TPU v7x, 32 devices: a whole 2x2x4 slice. The times are simulated.
32 devices in a mesh: dp: 8 (over z, y), expert: 4 (over x, core).
Axes of the slice: x: 2, y: 2, z: 4, core: 2. Of those that a mesh axis runs over, the one named last changes fastest.
Arguments:
- hidden_in: float32 [4, 2560, 1536], P('expert', 'dp'), may hold values from -6 to 6
- gain_attn: float32 [1536], replicated, may hold values from 0.5 to 1.5
- w_query: bfloat16 [1536, 1536], replicated, may hold values from -0.15625 to 0.15625
- w_key: bfloat16 [1536, 512], replicated, may hold values from -0.15625 to 0.15625
- w_value: bfloat16 [1536, 512], replicated, may hold values from -0.15625 to 0.15625
- w_output: bfloat16 [1536, 1536], replicated, may hold values from -1.25 to 1.25
- gain_mlp: float32 [1536], replicated, may hold values from 0.5 to 1.5
- w_router: bfloat16 [1536, 40], replicated, may hold values from -0.078125 to 0.078125
- w_gate: bfloat16 [40, 1536, 512], P('expert'), may hold values from -0.15625 to 0.15625
- w_up: bfloat16 [40, 1536, 512], P('expert'), may hold values from -0.15625 to 0.15625
- w_down: bfloat16 [40, 512, 1536], P('expert'), may hold values from -1 to 1
- expert_ids: int32 [4, 2560, 8], P('expert', 'dp'), may hold values from 0 to 39, all different within a row
- slot_order: int32 [4, 8, 2560], P('expert', 'dp'), may hold values from 0 to 2559, each once within a row
- grad_out: float32 [4, 2560, 1536], P('expert', 'dp'), may hold values from -6 to 6
Outputs:
- hidden_out: float32 [4, 2560, 1536], P('expert', 'dp')
- grad_in: float32 [4, 2560, 1536], P('expert', 'dp')
- grad_gain_attn: float32 [1536], P(('dp', 'expert'))
- grad_query: float32 [1536, 1536], P(('dp', 'expert'))
- grad_key: float32 [1536, 512], P(('dp', 'expert'))
- grad_value: float32 [1536, 512], P(('dp', 'expert'))
- grad_output: float32 [1536, 1536], P(('dp', 'expert'))
- grad_gain_mlp: float32 [1536], P(('dp', 'expert'))
- grad_router: float32 [1536, 40], P(('dp', 'expert'))
- grad_gate: float32 [40, 1536, 512], P('expert', 'dp')
- grad_up: float32 [40, 1536, 512], P('expert', 'dp')
- grad_down: float32 [40, 512, 1536], P('expert', 'dp')
Inputs may be any that keep to these rules, and one draw needn't show every extreme that they name: `expert_ids`: each token names 8 different experts. `slot_order`: for every sequence and block, the 2560 ranks of the block's pairs are each of 0 to 2559 once.
All inputs are finite; a program needn't handle non-finite values.
Results may differ from a plain program's by a relative error of at most 0.019.
Values may be sent and summed in bfloat16 or wider, within the bound.
A program may use at most 320 MiB of HBM per device.

v0:
```python
import math

import jax
import jax.numpy as jnp
from jax import lax
from jax.sharding import PartitionSpec as P

HEADS = 24
KV_HEADS = 8
HEAD_DIM = 64


EPS = 1e-05
MASKED = -1e30


def rotary_tables(positions):
    half = HEAD_DIM // 2
    frequency = jnp.exp(-math.log(10000.0) * jnp.arange(half, dtype=jnp.float32) * 2.0 / HEAD_DIM)
    angles = positions.astype(jnp.float32)[:, None] * frequency[None, :]
    return (jnp.cos(angles)[:, None, :], jnp.sin(angles)[:, None, :])


def rotate(values, cosine, sine):
    half = values.shape[-1] // 2
    first = values[..., :half]
    second = values[..., half:]
    return jnp.concatenate(
        [first * cosine - second * sine, second * cosine + first * sine], axis=-1
    )


def rotate_back(values, cosine, sine):
    half = values.shape[-1] // 2
    first = values[..., :half]
    second = values[..., half:]
    return jnp.concatenate(
        [first * cosine + second * sine, second * cosine - first * sine], axis=-1
    )


def assign_slots(row_chosen, row_ranks, all_experts, capacity):
    pairs = row_chosen.shape[0]
    by_rank = jnp.zeros((pairs,), jnp.int32).at[row_ranks].set(jnp.arange(pairs, dtype=jnp.int32))
    ordered = row_chosen[by_rank]
    table = (ordered[:, None] == jnp.arange(all_experts, dtype=jnp.int32)[None, :]).astype(
        jnp.int32
    )
    before = jnp.sum(table * (jnp.cumsum(table, axis=0) - 1), axis=1)
    slot = before[row_ranks]
    target = jnp.where(slot < capacity, row_chosen * capacity + slot, all_experts * capacity)
    owner = (
        jnp.full((all_experts * capacity,), pairs, jnp.int32)
        .at[target]
        .set(jnp.arange(pairs, dtype=jnp.int32), mode="drop")
    )
    return (target, owner)


def body(
    hidden_in,
    gain_attn,
    w_query,
    w_key,
    w_value,
    w_output,
    gain_mlp,
    w_router,
    w_gate,
    w_up,
    w_down,
    expert_ids,
    slot_order,
    grad_out,
):
    inputs = hidden_in[0]
    cotangent = grad_out[0]
    chosen = expert_ids[0]
    tokens, width = inputs.shape
    top = chosen.shape[1]
    local_experts = w_gate.shape[0]
    peers = lax.axis_size("expert")
    all_experts = local_experts * peers
    pairs = tokens * top
    capacity = pairs // all_experts
    shards = lax.axis_size("dp")
    index = lax.axis_index("dp")
    length = shards * tokens
    block = math.gcd(length, 512)
    groups = HEADS // KV_HEADS
    scale = HEAD_DIM ** (-0.5)
    query_pos = index * tokens + jnp.arange(tokens, dtype=jnp.int32)
    cosine, sine = rotary_tables(query_pos)
    count = ((index + 1) * tokens + block - 1) // block
    inv_one = lax.rsqrt(jnp.mean(inputs * inputs, axis=-1, keepdims=True) + EPS)
    normed = (inputs * inv_one * gain_attn).astype(jnp.bfloat16)
    query_pre = jnp.dot(normed, w_query, preferred_element_type=jnp.float32).reshape(
        tokens, HEADS, HEAD_DIM
    )
    queries = rotate(query_pre, cosine, sine).astype(jnp.bfloat16)
    key_pre = jnp.dot(normed, w_key, preferred_element_type=jnp.float32).reshape(
        tokens, KV_HEADS, HEAD_DIM
    )
    keys_low = rotate(key_pre, cosine, sine).astype(jnp.bfloat16)
    values_low = (
        jnp.dot(normed, w_value, preferred_element_type=jnp.float32)
        .astype(jnp.bfloat16)
        .reshape(tokens, KV_HEADS, HEAD_DIM)
    )
    keys_all, values_all = (
        lax.all_gather(keys_low, "dp", axis=0, tiled=True),
        lax.all_gather(values_low, "dp", axis=0, tiled=True),
    )
    query_groups = queries.reshape(tokens, KV_HEADS, groups, HEAD_DIM)

    def block_scores(key_block, start):
        raw = (
            jnp.einsum(
                "qkgd,skd->kgqs", query_groups, key_block, preferred_element_type=jnp.float32
            )
            * scale
        )
        key_pos = start + jnp.arange(block, dtype=jnp.int32)
        allowed = key_pos[None, :] <= query_pos[:, None]
        return jnp.where(allowed, raw, MASKED)

    def stats_step(step, carry):
        running, total = carry
        scores = block_scores(
            lax.dynamic_slice_in_dim(keys_all, step * block, block, 0), step * block
        )
        newest = jnp.maximum(running, jnp.max(scores, axis=-1))
        total = total * jnp.exp(running - newest) + jnp.sum(
            jnp.exp(scores - newest[..., None]), axis=-1
        )
        return (newest, total)

    stat_init = (
        jnp.full((KV_HEADS, groups, tokens), MASKED, jnp.float32),
        jnp.zeros((KV_HEADS, groups, tokens), jnp.float32),
    )
    running, total = lax.fori_loop(0, count, stats_step, stat_init)
    log_total = running + jnp.log(total)

    def output_step(step, accum):
        start = step * block
        scores = block_scores(lax.dynamic_slice_in_dim(keys_all, start, block, 0), start)
        probs = jnp.exp(scores - log_total[..., None]).astype(jnp.bfloat16)
        value_block = lax.dynamic_slice_in_dim(values_all, start, block, 0)
        return accum + jnp.einsum(
            "kgqs,skd->qkgd", probs, value_block, preferred_element_type=jnp.float32
        )

    attended_groups = lax.fori_loop(
        0, count, output_step, jnp.zeros((tokens, KV_HEADS, groups, HEAD_DIM), jnp.float32)
    )
    attended = attended_groups.reshape(tokens, HEADS * HEAD_DIM)
    attended_low = attended.astype(jnp.bfloat16)
    branch = jnp.dot(attended_low, w_output, preferred_element_type=jnp.float32)
    middle = inputs + branch
    inv_two = lax.rsqrt(jnp.mean(middle * middle, axis=-1, keepdims=True) + EPS)
    normed_two = (middle * inv_two * gain_mlp).astype(jnp.bfloat16)
    logits = jnp.dot(normed_two, w_router, preferred_element_type=jnp.float32)
    onehot = (chosen[:, :, None] == jnp.arange(all_experts, dtype=jnp.int32)[None, None, :]).astype(
        jnp.float32
    )
    picked = jnp.sum(onehot * logits[:, None, :], axis=-1)
    gates = jax.nn.softmax(picked, axis=-1)
    target, owner = assign_slots(chosen.reshape(pairs), slot_order[0, 0], all_experts, capacity)
    valid = owner < pairs
    source = jnp.minimum(owner, pairs - 1)
    rows_send = jnp.where(valid[:, None], normed_two[source // top], 0).reshape(
        peers, local_experts, capacity, width
    )
    received = lax.all_to_all(rows_send, "expert", split_axis=0, concat_axis=0, tiled=True)
    gate_pre = jnp.einsum("necd,edf->necf", received, w_gate, preferred_element_type=jnp.float32)
    up_pre = jnp.einsum("necd,edf->necf", received, w_up, preferred_element_type=jnp.float32)
    hidden = (jax.nn.silu(gate_pre) * up_pre).astype(jnp.bfloat16)
    result = jnp.einsum(
        "necf,efd->necd", hidden, w_down, preferred_element_type=jnp.float32
    ).astype(jnp.bfloat16)
    returned = lax.all_to_all(result, "expert", split_axis=0, concat_axis=0, tiled=True)
    returned, received, gate_pre, up_pre = (returned, received, gate_pre, up_pre)
    zero_row = jnp.zeros((1, width), jnp.bfloat16)
    pair_out = jnp.concatenate([returned.reshape(all_experts * capacity, width), zero_row], axis=0)[
        target
    ].reshape(tokens, top, width)
    mixed = jnp.einsum("tk,tkd->td", gates, pair_out, preferred_element_type=jnp.float32)
    hidden_out = middle + mixed
    dy_pairs = (
        (gates[:, :, None] * cotangent[:, None, :]).astype(jnp.bfloat16).reshape(pairs, width)
    )
    dy_send = jnp.where(valid[:, None], dy_pairs[source], 0).reshape(
        peers, local_experts, capacity, width
    )
    dy_received = lax.all_to_all(dy_send, "expert", split_axis=0, concat_axis=0, tiled=True)
    sigmoid_gate = jax.nn.sigmoid(gate_pre)
    silu_gate = gate_pre * sigmoid_gate
    hidden = (silu_gate * up_pre).astype(jnp.bfloat16)
    grad_down_part = jnp.einsum(
        "necf,necd->efd", hidden, dy_received, preferred_element_type=jnp.float32
    )
    d_hidden = jnp.einsum("necd,efd->necf", dy_received, w_down, preferred_element_type=jnp.float32)
    d_gate = (d_hidden * up_pre * sigmoid_gate * (1.0 + gate_pre * (1.0 - sigmoid_gate))).astype(
        jnp.bfloat16
    )
    d_up = (d_hidden * silu_gate).astype(jnp.bfloat16)
    grad_gate_part = jnp.einsum(
        "necd,necf->edf", received, d_gate, preferred_element_type=jnp.float32
    )
    grad_up_part = jnp.einsum("necd,necf->edf", received, d_up, preferred_element_type=jnp.float32)
    gate_total, up_total, down_total = (
        lax.psum_scatter(
            grad_gate_part.astype(jnp.bfloat16), "dp", scatter_dimension=1, tiled=True
        ).astype(jnp.float32),
        lax.psum_scatter(
            grad_up_part.astype(jnp.bfloat16), "dp", scatter_dimension=1, tiled=True
        ).astype(jnp.float32),
        lax.psum_scatter(
            grad_down_part.astype(jnp.bfloat16), "dp", scatter_dimension=1, tiled=True
        ).astype(jnp.float32),
    )
    d_rows = jnp.einsum("necf,edf->necd", d_gate, w_gate, preferred_element_type=jnp.float32)
    d_rows = (
        d_rows + jnp.einsum("necf,edf->necd", d_up, w_up, preferred_element_type=jnp.float32)
    ).astype(jnp.bfloat16)
    d_back = lax.all_to_all(d_rows, "expert", split_axis=0, concat_axis=0, tiled=True)
    d_pairs = jnp.concatenate([d_back.reshape(all_experts * capacity, width), zero_row], axis=0)[
        target
    ].reshape(tokens, top, width)
    d_normed_two = jnp.sum(d_pairs, axis=1, dtype=jnp.float32)
    d_gates = jnp.einsum("td,tkd->tk", cotangent, pair_out, preferred_element_type=jnp.float32)
    d_picked = gates * (d_gates - jnp.sum(gates * d_gates, axis=-1, keepdims=True))
    d_logits = jnp.sum(onehot * d_picked[:, :, None], axis=1).astype(jnp.bfloat16)
    grad_router_part = jnp.einsum(
        "td,te->de", normed_two, d_logits, preferred_element_type=jnp.float32
    )
    d_normed_two = d_normed_two + jnp.einsum(
        "te,de->td", d_logits, w_router, preferred_element_type=jnp.float32
    )
    scaled_two = d_normed_two * gain_mlp
    grad_gain_mlp_part = jnp.sum(d_normed_two * middle * inv_two, axis=0)
    d_middle = (
        cotangent
        + inv_two * scaled_two
        - middle * inv_two**3 * jnp.mean(middle * scaled_two, axis=-1, keepdims=True)
    )
    d_branch = d_middle.astype(jnp.bfloat16)
    grad_output_part = jnp.einsum(
        "tf,td->fd", attended_low, d_branch, preferred_element_type=jnp.float32
    )
    d_attended = jnp.einsum(
        "td,fd->tf", d_branch, w_output, preferred_element_type=jnp.float32
    ).astype(jnp.bfloat16)
    d_groups = d_attended.reshape(tokens, KV_HEADS, groups, HEAD_DIM)
    delta = jnp.einsum(
        "qkgd,qkgd->kgq", d_groups, attended_groups, preferred_element_type=jnp.float32
    )
    keys_back, values_back = (
        lax.all_gather(keys_low, "dp", axis=0, tiled=True),
        lax.all_gather(values_low, "dp", axis=0, tiled=True),
    )

    def grad_step(step, carry):
        d_query, d_keys, d_values = carry
        start = step * block
        key_block = lax.dynamic_slice_in_dim(keys_back, start, block, 0)
        value_block = lax.dynamic_slice_in_dim(values_back, start, block, 0)
        scores = block_scores(key_block, start)
        probs = jnp.exp(scores - log_total[..., None])
        probs_low = probs.astype(jnp.bfloat16)
        d_probs = jnp.einsum(
            "qkgd,skd->kgqs", d_groups, value_block, preferred_element_type=jnp.float32
        )
        d_scores = (probs * (d_probs - delta[..., None])).astype(jnp.bfloat16)
        d_query = d_query + jnp.einsum(
            "kgqs,skd->qkgd", d_scores, key_block, preferred_element_type=jnp.float32
        )
        key_part = jnp.einsum(
            "kgqs,qkgd->skd", d_scores, query_groups, preferred_element_type=jnp.float32
        )
        value_part = jnp.einsum(
            "kgqs,qkgd->skd", probs_low, d_groups, preferred_element_type=jnp.float32
        )
        d_keys = lax.dynamic_update_slice_in_dim(
            d_keys, lax.dynamic_slice_in_dim(d_keys, start, block, 0) + key_part, start, 0
        )
        d_values = lax.dynamic_update_slice_in_dim(
            d_values, lax.dynamic_slice_in_dim(d_values, start, block, 0) + value_part, start, 0
        )
        return (d_query, d_keys, d_values)

    grad_init = (
        jnp.zeros((tokens, KV_HEADS, groups, HEAD_DIM), jnp.float32),
        jnp.zeros((length, KV_HEADS, HEAD_DIM), jnp.float32),
        jnp.zeros((length, KV_HEADS, HEAD_DIM), jnp.float32),
    )
    d_query, d_keys, d_values = lax.fori_loop(0, count, grad_step, grad_init)
    key_sum, value_sum = (
        lax.psum_scatter(
            (d_keys * scale).reshape(length, KV_HEADS * HEAD_DIM).astype(jnp.bfloat16),
            "dp",
            scatter_dimension=0,
            tiled=True,
        ).astype(jnp.float32),
        lax.psum_scatter(
            d_values.reshape(length, KV_HEADS * HEAD_DIM).astype(jnp.bfloat16),
            "dp",
            scatter_dimension=0,
            tiled=True,
        ).astype(jnp.float32),
    )
    d_query_low = (
        rotate_back((d_query * scale).reshape(tokens, HEADS, HEAD_DIM), cosine, sine)
        .astype(jnp.bfloat16)
        .reshape(tokens, HEADS * HEAD_DIM)
    )
    d_key_low = (
        rotate_back(key_sum.reshape(tokens, KV_HEADS, HEAD_DIM), cosine, sine)
        .astype(jnp.bfloat16)
        .reshape(tokens, KV_HEADS * HEAD_DIM)
    )
    d_value_low = value_sum.astype(jnp.bfloat16)
    grad_query_part = jnp.einsum(
        "td,tf->df", normed, d_query_low, preferred_element_type=jnp.float32
    )
    grad_key_part = jnp.einsum("td,tf->df", normed, d_key_low, preferred_element_type=jnp.float32)
    grad_value_part = jnp.einsum(
        "td,tf->df", normed, d_value_low, preferred_element_type=jnp.float32
    )
    d_normed = jnp.einsum("tf,df->td", d_query_low, w_query, preferred_element_type=jnp.float32)
    d_normed = d_normed + jnp.einsum(
        "tf,df->td", d_key_low, w_key, preferred_element_type=jnp.float32
    )
    d_normed = d_normed + jnp.einsum(
        "tf,df->td", d_value_low, w_value, preferred_element_type=jnp.float32
    )
    scaled_one = d_normed * gain_attn
    grad_gain_attn_part = jnp.sum(d_normed * inputs * inv_one, axis=0)
    grad_in = (
        d_middle
        + inv_one * scaled_one
        - inputs * inv_one**3 * jnp.mean(inputs * scaled_one, axis=-1, keepdims=True)
    )
    dense = (
        lax.psum_scatter(grad_gain_attn_part, ("dp", "expert"), scatter_dimension=0, tiled=True),
        lax.psum_scatter(grad_query_part, ("dp", "expert"), scatter_dimension=0, tiled=True),
        lax.psum_scatter(grad_key_part, ("dp", "expert"), scatter_dimension=0, tiled=True),
        lax.psum_scatter(grad_value_part, ("dp", "expert"), scatter_dimension=0, tiled=True),
        lax.psum_scatter(grad_output_part, ("dp", "expert"), scatter_dimension=0, tiled=True),
        lax.psum_scatter(grad_gain_mlp_part, ("dp", "expert"), scatter_dimension=0, tiled=True),
        lax.psum_scatter(grad_router_part, ("dp", "expert"), scatter_dimension=0, tiled=True),
    )
    return (
        hidden_out[None],
        grad_in[None],
        dense[0],
        dense[1],
        dense[2],
        dense[3],
        dense[4],
        dense[5],
        dense[6],
        gate_total,
        up_total,
        down_total,
    )


def solution(mesh):
    in_specs = (
        P("expert", "dp", None),
        P(),
        P(),
        P(),
        P(),
        P(),
        P(),
        P(),
        P("expert", None, None),
        P("expert", None, None),
        P("expert", None, None),
        P("expert", "dp", None),
        P("expert", "dp", None),
        P("expert", "dp", None),
    )
    out_specs = (
        P("expert", "dp", None),
        P("expert", "dp", None),
        P(("dp", "expert")),
        P(("dp", "expert"), None),
        P(("dp", "expert"), None),
        P(("dp", "expert"), None),
        P(("dp", "expert"), None),
        P(("dp", "expert")),
        P(("dp", "expert"), None),
        P("expert", "dp", None),
        P("expert", "dp", None),
        P("expert", "dp", None),
    )
    return jax.shard_map(body, mesh=mesh, in_specs=in_specs, out_specs=out_specs, check_vma=False)
```

profile of v0, /device:TPU:0, one launch (start us, length us, event | category | flops | bytes accessed | tf_op | source)
XLA Modules:
  0.0 2534.0 jit_solution(5355342469741384523)
XLA Ops:
  124.9 70.6 %all-gather.3.cloned.1.call-done = bf16[2560,8,64]{2,1,0:T(8,128)(2,1)} async-done(((bf16[320,8,64]{2,1,0:T(8,128)(2,1)}), bf16[2560,8,64]{2,1,0:T(8,128)(2,1)}) %all-gather.3.cloned.1.call-update) | async-done | bytes 2621456 | tf_op jit(solution)/shard_map/all_gather | solution.py:112
  238.5 95.0 %all_to_all.20 = bf16[4,10,64,1536]{3,2,1,0:T(8,128)(2,1)} all-to-all(bf16[4,10,64,1536]{3,2,1,0:T(8,128)(2,1)} %broadcast_select_fusion.1), channel_id=1, replica_groups=mesh['dp'=8,'expert'=4] {'expert'}, dimensions={0} | all-to-all | bytes 15728640 | tf_op jit(solution)/shard_map/all_to_all | solution.py:175
  333.6 14.2 fusion.62
  347.8 16.7 fusion.86
  393.1 85.8 %all-to-all-done.1 = bf16[4,10,64,1536]{3,2,1,0:T(8,128)(2,1)} async-done(((bf16[4,10,64,1536]{3,2,1,0:T(8,128)(2,1)}), bf16[4,10,64,1536]{3,2,1,0:T(8,128)(2,1)}, u32[]{:S(2)}, u32[]{:S(2)}) %all-to-all-start.1) | async-done | bytes 7864352 | tf_op jit(solution)/shard_map/all_to_all | solution.py:182
  485.7 20.9 gather_fusion.3
  526.1 20.6 gather_fusion.4
  553.7 95.3 %all_to_all.21 = bf16[4,10,64,1536]{3,2,1,0:T(8,128)(2,1)} all-to-all(bf16[4,10,64,1536]{3,2,1,0:T(8,128)(2,1)} %broadcast_select_fusion), channel_id=1, replica_groups=mesh['dp'=8,'expert'=4] {'expert'}, dimensions={0} | all-to-all | bytes 15728640 | tf_op jit(solution)/shard_map/all_to_all | solution.py:196
  649.0 15.8 fusion.84
  676.7 15.9 fusion.69
  712.7 80.4 %all-to-all-done.3 = bf16[4,10,64,1536]{3,2,1,0:T(8,128)(2,1)} async-done(((bf16[4,10,64,1536]{3,2,1,0:T(8,128)(2,1)}), bf16[4,10,64,1536]{3,2,1,0:T(8,128)(2,1)}, u32[]{:S(2)}, u32[]{:S(2)}) %all-to-all-start.3) | async-done | bytes 7864352 | tf_op jit(solution)/shard_map/all_to_all | solution.py:227
  800.0 20.8 gather_fusion.5
  850.3 26.7 %while.41 = (s32[]{:T(128)}, f32[320,8,3,64]{0,3,2,1:T(8,128)}, f32[2560,8,64]{0,2,1:T(8,128)}, f32[2560,8,64]{0,2,1:T(8,128)}, s32[]{:T(128)}, /*index=5*/bf16[...) while((s32[]{:T(128)}, f32[320,8,3,64]{0,3,2,1:T(8,128)}, ...), condition=%wide.region_21.22_spmd.clone, body=%wide.region_20.21_spmd.clone.sunk | while | flops 2557084416 | bytes 89326328 | solution.py:298
  929.8 166.8 %reduce-scatter.31.cloned.1.call-done = bf16[320,512]{1,0:T(8,128)(2,1)} async-done(((bf16[2560,512]{1,0:T(8,128)(2,1)}), bf16[320,512]{1,0:T(8,128)(2,1)}) %reduce-scatter.31.cloned.1.call-update) | async-done | bytes 327696
  1101.6 67.8 %reduce-scatter.33.cloned.1.call-done = bf16[320,512]{1,0:T(8,128)(2,1)} async-done(((bf16[2560,512]{1,0:T(8,128)(2,1)}), bf16[320,512]{1,0:T(8,128)(2,1)}) %reduce-scatter.33.cloned.1.call-update) | async-done | bytes 327696
  1190.3 78.3 %reduce-scatter.35.cloned.1.call-done = f32[48,40]{1,0:T(8,128)} async-done(((f32[1536,40]{1,0:T(8,128)}), f32[48,40]{1,0:T(8,128)}) %reduce-scatter.35.cloned.1.call-update) | async-done | bytes 7696
  1278.8 46.2 %all-reduce.4 = (f32[1536]{0:T(1024)}, f32[1536]{0:T(1024)}) all-reduce(f32[1536]{0:T(1024)} %get-tuple-element.315, f32[1536]{0:T(1024)} %get-tuple-element.313), channel_id=4, replica_groups=mesh['dp'=8,'expert'=4] {'dp','expert'}, use_global_device_ids=true, to_apply=%region_26.27.clone | all-reduce | flops 3072 | bytes 24576
  1332.2 191.2 %reduce-scatter.29.cloned.1.call-done = bf16[10,64,1536]{2,1,0:T(8,128)(2,1)} async-done(((bf16[10,512,1536]{2,1,0:T(8,128)(2,1)}), bf16[10,64,1536]{2,1,0:T(8,128)(2,1)}) %reduce-scatter.29.cloned.1.call-update) | async-done | bytes 1966096 | tf_op jit(solution)/shard_map/reduce_scatter | solution.py:219
  1527.4 249.9 %reduce-scatter.25.cloned.1.call-done = bf16[10,192,512]{2,1,0:T(8,128)(2,1)} async-done(((bf16[10,1536,512]{2,1,0:T(8,128)(2,1)}), bf16[10,192,512]{2,1,0:T(8,128)(2,1)}) %reduce-scatter.25.cloned.1.call-update) | async-done | bytes 1966096 | tf_op jit(solution)/shard_map/reduce_scatter | solution.py:213
  1781.2 249.8 %reduce-scatter.27.cloned.1.call-done = bf16[10,192,512]{2,1,0:T(8,128)(2,1)} async-done(((bf16[10,1536,512]{2,1,0:T(8,128)(2,1)}), bf16[10,192,512]{2,1,0:T(8,128)(2,1)}) %reduce-scatter.27.cloned.1.call-update) | async-done | bytes 1966096 | tf_op jit(solution)/shard_map/reduce_scatter | solution.py:216
  2035.0 102.7 %reduce-scatter.19.cloned.1.call-done = f32[48,512]{1,0:T(8,128)} async-done(((f32[1536,512]{1,0:T(8,128)}), f32[48,512]{1,0:T(8,128)}) %reduce-scatter.19.cloned.1.call-update) | async-done | bytes 98320 | tf_op jit(solution)/shard_map/reduce_scatter | solution.py:348
  2137.7 106.4 %reduce-scatter.21.cloned.1.call-done = f32[48,512]{1,0:T(8,128)} async-done(((f32[1536,512]{1,0:T(8,128)}), f32[48,512]{1,0:T(8,128)}) %reduce-scatter.21.cloned.1.call-update) | async-done | bytes 98320 | tf_op jit(solution)/shard_map/reduce_scatter | solution.py:349
  2244.0 141.0 %reduce-scatter.23.cloned.1.call-done = f32[48,1536]{1,0:T(8,128)} async-done(((f32[1536,1536]{1,0:T(8,128)}), f32[48,1536]{1,0:T(8,128)}) %reduce-scatter.23.cloned.1.call-update) | async-done | bytes 294928 | tf_op jit(solution)/shard_map/reduce_scatter | solution.py:350
  2385.0 142.0 %reduce-scatter.17.cloned.1.call-done = f32[48,1536]{1,0:T(8,128)} async-done(((f32[1536,1536]{1,0:T(8,128)}), f32[48,1536]{1,0:T(8,128)}) %reduce-scatter.17.cloned.1.call-update) | async-done | bytes 294928 | tf_op jit(solution)/shard_map/reduce_scatter | solution.py:347
  (297 shorter events, 443.0 us)
Async XLA Ops:
  7.2 101.0 %all-gather.5.cloned.1.call-start = ((), (), s32[]{:S(2)}) async-start(), calls=%async_computation.15 | async-start | bytes 5898240 | tf_op jit(solution)/shard_map/all_gather | solution.py:111
  19.1 176.5 %all-gather.3.cloned.1.call-start = ((), (), s32[]{:S(2)}) async-start(), calls=%async_computation.14 | async-start | bytes 5898240 | tf_op jit(solution)/shard_map/all_gather | solution.py:112
  84.8 146.8 %copy-start.45 = (pred[4,10,64]{2,1,0:T(8,128)(4,1)}, pred[4,10,64]{2,1,0:T(8,128)(4,1)S(1)}, u32[]{:S(2)}) copy-start(pred[4,10,64]{2,1,0:T(8,128)(4,1)S(1)} %broadcast_in_dim.67) | copy-start | bytes 7684
  222.0 170.0 %copy-start.1 = (bf16[320,1536]{1,0:T(8,128)(2,1)}, bf16[320,1536]{1,0:T(8,128)(2,1)S(1)}, u32[]{:S(2)}) copy-start(bf16[320,1536]{1,0:T(8,128)(2,1)S(1)} %multiply_convert_fusion.1) | copy-start | bytes 2949124
  385.4 93.5 %all-to-all-start.1 = ((bf16[4,10,64,1536]{3,2,1,0:T(8,128)(2,1)}), bf16[4,10,64,1536]{3,2,1,0:T(8,128)(2,1)}, u32[]{:S(2)}, u32[]{:S(2)}) async-start(bf16[4,10,64,1536]{3,2,1,0:T(8,128)(2,1)} %copy.90), calls=%async_computation.1 | async-start | bytes 15728640 | tf_op jit(solution)/shard_map/all_to_all | solution.py:182
  485.7 20.9 copy-start.16
  699.9 93.2 %all-to-all-start.3 = ((bf16[4,10,64,1536]{3,2,1,0:T(8,128)(2,1)}), bf16[4,10,64,1536]{3,2,1,0:T(8,128)(2,1)}, u32[]{:S(2)}, u32[]{:S(2)}) async-start(bf16[4,10,64,1536]{3,2,1,0:T(8,128)(2,1)} %copy.93), calls=%async_computation.3 | async-start | bytes 15728640 | tf_op jit(solution)/shard_map/all_to_all | solution.py:227
  705.6 391.0 %reduce-scatter.31.cloned.1.call-start = ((), (), s32[]{:S(2)}) async-start(), calls=%async_computation.23 | async-start | bytes 2949120
  885.9 283.4 %reduce-scatter.33.cloned.1.call-start = ((), (), s32[]{:S(2)}) async-start(), calls=%async_computation.24 | async-start | bytes 2949120
  894.7 374.0 %reduce-scatter.35.cloned.1.call-start = ((), (), s32[]{:S(2)}) async-start(), calls=%async_computation.25 | async-start | bytes 811008
  897.3 626.1 %reduce-scatter.29.cloned.1.call-start = ((), (), s32[]{:S(2)}) async-start(), calls=%async_computation.22 | async-start | bytes 17694720 | tf_op jit(solution)/shard_map/reduce_scatter | solution.py:219
  908.2 869.0 %reduce-scatter.25.cloned.1.call-start = ((), (), s32[]{:S(2)}) async-start(), calls=%async_computation.20 | async-start | bytes 17694720 | tf_op jit(solution)/shard_map/reduce_scatter | solution.py:213
  918.9 1112.1 %reduce-scatter.27.cloned.1.call-start = ((), (), s32[]{:S(2)}) async-start(), calls=%async_computation.21 | async-start | bytes 17694720 | tf_op jit(solution)/shard_map/reduce_scatter | solution.py:216
  929.7 168.2 %copy-start.27 = (f32[320,32]{0,1:T(8,128)S(1)}, f32[320,32]{0,1:T(8,128)}, u32[]{:S(2)}) copy-start(f32[320,32]{0,1:T(8,128)} %copy-done.25) | copy-start | bytes 122884
  929.7 168.2 %copy-start.31 = (f32[320,32]{0,1:T(8,128)S(1)}, f32[320,32]{0,1:T(8,128)}, u32[]{:S(2)}) copy-start(f32[320,32]{0,1:T(8,128)} %copy-done.29) | copy-start | bytes 122884
  929.7 169.1 %copy-start.14 = (bf16[1,320,1536]{2,1,0:T(8,128)(2,1)S(1)}, bf16[1,320,1536]{2,1,0:T(8,128)(2,1)}, u32[]{:S(2)}) copy-start(bf16[1,320,1536]{2,1,0:T(8,128)(2,1)} %copy-done.12) | copy-start | bytes 2949124
  929.7 1208.0 %reduce-scatter.19.cloned.1.call-start = ((), (), s32[]{:S(2)}) async-start(), calls=%async_computation.17 | async-start | bytes 3244032 | tf_op jit(solution)/shard_map/reduce_scatter | solution.py:348
  1101.5 67.9 %copy-start.7 = (f32[1,320,1536]{2,1,0:T(8,128)S(1)}, f32[1,320,1536]{2,1,0:T(8,128)}, u32[]{:S(2)}) copy-start(f32[1,320,1536]{2,1,0:T(8,128)} %param.20) | copy-start | bytes 5898244
  1101.5 67.9 %copy-start.42 = (f32[1536]{0:T(1024)S(1)}, f32[1536]{0:T(1024)}, u32[]{:S(2)}) copy-start(f32[1536]{0:T(1024)} %param.21) | copy-start | bytes 18436
  1101.5 67.9 %copy-start.50 = (f32[320]{0:T(512)S(1)}, f32[320]{0:T(512)}, u32[]{:S(2)}) copy-start(f32[320]{0:T(512)} %copy-done.49) | copy-start | bytes 3844
  1101.5 1142.5 %reduce-scatter.21.cloned.1.call-start = ((), (), s32[]{:S(2)}) async-start(), calls=%async_computation.18 | async-start | bytes 3244032 | tf_op jit(solution)/shard_map/reduce_scatter | solution.py:349
  1173.2 1211.8 %reduce-scatter.23.cloned.1.call-start = ((), (), s32[]{:S(2)}) async-start(), calls=%async_computation.19 | async-start | bytes 9732096 | tf_op jit(solution)/shard_map/reduce_scatter | solution.py:350
  1181.5 1345.5 %reduce-scatter.17.cloned.1.call-start = ((), (), s32[]{:S(2)}) async-start(), calls=%async_computation.16 | async-start | bytes 9732096 | tf_op jit(solution)/shard_map/reduce_scatter | solution.py:347
  1276.1 52.2 %copy-start.58 = (f32[320]{0:T(512)S(1)}, f32[320]{0:T(512)}, u32[]{:S(2)}) copy-start(f32[320]{0:T(512)} %get-tuple-element.395) | copy-start | bytes 3844
  (54 other events, 273.1 us)
Sparse Core Ops, SparseCore 0:
  19.2 88.9 all-gather.4
  110.9 84.5 all-gather.2
  886.1 210.4 reduce-scatter.30
  1100.0 69.3 reduce-scatter.32
  1174.3 94.2 reduce-scatter.34
  1272.1 251.2 reduce-scatter.28
  1526.9 250.2 reduce-scatter.24
  1780.8 250.1 reduce-scatter.26
  2037.0 100.6 reduce-scatter.18
  2143.5 100.4 reduce-scatter.20
  2250.5 134.4 reduce-scatter.22
  2392.4 134.5 reduce-scatter.16
where the time goes:
time: 2540 us; the launch traced here: 2530 us
  waiting for transfers between devices  1740 us (69%)
  blocking collectives  237 us (9%)
  matrix products  220 us (9%)
  local copies, waits for them, and re-layouts  212 us (8%)
  other arithmetic  95.4 us (4%)
    unnamed x15, waiting for transfers between devices  313 us
    reduce_scatter x1, waiting for transfers between devices, body(): lax.psum_scatter(grad_gate_part.astype(jnp.bfloat16), 'dp', scatter_dimen...  250 us
    reduce_scatter x1, waiting for transfers between devices, body(): lax.psum_scatter(grad_up_part.astype(jnp.bfloat16), 'dp', scatter_dimensi...  250 us
    reduce_scatter x1, waiting for transfers between devices, body(): lax.psum_scatter(grad_down_part.astype(jnp.bfloat16), 'dp', scatter_dimen...  191 us
    reduce_scatter x1, waiting for transfers between devices, body(): lax.psum_scatter(grad_query_part, ('dp', 'expert'), scatter_dimension=0,...  142 us
    reduce_scatter x1, waiting for transfers between devices, body(): lax.psum_scatter(grad_output_part, ('dp', 'expert'), scatter_dimension=0,...  141 us
    reduce_scatter x1, waiting for transfers between devices, body(): lax.psum_scatter(grad_value_part, ('dp', 'expert'), scatter_dimension=0,...  106 us
    reduce_scatter x1, waiting for transfers between devices, body(): lax.psum_scatter(grad_key_part, ('dp', 'expert'), scatter_dimension=0, ti...  103 us
  transfers between devices with their start and end apart: 14, of which 14 were waited for; matrix products, arithmetic and copies ran while one was open for 8% of the time, Pallas kernels for 0%

commit v1 on v0

--- a/solution.py
+++ b/solution.py
@@ -3,6 +3,8 @@
 import jax
 import jax.numpy as jnp
 from jax import lax
+from jax.experimental import pallas as pl
+from jax.experimental.pallas import tpu as pltpu
 from jax.sharding import PartitionSpec as P
 
 HEADS = 24
@@ -366,6 +368,941 @@
         down_total,
     )
 
+BF = jnp.bfloat16
+F32 = jnp.float32
+WIDTH = 1536
+LANES = 128
+PER_KV = HEADS // KV_HEADS
+ROWS_Q = PER_KV * HEAD_DIM
+PACK = ROWS_Q + 2 * HEAD_DIM
+BIT_Y, BIT_ZL, BIT_ZH = 1, 2, 4
+BIT_C, BIT_X = 1, 2
+BLOCK_Q = 256
+BLOCK_K = 512
+SLOTS = 64
+CHUNK = 512
+MIB = 1 << 20
+
+
+def dot_nn(a, b):
+    return lax.dot_general(a, b, (((1,), (0,)), ((), ())), preferred_element_type=F32)
+
+
+def dot_nt(a, b):
+    return lax.dot_general(a, b, (((1,), (1,)), ((), ())), preferred_element_type=F32)
+
+
+def dot_tn(a, b):
+    return lax.dot_general(a, b, (((0,), (0,)), ((), ())), preferred_element_type=F32)
+
+
+def cost(flops, moved, transcendentals=0):
+    return pl.CostEstimate(
+        flops=int(flops), bytes_accessed=int(moved), transcendentals=int(transcendentals)
+    )
+
+
+def params(mib, dims=None):
+    return pltpu.CompilerParams(vmem_limit_bytes=mib * MIB, dimension_semantics=dims)
+
+
+def swap(values, axis, mask):
+    size = lax.axis_size(axis)
+    return lax.ppermute(values, axis, [(i, i ^ mask) for i in range(size)])
+
+
+def swap_bit(values, bit):
+    axis, mask = bit
+    return swap(values, axis, mask)
+
+
+C_BIT = ("expert", BIT_C)
+X_BIT = ("expert", BIT_X)
+Y_BIT = ("dp", BIT_Y)
+ZL_BIT = ("dp", BIT_ZL)
+ZH_BIT = ("dp", BIT_ZH)
+
+
+def pre_kernel(hid_ref, gain_ref, wq_ref, wk_ref, wv_ref, cos_ref, sin_ref, norm_ref, pack_ref):
+    tokens = hid_ref.shape[0]
+    inputs = hid_ref[...]
+    inv = lax.rsqrt(jnp.mean(inputs * inputs, axis=-1, keepdims=True) + EPS)
+    normed = (inputs * inv * gain_ref[...]).astype(BF)
+    norm_ref[...] = normed
+    low = (lax.broadcasted_iota(jnp.int32, (tokens, LANES), 1) % HEAD_DIM) < HEAD_DIM // 2
+    cosine, sine = cos_ref[...], sin_ref[...]
+
+    def turn(tile):
+        other = jnp.where(
+            low,
+            pltpu.roll(tile, LANES - HEAD_DIM // 2, 1),
+            pltpu.roll(tile, HEAD_DIM // 2, 1),
+        )
+        return (tile * cosine + other * sine).astype(BF)
+
+    def put_heads(tiles, width, start):
+        flat = jnp.concatenate(tiles, axis=1)
+        for g in range(KV_HEADS):
+            pack_ref[g, :, start : start + width] = flat[:, g * width : (g + 1) * width]
+
+    tiles = []
+    for n in range(wq_ref.shape[1] // CHUNK):
+        pre = dot_nn(normed, wq_ref[:, n * CHUNK : (n + 1) * CHUNK])
+        tiles += [turn(pre[:, m * LANES : (m + 1) * LANES]) for m in range(CHUNK // LANES)]
+    put_heads(tiles, ROWS_Q, 0)
+    pre = dot_nn(normed, wk_ref[...])
+    put_heads(
+        [turn(pre[:, m * LANES : (m + 1) * LANES]) for m in range(pre.shape[1] // LANES)],
+        HEAD_DIM,
+        ROWS_Q,
+    )
+    put_heads([dot_nn(normed, wv_ref[...]).astype(BF)], HEAD_DIM, ROWS_Q + HEAD_DIM)
+
+
+def run_pre(inputs, gain, w_query, w_key, w_value, cos_tab, sin_tab):
+    tokens = inputs.shape[0]
+    return pl.pallas_call(
+        pre_kernel,
+        out_shape=(
+            jax.ShapeDtypeStruct((tokens, WIDTH), BF),
+            jax.ShapeDtypeStruct((KV_HEADS, tokens, PACK), BF),
+        ),
+        compiler_params=params(48),
+        cost_estimate=cost(2 * tokens * WIDTH * 2560, 14e6),
+    )(inputs, gain[None], w_query, w_key, w_value, cos_tab, sin_tab)
+
+
+def heads_t(block, width):
+    return jnp.concatenate(
+        [block[:, h * HEAD_DIM : (h + 1) * HEAD_DIM].astype(F32).T for h in range(width)], axis=1
+    )
+
+
+def heads_rows(block, width):
+    return jnp.concatenate(
+        [block[:, h * HEAD_DIM : (h + 1) * HEAD_DIM] for h in range(width)], axis=0
+    )
+
+
+def allowed_t(step, block):
+    shape = (BLOCK_K, PER_KV * BLOCK_Q)
+    key_pos = step * BLOCK_K + lax.broadcasted_iota(jnp.int32, shape, 0)
+    query_pos = block * BLOCK_Q + lax.broadcasted_iota(jnp.int32, shape, 1) % BLOCK_Q
+    return key_pos <= query_pos
+
+
+def forward_kernel(pack_ref, out_ref, out_t_ref, lse_ref, k_s, vt_s):
+    block = pl.program_id(0)
+
+    @pl.when(block == 0)
+    def _():
+        k_s[...] = pack_ref[:, ROWS_Q : ROWS_Q + HEAD_DIM]
+        vt_s[...] = pack_ref[:, ROWS_Q + HEAD_DIM : PACK].astype(F32).T.astype(BF)
+
+    rows = pl.ds(pl.multiple_of(block * BLOCK_Q, BLOCK_Q), BLOCK_Q)
+    scale = HEAD_DIM ** (-0.5)
+    q_t = (heads_t(pack_ref[rows, 0:ROWS_Q], PER_KV) * scale).astype(BF)
+    columns = PER_KV * BLOCK_Q
+
+    def step(j, carry, masked):
+        running, total, accum = carry
+        keys = pl.ds(pl.multiple_of(j * BLOCK_K, BLOCK_K), BLOCK_K)
+        scores = dot_nn(k_s[keys, :], q_t)
+        if masked:
+            scores = jnp.where(allowed_t(j, block), scores, MASKED)
+        newest = jnp.maximum(running, jnp.max(scores, axis=0, keepdims=True))
+        fade = jnp.exp(running - newest)
+        probs = jnp.exp(scores - newest)
+        total = total * fade + jnp.sum(probs, axis=0, keepdims=True)
+        accum = accum * fade + dot_nn(vt_s[:, keys], probs.astype(BF))
+        return newest, total, accum
+
+    carry = (
+        jnp.full((1, columns), MASKED, F32),
+        jnp.zeros((1, columns), F32),
+        jnp.zeros((HEAD_DIM, columns), F32),
+    )
+    last = (block * BLOCK_Q) // BLOCK_K
+    carry = lax.fori_loop(0, last, lambda j, c: step(j, c, False), carry)
+    running, total, accum = step(last, carry, True)
+    out_t = accum / total
+    out_t_ref[0] = out_t
+    lse_ref[0] = running + jnp.log(total)
+    out_ref[...] = jnp.concatenate(
+        [out_t[:, h * BLOCK_Q : (h + 1) * BLOCK_Q].T for h in range(PER_KV)], axis=1
+    ).astype(BF)
+
+
+def run_forward(pack):
+    length = pack.shape[0]
+    blocks = length // BLOCK_Q
+    columns = PER_KV * BLOCK_Q
+    return pl.pallas_call(
+        forward_kernel,
+        grid=(blocks,),
+        in_specs=[pl.BlockSpec((length, PACK), lambda i: (0, 0))],
+        out_specs=(
+            pl.BlockSpec((BLOCK_Q, ROWS_Q), lambda i: (i, 0)),
+            pl.BlockSpec((1, HEAD_DIM, columns), lambda i: (i, 0, 0)),
+            pl.BlockSpec((1, 1, columns), lambda i: (i, 0, 0)),
+        ),
+        out_shape=(
+            jax.ShapeDtypeStruct((length, ROWS_Q), BF),
+            jax.ShapeDtypeStruct((blocks, HEAD_DIM, columns), F32),
+            jax.ShapeDtypeStruct((blocks, 1, columns), F32),
+        ),
+        scratch_shapes=[pltpu.VMEM((length, HEAD_DIM), BF), pltpu.VMEM((HEAD_DIM, length), BF)],
+        compiler_params=params(40, ("arbitrary",)),
+        cost_estimate=cost(8 * length * length * ROWS_Q, 6e6, length * length * PER_KV),
+    )(pack)
+
+
+def backward_kernel(
+    pack_ref, grad_ref, out_t_ref, lse_ref, cos_ref, sin_ref, res_ref, k_s, v_s, kt_s, dk_s, dv_s
+):
+    block = pl.program_id(0)
+
+    @pl.when(block == 0)
+    def _():
+        keys = pack_ref[:, ROWS_Q : ROWS_Q + HEAD_DIM]
+        k_s[...] = keys
+        kt_s[...] = keys.astype(F32).T.astype(BF)
+        v_s[...] = pack_ref[:, ROWS_Q + HEAD_DIM : PACK]
+        dk_s[...] = jnp.zeros_like(dk_s)
+        dv_s[...] = jnp.zeros_like(dv_s)
+
+    scale = HEAD_DIM ** (-0.5)
+    half = HEAD_DIM // 2
+    rows = pl.ds(pl.multiple_of(block * BLOCK_Q, BLOCK_Q), BLOCK_Q)
+    q_block = pack_ref[rows, 0:ROWS_Q]
+    q_t = (heads_t(q_block, PER_KV) * scale).astype(BF)
+    q_rows = (heads_rows(q_block, PER_KV).astype(F32) * scale).astype(BF)
+    do_block = grad_ref[...]
+    do_f32 = heads_t(do_block, PER_KV)
+    do_t = do_f32.astype(BF)
+    do_rows = heads_rows(do_block, PER_KV)
+    delta = jnp.sum(do_f32 * out_t_ref[0], axis=0, keepdims=True)
+    lse = lse_ref[0]
+
+    def step(j, dq_t, masked):
+        keys = pl.ds(pl.multiple_of(j * BLOCK_K, BLOCK_K), BLOCK_K)
+        scores = dot_nn(k_s[keys, :], q_t)
+        if masked:
+            scores = jnp.where(allowed_t(j, block), scores, MASKED)
+        probs = jnp.exp(scores - lse)
+        d_probs = dot_nn(v_s[keys, :], do_t)
+        d_scores = (probs * (d_probs - delta)).astype(BF)
+        dv_s[keys, :] += dot_nn(probs.astype(BF), do_rows)
+        dk_s[keys, :] += dot_nn(d_scores, q_rows)
+        return dq_t + dot_nn(kt_s[:, keys], d_scores)
+
+    last = (block * BLOCK_Q) // BLOCK_K
+    dq_t = jnp.zeros((HEAD_DIM, PER_KV * BLOCK_Q), F32)
+    dq_t = lax.fori_loop(0, last, lambda j, c: step(j, c, False), dq_t)
+    dq_t = step(last, dq_t, True) * scale
+
+    def turn_back(values, cosine, sine):
+        first, second = values[:half], values[half:]
+        return jnp.concatenate(
+            [first * cosine + second * sine, second * cosine - first * sine], axis=0
+        )
+
+    columns = pl.ds(pl.multiple_of(block * BLOCK_Q, BLOCK_Q), BLOCK_Q)
+    cosine, sine = cos_ref[:, columns], sin_ref[:, columns]
+    res_ref[rows, 0:ROWS_Q] = jnp.concatenate(
+        [
+            turn_back(dq_t[:, h * BLOCK_Q : (h + 1) * BLOCK_Q], cosine, sine).T
+            for h in range(PER_KV)
+        ],
+        axis=1,
+    ).astype(BF)
+
+    @pl.when(block == pl.num_programs(0) - 1)
+    def _():
+        dk_t = turn_back(dk_s[...].T, cos_ref[...], sin_ref[...])
+        res_ref[:, ROWS_Q : ROWS_Q + HEAD_DIM] = dk_t.T.astype(BF)
+        res_ref[:, ROWS_Q + HEAD_DIM : PACK] = dv_s[...].astype(BF)
+
+
+def run_backward(pack, grad, out_t, lse, cos_t, sin_t):
+    length = pack.shape[0]
+    blocks = length // BLOCK_Q
+    columns = PER_KV * BLOCK_Q
+    half = HEAD_DIM // 2
+    return pl.pallas_call(
+        backward_kernel,
+        grid=(blocks,),
+        in_specs=[
+            pl.BlockSpec((length, PACK), lambda i: (0, 0)),
+            pl.BlockSpec((BLOCK_Q, ROWS_Q), lambda i: (i, 0)),
+            pl.BlockSpec((1, HEAD_DIM, columns), lambda i: (i, 0, 0)),
+            pl.BlockSpec((1, 1, columns), lambda i: (i, 0, 0)),
+            pl.BlockSpec((half, length), lambda i: (0, 0)),
+            pl.BlockSpec((half, length), lambda i: (0, 0)),
+        ],
+        out_specs=pl.BlockSpec((length, PACK), lambda i: (0, 0)),
+        out_shape=jax.ShapeDtypeStruct((length, PACK), BF),
+        scratch_shapes=[
+            pltpu.VMEM((length, HEAD_DIM), BF),
+            pltpu.VMEM((length, HEAD_DIM), BF),
+            pltpu.VMEM((HEAD_DIM, length), BF),
+            pltpu.VMEM((length, HEAD_DIM), F32),
+            pltpu.VMEM((length, HEAD_DIM), F32),
+        ],
+        compiler_params=params(48, ("arbitrary",)),
+        cost_estimate=cost(20 * length * length * ROWS_Q, 8e6, length * length * PER_KV),
+    )(pack, grad, out_t, lse, cos_t, sin_t)
+
+
+def mid_kernel(att_ref, wo_ref, hid_ref, gain_ref, mid_ref, norm_ref, full_ref):
+    for g in range(KV_HEADS):
+        full_ref[:, g * ROWS_Q : (g + 1) * ROWS_Q] = att_ref[g]
+    middle = hid_ref[...] + dot_nn(full_ref[...], wo_ref[...])
+    mid_ref[...] = middle
+    inv = lax.rsqrt(jnp.mean(middle * middle, axis=-1, keepdims=True) + EPS)
+    norm_ref[...] = (middle * inv * gain_ref[...]).astype(BF)
+
+
+def run_mid(att, w_output, inputs, gain):
+    tokens = inputs.shape[0]
+    return pl.pallas_call(
+        mid_kernel,
+        out_shape=(
+            jax.ShapeDtypeStruct((tokens, WIDTH), F32),
+            jax.ShapeDtypeStruct((tokens, WIDTH), BF),
+            jax.ShapeDtypeStruct((tokens, WIDTH), BF),
+        ),
+        compiler_params=params(40),
+        cost_estimate=cost(2 * tokens * WIDTH * WIDTH, 12e6),
+    )(att, w_output, inputs, gain[None])
+
+
+def expert_kernel(
+    place_ref,
+    x_ref,
+    g_ref,
+    map_ref,
+    wr_ref,
+    wg0_ref,
+    wg1_ref,
+    wu0_ref,
+    wu1_ref,
+    wd0_ref,
+    wd1_ref,
+    mix_keep,
+    mix_send,
+    dx_keep,
+    dx_send,
+    gate_keep,
+    gate_send,
+    up_keep,
+    up_send,
+    down_keep,
+    down_send,
+    xs,
+    gs,
+    gate_s,
+    wide_s,
+    tall_s,
+):
+    step = pl.program_id(0)
+    sources = map_ref.shape[0]
+    experts = xs.shape[0]
+    tokens = x_ref.shape[1]
+    rows = experts * SLOTS
+    count = WIDTH // CHUNK
+
+    def one_hot(source):
+        slots = map_ref[source, 0:experts, :]
+        wide = jnp.broadcast_to(slots[:, None, :], (experts, SLOTS, tokens))
+        rank = lax.broadcasted_iota(jnp.int32, (experts, SLOTS, tokens), 1).astype(F32)
+        return (wide == rank).astype(F32).reshape(rows, tokens)
+
+    @pl.when(step < sources)
+    def _():
+        slot_map = map_ref[step]
+        chosen = slot_map >= 0.0
+        logits = dot_nt(wr_ref[...], x_ref[0])[0 : slot_map.shape[0]]
+        logits = jnp.where(chosen, logits, MASKED)
+        raised = jnp.exp(logits - jnp.max(logits, axis=0, keepdims=True))
+        raised = jnp.where(chosen, raised, 0.0)
+        gates = raised / jnp.sum(raised, axis=0, keepdims=True)
+        pick = one_hot(step)
+        wide = jnp.broadcast_to(gates[0:experts, None, :], (experts, SLOTS, tokens))
+        gate_rows = jnp.sum(pick * wide.reshape(rows, tokens), axis=1, keepdims=True)
+        pick = pick.astype(BF)
+        here = pl.ds(pl.multiple_of(step * SLOTS, SLOTS), SLOTS)
+        for e in range(experts):
+            gate_s[e, here, :] = gate_rows[e * SLOTS : (e + 1) * SLOTS]
+        for n in range(count):
+            cols = slice(n * CHUNK, (n + 1) * CHUNK)
+            got = dot_nn(pick, x_ref[0, :, cols]).astype(BF)
+            xs[:, here, cols] = got.reshape(experts, SLOTS, CHUNK)
+            got = dot_nn(pick, g_ref[0, :, cols]).astype(BF)
+            gs[:, here, cols] = got.reshape(experts, SLOTS, CHUNK)
+
+    @pl.when((step >= sources) & (step < sources + experts))
+    def _():
+        e = step - sources
+        x = xs[e]
+        w_gate = jnp.concatenate([wg0_ref[0], wg1_ref[0]], axis=1)
+        w_up = jnp.concatenate([wu0_ref[0], wu1_ref[0]], axis=1)
+        gate_pre = dot_nn(x, w_gate)
+        up_pre = dot_nn(x, w_up)
+        sig = jax.nn.sigmoid(gate_pre)
+        silu = gate_pre * sig
+        hidden = (silu * up_pre).astype(BF)
+        gate = gate_s[e]
+        d_hidden = jnp.zeros(hidden.shape, F32)
+        d_gates = jnp.zeros(gate.shape, F32)
+        for n in range(count):
+            cols = slice(n * CHUNK, (n + 1) * CHUNK)
+            w_down = jnp.concatenate([wd0_ref[0, :, cols], wd1_ref[0, :, cols]], axis=0)
+            grad = gs[e, :, cols].astype(F32)
+            d_y = (gate * grad).astype(BF)
+            y = dot_nn(hidden, w_down)
+            d_gates += jnp.sum(y * grad, axis=1, keepdims=True)
+            gs[e, :, cols] = (gate * y).astype(BF)
+            d_hidden += dot_nt(d_y, w_down)
+            wide_s[:, cols] = dot_tn(hidden, d_y).astype(BF)
+        gate_s[e] = d_gates
+        d_gate = (d_hidden * up_pre * sig * (1.0 + gate_pre * (1.0 - sig))).astype(BF)
+        d_up = (d_hidden * silu).astype(BF)
+
+        y_at, zl_at, zh_at = place_ref[1], place_ref[2], place_ref[3]
+        part = down_keep.shape[2]
+        for z in range(2):
+            base = (zh_at ^ z) * 2
+            down_keep[z, 0] = wide_s[pl.ds(pl.multiple_of((base + y_at) * part, part), part), :]
+            down_send[z, 0] = wide_s[
+                pl.ds(pl.multiple_of((base + (1 - y_at)) * part, part), part), :
+            ]
+
+        def spread(keep, send):
+            part = keep.shape[3]
+            for z in range(2):
+                for low in range(2):
+                    base = ((zh_at ^ z) * 2 + (zl_at ^ low)) * 2
+                    keep[z, 0, low] = tall_s[
+                        pl.ds(pl.multiple_of((base + y_at) * part, part), part), :
+                    ]
+                    send[z, 0, low] = tall_s[
+                        pl.ds(pl.multiple_of((base + (1 - y_at)) * part, part), part), :
+                    ]
+
+        for n in range(count):
+            cols = slice(n * CHUNK, (n + 1) * CHUNK)
+            tall_s[cols, :] = dot_tn(x[:, cols], d_gate).astype(BF)
+        spread(gate_keep, gate_send)
+        for n in range(count):
+            cols = slice(n * CHUNK, (n + 1) * CHUNK)
+            tall_s[cols, :] = dot_tn(x[:, cols], d_up).astype(BF)
+        spread(up_keep, up_send)
+        for n in range(count):
+            cols = slice(n * CHUNK, (n + 1) * CHUNK)
+            d_x = dot_nt(d_gate, w_gate[cols]) + dot_nt(d_up, w_up[cols])
+            xs[e, :, cols] = d_x.astype(BF)
+
+    def combine(source, mix_out, dx_out):
+        here = pl.ds(pl.multiple_of(source * SLOTS, SLOTS), SLOTS)
+        pick = one_hot(source).astype(BF)
+        for n in range(count):
+            cols = slice(n * CHUNK, (n + 1) * CHUNK)
+            dx_out[0, :, cols] = dot_tn(pick, xs[:, here, cols].reshape(rows, CHUNK)).astype(BF)
+            mix_out[0, :, cols] = dot_tn(pick, gs[:, here, cols].reshape(rows, CHUNK)).astype(BF)
+        values = gate_s[:, here, :].reshape(rows, 1)
+        column = lax.broadcasted_iota(jnp.int32, (rows, LANES), 1)
+        owner = lax.broadcasted_iota(jnp.int32, (rows, LANES), 0) // SLOTS
+        spread_out = jnp.where(column == owner + place_ref[4], values, 0.0).astype(BF)
+        dx_out[0, :, WIDTH:] = dot_tn(pick, spread_out).astype(BF)
+
+    @pl.when((step >= sources + experts) & (step < sources + experts + sources // 2))
+    def _():
+        combine(step - experts - sources // 2, mix_send, dx_send)
+
+    @pl.when(step >= sources + experts + sources // 2)
+    def _():
+        combine(step - experts - sources - sources // 2, mix_keep, dx_keep)
+
+
+def run_experts(place, x_all, g_all, maps, wr_t, w_gate, w_up, w_down):
+    sources, tokens, width = x_all.shape
+    experts = w_gate.shape[0]
+    ffe = w_gate.shape[2]
+    part = ffe // 8
+    quarter = width // 8
+    half = ffe // 2
+    slots = sources * SLOTS
+    extra = width + LANES
+    first = sources
+    second = sources + experts
+    third = second + sources // 2
+
+    def at(i, low, size):
+        return jnp.clip(i - low, 0, size - 1)
+
+    def expert_of(i):
+        return at(i, first, experts)
+
+    def w_cols(block):
+        return pl.BlockSpec((1, width, LANES), lambda i, p: (expert_of(i), 0, p[0] + 2 * block))
+
+    def w_rows(block):
+        return pl.BlockSpec((1, LANES, width), lambda i, p: (expert_of(i), p[0] + 2 * block, 0))
+
+    token_spec = pl.BlockSpec(
+        (1, tokens, width),
+        lambda i, p: (at(i, 0, sources), 0, 0),
+        pipeline_mode=pl.Buffered(1),
+    )
+
+    def out_tokens(low, cols):
+        return pl.BlockSpec((1, tokens, cols), lambda i, p: (at(i, low, sources // 2), 0, 0))
+
+    tall_spec = pl.BlockSpec(
+        (2, 1, 2, quarter, half), lambda i, p: (0, expert_of(i), 0, 0, 0)
+    )
+    wide_spec = pl.BlockSpec((2, 1, part, width), lambda i, p: (0, expert_of(i), 0, 0))
+    tall = jax.ShapeDtypeStruct((2, experts, 2, quarter, half), BF)
+    wide = jax.ShapeDtypeStruct((2, experts, part, width), BF)
+    mixed = jax.ShapeDtypeStruct((sources // 2, tokens, width), BF)
+    d_x = jax.ShapeDtypeStruct((sources // 2, tokens, extra), BF)
+    return pl.pallas_call(
+        expert_kernel,
+        grid_spec=pltpu.PrefetchScalarGridSpec(
+            num_scalar_prefetch=1,
+            grid=(third + sources // 2,),
+            in_specs=[
+                token_spec,
+                token_spec,
+                pl.BlockSpec(maps.shape, lambda i, p: (0, 0, 0)),
+                pl.BlockSpec(wr_t.shape, lambda i, p: (0, 0)),
+                w_cols(0),
+                w_cols(1),
+                w_cols(0),
+                w_cols(1),
+                w_rows(0),
+                w_rows(1),
+            ],
+            out_specs=(
+                out_tokens(third, width),
+                out_tokens(second, width),
+                out_tokens(third, extra),
+                out_tokens(second, extra),
+                tall_spec,
+                tall_spec,
+                tall_spec,
+                tall_spec,
+                wide_spec,
+                wide_spec,
+            ),
+            scratch_shapes=[
+                pltpu.VMEM((experts, slots, width), BF),
+                pltpu.VMEM((experts, slots, width), BF),
+                pltpu.VMEM((experts, slots, 1), F32),
+                pltpu.VMEM((half, width), BF),
+                pltpu.VMEM((width, half), BF),
+            ],
+        ),
+        out_shape=(mixed, mixed, d_x, d_x, tall, tall, tall, tall, wide, wide),
+        compiler_params=params(63, ("arbitrary",)),
+        cost_estimate=cost(60e9, 90e6),
+    )(place, x_all, g_all, maps, wr_t, w_gate, w_gate, w_up, w_up, w_down, w_down)
+
+
+def post_kernel(
+    dx_ref,
+    mid_ref,
+    cot_ref,
+    norm_ref,
+    wr_ref,
+    map_ref,
+    gain_ref,
+    wo_ref,
+    datt_ref,
+    dmid_ref,
+    dlow_ref,
+    dlog_ref,
+    ggain_ref,
+):
+    middle = mid_ref[...]
+    inv = lax.rsqrt(jnp.mean(middle * middle, axis=-1, keepdims=True) + EPS)
+    chosen = map_ref[...] >= 0.0
+    logits = jnp.where(chosen, dot_nn(norm_ref[...], wr_ref[...]), MASKED)
+    raised = jnp.exp(logits - jnp.max(logits, axis=-1, keepdims=True))
+    raised = jnp.where(chosen, raised, 0.0)
+    gates = raised / jnp.sum(raised, axis=-1, keepdims=True)
+    d_gates = dx_ref[:, WIDTH:]
+    d_picked = gates * (d_gates - jnp.sum(gates * d_gates, axis=-1, keepdims=True))
+    d_logits = d_picked.astype(BF)
+    dlog_ref[...] = d_logits
+    d_norm = dx_ref[:, :WIDTH] + dot_nt(d_logits, wr_ref[...])
+    scaled = d_norm * gain_ref[...]
+    ggain_ref[...] = jnp.sum(d_norm * middle * inv, axis=0, keepdims=True)
+    d_mid = (
+        cot_ref[...]
+        + inv * scaled
+        - middle * inv**3 * jnp.mean(middle * scaled, axis=-1, keepdims=True)
+    )
+    dmid_ref[...] = d_mid
+    d_low = d_mid.astype(BF)
+    dlow_ref[...] = d_low
+    d_att = dot_nt(d_low, wo_ref[...]).astype(BF)
+    for g in range(KV_HEADS):
+        datt_ref[g] = d_att[:, g * ROWS_Q : (g + 1) * ROWS_Q]
+
+
+def run_post(dx_sum, middle, cotangent, normed_two, wr_pad, map_rows, gain, w_output):
+    tokens = middle.shape[0]
+    return pl.pallas_call(
+        post_kernel,
+        out_shape=(
+            jax.ShapeDtypeStruct((KV_HEADS, tokens, ROWS_Q), BF),
+            jax.ShapeDtypeStruct((tokens, WIDTH), F32),
+            jax.ShapeDtypeStruct((tokens, WIDTH), BF),
+            jax.ShapeDtypeStruct((tokens, LANES), BF),
+            jax.ShapeDtypeStruct((1, WIDTH), F32),
+        ),
+        compiler_params=params(48),
+        cost_estimate=cost(2 * tokens * WIDTH * WIDTH, 14e6),
+    )(dx_sum, middle, cotangent, normed_two, wr_pad, map_rows, gain[None], w_output)
+
+
+def put_rows(place_ref, held, keep, send):
+    part = keep.shape[1]
+    for b in range(keep.shape[0]):
+        own = (2 * b) ^ place_ref[5]
+        keep[b] = held[pl.ds(pl.multiple_of(own * part, part), part), :]
+        other = own ^ 1
+        send[b] = held[pl.ds(pl.multiple_of(other * part, part), part), :]
+
+
+def outgrad_kernel(place_ref, a_ref, b_ref, keep, send, held):
+    held[...] = dot_tn(a_ref[...], b_ref[...]).astype(BF)
+    put_rows(place_ref, held, keep, send)
+
+
+def run_outgrad(place, left, right, blocks):
+    tokens, rows = left.shape
+    cols = right.shape[1]
+    part = rows // blocks
+    spec = pl.BlockSpec((blocks // 2, part, 256), lambda i, p: (0, 0, i))
+    shape = jax.ShapeDtypeStruct((blocks // 2, part, cols), BF)
+    return pl.pallas_call(
+        outgrad_kernel,
+        grid_spec=pltpu.PrefetchScalarGridSpec(
+            num_scalar_prefetch=1,
+            grid=(cols // 256,),
+            in_specs=[
+                pl.BlockSpec((tokens, rows), lambda i, p: (0, 0)),
+                pl.BlockSpec((tokens, 256), lambda i, p: (0, i)),
+            ],
+            out_specs=(spec, spec),
+            scratch_shapes=[pltpu.VMEM((rows, 256), BF)],
+        ),
+        out_shape=(shape, shape),
+        compiler_params=params(32, ("arbitrary",)),
+        cost_estimate=cost(2 * tokens * rows * cols, 8e6),
+    )(place, left, right)
+
+
+def qkvgrad_kernel(
+    place_ref, a_ref, d_ref, full_ref, keep0, send0, keep1, send1, keep2, send2, held
+):
+    step = pl.program_id(0)
+
+    @pl.when(step == 0)
+    def _():
+        key_at = KV_HEADS * ROWS_Q
+        value_at = key_at + KV_HEADS * HEAD_DIM
+        for g in range(KV_HEADS):
+            full_ref[:, g * ROWS_Q : (g + 1) * ROWS_Q] = d_ref[g, :, 0:ROWS_Q]
+            full_ref[:, key_at + g * HEAD_DIM : key_at + (g + 1) * HEAD_DIM] = d_ref[
+                g, :, ROWS_Q : ROWS_Q + HEAD_DIM
+            ]
+            full_ref[:, value_at + g * HEAD_DIM : value_at + (g + 1) * HEAD_DIM] = d_ref[
+                g, :, ROWS_Q + HEAD_DIM : PACK
+            ]
+
+    cols = pl.ds(pl.multiple_of(step * 256, 256), 256)
+    held[...] = dot_tn(a_ref[...], full_ref[:, cols]).astype(BF)
+
+    @pl.when(step < 3)
+    def _():
+        put_rows(place_ref, held, keep0, send0)
+
+    @pl.when((step >= 3) & (step < 6))
+    def _():
+        put_rows(place_ref, held, keep1, send1)
+
+    @pl.when(step >= 6)
+    def _():
+        put_rows(place_ref, held, keep2, send2)
+
+
+def run_qkvgrad(place, normed, d_pack, blocks):
+    tokens, rows = normed.shape
+    cols = KV_HEADS * PACK
+    part = rows // blocks
+
+    def spec(low, size):
+        return pl.BlockSpec(
+            (blocks // 2, part, 256), lambda i, p: (0, 0, jnp.clip(i - low, 0, size - 1))
+        )
+
+    def shape(size):
+        return jax.ShapeDtypeStruct((blocks // 2, part, size * 256), BF)
+
+    return pl.pallas_call(
+        qkvgrad_kernel,
+        grid_spec=pltpu.PrefetchScalarGridSpec(
+            num_scalar_prefetch=1,
+            grid=(cols // 256,),
+            in_specs=[
+                pl.BlockSpec((tokens, rows), lambda i, p: (0, 0)),
+                pl.BlockSpec(d_pack.shape, lambda i, p: (0, 0, 0)),
+            ],
+            out_specs=(
+                pl.BlockSpec((tokens, cols), lambda i, p: (0, 0)),
+                spec(0, 3),
+                spec(0, 3),
+                spec(3, 3),
+                spec(3, 3),
+                spec(6, 4),
+                spec(6, 4),
+            ),
+            scratch_shapes=[pltpu.VMEM((rows, 256), BF)],
+        ),
+        out_shape=(
+            jax.ShapeDtypeStruct((tokens, cols), BF),
+            shape(3),
+            shape(3),
+            shape(3),
+            shape(3),
+            shape(4),
+            shape(4),
+        ),
+        compiler_params=params(40, ("arbitrary",)),
+        cost_estimate=cost(2 * tokens * rows * cols, 12e6),
+    )(place, normed, d_pack)
+
+
+def last_kernel(d_ref, wq_ref, wk_ref, wv_ref, dmid_ref, hid_ref, gain_ref, out_ref, ggain_ref):
+    key_at = KV_HEADS * ROWS_Q
+    value_at = key_at + KV_HEADS * HEAD_DIM
+    d_norm = dot_nt(d_ref[:, 0:key_at], wq_ref[...])
+    d_norm += dot_nt(d_ref[:, key_at:value_at], wk_ref[...])
+    d_norm += dot_nt(d_ref[:, value_at:], wv_ref[...])
+    inputs = hid_ref[...]
+    inv = lax.rsqrt(jnp.mean(inputs * inputs, axis=-1, keepdims=True) + EPS)
+    scaled = d_norm * gain_ref[...]
+    ggain_ref[...] = jnp.sum(d_norm * inputs * inv, axis=0, keepdims=True)
+    out_ref[...] = (
+        dmid_ref[...]
+        + inv * scaled
+        - inputs * inv**3 * jnp.mean(inputs * scaled, axis=-1, keepdims=True)
+    )
+
+
+def run_last(d_full, w_query, w_key, w_value, d_middle, inputs, gain):
+    tokens = inputs.shape[0]
+    return pl.pallas_call(
+        last_kernel,
+        out_shape=(
+            jax.ShapeDtypeStruct((tokens, WIDTH), F32),
+            jax.ShapeDtypeStruct((1, WIDTH), F32),
+        ),
+        compiler_params=params(48),
+        cost_estimate=cost(2 * tokens * WIDTH * 2560, 16e6),
+    )(d_full, w_query, w_key, w_value, d_middle, inputs, gain[None])
+
+
+def gather_relative(values):
+    held = values[None]
+    for bit in (X_BIT, ZL_BIT, C_BIT):
+        held = jnp.concatenate([held, swap_bit(held, bit)], axis=0)
+    return held
+
+
+def sum_pair(kept, received):
+    return kept.astype(F32) + received.astype(F32)
+
+
+def scatter_tokens(keep, send):
+    tokens, cols = keep.shape[1:]
+    got = swap_bit(send, C_BIT)
+    both = sum_pair(keep, got).reshape(2, 2, tokens, cols)
+    half = tokens // 2
+    results = []
+    for part in range(2):
+        rows = slice(part * half, (part + 1) * half)
+        if part == 0:
+            mine, other = both[:, 0, rows], both[:, 1, rows]
+            bits = (X_BIT, ZL_BIT)
+        else:
+            mine, other = both[0, :, rows], both[1, :, rows]
+            bits = (ZL_BIT, X_BIT)
+        held = sum_pair(mine, swap_bit(other.astype(BF), bits[0]))
+        results.append(sum_pair(held[0], swap_bit(held[1].astype(BF), bits[1])))
+    return jnp.concatenate(results, axis=0)
+
+
+BITS = {"zh": ZH_BIT, "zl": ZL_BIT, "y": Y_BIT, "x": X_BIT}
+
+
+def scatter_dense(keep, send, order, low=BF):
+    part, cols = keep.shape[1:]
+    held = sum_pair(keep, swap_bit(send, C_BIT)).reshape(2, 2, 2, 2, part, cols)
+    names = ["zh", "zl", "y", "x"]
+    for name in order:
+        axis = names.index(name)
+        mine = lax.index_in_dim(held, 0, axis, keepdims=False)
+        other = lax.index_in_dim(held, 1, axis, keepdims=False)
+        held = sum_pair(mine, swap_bit(other.astype(low), BITS[name]))
+        names.remove(name)
+    return held
+
+
+def scatter_expert(keep, send):
+    held = sum_pair(keep, swap_bit(send, Y_BIT))
+    return sum_pair(held[0], swap_bit(held[1].astype(BF), ZH_BIT))
+
+
+def join_columns(total, zl_at):
+    mine = total[:, 0]
+    other = swap_bit(total[:, 1].astype(BF), ZL_BIT).astype(F32)
+    experts, rows, cols = mine.shape
+    mine = mine.reshape(experts, rows, 2, 1, LANES)
+    other = other.reshape(experts, rows, 2, 1, LANES)
+    low = jnp.where(zl_at == 0, mine, other)
+    high = jnp.where(zl_at == 0, other, mine)
+    return jnp.concatenate([low, high], axis=3).reshape(experts, rows, 2 * cols)
+
+
+def fast_body(
+    hidden_in,
+    gain_attn,
+    w_query,
+    w_key,
+    w_value,
+    w_output,
+    gain_mlp,
+    w_router,
+    w_gate,
+    w_up,
+    w_down,
+    expert_ids,
+    slot_order,
+    grad_out,
+):
+    inputs = hidden_in[0]
+    cotangent = grad_out[0]
+    chosen = expert_ids[0]
+    tokens = inputs.shape[0]
+    top = chosen.shape[1]
+    local_experts = w_gate.shape[0]
+    peers = lax.axis_size("expert")
+    all_experts = local_experts * peers
+    shards = lax.axis_size("dp")
+    length = shards * tokens
+    devices = shards * peers
+    index = lax.axis_index("dp")
+    column = lax.axis_index("expert")
+    y_at = index % 2
+    zl_at = (index // 2) % 2
+    zh_at = index // 4
+    place = jnp.stack(
+        [zl_at, y_at, zl_at, zh_at, column * local_experts, index * peers + column]
+    ).astype(jnp.int32)
+
+    ranks = slot_order[0, 0].reshape(tokens, top)
+    far = tokens * top
+    match = chosen.T[None] == jnp.arange(all_experts, dtype=jnp.int32)[:, None, None]
+    rank_map = jnp.min(jnp.where(match, ranks.T[None], far), axis=1)
+    before = jnp.sum((rank_map[:, None, :] < rank_map[:, :, None]).astype(jnp.int32), axis=-1)
+    slot_map = jnp.where(rank_map < far, jnp.minimum(before, SLOTS), -1).astype(BF)
+    map_rows = jnp.pad(slot_map.T.astype(F32), ((0, 0), (0, LANES - all_experts)), constant_values=-1.0)
+    maps = gather_relative(slot_map).astype(F32)
+    maps = jnp.roll(maps, -column * local_experts, axis=1)
+    g_all = gather_relative(cotangent.astype(BF))
+    wr_pad = jnp.pad(w_router, ((0, 0), (0, LANES - all_experts)))
+    wr_t = jnp.roll(w_router.T, -column * local_experts, axis=0)
+    wr_t = jnp.pad(wr_t, ((0, LANES - all_experts), (0, 0)))
+
+    half = HEAD_DIM // 2
+    frequency = jnp.exp(-math.log(10000.0) * jnp.arange(half, dtype=F32) * 2.0 / HEAD_DIM)
+    own_angles = (index * tokens + jnp.arange(tokens, dtype=jnp.int32)).astype(F32)[:, None] * frequency
+    cos_own, sin_own = jnp.cos(own_angles), jnp.sin(own_angles)
+    cos_tab = jnp.concatenate([cos_own] * 4, axis=1)
+    sin_tab = jnp.concatenate([-sin_own, sin_own] * 2, axis=1)
+    angles = frequency[:, None] * jnp.arange(length, dtype=jnp.int32).astype(F32)[None]
+    cos_t, sin_t = jnp.cos(angles), jnp.sin(angles)
+
+    normed, pack = run_pre(inputs, gain_attn, w_query, w_key, w_value, cos_tab, sin_tab)
+    pack = lax.all_to_all(pack, "dp", 0, 0, tiled=True).reshape(length, PACK)
+    out, out_t, lse = run_forward(pack)
+    att = lax.all_to_all(out.reshape(shards, tokens, ROWS_Q), "dp", 0, 0, tiled=True)
+    middle, normed_two, att_full = run_mid(att, w_output, inputs, gain_mlp)
+    x_all = gather_relative(normed_two)
+    (
+        mix_keep,
+        mix_send,
+        dx_keep,
+        dx_send,
+        gate_keep,
+        gate_send,
+        up_keep,
+        up_send,
+        down_keep,
+        down_send,
+    ) = run_experts(place, x_all, g_all, maps, wr_t, w_gate, w_up, w_down)
+    dx_sum = scatter_tokens(dx_keep, dx_send)
+    hidden_out = middle + scatter_tokens(mix_keep, mix_send)
+    gate_total = join_columns(scatter_expert(gate_keep, gate_send), zl_at)
+    up_total = join_columns(scatter_expert(up_keep, up_send), zl_at)
+    down_total = scatter_expert(down_keep, down_send)
+
+    d_att, d_middle, d_low, d_log, ggain_mlp = run_post(
+        dx_sum, middle, cotangent, normed_two, wr_pad, map_rows, gain_mlp, w_output
+    )
+    d_out = lax.all_to_all(d_att, "dp", 0, 0, tiled=True).reshape(length, ROWS_Q)
+    out_keep, out_send = run_outgrad(place, att_full, d_low, devices)
+    output_total = scatter_dense(out_keep, out_send, ("x", "y", "zl", "zh"))
+    router_part = dot_tn(normed_two, d_log)[:, :all_experts]
+
+    d_pack = run_backward(pack, d_out, out_t, lse, cos_t, sin_t)
+    d_pack = lax.all_to_all(
+        d_pack.reshape(shards, tokens, PACK), "dp", 0, 0, tiled=True
+    )
+    d_full, keep0, send0, keep1, send1, keep2, send2 = run_qkvgrad(place, normed, d_pack, devices)
+    total0 = scatter_dense(keep0, send0, ("x", "y", "zl", "zh"))
+    total1 = scatter_dense(keep1, send1, ("y", "zl", "x", "zh"))
+    total2 = scatter_dense(keep2, send2, ("zl", "x", "y", "zh"))
+    grad_in, ggain_attn = run_last(
+        d_full, w_query, w_key, w_value, d_middle, inputs, gain_attn
+    )
+    small = jnp.concatenate([router_part, ggain_mlp.T, ggain_attn.T], axis=1)
+    small = lax.psum_scatter(small, ("dp", "expert"), scatter_dimension=0, tiled=True)
+    key_width = KV_HEADS * HEAD_DIM
+    return (
+        hidden_out[None],
+        grad_in[None],
+        small[:, all_experts + 1],
+        jnp.concatenate([total0, total1], axis=1),
+        total2[:, :key_width],
+        total2[:, key_width:],
+        output_total,
+        small[:, all_experts],
+        small[:, :all_experts],
+        gate_total,
+        up_total,
+        down_total,
+    )
+
+
+def fits(mesh):
+    return mesh.shape["dp"] == KV_HEADS and mesh.shape["expert"] == 4
+
 
 def solution(mesh):
     in_specs = (
@@ -398,4 +1335,5 @@
         P("expert", "dp", None),
         P("expert", "dp", None),
     )
-    return jax.shard_map(body, mesh=mesh, in_specs=in_specs, out_specs=out_specs, check_vma=False)
+    chosen = fast_body if fits(mesh) else body
+    return jax.shard_map(chosen, mesh=mesh, in_specs=in_specs, out_specs=out_specs, check_vma=False)

time: 2540 us -> 1140 us (0.45)
  waiting for transfers between devices: 1740 us -> 603 us
  matrix products: 220 us -> 1.02 us
  Pallas kernels: 0 us -> 209 us
  blocking collectives: 237 us -> 53.1 us
  local copies, waits for them, and re-layouts: 212 us -> 89.6 us
  starting transfers between devices: 12.3 us -> 60.5 us
    reduce_scatter x7 -> x0, waiting for transfers between devices: 1180 us -> none  [the longest x1 250 us: body(): lax.psum_scatter(grad_gate_part.astype(jnp.bfloat16), 'dp', scatter_dimen...]
    ppermute x0 -> x47, waiting for transfers between devices: none -> 488 us  [swap(): return lax.ppermute(values, axis, [(i, i ^ mask) for i in range(size)])]
    unnamed x15 -> x2, waiting for transfers between devices: 313 us -> 91 us
    dot_general x32 -> x1, matrix products: 219 us -> 1.02 us  [dot_tn(): lax.dot_general(a, b, (((0,), (0,)), ((), ())), preferred_element_type=F32)]
    pallas_call x0 -> x9, Pallas kernels: none -> 209 us  [the longest x1 100 us: run_experts(): pl.pallas_call(expert_kernel, grid_spec=pltpu.PrefetchScalarGridSpec(num_...]
    all_to_all x2 -> x3, waiting for transfers between devices: 166 us -> 23.9 us  [the longest x1 23.9 us: fast_body(): lax.all_to_all(out.reshape(shards, tokens, ROWS_Q), 'dp', 0, 0, tiled=True)]
    all_to_all x2 -> x1, blocking collectives: 190 us -> 53.1 us  [fast_body(): pack = lax.all_to_all(pack, 'dp', 0, 0, tiled=True).reshape(length, PACK)]
    gather x6 -> x0, local copies, waits for them, and re-layouts: 99.1 us -> none  [the longest x1 20.9 us: body(): jnp.concatenate([returned.reshape(all_experts * capacity, width), zero_ro...]
  transfers between devices with their start and end apart: 14 -> 51, of which waited for: 14 -> 29; matrix products, arithmetic and copies ran while one was open for 8% -> 14% of each run, Pallas kernels for 0% -> 6%
where the time goes in v1:
time: 1140 us
  waiting for transfers between devices  603 us (53%)
  Pallas kernels  209 us (18%)
  other arithmetic  105 us (9%)
  local copies, waits for them, and re-layouts  89.6 us (8%)
  starting transfers between devices  60.5 us (5%)
  blocking collectives  53.1 us (5%)
  between operations  15.5 us (1%)
    ppermute x47, waiting for transfers between devices, swap(): return lax.ppermute(values, axis, [(i, i ^ mask) for i in range(size)])  488 us
    pallas_call x1, Pallas kernels, run_experts(): pl.pallas_call(expert_kernel, grid_spec=pltpu.PrefetchScalarGridSpec(num_...  100 us
    unnamed x2, waiting for transfers between devices  91 us
    all_to_all x1, blocking collectives, fast_body(): pack = lax.all_to_all(pack, 'dp', 0, 0, tiled=True).reshape(length, PACK)  53.1 us
    add x34, other arithmetic, sum_pair(): return kept.astype(F32) + received.astype(F32)  52.1 us
    ppermute x47, starting transfers between devices, swap(): return lax.ppermute(values, axis, [(i, i ^ mask) for i in range(size)])  46.9 us
    pallas_call x1, Pallas kernels, run_backward(): pl.pallas_call(backward_kernel, grid=(blocks,), in_specs=[pl.BlockSpec((l...  40.5 us
    pallas_call x1, Pallas kernels, run_forward(): pl.pallas_call(forward_kernel, grid=(blocks,), in_specs=[pl.BlockSpec((le...  27.1 us
  transfers between devices with their start and end apart: 51, of which 29 were waited for; matrix products, arithmetic and copies ran while one was open for 14% of the time, Pallas kernels for 6%

profile of v1, /device:TPU:0, one launch (start us, length us, event | category | flops | bytes accessed | tf_op | source)
XLA Modules:
  0.0 1136.2 jit_solution(10455965636863522557)
XLA Ops:
  11.7 7.2 shard_map.229
  19.0 53.1 %all_to_all.20 = bf16[8,320,320]{2,1,0:T(8,128)(2,1)S(1)} all-to-all(bf16[8,320,320]{2,1,0:T(8,128)(2,1)} %get-tuple-element.46), channel_id=1, replica_groups=mesh['dp'=8,'expert'=4] {'dp'}, dimensions={0} | all-to-all | bytes 3276800 | tf_op jit(solution)/shard_map/all_to_all | solution.py:1242
  72.1 27.1 %shard_map.230 = (bf16[2560,192]{1,0:T(8,128)(2,1)S(1)}, f32[10,64,768]{2,1,0:T(8,128)S(1)}, f32[10,1,768]{2,1,0:T(1,128)S(1)}) custom-call(bf16[2560,320]{1,0:T(8,128)(2,1)S(1)} %bitcast.226), custom_call_target="tpu_custom_call" | custom-call | flops 10066329600 | bytes 6000000 | tf_op jit(solution)/shard_map/pallas_call | solution.py:540
  110.8 23.9 %all-to-all-done.1 = bf16[8,320,192]{1,2,0:T(8,128)(2,1)S(1)} async-done(((bf16[8,320,192]{1,2,0:T(8,128)(2,1)}), bf16[8,320,192]{1,2,0:T(8,128)(2,1)S(1)}, u32[]{:S(2)}, u32[]{:S(2)}) %all-to-all-start.1) | async-done | bytes 983072 | tf_op jit(solution)/shard_map/all_to_all | solution.py:1244
  145.2 18.5 %collective-permute-done = bf16[1,320,1536]{2,1,0:T(8,128)(2,1)S(1)} collective-permute-done((bf16[1,320,1536]{2,1,0:T(8,128)(2,1)S(1)}, bf16[1,320,1536]{2,1,0:T(8,128)(2,1)S(1)}, u32[]{:S(2)}, u32[]{:S(2)}) %collective-permute-start) | collective-permute-done | bytes 983072 | tf_op jit(solution)/shard_map/ppermute | solution.py:411
  164.0 26.9 %collective-permute-done.4 = bf16[2,320,1536]{2,1,0:T(8,128)(2,1)S(1)} collective-permute-done((bf16[2,320,1536]{2,1,0:T(8,128)(2,1)S(1)}, bf16[2,320,1536]{2,1,0:T(8,128)(2,1)S(1)}, u32[]{:S(2)}, u32[]{:S(2)}) %collective-permute-start.4) | collective-permute-done | bytes 1966112 | tf_op jit(solution)/shard_map/ppermute | solution.py:411
  195.0 34.8 %collective-permute-done.1 = bf16[2,320,1536]{2,1,0:T(8,128)(2,1)S(1)} collective-permute-done((bf16[2,320,1536]{2,1,0:T(8,128)(2,1)S(1)}, bf16[2,320,1536]{2,1,0:T(8,128)(2,1)S(1)}, u32[]{:S(2)}, u32[]{:S(2)}) %collective-permute-start.1) | collective-permute-done | bytes 1966112 | tf_op jit(solution)/shard_map/ppermute | solution.py:411
  262.9 100.3 %shard_map.232 = (bf16[4,320,1536]{2,1,0:T(8,128)(2,1)}, bf16[4,320,1536]{2,1,0:T(8,128)(2,1)}, bf16[4,320,1664]{2,1,0:T(8,128)(2,1)}, bf16[4,320,1664]{2,1,0:T(...) custom-call(s32[6]{0:T(128)} %stack.24.place_ref, ...), custom_call_target="tpu_custom_call" | custom-call | flops 60000002048 | bytes 90000000 | tf_op jit(solution)/shard_map/pallas_call | solution.py:870
  373.6 78.0 %collective-permute-done.45 = bf16[2,10,64,1536]{3,2,1,0:T(8,128)(2,1)} collective-permute-done((bf16[2,10,64,1536]{3,2,1,0:T(8,128)(2,1)}, bf16[2,10,64,1536]{3,2,1,0:T(8,128)(2,1)}, u32[]{:S(2)}, u32[]{:S(2)}) %collective-permute-start.45) | collective-permute-done | bytes 3932192 | tf_op jit(solution)/shard_map/ppermute | solution.py:411
  459.1 76.7 %collective-permute-done.42 = bf16[2,10,2,192,256]{4,3,2,1,0:T(8,128)(2,1)} collective-permute-done((bf16[2,10,2,192,256]{4,3,2,1,0:T(8,128)(2,1)}, bf16[2,10,2,192,256]{4,3,2,1,0:T(8,128)(2,1)}, u32[]{:S(2)}, u32[]{:S(2)}) %collective-permute-start.42) | collective-permute-done | bytes 3932192 | tf_op jit(solution)/shard_map/ppermute | solution.py:411
  542.4 77.5 %collective-permute-done.39 = bf16[2,10,2,192,256]{4,3,2,1,0:T(8,128)(2,1)} collective-permute-done((bf16[2,10,2,192,256]{4,3,2,1,0:T(8,128)(2,1)}, bf16[2,10,2,192,256]{4,3,2,1,0:T(8,128)(2,1)}, u32[]{:S(2)}, u32[]{:S(2)}) %collective-permute-start.39) | collective-permute-done | bytes 3932192 | tf_op jit(solution)/shard_map/ppermute | solution.py:411
  643.1 17.6 %collective-permute-done.10 = bf16[2,160,1536]{2,1,0:T(8,128)(2,1)S(1)} collective-permute-done((bf16[2,160,1536]{2,1,0:T(8,128)(2,1)}, bf16[2,160,1536]{2,1,0:T(8,128)(2,1)S(1)}, u32[]{:S(2)}, u32[]{:S(2)}) %collective-permute-start.10) | collective-permute-done | bytes 983072 | tf_op jit(solution)/shard_map/ppermute | solution.py:411
  661.9 28.0 %collective-permute-done.12 = bf16[2,160,1536]{2,1,0:T(8,128)(2,1)S(1)} collective-permute-done((bf16[2,160,1536]{2,1,0:T(8,128)(2,1)}, bf16[2,160,1536]{2,1,0:T(8,128)(2,1)S(1)}, u32[]{:S(2)}, u32[]{:S(2)}) %collective-permute-start.12) | collective-permute-done | bytes 983072 | tf_op jit(solution)/shard_map/ppermute | solution.py:411
  696.7 40.0 %collective-permute-done.17 = bf16[2,160,1664]{2,1,0:T(8,128)(2,1)S(1)} collective-permute-done((bf16[2,160,1664]{2,1,0:T(8,128)(2,1)S(1)}, bf16[2,160,1664]{2,1,0:T(8,128)(2,1)S(1)}, u32[]{:S(2)}, u32[]{:S(2)}) %collective-permute-start.17) | collective-permute-done | bytes 1064992 | tf_op jit(solution)/shard_map/ppermute | solution.py:411
  738.6 8.5 collective-permute-done.11
  752.6 8.5 collective-permute-done.16
  764.4 8.0 shard_map.233
  817.4 12.7 %collective-permute-done.44 = bf16[10,192,256]{2,1,0:T(8,128)(2,1)S(1)} collective-permute-done((bf16[10,192,256]{2,1,0:T(8,128)(2,1)}, bf16[10,192,256]{2,1,0:T(8,128)(2,1)S(1)}, u32[]{:S(2)}, u32[]{:S(2)}) %collective-permute-start.44) | collective-permute-done | bytes 983072 | tf_op jit(solution)/shard_map/ppermute | solution.py:411
  845.0 40.5 %shard_map.234 = bf16[2560,320]{1,0:T(8,128)(2,1)S(1)} custom-call(bf16[2560,320]{1,0:T(8,128)(2,1)S(1)} %bitcast.227, bf16[2560,192]{1,0:T(8,128)(2,1)S(1)} %bitcast.229, f32[10,64,768]{2,1,0:T(8,128)} %copy-done.33, f32[10,1,768]{2,1,0:T(1,128)S(1)} %copy-done.35, f32[32,2560]{1,0:T(8,128)S(1)} %copy-done.20, f32[32,2560]{1,0:T(8,128)S(1)} %copy-done.19), custom_call_target="tpu_custom_call" | custom-call | flops 25165824000 | bytes 8000000 | tf_op jit(solution)/shard_map/pallas_call | solution.py:632
  915.8 10.6 collective-permute-done.36
  945.2 10.1 shard_map.235
  960.2 7.9 shard_map.236
  972.8 91.0 %reduce-scatter.4.cloned.1.call-done = f32[48,42]{1,0:T(8,128)} async-done(((f32[1536,42]{1,0:T(8,128)}), f32[48,42]{1,0:T(8,128)}) %reduce-scatter.4.cloned.1.call-update) | async-done | bytes 8080
  1093.2 7.6 collective-permute-done.26
  (347 shorter events, 305.5 us)
Async XLA Ops:
  145.1 45.8 %collective-permute-start.4 = (bf16[2,320,1536]{2,1,0:T(8,128)(2,1)S(1)}, bf16[2,320,1536]{2,1,0:T(8,128)(2,1)S(1)}, u32[]{:S(2)}, u32[]{:S(2)}) collective-permute-start(bf16[2,320,1536]{2,1,0:T(8,128)(2,1)S(1)} %pad_maximum_fusion.8), channel_id=1, source_target_pairs={{0,8},{4,12},{8,0},{12,4},{16,24},{20,28},{24,16},{28,20},{1,9},{5... | collective-permute-start | bytes 5898248 | tf_op jit(solution)/shard_map/ppermute | solution.py:411
  163.9 66.0 %collective-permute-start.1 = (bf16[2,320,1536]{2,1,0:T(8,128)(2,1)S(1)}, bf16[2,320,1536]{2,1,0:T(8,128)(2,1)S(1)}, u32[]{:S(2)}, u32[]{:S(2)}) collective-permute-start(bf16[2,320,1536]{2,1,0:T(8,128)(2,1)S(1)} %pad_maximum_fusion.7), channel_id=1, source_target_pairs={{0,8},{4,12},{8,0},{12,4},{16,24},{20,28},{24,16},{28,20},{1,9},{5... | collective-permute-start | bytes 5898248 | tf_op jit(solution)/shard_map/ppermute | solution.py:411
  194.9 55.1 %collective-permute-start.5 = (bf16[4,320,1536]{2,1,0:T(8,128)(2,1)}, bf16[4,320,1536]{2,1,0:T(8,128)(2,1)}, u32[]{:S(2)}, u32[]{:S(2)}) collective-permute-start(bf16[4,320,1536]{2,1,0:T(8,128)(2,1)} %pad_maximum_fusion.3), channel_id=1, source_target_pairs={{0,1},{1,0},{2,3},{3,2},{4,5},{5,4},{6,7},{7,6},{8,9},{9,8},{10,11... | collective-permute-start | bytes 11796488 | tf_op jit(solution)/shard_map/ppermute | solution.py:411
  363.2 88.4 %collective-permute-start.45 = (bf16[2,10,64,1536]{3,2,1,0:T(8,128)(2,1)}, bf16[2,10,64,1536]{3,2,1,0:T(8,128)(2,1)}, u32[]{:S(2)}, u32[]{:S(2)}) collective-permute-start(bf16[2,10,64,1536]{3,2,1,0:T(8,128)(2,1)} %get-tuple-element.79), channel_id=1, source_target_pairs={{0,4},{4,0},{8,12},{12,8},{16,20},{20,16},{24,28},{28,24},{1,5},{5... | collective-permute-start | bytes 11796488 | tf_op jit(solution)/shard_map/ppermute | solution.py:411
  365.5 170.4 %collective-permute-start.42 = (bf16[2,10,2,192,256]{4,3,2,1,0:T(8,128)(2,1)}, bf16[2,10,2,192,256]{4,3,2,1,0:T(8,128)(2,1)}, u32[]{:S(2)}, u32[]{:S(2)}) collective-permute-start(bf16[2,10,2,192,256]{4,3,2,1,0:T(8,128)(2,1)} %get-tuple-element.77), channel_id=1, source_target_pairs={{0,4},{4,0},{8,12},{12,8},{16,20},{20,16},{24,28},{28,24},{1,5},{5... | collective-permute-start | bytes 11796488 | tf_op jit(solution)/shard_map/ppermute | solution.py:411
  365.5 254.4 %collective-permute-start.39 = (bf16[2,10,2,192,256]{4,3,2,1,0:T(8,128)(2,1)}, bf16[2,10,2,192,256]{4,3,2,1,0:T(8,128)(2,1)}, u32[]{:S(2)}, u32[]{:S(2)}) collective-permute-start(bf16[2,10,2,192,256]{4,3,2,1,0:T(8,128)(2,1)} %get-tuple-element.75), channel_id=1, source_target_pairs={{0,4},{4,0},{8,12},{12,8},{16,20},{20,16},{24,28},{28,24},{1,5},{5... | collective-permute-start | bytes 11796488 | tf_op jit(solution)/shard_map/ppermute | solution.py:411
  371.9 254.5 %collective-permute-start.9 = (bf16[4,320,1536]{2,1,0:T(8,128)(2,1)}, bf16[4,320,1536]{2,1,0:T(8,128)(2,1)}, u32[]{:S(2)}, u32[]{:S(2)}) collective-permute-start(bf16[4,320,1536]{2,1,0:T(8,128)(2,1)} %get-tuple-element.51), channel_id=1, source_target_pairs={{0,1},{1,0},{2,3},{3,2},{4,5},{5,4},{6,7},{7,6},{8,9},{9,8},{10,11... | collective-permute-start | bytes 11796488 | tf_op jit(solution)/shard_map/ppermute | solution.py:411
  373.0 266.2 %collective-permute-start.14 = (bf16[4,320,1664]{2,1,0:T(8,128)(2,1)}, bf16[4,320,1664]{2,1,0:T(8,128)(2,1)}, u32[]{:S(2)}, u32[]{:S(2)}) collective-permute-start(bf16[4,320,1664]{2,1,0:T(8,128)(2,1)} %get-tuple-element.54), channel_id=1, source_target_pairs={{0,1},{1,0},{2,3},{3,2},{4,5},{5,4},{6,7},{7,6},{8,9},{9,8},{10,11... | collective-permute-start | bytes 12779528 | tf_op jit(solution)/shard_map/ppermute | solution.py:411
  457.8 354.3 %collective-permute-start.46 = (bf16[10,64,1536]{2,1,0:T(8,128)(2,1)}, bf16[10,64,1536]{2,1,0:T(8,128)(2,1)}, u32[]{:S(2)}, u32[]{:S(2)}) collective-permute-start(bf16[10,64,1536]{2,1,0:T(8,128)(2,1)} %fusion.8), channel_id=1, source_target_pairs={{0,16},{4,20},{8,24},{12,28},{16,0},{20,4},{24,8},{28,12},{1,17},{... | collective-permute-start | bytes 5898248 | tf_op jit(solution)/shard_map/ppermute | solution.py:411
  541.1 246.2 %collective-permute-start.43 = (bf16[10,2,192,256]{3,2,1,0:T(8,128)(2,1)}, bf16[10,2,192,256]{3,2,1,0:T(8,128)(2,1)}, u32[]{:S(2)}, u32[]{:S(2)}) collective-permute-start(bf16[10,2,192,256]{3,2,1,0:T(8,128)(2,1)} %fusion.7), channel_id=1, source_target_pairs={{0,16},{4,20},{8,24},{12,28},{16,0},{20,4},{24,8},{28,12},{1,17},{... | collective-permute-start | bytes 5898248 | tf_op jit(solution)/shard_map/ppermute | solution.py:411
  625.1 168.4 %collective-permute-start.40 = (bf16[10,2,192,256]{3,2,1,0:T(8,128)(2,1)}, bf16[10,2,192,256]{3,2,1,0:T(8,128)(2,1)}, u32[]{:S(2)}, u32[]{:S(2)}) collective-permute-start(bf16[10,2,192,256]{3,2,1,0:T(8,128)(2,1)} %fusion.6), channel_id=1, source_target_pairs={{0,16},{4,20},{8,24},{12,28},{16,0},{20,4},{24,8},{28,12},{1,17},{... | collective-permute-start | bytes 5898248 | tf_op jit(solution)/shard_map/ppermute | solution.py:411
  639.2 50.7 %collective-permute-start.12 = (bf16[2,160,1536]{2,1,0:T(8,128)(2,1)}, bf16[2,160,1536]{2,1,0:T(8,128)(2,1)S(1)}, u32[]{:S(2)}, u32[]{:S(2)}) collective-permute-start(bf16[2,160,1536]{2,1,0:T(8,128)(2,1)} %slice_bitcast_fusion.13), channel_id=1, source_target_pairs={{0,8},{4,12},{8,0},{12,4},{16,24},{20,28},{24,16},{28,20},{1,9},{5... | collective-permute-start | bytes 2949128 | tf_op jit(solution)/shard_map/ppermute | solution.py:411
  690.9 45.8 %collective-permute-start.17 = (bf16[2,160,1664]{2,1,0:T(8,128)(2,1)S(1)}, bf16[2,160,1664]{2,1,0:T(8,128)(2,1)S(1)}, u32[]{:S(2)}, u32[]{:S(2)}) collective-permute-start(bf16[2,160,1664]{2,1,0:T(8,128)(2,1)S(1)} %slice_bitcast_fusion.9), channel_id=1, source_target_pairs={{0,8},{4,12},{8,0},{12,4},{16,24},{20,28},{24,16},{28,20},{1,9},{5... | collective-permute-start | bytes 3194888 | tf_op jit(solution)/shard_map/ppermute | solution.py:411
  696.6 50.5 %collective-permute-start.11 = (bf16[160,1536]{1,0:T(8,128)(2,1)S(1)}, bf16[160,1536]{1,0:T(8,128)(2,1)S(1)}, u32[]{:S(2)}, u32[]{:S(2)}) collective-permute-start(bf16[160,1536]{1,0:T(8,128)(2,1)S(1)} %fusion.33), channel_id=1, source_target_pairs={{0,8},{4,12},{8,0},{12,4},{16,24},{20,28},{24,16},{28,20},{1,9},{5... | collective-permute-start | bytes 1474568 | tf_op jit(solution)/shard_map/ppermute | solution.py:411
  779.1 60.1 %collective-permute-start.34 = (bf16[16,48,1536]{2,1,0:T(8,128)(2,1)}, bf16[16,48,1536]{2,1,0:T(8,128)(2,1)}, u32[]{:S(2)}, u32[]{:S(2)}) collective-permute-start(bf16[16,48,1536]{2,1,0:T(8,128)(2,1)} %get-tuple-element.73), channel_id=1, source_target_pairs={{0,1},{1,0},{2,3},{3,2},{4,5},{5,4},{6,7},{7,6},{8,9},{9,8},{10,11... | collective-permute-start | bytes 7077896 | tf_op jit(solution)/shard_map/ppermute | solution.py:411
  781.6 55.1 %all-to-all-start.2 = ((bf16[8,320,192]{1,2,0:T(8,128)(2,1)}), bf16[8,320,192]{1,2,0:T(8,128)(2,1)}, u32[]{:S(2)}, u32[]{:S(2)}) async-start(bf16[8,320,192]{1,2,0:T(8,128)(2,1)} %copy.127), calls=%async_computation.2 | async-start | bytes 2359296 | tf_op jit(solution)/shard_map/all_to_all | solution.py:1268
  791.5 38.5 %collective-permute-start.44 = (bf16[10,192,256]{2,1,0:T(8,128)(2,1)}, bf16[10,192,256]{2,1,0:T(8,128)(2,1)S(1)}, u32[]{:S(2)}, u32[]{:S(2)}) collective-permute-start(bf16[10,192,256]{2,1,0:T(8,128)(2,1)} %fusion.20), channel_id=1, source_target_pairs={{0,8},{4,12},{8,0},{12,4},{16,24},{20,28},{24,16},{28,20},{1,9},{5... | collective-permute-start | bytes 2949128 | tf_op jit(solution)/shard_map/ppermute | solution.py:411
  808.9 101.2 %collective-permute-start.41 = (bf16[10,192,256]{2,1,0:T(8,128)(2,1)}, bf16[10,192,256]{2,1,0:T(8,128)(2,1)}, u32[]{:S(2)}, u32[]{:S(2)}) collective-permute-start(bf16[10,192,256]{2,1,0:T(8,128)(2,1)} %fusion.19), channel_id=1, source_target_pairs={{0,8},{4,12},{8,0},{12,4},{16,24},{20,28},{24,16},{28,20},{1,9},{5... | collective-permute-start | bytes 2949128 | tf_op jit(solution)/shard_map/ppermute | solution.py:411
  841.9 50.0 %collective-permute-start.35 = (bf16[2,2,2,48,1536]{4,3,0,1,2:T(8,128)(2,1)S(1)}, bf16[2,2,2,48,1536]{4,3,0,1,2:T(8,128)(2,1)}, u32[]{:S(2)}, u32[]{:S(2)}) collective-permute-start(bf16[2,2,2,48,1536]{4,3,0,1,2:T(8,128)(2,1)S(1)} %fusion.13), channel_id=1, source_target_pairs={{0,2},{1,3},{2,0},{3,1},{4,6},{5,7},{6,4},{7,5},{8,10},{9,11},{10,... | collective-permute-start | bytes 3538952 | tf_op jit(solution)/shard_map/ppermute | solution.py:411
  886.8 57.2 %all-to-all-start.3 = ((bf16[8,320,320]{2,1,0:T(8,128)(2,1)}), bf16[8,320,320]{2,1,0:T(8,128)(2,1)S(1)}, u32[]{:S(2)}, u32[]{:S(2)}) async-start(bf16[8,320,320]{2,1,0:T(8,128)(2,1)} %bitcast.228), calls=%async_computation.3 | async-start | bytes 3932160 | tf_op jit(solution)/shard_map/all_to_all | solution.py:1274
  891.4 172.4 %reduce-scatter.4.cloned.1.call-start = ((), (), s32[]{:S(2)}) async-start(), calls=%async_computation.5 | async-start | bytes 811008
  955.3 111.9 %collective-permute-start.19 = (bf16[16,48,768]{2,1,0:T(8,128)(2,1)}, bf16[16,48,768]{2,1,0:T(8,128)(2,1)}, u32[]{:S(2)}, u32[]{:S(2)}) collective-permute-start(bf16[16,48,768]{2,1,0:T(8,128)(2,1)} %get-tuple-element.65), channel_id=1, source_target_pairs={{0,1},{1,0},{2,3},{3,2},{4,5},{5,4},{6,7},{7,6},{8,9},{9,8},{10,11... | collective-permute-start | bytes 3538952 | tf_op jit(solution)/shard_map/ppermute | solution.py:411
  959.7 114.0 %collective-permute-start.29 = (bf16[16,48,1024]{2,1,0:T(8,128)(2,1)}, bf16[16,48,1024]{2,1,0:T(8,128)(2,1)}, u32[]{:S(2)}, u32[]{:S(2)}) collective-permute-start(bf16[16,48,1024]{2,1,0:T(8,128)(2,1)} %get-tuple-element.69), channel_id=1, source_target_pairs={{0,1},{1,0},{2,3},{3,2},{4,5},{5,4},{6,7},{7,6},{8,9},{9,8},{10,11... | collective-permute-start | bytes 4718600 | tf_op jit(solution)/shard_map/ppermute | solution.py:411
  959.7 110.8 %collective-permute-start.24 = (bf16[16,48,768]{2,1,0:T(8,128)(2,1)}, bf16[16,48,768]{2,1,0:T(8,128)(2,1)}, u32[]{:S(2)}, u32[]{:S(2)}) collective-permute-start(bf16[16,48,768]{2,1,0:T(8,128)(2,1)} %get-tuple-element.67), channel_id=1, source_target_pairs={{0,1},{1,0},{2,3},{3,2},{4,5},{5,4},{6,7},{7,6},{8,9},{9,8},{10,11... | collective-permute-start | bytes 3538952 | tf_op jit(solution)/shard_map/ppermute | solution.py:411
  (91 other events, 1501.6 us)
Sparse Core Ops, SparseCore 0:
  971.2 92.5 reduce-scatter.3

commit v2 on v1

--- a/solution.py
+++ b/solution.py
@@ -1,3 +1,4 @@
+import functools
 import math
 
 import jax
@@ -416,6 +417,10 @@
     return swap(values, axis, mask)
 
 
+def fence(*values):
+    return lax.optimization_barrier(values)
+
+
 C_BIT = ("expert", BIT_C)
 X_BIT = ("expert", BIT_X)
 Y_BIT = ("dp", BIT_Y)
@@ -689,6 +694,15 @@
     wu1_ref,
     wd0_ref,
     wd1_ref,
+    *refs,
+    first,
+):
+    if first:
+        mix_prior = dx_prior = None
+    else:
+        mix_prior, dx_prior = refs[0:2], refs[2:4]
+        refs = refs[4:]
+    (
     mix_keep,
     mix_send,
     dx_keep,
@@ -704,16 +718,17 @@
     gate_s,
     wide_s,
     tall_s,
-):
+    ) = refs
     step = pl.program_id(0)
     sources = map_ref.shape[0]
     experts = xs.shape[0]
+    low = 0 if first else experts
     tokens = x_ref.shape[1]
     rows = experts * SLOTS
     count = WIDTH // CHUNK
 
     def one_hot(source):
-        slots = map_ref[source, 0:experts, :]
+        slots = map_ref[source, low : low + experts, :]
         wide = jnp.broadcast_to(slots[:, None, :], (experts, SLOTS, tokens))
         rank = lax.broadcasted_iota(jnp.int32, (experts, SLOTS, tokens), 1).astype(F32)
         return (wide == rank).astype(F32).reshape(rows, tokens)
@@ -728,7 +743,7 @@
         raised = jnp.where(chosen, raised, 0.0)
         gates = raised / jnp.sum(raised, axis=0, keepdims=True)
         pick = one_hot(step)
-        wide = jnp.broadcast_to(gates[0:experts, None, :], (experts, SLOTS, tokens))
+        wide = jnp.broadcast_to(gates[low : low + experts, None, :], (experts, SLOTS, tokens))
         gate_rows = jnp.sum(pick * wide.reshape(rows, tokens), axis=1, keepdims=True)
         pick = pick.astype(BF)
         here = pl.ds(pl.multiple_of(step * SLOTS, SLOTS), SLOTS)
@@ -783,10 +798,10 @@
             for z in range(2):
                 for low in range(2):
                     base = ((zh_at ^ z) * 2 + (zl_at ^ low)) * 2
-                    keep[z, 0, low] = tall_s[
+                    keep[z, low, 0] = tall_s[
                         pl.ds(pl.multiple_of((base + y_at) * part, part), part), :
                     ]
-                    send[z, 0, low] = tall_s[
+                    send[z, low, 0] = tall_s[
                         pl.ds(pl.multiple_of((base + (1 - y_at)) * part, part), part), :
                     ]
 
@@ -803,38 +818,47 @@
             d_x = dot_nt(d_gate, w_gate[cols]) + dot_nt(d_up, w_up[cols])
             xs[e, :, cols] = d_x.astype(BF)
 
-    def combine(source, mix_out, dx_out):
+    def combine(source, mix_out, dx_out, mix_in, dx_in):
+        def put(out, prior, cols, values):
+            if prior is not None:
+                values += prior[0, :, cols].astype(F32)
+            out[0, :, cols] = values.astype(BF)
+
         here = pl.ds(pl.multiple_of(source * SLOTS, SLOTS), SLOTS)
         pick = one_hot(source).astype(BF)
         for n in range(count):
             cols = slice(n * CHUNK, (n + 1) * CHUNK)
-            dx_out[0, :, cols] = dot_tn(pick, xs[:, here, cols].reshape(rows, CHUNK)).astype(BF)
-            mix_out[0, :, cols] = dot_tn(pick, gs[:, here, cols].reshape(rows, CHUNK)).astype(BF)
+            put(dx_out, dx_in, cols, dot_tn(pick, xs[:, here, cols].reshape(rows, CHUNK)))
+            put(mix_out, mix_in, cols, dot_tn(pick, gs[:, here, cols].reshape(rows, CHUNK)))
         values = gate_s[:, here, :].reshape(rows, 1)
         column = lax.broadcasted_iota(jnp.int32, (rows, LANES), 1)
         owner = lax.broadcasted_iota(jnp.int32, (rows, LANES), 0) // SLOTS
-        spread_out = jnp.where(column == owner + place_ref[4], values, 0.0).astype(BF)
-        dx_out[0, :, WIDTH:] = dot_tn(pick, spread_out).astype(BF)
+        spread_out = jnp.where(column == owner + (place_ref[4] + low), values, 0.0).astype(BF)
+        put(dx_out, dx_in, slice(WIDTH, WIDTH + LANES), dot_tn(pick, spread_out))
 
     @pl.when((step >= sources + experts) & (step < sources + experts + sources // 2))
     def _():
-        combine(step - experts - sources // 2, mix_send, dx_send)
+        source = step - experts - sources // 2
+        prior = (None, None) if first else (mix_prior[1], dx_prior[1])
+        combine(source, mix_send, dx_send, *prior)
 
     @pl.when(step >= sources + experts + sources // 2)
     def _():
-        combine(step - experts - sources - sources // 2, mix_keep, dx_keep)
-
-
-def run_experts(place, x_all, g_all, maps, wr_t, w_gate, w_up, w_down):
+        source = step - experts - sources - sources // 2
+        prior = (None, None) if first else (mix_prior[0], dx_prior[0])
+        combine(source, mix_keep, dx_keep, *prior)
+
+
+def run_experts(place, x_all, g_all, maps, wr_t, w_gate, w_up, w_down, prior=()):
     sources, tokens, width = x_all.shape
-    experts = w_gate.shape[0]
+    experts = w_gate.shape[0] // 2
+    low = experts if prior else 0
     ffe = w_gate.shape[2]
     part = ffe // 8
     quarter = width // 8
     half = ffe // 2
     slots = sources * SLOTS
     extra = width + LANES
-    first = sources
     second = sources + experts
     third = second + sources // 2
 
@@ -842,33 +866,42 @@
         return jnp.clip(i - low, 0, size - 1)
 
     def expert_of(i):
-        return at(i, first, experts)
+        return at(i, sources, experts)
 
     def w_cols(block):
-        return pl.BlockSpec((1, width, LANES), lambda i, p: (expert_of(i), 0, p[0] + 2 * block))
+        return pl.BlockSpec(
+            (1, width, LANES), lambda i, p: (expert_of(i) + low, 0, p[0] + 2 * block)
+        )
 
     def w_rows(block):
-        return pl.BlockSpec((1, LANES, width), lambda i, p: (expert_of(i), p[0] + 2 * block, 0))
+        return pl.BlockSpec(
+            (1, LANES, width), lambda i, p: (expert_of(i) + low, p[0] + 2 * block, 0)
+        )
 
     token_spec = pl.BlockSpec(
         (1, tokens, width),
         lambda i, p: (at(i, 0, sources), 0, 0),
-        pipeline_mode=pl.Buffered(1),
     )
 
     def out_tokens(low, cols):
         return pl.BlockSpec((1, tokens, cols), lambda i, p: (at(i, low, sources // 2), 0, 0))
 
     tall_spec = pl.BlockSpec(
-        (2, 1, 2, quarter, half), lambda i, p: (0, expert_of(i), 0, 0, 0)
+        (2, 2, 1, quarter, half), lambda i, p: (0, 0, expert_of(i), 0, 0)
     )
     wide_spec = pl.BlockSpec((2, 1, part, width), lambda i, p: (0, expert_of(i), 0, 0))
-    tall = jax.ShapeDtypeStruct((2, experts, 2, quarter, half), BF)
+    tall = jax.ShapeDtypeStruct((2, 2, experts, quarter, half), BF)
     wide = jax.ShapeDtypeStruct((2, experts, part, width), BF)
     mixed = jax.ShapeDtypeStruct((sources // 2, tokens, width), BF)
     d_x = jax.ShapeDtypeStruct((sources // 2, tokens, extra), BF)
+    sums = (
+        out_tokens(third, width),
+        out_tokens(second, width),
+        out_tokens(third, extra),
+        out_tokens(second, extra),
+    )
     return pl.pallas_call(
-        expert_kernel,
+        functools.partial(expert_kernel, first=not prior),
         grid_spec=pltpu.PrefetchScalarGridSpec(
             num_scalar_prefetch=1,
             grid=(third + sources // 2,),
@@ -883,12 +916,10 @@
                 w_cols(1),
                 w_rows(0),
                 w_rows(1),
+                *(sums if prior else ()),
             ],
             out_specs=(
-                out_tokens(third, width),
-                out_tokens(second, width),
-                out_tokens(third, extra),
-                out_tokens(second, extra),
+                *sums,
                 tall_spec,
                 tall_spec,
                 tall_spec,
@@ -905,9 +936,9 @@
             ],
         ),
         out_shape=(mixed, mixed, d_x, d_x, tall, tall, tall, tall, wide, wide),
-        compiler_params=params(63, ("arbitrary",)),
-        cost_estimate=cost(60e9, 90e6),
-    )(place, x_all, g_all, maps, wr_t, w_gate, w_gate, w_up, w_up, w_down, w_down)
+        compiler_params=params(56, ("arbitrary",)),
+        cost_estimate=cost(30e9, 60e6),
+    )(place, x_all, g_all, maps, wr_t, w_gate, w_gate, w_up, w_up, w_down, w_down, *prior)
 
 
 def post_kernel(
@@ -1006,9 +1037,7 @@
     )(place, left, right)
 
 
-def qkvgrad_kernel(
-    place_ref, a_ref, d_ref, full_ref, keep0, send0, keep1, send1, keep2, send2, held
-):
+def qkvgrad_kernel(place_ref, a_ref, d_ref, full_ref, keep, send, held):
     step = pl.program_id(0)
 
     @pl.when(step == 0)
@@ -1026,33 +1055,15 @@
 
     cols = pl.ds(pl.multiple_of(step * 256, 256), 256)
     held[...] = dot_tn(a_ref[...], full_ref[:, cols]).astype(BF)
-
-    @pl.when(step < 3)
-    def _():
-        put_rows(place_ref, held, keep0, send0)
-
-    @pl.when((step >= 3) & (step < 6))
-    def _():
-        put_rows(place_ref, held, keep1, send1)
-
-    @pl.when(step >= 6)
-    def _():
-        put_rows(place_ref, held, keep2, send2)
+    put_rows(place_ref, held, keep, send)
 
 
 def run_qkvgrad(place, normed, d_pack, blocks):
     tokens, rows = normed.shape
     cols = KV_HEADS * PACK
     part = rows // blocks
-
-    def spec(low, size):
-        return pl.BlockSpec(
-            (blocks // 2, part, 256), lambda i, p: (0, 0, jnp.clip(i - low, 0, size - 1))
-        )
-
-    def shape(size):
-        return jax.ShapeDtypeStruct((blocks // 2, part, size * 256), BF)
-
+    spec = pl.BlockSpec((blocks // 2, part, 256), lambda i, p: (0, 0, i))
+    shape = jax.ShapeDtypeStruct((blocks // 2, part, cols), BF)
     return pl.pallas_call(
         qkvgrad_kernel,
         grid_spec=pltpu.PrefetchScalarGridSpec(
@@ -1062,26 +1073,10 @@
                 pl.BlockSpec((tokens, rows), lambda i, p: (0, 0)),
                 pl.BlockSpec(d_pack.shape, lambda i, p: (0, 0, 0)),
             ],
-            out_specs=(
-                pl.BlockSpec((tokens, cols), lambda i, p: (0, 0)),
-                spec(0, 3),
-                spec(0, 3),
-                spec(3, 3),
-                spec(3, 3),
-                spec(6, 4),
-                spec(6, 4),
-            ),
+            out_specs=(pl.BlockSpec((tokens, cols), lambda i, p: (0, 0)), spec, spec),
             scratch_shapes=[pltpu.VMEM((rows, 256), BF)],
         ),
-        out_shape=(
-            jax.ShapeDtypeStruct((tokens, cols), BF),
-            shape(3),
-            shape(3),
-            shape(3),
-            shape(3),
-            shape(4),
-            shape(4),
-        ),
+        out_shape=(jax.ShapeDtypeStruct((tokens, cols), BF), shape, shape),
         compiler_params=params(40, ("arbitrary",)),
         cost_estimate=cost(2 * tokens * rows * cols, 12e6),
     )(place, normed, d_pack)
@@ -1117,66 +1112,399 @@
     )(d_full, w_query, w_key, w_value, d_middle, inputs, gain[None])
 
 
-def gather_relative(values):
-    held = values[None]
-    for bit in (X_BIT, ZL_BIT, C_BIT):
-        held = jnp.concatenate([held, swap_bit(held, bit)], axis=0)
-    return held
+def small_kernel(place_ref, norm_ref, dlog_ref, gmlp_ref, gattn_ref, keep, send, held):
+    columns = dot_tn(norm_ref[...], dlog_ref[...])
+    lane = lax.broadcasted_iota(jnp.int32, columns.shape, 1)
+    for n, ref in enumerate((gmlp_ref, gattn_ref)):
+        turned = jnp.broadcast_to(ref[...], (8, ref.shape[1])).T[:, 0:1]
+        columns = jnp.where(lane == LANES - 2 + n, turned, columns)
+    held[...] = columns
+    put_rows(place_ref, held, keep, send)
+
+
+def run_small(place, normed_two, d_log, ggain_mlp, ggain_attn, blocks):
+    part = WIDTH // blocks
+    shape = jax.ShapeDtypeStruct((blocks // 2, part, LANES), F32)
+    smem = pl.BlockSpec(memory_space=pltpu.SMEM)
+    vmem = pl.BlockSpec(memory_space=pltpu.VMEM)
+    return pl.pallas_call(
+        small_kernel,
+        in_specs=[smem] + [vmem] * 4,
+        out_shape=(shape, shape),
+        scratch_shapes=[pltpu.VMEM((WIDTH, LANES), F32)],
+        compiler_params=params(24),
+        cost_estimate=cost(1e8, 3e6),
+    )(place, normed_two, d_log, ggain_mlp, ggain_attn)
+
+
+def stack_swap(values, bit):
+    return jnp.concatenate([values, swap_bit(values, bit)], axis=0)
+
+
+MESH = pl.DeviceIdType.MESH
+
+
+def peer_of(bit):
+    axis, mask = bit
+    return {axis: lax.axis_index(axis) ^ mask}
+
+
+def greet(ids):
+    barrier = pltpu.get_barrier_semaphore()
+    for device in ids:
+        pl.semaphore_signal(barrier, inc=1, device_id=device, device_id_type=MESH)
+    pl.semaphore_wait(barrier, len(ids))
+
+
+GATHER_BITS = (X_BIT, ZL_BIT, C_BIT)
+
+
+def gather_steps(x_ref, all_ref, send_sem, recv_sem, local_sem):
+    half = x_ref.shape[0] // 2
+    own = pltpu.make_async_copy(x_ref, all_ref.at[0], local_sem)
+    own.start()
+    copies = []
+
+    def send(source, slot, rows, bit):
+        n = len(copies)
+        copy = pltpu.make_async_remote_copy(
+            src_ref=source if rows is None else source.at[rows],
+            dst_ref=all_ref.at[slot] if rows is None else all_ref.at[slot, rows],
+            send_sem=send_sem.at[n],
+            recv_sem=recv_sem.at[n],
+            device_id=peer_of(bit),
+            device_id_type=MESH,
+        )
+        copy.start()
+        copies.append(copy)
+        return copy
+
+    top, low = pl.ds(0, half), pl.ds(half, half)
+    x_top = send(x_ref, 1, top, X_BIT)
+    z_low = send(x_ref, 2, low, ZL_BIT)
+    x_low = send(x_ref, 1, low, X_BIT)
+    z_top = send(x_ref, 2, top, ZL_BIT)
+    last = [send(x_ref, 4, None, C_BIT)]
+    x_top.wait_recv()
+    far_top = send(all_ref.at[1], 3, top, ZL_BIT)
+    z_low.wait_recv()
+    far_low = send(all_ref.at[2], 3, low, X_BIT)
+    x_low.wait_recv()
+    last.append(send(all_ref.at[1], 5, None, C_BIT))
+    z_top.wait_recv()
+    last.append(send(all_ref.at[2], 6, None, C_BIT))
+    far_top.wait_recv()
+    far_low.wait_recv()
+    last.append(send(all_ref.at[3], 7, None, C_BIT))
+    for copy in last:
+        copy.wait_recv()
+    for copy in copies:
+        copy.wait_send()
+    own.wait()
+
+
+def gather_kernel(*refs):
+    x_ref, blocks = refs[0], refs[1:5]
+    all_ref, other_ref = refs[5:7]
+    send_sem, recv_sem, more_send, more_recv, local_sem = refs[7:]
+    greet([peer_of(bit) for bit in GATHER_BITS])
+    local = []
+    remote = []
+    for n, block in enumerate(blocks):
+        copy = pltpu.make_async_remote_copy(
+            src_ref=block,
+            dst_ref=other_ref.at[4 + n],
+            send_sem=more_send.at[n],
+            recv_sem=more_recv.at[n],
+            device_id=peer_of(C_BIT),
+            device_id_type=MESH,
+        )
+        copy.start()
+        remote.append(copy)
+        copy = pltpu.make_async_copy(block, other_ref.at[n], local_sem.at[1 + n])
+        copy.start()
+        local.append(copy)
+    gather_steps(x_ref, all_ref, send_sem, recv_sem, local_sem.at[0])
+    for copy in local:
+        copy.wait()
+    for copy in remote:
+        copy.wait()
+
+
+def run_gather(values, blocks):
+    tokens, width = values.shape
+    hbm = pl.BlockSpec(memory_space=pl.ANY)
+    shape = jax.ShapeDtypeStruct((8, tokens, width), values.dtype)
+    return pl.pallas_call(
+        gather_kernel,
+        in_specs=[hbm] * 5,
+        out_specs=(hbm, hbm),
+        out_shape=(shape, shape),
+        scratch_shapes=[pltpu.SemaphoreType.DMA((n,)) for n in (10, 10, 4, 4, 5)],
+        compiler_params=pltpu.CompilerParams(
+            collective_id=1, has_side_effects=True, vmem_limit_bytes=16 * MIB
+        ),
+        cost_estimate=cost(0, 150e6),
+    )(values, *blocks)
+
+
+def trade_peers(size):
+    me = lax.axis_index("dp")
+    return [{"dp": me ^ k} for k in range(size - 1, 0, -1)]
+
+
+def trade_start(a_ref, out_ref, send_sem, recv_sem, local_sem):
+    me = lax.axis_index("dp")
+    copies = []
+    for n, device in enumerate(trade_peers(a_ref.shape[0])):
+        copy = pltpu.make_async_remote_copy(
+            src_ref=a_ref.at[device["dp"]],
+            dst_ref=out_ref.at[me],
+            send_sem=send_sem.at[n],
+            recv_sem=recv_sem.at[n],
+            device_id=device,
+            device_id_type=MESH,
+        )
+        copy.start()
+        copies.append(copy)
+    own = pltpu.make_async_copy(a_ref.at[me], out_ref.at[me], local_sem)
+    own.start()
+    return copies, own
+
+
+def trade_end(copies, own):
+    own.wait()
+    for copy in copies:
+        copy.wait_recv()
+    for copy in copies:
+        copy.wait_send()
+
+
+def trade_kernel(a_ref, out_ref, send_sem, recv_sem, local_sem):
+    greet(trade_peers(a_ref.shape[0]))
+    trade_end(*trade_start(a_ref, out_ref, send_sem, recv_sem, local_sem.at[0]))
+
+
+def run_trade(values, number):
+    size = values.shape[0]
+    return pl.pallas_call(
+        trade_kernel,
+        in_specs=[pl.BlockSpec(memory_space=pl.ANY)],
+        out_specs=pl.BlockSpec(memory_space=pl.ANY),
+        out_shape=jax.ShapeDtypeStruct(values.shape, values.dtype),
+        scratch_shapes=[
+            pltpu.SemaphoreType.DMA((size - 1,)),
+            pltpu.SemaphoreType.DMA((size - 1,)),
+            pltpu.SemaphoreType.DMA((1,)),
+        ],
+        compiler_params=pltpu.CompilerParams(
+            collective_id=number, has_side_effects=True, vmem_limit_bytes=8 * MIB
+        ),
+        cost_estimate=cost(0, 170e6),
+    )(values)
+
+
+def reduce_chain(job, part, keep_ref, send_ref, out_ref, acc, got, staged, send_sem, recv_sem):
+    bits, row, rows, column, columns, order = part
+    blocks = keep_ref.shape[0]
+    stages = len(bits) + 1
+    low = send_ref.dtype
+    at = (pl.ds(row, rows), pl.ds(column, columns))
+    copies = []
+
+    def exchange(source, target, bit):
+        n = job * stages + len(copies)
+        copy = pltpu.make_async_remote_copy(
+            src_ref=source,
+            dst_ref=target,
+            send_sem=send_sem.at[n],
+            recv_sem=recv_sem.at[n],
+            device_id=peer_of(bit),
+            device_id_type=MESH,
+        )
+        copy.start()
+        copies.append(copy)
+
+    live = list(range(blocks))
+    base_got, base_sent = 0, 0
+    exchange(send_ref.at[(slice(None),) + at], got.at[(pl.ds(0, blocks),) + at], C_BIT)
+    yield
+    for stage in range(stages):
+        copies[-1].wait_recv()
+
+        def total(position):
+            index = live[position]
+            kept = keep_ref[(index,) + at].astype(F32) if stage == 0 else acc[(index,) + at]
+            return kept + got[(base_got + position,) + at].astype(F32)
+
+        if stage == stages - 1:
+            out_ref[at] = total(0)
+            break
+        mask = 1 << order[stage]
+        rest = [i for i in live if not i & mask]
+        for m, i in enumerate(rest):
+            staged[(base_sent + m,) + at] = total(live.index(i ^ mask)).astype(low)
+        exchange(
+            staged.at[(pl.ds(base_sent, len(rest)),) + at],
+            got.at[(pl.ds(base_got + len(live), len(rest)),) + at],
+            bits[order[stage]],
+        )
+        for i in rest:
+            acc[(i,) + at] = total(live.index(i))
+        base_got += len(live)
+        base_sent += len(rest)
+        live = rest
+        yield
+    for copy in copies:
+        copy.wait_send()
+
+
+def reduce_kernel(*refs, parts, bits):
+    jobs = len(parts)
+    keeps, sends, outs = refs[:jobs], refs[jobs : 2 * jobs], refs[2 * jobs : 3 * jobs]
+    scratch = refs[3 * jobs :]
+    greet([peer_of(bit) for bit in (C_BIT,) + bits])
+    send_sem, recv_sem = scratch[-2:]
+    chains, number = [], 0
+    for n in range(jobs):
+        buffers = scratch[3 * n : 3 * n + 3]
+        for part in parts[n]:
+            chains.append(
+                reduce_chain(
+                    number, (bits,) + part, keeps[n], sends[n], outs[n], *buffers, send_sem, recv_sem
+                )
+            )
+            number += 1
+    while chains:
+        rest = []
+        for chain in chains:
+            try:
+                next(chain)
+                rest.append(chain)
+            except StopIteration:
+                pass
+        chains = rest
+
+
+def run_reduce(pairs, parts, bits, number):
+    slots = sum(len(part) for part in parts) * (len(bits) + 1)
+    vmem = pl.BlockSpec(memory_space=pltpu.VMEM)
+    scratch, shapes = [], []
+    for keep, send in pairs:
+        blocks, rows, cols = keep.shape
+        scratch += [
+            pltpu.VMEM((blocks, rows, cols), F32),
+            pltpu.VMEM((2 * blocks - 1, rows, cols), send.dtype),
+            pltpu.VMEM((max(blocks - 1, 1), rows, cols), send.dtype),
+        ]
+        shapes.append(jax.ShapeDtypeStruct((rows, cols), F32))
+    return pl.pallas_call(
+        functools.partial(reduce_kernel, parts=parts, bits=bits),
+        in_specs=[vmem] * len(pairs) + [pl.BlockSpec(memory_space=pl.ANY)] * len(pairs),
+        out_specs=tuple(vmem for _ in pairs),
+        out_shape=tuple(shapes),
+        scratch_shapes=scratch
+        + [pltpu.SemaphoreType.DMA((slots,)), pltpu.SemaphoreType.DMA((slots,))],
+        compiler_params=pltpu.CompilerParams(
+            collective_id=number, has_side_effects=True, vmem_limit_bytes=56 * MIB
+        ),
+        cost_estimate=cost(0, 170e6),
+    )(*(keep for keep, _ in pairs), *(send for _, send in pairs))
 
 
 def sum_pair(kept, received):
     return kept.astype(F32) + received.astype(F32)
 
 
-def scatter_tokens(keep, send):
-    tokens, cols = keep.shape[1:]
-    got = swap_bit(send, C_BIT)
-    both = sum_pair(keep, got).reshape(2, 2, tokens, cols)
-    half = tokens // 2
-    results = []
+def first_sum(keep, got):
+    return sum_pair(keep[1], got[1]).astype(BF)
+
+
+def low_sum(keep, got, more):
+    return (sum_pair(keep[0, 1], got[0, 1]) + more[1].astype(F32)).astype(BF)
+
+
+def join_down_kernel(*refs):
+    out = refs[-1]
+    step = pl.program_id(0)
     for part in range(2):
-        rows = slice(part * half, (part + 1) * half)
-        if part == 0:
-            mine, other = both[:, 0, rows], both[:, 1, rows]
-            bits = (X_BIT, ZL_BIT)
-        else:
-            mine, other = both[0, :, rows], both[1, :, rows]
-            bits = (ZL_BIT, X_BIT)
-        held = sum_pair(mine, swap_bit(other.astype(BF), bits[0]))
-        results.append(sum_pair(held[0], swap_bit(held[1].astype(BF), bits[1])))
-    return jnp.concatenate(results, axis=0)
-
-
-BITS = {"zh": ZH_BIT, "zl": ZL_BIT, "y": Y_BIT, "x": X_BIT}
-
-
-def scatter_dense(keep, send, order, low=BF):
-    part, cols = keep.shape[1:]
-    held = sum_pair(keep, swap_bit(send, C_BIT)).reshape(2, 2, 2, 2, part, cols)
-    names = ["zh", "zl", "y", "x"]
-    for name in order:
-        axis = names.index(name)
-        mine = lax.index_in_dim(held, 0, axis, keepdims=False)
-        other = lax.index_in_dim(held, 1, axis, keepdims=False)
-        held = sum_pair(mine, swap_bit(other.astype(low), BITS[name]))
-        names.remove(name)
-    return held
-
-
-def scatter_expert(keep, send):
-    held = sum_pair(keep, swap_bit(send, Y_BIT))
-    return sum_pair(held[0], swap_bit(held[1].astype(BF), ZH_BIT))
-
-
-def join_columns(total, zl_at):
-    mine = total[:, 0]
-    other = swap_bit(total[:, 1].astype(BF), ZL_BIT).astype(F32)
-    experts, rows, cols = mine.shape
-    mine = mine.reshape(experts, rows, 2, 1, LANES)
-    other = other.reshape(experts, rows, 2, 1, LANES)
-    low = jnp.where(zl_at == 0, mine, other)
-    high = jnp.where(zl_at == 0, other, mine)
-    return jnp.concatenate([low, high], axis=3).reshape(experts, rows, 2 * cols)
+        keep, got, more = refs[3 * part : 3 * part + 3]
+
+        @pl.when((step >= 5 * part) & (step < 5 * part + 5))
+        def _():
+            total = keep[0, 0].astype(F32) + got[0, 0].astype(F32)
+            out[0] = total + more[0].astype(F32)
+
+
+def join_tall_kernel(place_ref, *refs):
+    out = refs[-1]
+    step = pl.program_id(0)
+    zl_at = place_ref[0]
+    for part in range(2):
+        keep, got, more, other = refs[4 * part : 4 * part + 4]
+
+        @pl.when((step >= 5 * part) & (step < 5 * part + 5))
+        def _():
+            total = keep[0, 0, 0].astype(F32) + got[0, 0, 0].astype(F32)
+            total += more[0, 0].astype(F32)
+            across = other[0].astype(F32)
+            for n in range(2):
+                cols = slice(n * LANES, (n + 1) * LANES)
+                mine = pl.multiple_of((2 * n + zl_at) * LANES, LANES)
+                theirs = pl.multiple_of((2 * n + 1 - zl_at) * LANES, LANES)
+                out[0, :, pl.ds(mine, LANES)] = total[:, cols]
+                out[0, :, pl.ds(theirs, LANES)] = across[:, cols]
+
+
+def run_join_down(parts):
+    experts, rows, cols = parts[0][2].shape
+    specs = []
+    for part in range(2):
+        def of(i, part=part):
+            return jnp.clip(i - part * experts, 0, experts - 1)
+
+        specs += [
+            pl.BlockSpec((1, 1, rows, cols), lambda i, of=of: (0, of(i), 0, 0)),
+            pl.BlockSpec((1, 1, rows, cols), lambda i, of=of: (0, of(i), 0, 0)),
+            pl.BlockSpec((1, rows, cols), lambda i, of=of: (of(i), 0, 0)),
+        ]
+    return pl.pallas_call(
+        join_down_kernel,
+        grid=(2 * experts,),
+        in_specs=specs,
+        out_specs=pl.BlockSpec((1, rows, cols), lambda i: (i, 0, 0)),
+        out_shape=jax.ShapeDtypeStruct((2 * experts, rows, cols), F32),
+        compiler_params=params(24, ("arbitrary",)),
+        cost_estimate=cost(1e6, 10e6),
+    )(*parts[0], *parts[1])
+
+
+def run_join_tall(place, parts):
+    experts, rows, cols = parts[0][3].shape
+    specs = []
+    for part in range(2):
+        def of(i, part=part):
+            return jnp.clip(i - part * experts, 0, experts - 1)
+
+        wide = pl.BlockSpec((1, 1, 1, rows, cols), lambda i, p, of=of: (0, 0, of(i), 0, 0))
+        specs += [
+            wide,
+            wide,
+            pl.BlockSpec((1, 1, rows, cols), lambda i, p, of=of: (0, of(i), 0, 0)),
+            pl.BlockSpec((1, rows, cols), lambda i, p, of=of: (of(i), 0, 0)),
+        ]
+    return pl.pallas_call(
+        join_tall_kernel,
+        grid_spec=pltpu.PrefetchScalarGridSpec(
+            num_scalar_prefetch=1,
+            grid=(2 * experts,),
+            in_specs=specs,
+            out_specs=pl.BlockSpec((1, rows, 2 * cols), lambda i, p: (i, 0, 0)),
+        ),
+        out_shape=jax.ShapeDtypeStruct((2 * experts, rows, 2 * cols), F32),
+        compiler_params=params(24, ("arbitrary",)),
+        cost_estimate=cost(1e6, 12e6),
+    )(place, *parts[0], *parts[1])
 
 
 def fast_body(
@@ -1222,9 +1550,6 @@
     before = jnp.sum((rank_map[:, None, :] < rank_map[:, :, None]).astype(jnp.int32), axis=-1)
     slot_map = jnp.where(rank_map < far, jnp.minimum(before, SLOTS), -1).astype(BF)
     map_rows = jnp.pad(slot_map.T.astype(F32), ((0, 0), (0, LANES - all_experts)), constant_values=-1.0)
-    maps = gather_relative(slot_map).astype(F32)
-    maps = jnp.roll(maps, -column * local_experts, axis=1)
-    g_all = gather_relative(cotangent.astype(BF))
     wr_pad = jnp.pad(w_router, ((0, 0), (0, LANES - all_experts)))
     wr_t = jnp.roll(w_router.T, -column * local_experts, axis=0)
     wr_t = jnp.pad(wr_t, ((0, LANES - all_experts), (0, 0)))
@@ -1239,60 +1564,137 @@
     cos_t, sin_t = jnp.cos(angles), jnp.sin(angles)
 
     normed, pack = run_pre(inputs, gain_attn, w_query, w_key, w_value, cos_tab, sin_tab)
-    pack = lax.all_to_all(pack, "dp", 0, 0, tiled=True).reshape(length, PACK)
+    g_own = cotangent.astype(BF)
+    pack, g_own, slot_map = fence(pack, g_own, slot_map)
+    g_x = swap_bit(g_own, X_BIT)
+    maps = stack_swap(slot_map[None], X_BIT)
+    pack = run_trade(pack, 2).reshape(length, PACK)
+    pack, g_x, maps, g_own = fence(pack, g_x, maps, g_own)
+    g_z = swap_bit(g_own, ZL_BIT)
+    maps = stack_swap(maps, ZL_BIT)
     out, out_t, lse = run_forward(pack)
-    att = lax.all_to_all(out.reshape(shards, tokens, ROWS_Q), "dp", 0, 0, tiled=True)
+    out, g_z, maps = fence(out, g_z, maps)
+    g_zx = swap_bit(g_z, X_BIT)
+    maps = stack_swap(maps, C_BIT)
+    att = run_trade(out.reshape(shards, tokens, ROWS_Q), 3)
+    att, g_zx, maps = fence(att, g_zx, maps)
+    maps = jnp.roll(maps.astype(F32), -column * local_experts, axis=1)
     middle, normed_two, att_full = run_mid(att, w_output, inputs, gain_mlp)
-    x_all = gather_relative(normed_two)
+    x_all, g_all = run_gather(normed_two, (g_own, g_x, g_z, g_zx))
+    expert_args = (place, x_all, g_all, maps, wr_t, w_gate, w_up, w_down)
+    *sums, gate_ka, gate_sa, up_ka, up_sa, down_ka, down_sa = run_experts(*expert_args)
+    down_ga = swap_bit(down_sa, Y_BIT)
     (
         mix_keep,
         mix_send,
         dx_keep,
         dx_send,
-        gate_keep,
-        gate_send,
-        up_keep,
-        up_send,
-        down_keep,
-        down_send,
-    ) = run_experts(place, x_all, g_all, maps, wr_t, w_gate, w_up, w_down)
-    dx_sum = scatter_tokens(dx_keep, dx_send)
-    hidden_out = middle + scatter_tokens(mix_keep, mix_send)
-    gate_total = join_columns(scatter_expert(gate_keep, gate_send), zl_at)
-    up_total = join_columns(scatter_expert(up_keep, up_send), zl_at)
-    down_total = scatter_expert(down_keep, down_send)
-
+        gate_kb,
+        gate_sb,
+        up_kb,
+        up_sb,
+        down_kb,
+        down_sb,
+    ) = run_experts(*expert_args, prior=tuple(sums))
+    dx_send, gate_sa, down_ga, mix_send = fence(dx_send, gate_sa, down_ga, mix_send)
+    down_ma = swap_bit(first_sum(down_ka, down_ga), ZH_BIT)
+    gate_ga = swap_bit(gate_sa, Y_BIT)
+    quarter = tokens // 4
+    extra = dx_keep.shape[2]
+    token_parts = tuple((n * quarter, quarter, 0, extra, (0, 1)) for n in range(4))
+    (dx_sum,) = run_reduce(((dx_keep, dx_send),), (token_parts,), (X_BIT, ZL_BIT), 6)
+    dx_sum, gate_ga, down_ma = fence(dx_sum, gate_ga, down_ma)
     d_att, d_middle, d_low, d_log, ggain_mlp = run_post(
         dx_sum, middle, cotangent, normed_two, wr_pad, map_rows, gain_mlp, w_output
     )
-    d_out = lax.all_to_all(d_att, "dp", 0, 0, tiled=True).reshape(length, ROWS_Q)
+    mix_got = swap_bit(mix_send, C_BIT)
     out_keep, out_send = run_outgrad(place, att_full, d_low, devices)
-    output_total = scatter_dense(out_keep, out_send, ("x", "y", "zl", "zh"))
-    router_part = dot_tn(normed_two, d_log)[:, :all_experts]
-
+    d_att, up_sa, out_send, mix_got = fence(d_att, up_sa, out_send, mix_got)
+    gate_ma = swap_bit(first_sum(gate_ka, gate_ga), ZH_BIT)
+    up_ga = swap_bit(up_sa, Y_BIT)
+    out_got = swap_bit(out_send, C_BIT)
+    mix_keep = mix_keep.reshape(2, 2, tokens, WIDTH)
+    mix_got = mix_got.reshape(2, 2, tokens, WIDTH)
+    mix_x = swap_bit(sum_pair(mix_keep[:, 1], mix_got[:, 1]).astype(BF), X_BIT)
+    d_out = run_trade(d_att, 4).reshape(length, ROWS_Q)
+    d_out, up_ga, gate_ma, gate_sb, mix_x, out_got = fence(
+        d_out, up_ga, gate_ma, gate_sb, mix_x, out_got
+    )
+    up_ma = swap_bit(first_sum(up_ka, up_ga), ZH_BIT)
+    gate_gb = swap_bit(gate_sb, Y_BIT)
+    gate_oa = swap_bit(low_sum(gate_ka, gate_ga, gate_ma), ZL_BIT)
+    mix_z = swap_bit(
+        (sum_pair(mix_keep[1, 0], mix_got[1, 0]) + mix_x[1].astype(F32)).astype(BF), ZL_BIT
+    )
+    split = (2, 2, 2, 2, WIDTH // devices, WIDTH)
+    out_keep, out_got = out_keep.reshape(split), out_got.reshape(split)
+    out_x = swap_bit(sum_pair(out_keep[:, :, :, 1], out_got[:, :, :, 1]).astype(BF), X_BIT)
     d_pack = run_backward(pack, d_out, out_t, lse, cos_t, sin_t)
-    d_pack = lax.all_to_all(
-        d_pack.reshape(shards, tokens, PACK), "dp", 0, 0, tiled=True
-    )
-    d_full, keep0, send0, keep1, send1, keep2, send2 = run_qkvgrad(place, normed, d_pack, devices)
-    total0 = scatter_dense(keep0, send0, ("x", "y", "zl", "zh"))
-    total1 = scatter_dense(keep1, send1, ("y", "zl", "x", "zh"))
-    total2 = scatter_dense(keep2, send2, ("zl", "x", "y", "zh"))
+    d_pack, gate_gb, up_ma, up_sb, gate_oa, mix_z, out_x = fence(
+        d_pack, gate_gb, up_ma, up_sb, gate_oa, mix_z, out_x
+    )
+    gate_mb, up_oa = first_sum(gate_kb, gate_gb), low_sum(up_ka, up_ga, up_ma)
+    out_held = sum_pair(out_keep[:, :, :, 0], out_got[:, :, :, 0]) + out_x.astype(F32)
+    out_z = out_held[:, 1].astype(BF)
+    d_pack, gate_mb, up_oa, out_z = fence(d_pack, gate_mb, up_oa, out_z)
+    gate_mb = swap_bit(gate_mb, ZH_BIT)
+    up_gb = swap_bit(up_sb, Y_BIT)
+    up_oa = swap_bit(up_oa, ZL_BIT)
+    out_z = swap_bit(out_z, ZL_BIT)
+    d_pack = run_trade(d_pack.reshape(shards, tokens, PACK), 5)
+    d_pack, up_gb, gate_mb, down_sb, up_oa, out_z = fence(
+        d_pack, up_gb, gate_mb, down_sb, up_oa, out_z
+    )
+    up_mb = swap_bit(first_sum(up_kb, up_gb), ZH_BIT)
+    down_gb = swap_bit(down_sb, Y_BIT)
+    gate_ob = swap_bit(low_sum(gate_kb, gate_gb, gate_mb), ZL_BIT)
+    out_held = out_held[:, 0] + out_z.astype(F32)
+    out_y = swap_bit(out_held[:, 1].astype(BF), Y_BIT)
+    d_full, qkv_keep, qkv_send = run_qkvgrad(place, normed, d_pack, devices)
     grad_in, ggain_attn = run_last(
         d_full, w_query, w_key, w_value, d_middle, inputs, gain_attn
     )
-    small = jnp.concatenate([router_part, ggain_mlp.T, ggain_attn.T], axis=1)
-    small = lax.psum_scatter(small, ("dp", "expert"), scatter_dimension=0, tiled=True)
+    small_keep, small_send = run_small(place, normed_two, d_log, ggain_mlp, ggain_attn, devices)
+    mixed = sum_pair(mix_keep[0, 0], mix_got[0, 0]) + sum_pair(mix_x[0], mix_z)
+    hidden_out = middle + mixed
+    qkv_send, small_send, up_mb, down_gb, gate_ob, out_y, hidden_out = fence(
+        qkv_send, small_send, up_mb, down_gb, gate_ob, out_y, hidden_out
+    )
+    down_mb = swap_bit(first_sum(down_kb, down_gb), ZH_BIT)
+    up_ob = swap_bit(low_sum(up_kb, up_gb, up_mb), ZL_BIT)
+    out_held = out_held[:, 0] + out_y.astype(F32)
+    out_h = swap_bit(out_held[1].astype(BF), ZH_BIT)
+    rows = WIDTH // devices
+    dense_parts = (
+        (0, rows, 0, 768, (0, 1, 2, 3)),
+        (0, rows, 768, 768, (1, 2, 0, 3)),
+        (0, rows, 1536, 1024, (2, 0, 1, 3)),
+    )
+    qkv_total, small = run_reduce(
+        ((qkv_keep, qkv_send), (small_keep, small_send)),
+        (dense_parts, ((0, rows, 0, LANES, (0, 1, 2, 3)),)),
+        (X_BIT, Y_BIT, ZL_BIT, ZH_BIT),
+        7,
+    )
+    qkv_total, small, down_mb, up_ob, out_h = fence(qkv_total, small, down_mb, up_ob, out_h)
+    output_total = sum_pair(out_held[0], out_h)
+    down_total = run_join_down(((down_ka, down_ga, down_ma), (down_kb, down_gb, down_mb)))
+    gate_total = run_join_tall(
+        place, ((gate_ka, gate_ga, gate_ma, gate_oa), (gate_kb, gate_gb, gate_mb, gate_ob))
+    )
+    up_total = run_join_tall(
+        place, ((up_ka, up_ga, up_ma, up_oa), (up_kb, up_gb, up_mb, up_ob))
+    )
     key_width = KV_HEADS * HEAD_DIM
     return (
         hidden_out[None],
         grad_in[None],
-        small[:, all_experts + 1],
-        jnp.concatenate([total0, total1], axis=1),
-        total2[:, :key_width],
-        total2[:, key_width:],
+        small[:, LANES - 1],
+        qkv_total[:, :WIDTH],
+        qkv_total[:, WIDTH : WIDTH + key_width],
+        qkv_total[:, WIDTH + key_width :],
         output_total,
-        small[:, all_experts],
+        small[:, LANES - 2],
         small[:, :all_experts],
         gate_total,
         up_total,

time: 1140 us -> 831 us (0.73)
  waiting for transfers between devices: 603 us -> 43.4 us
  Pallas kernels: 209 us -> 663 us
  other arithmetic: 105 us -> 44.4 us
  blocking collectives: 53.1 us -> 0 us
  local copies, waits for them, and re-layouts: 89.6 us -> 41.5 us
  starting transfers between devices: 60.5 us -> 28 us
  between operations: 15.5 us -> 1.81 us
    pallas_call x1 -> x13, Pallas kernels: 100 us -> 556 us  [the longest x4 240 us: run_trade(): pl.pallas_call(trade_kernel, in_specs=[pl.BlockSpec(memory_space=pl.ANY)]...]
    ppermute x47 -> x30, waiting for transfers between devices: 488 us -> 43.4 us  [swap(): return lax.ppermute(values, axis, [(i, i ^ mask) for i in range(size)])]
    unnamed x2 -> x0, waiting for transfers between devices: 91 us -> none
    all_to_all x1 -> x0, blocking collectives: 53.1 us -> none  [fast_body(): pack = lax.all_to_all(pack, 'dp', 0, 0, tiled=True).reshape(length, PACK)]
    add x34 -> x1, other arithmetic: 52.1 us -> 0.75 us  [sum_pair(): return kept.astype(F32) + received.astype(F32)]
    concatenate x14 -> x4, other arithmetic: 30.1 us -> 2.67 us  [the longest x3 1.7 us: stack_swap(): return jnp.concatenate([values, swap_bit(values, bit)], axis=0)]
    all_to_all x3 -> x0, waiting for transfers between devices: 23.9 us -> none  [the longest x1 23.9 us: fast_body(): lax.all_to_all(out.reshape(shards, tokens, ROWS_Q), 'dp', 0, 0, tiled=True)]
    convert_element_type x2 -> x14, other arithmetic: 3.78 us -> 23.8 us  [the longest x4 7.73 us: low_sum(): return (sum_pair(keep[0, 1], got[0, 1]) + more[1].astype(F32)).astype(BF)]
  transfers between devices with their start and end apart: 51 -> 30, of which waited for: 29 -> 4; matrix products, arithmetic and copies ran while one was open for 14% -> 4% of each run, Pallas kernels for 6% -> 66%
where the time goes in v2:
time: 831 us; the launch traced here: 822 us
  Pallas kernels  663 us (80%)
  other arithmetic  44.4 us (5%)
  waiting for transfers between devices  43.4 us (5%)
  local copies, waits for them, and re-layouts  41.5 us (5%)
  starting transfers between devices  28 us (3%)
    pallas_call x4, Pallas kernels, run_trade(): pl.pallas_call(trade_kernel, in_specs=[pl.BlockSpec(memory_space=pl.ANY)]...  240 us
    pallas_call x2, Pallas kernels, run_reduce(): pl.pallas_call(functools.partial(reduce_kernel, parts=parts, bits=bits),...  142 us
    pallas_call x2, Pallas kernels, run_experts(): pl.pallas_call(functools.partial(expert_kernel, first=not prior), grid_sp...  114 us
    ppermute x30, waiting for transfers between devices, swap(): return lax.ppermute(values, axis, [(i, i ^ mask) for i in range(size)])  43.4 us
    pallas_call x1, Pallas kernels, run_backward(): pl.pallas_call(backward_kernel, grid=(blocks,), in_specs=[pl.BlockSpec((l...  40.7 us
    pallas_call x1, Pallas kernels, run_gather(): pl.pallas_call(gather_kernel, in_specs=[hbm] * 5, out_specs=(hbm, hbm), o...  37.1 us
    unnamed x136, local copies, waits for them, and re-layouts  31.1 us
    ppermute x30, starting transfers between devices, swap(): return lax.ppermute(values, axis, [(i, i ^ mask) for i in range(size)])  28 us
  transfers between devices with their start and end apart: 30, of which 4 were waited for; matrix products, arithmetic and copies ran while one was open for 4% of the time, Pallas kernels for 66%

profile of v2, /device:TPU:0, one launch (start us, length us, event | category | flops | bytes accessed | tf_op | source)
XLA Modules:
  0.0 822.1 jit_solution(14263009401430909260)
XLA Ops:
  2.6 4.7 convert_reduce_fusion
  14.3 7.2 shard_map.229
  27.2 49.9 %shard_map.230 = bf16[8,320,320]{2,1,0:T(8,128)(2,1)S(1)} custom-call(bf16[8,320,320]{2,1,0:T(8,128)(2,1)S(1)} %copy-done.37), custom_call_target="tpu_custom_call" | custom-call | bytes 170000000 | tf_op jit(solution)/shard_map/pallas_call | solution.py:1290
  80.3 27.1 %shard_map.231 = (bf16[2560,192]{1,0:T(8,128)(2,1)S(1)}, f32[10,64,768]{2,1,0:T(8,128)S(1)}, f32[10,1,768]{2,1,0:T(1,128)S(1)}) custom-call(bf16[2560,320]{1,0:T(8,128)(2,1)S(1)} %bitcast.104), custom_call_target="tpu_custom_call" | custom-call | flops 10066329600 | bytes 6000000 | tf_op jit(solution)/shard_map/pallas_call | solution.py:545
  113.4 33.3 %shard_map.232.att_ref = bf16[8,320,192]{2,1,0:T(8,128)(2,1)S(1)} custom-call(bf16[8,320,192]{2,1,0:T(8,128)(2,1)S(1)} %bitcast.107), custom_call_target="tpu_custom_call" | custom-call | bytes 170000000 | tf_op jit(solution)/shard_map/pallas_call | solution.py:1290
  153.0 37.1 %shard_map.234 = (bf16[8,320,1536]{2,1,0:T(8,128)(2,1)S(1)}, bf16[8,320,1536]{2,1,0:T(8,128)(2,1)S(1)}) custom-call(bf16[320,1536]{1,0:T(8,128)(2,1)S(1)} %get-tuple-element.130.refs_0_.norm_ref, bf16[320,1536]{1,0:T(8,128)(2,1)} %bitcast_convert_fusion.refs_1_, bf16[320,1536]{1,0:T(8,128)(2,1)S(1)} %copy-done.41, ...), custom_call_target="tpu_custom_call" | custom-call | bytes 150000000 | tf_op jit(solution)/shard_map/pallas_call | solution.py:1238
  196.4 55.4 %shard_map.235 = (bf16[4,320,1536]{2,1,0:T(8,128)(2,1)}, bf16[4,320,1536]{2,1,0:T(8,128)(2,1)}, bf16[4,320,1664]{2,1,0:T(8,128)(2,1)}, bf16[4,320,1664]{2,1,0:T(...) custom-call(s32[6]{0:T(128)} %stack.24.place_ref, ...), custom_call_target="tpu_custom_call" | custom-call | flops 30000001024 | bytes 60000000 | tf_op jit(solution)/shard_map/pallas_call | solution.py:903
  253.3 59.0 %shard_map.236 = (bf16[4,320,1536]{2,1,0:T(8,128)(2,1)}, bf16[4,320,1536]{2,1,0:T(8,128)(2,1)}, bf16[4,320,1664]{2,1,0:T(8,128)(2,1)}, bf16[4,320,1664]{2,1,0:T(...) custom-call(s32[6]{0:T(128)} %stack.24.place_ref, ...), custom_call_target="tpu_custom_call" | custom-call | flops 30000001024 | bytes 60000000 | tf_op jit(solution)/shard_map/pallas_call | solution.py:903
  317.1 66.5 %shard_map.237.dx_ref = f32[320,1664]{1,0:T(8,128)} custom-call(bf16[4,320,1664]{2,1,0:T(8,128)(2,1)} %get-tuple-element.140.refs_0_, bf16[4,320,1664]{2,1,0:T(8,128)(2,1)} %get-tuple-element.145.refs_1_), custom_call_target="tpu_custom_call" | custom-call | bytes 170000000 | tf_op jit(solution)/shard_map/pallas_call | solution.py:1401
  383.7 8.4 %shard_map.238 = (bf16[8,320,192]{2,1,0:T(8,128)(2,1)S(1)}, f32[320,1536]{1,0:T(8,128)S(1)}, bf16[320,1536]{1,0:T(8,128)(2,1)S(1)}, bf16[320,128]{1,0:T(8,128)(2,1)S(1)}, f32[1,1536]{1,0:T(1,128)S(1)}) custom-call(f32[320,1664]{1,0:T(8,128)} %shard_map.237.dx_ref, f32[320,1536]{1,0:T(8,128)} %copy-done.2, f32[320,1536]{1,0:T(8,128)} %bitcast.109, ...), custom_call_target="tpu_custom_call" | custom-call | flops 1509949440 | bytes 14000000 | tf_op jit(solution)/shard_map/pallas_call | solution.py:988
  392.1 5.1 shard_map.239
  405.2 71.0 %shard_map.240 = bf16[8,320,192]{2,1,0:T(8,128)(2,1)S(1)} custom-call(bf16[8,320,192]{2,1,0:T(8,128)(2,1)S(1)} %get-tuple-element.157.a_ref), custom_call_target="tpu_custom_call" | custom-call | bytes 170000000 | tf_op jit(solution)/shard_map/pallas_call | solution.py:1290
  488.7 40.7 %shard_map.241 = bf16[2560,320]{1,0:T(8,128)(2,1)S(1)} custom-call(bf16[2560,320]{1,0:T(8,128)(2,1)S(1)} %bitcast.105, bf16[2560,192]{1,0:T(8,128)(2,1)S(1)} %bitcast.108, f32[10,64,768]{2,1,0:T(8,128)} %copy-done.53, f32[10,1,768]{2,1,0:T(1,128)S(1)} %get-tuple-element.167.lse_ref, f32[32,2560]{1,0:T(8,128)S(1)} %get-tuple-element.291.cos_ref, ...), custom_call_target="tpu_custom_call" | custom-call | flops 25165824000 | bytes 8000000 | tf_op jit(solution)/shard_map/pallas_call | solution.py:637
  529.4 6.5 collective-permute-done.17
  541.3 86.1 %shard_map.242.d_ref = bf16[8,320,320]{2,1,0:T(8,128)(2,1)S(1)} custom-call(bf16[8,320,320]{2,1,0:T(8,128)(2,1)S(1)} %bitcast.106), custom_call_target="tpu_custom_call" | custom-call | bytes 170000000 | tf_op jit(solution)/shard_map/pallas_call | solution.py:1290
  633.2 8.3 %collective-permute-done.21.refs_3_ = bf16[5,192,256]{2,1,0:T(8,128)(2,1)S(1)} collective-permute-done((bf16[5,192,256]{2,1,0:T(8,128)(2,1)S(1)}, bf16[5,192,256]{2,1,0:T(8,128)(2,1)S(1)}, u32[]{:S(2)}, u32[]{:S(2)}) %collective-permute-start.21) | collective-permute-done | bytes 491552 | tf_op jit(solution)/shard_map/ppermute | solution.py:412
  641.5 11.7 %collective-permute-done.22 = bf16[2,2,48,1536]{3,2,0,1:T(8,128)(2,1)S(1)} collective-permute-done((bf16[2,2,48,1536]{3,2,0,1:T(8,128)(2,1)S(1)}, bf16[2,2,48,1536]{3,2,0,1:T(8,128)(2,1)S(1)}, u32[]{:S(2)}, u32[]{:S(2)}) %collective-permute-start.22) | collective-permute-done | bytes 589856 | tf_op jit(solution)/shard_map/ppermute | solution.py:412
  661.8 8.8 %shard_map.243 = (bf16[320,2560]{1,0:T(8,128)(2,1)S(1)}, bf16[16,48,2560]{2,1,0:T(8,128)(2,1)S(1)}, bf16[16,48,2560]{2,1,0:T(8,128)(2,1)S(1)}) custom-call(s32[6]{0:T(128)S(1)} %copy-done.48, bf16[320,1536]{1,0:T(8,128)(2,1)S(1)} %copy-done.50, bf16[8,320,320]{2,1,0:T(8,128)(2,1)S(1)} %shard_map.242.d_ref), custom_call_target="tpu_custom_call" | custom-call | flops 2516582400 | bytes 12000000 | tf_op jit(solution)/shard_map/pallas_call | solution.py:1067
  677.1 8.0 shard_map.244
  686.9 16.9 %collective-permute-done.26 = bf16[2,48,1536]{2,1,0:T(8,128)(2,1)} collective-permute-done((bf16[2,48,1536]{2,1,0:T(8,128)(2,1)}, bf16[2,48,1536]{2,1,0:T(8,128)(2,1)}, u32[]{:S(2)}, u32[]{:S(2)}) %collective-permute-start.26) | collective-permute-done | bytes 294944 | tf_op jit(solution)/shard_map/ppermute | solution.py:412
  713.4 75.6 %shard_map.246 = (f32[48,2560]{1,0:T(8,128)}, f32[48,128]{1,0:T(8,128)}) custom-call(bf16[16,48,2560]{2,1,0:T(8,128)(2,1)} %copy-done.30, f32[16,48,128]{2,1,0:T(8,128)} %copy-done.46, bf16[16,48,2560]{2,1,0:T(8,128)(2,1)} %copy-done.31, f32[16,48,128]{2,1,0:T(8,128)} %copy-done.47), custom_call_target="tpu_custom_call" | custom-call | bytes 170000000 | tf_op jit(solution)/shard_map/pallas_call | solution.py:1401
  793.6 4.8 shard_map.247
  806.6 7.9 shard_map.248
  814.6 7.3 shard_map.249
  (247 shorter events, 113.1 us)
Async XLA Ops:
  22.5 54.6 %collective-permute-start = (bf16[320,1536]{1,0:T(8,128)(2,1)}, bf16[320,1536]{1,0:T(8,128)(2,1)S(1)}, u32[]{:S(2)}, u32[]{:S(2)}) collective-permute-start(bf16[320,1536]{1,0:T(8,128)(2,1)} %bitcast_convert_fusion.refs_1_), channel_id=1, source_target_pairs={{0,2},{1,3},{2,0},{3,1},{4,6},{5,7},{6,4},{7,5},{8,10},{9,11},{10,... | collective-permute-start | bytes 2949128 | tf_op jit(solution)/shard_map/ppermute | solution.py:412
  25.5 51.6 %collective-permute-start.1 = (bf16[1,40,320]{1,2,0:T(8,128)(2,1)S(1)}, bf16[1,40,320]{1,2,0:T(8,128)(2,1)S(1)}, u32[]{:S(2)}, u32[]{:S(2)}) collective-permute-start(bf16[1,40,320]{1,2,0:T(8,128)(2,1)S(1)} %bitcast.115), channel_id=1, source_target_pairs={{0,2},{1,3},{2,0},{3,1},{4,6},{5,7},{6,4},{7,5},{8,10},{9,11},{10,... | collective-permute-start | bytes 76808 | tf_op jit(solution)/shard_map/ppermute | solution.py:412
  251.8 60.6 %collective-permute-start.6 = (bf16[2,5,64,1536]{3,2,1,0:T(8,128)(2,1)}, bf16[2,5,64,1536]{3,2,1,0:T(8,128)(2,1)S(1)}, u32[]{:S(2)}, u32[]{:S(2)}) collective-permute-start(bf16[2,5,64,1536]{3,2,1,0:T(8,128)(2,1)} %get-tuple-element.143), channel_id=1, source_target_pairs={{0,4},{4,0},{8,12},{12,8},{16,20},{20,16},{24,28},{28,24},{1,5},{5... | collective-permute-start | bytes 5898248 | tf_op jit(solution)/shard_map/ppermute | solution.py:412
  312.4 84.9 %collective-permute-start.9 = (bf16[4,320,1536]{2,1,0:T(8,128)(2,1)}, bf16[4,320,1536]{2,1,0:T(8,128)(2,1)}, u32[]{:S(2)}, u32[]{:S(2)}) collective-permute-start(bf16[4,320,1536]{2,1,0:T(8,128)(2,1)} %get-tuple-element.156), channel_id=1, source_target_pairs={{0,1},{1,0},{2,3},{3,2},{4,5},{5,4},{6,7},{7,6},{8,9},{9,8},{10,11... | collective-permute-start | bytes 11796488 | tf_op jit(solution)/shard_map/ppermute | solution.py:412
  312.5 71.1 %collective-permute-start.7 = (bf16[2,2,5,192,256]{4,3,2,1,0:T(8,128)(2,1)}, bf16[2,2,5,192,256]{4,3,2,1,0:T(8,128)(2,1)S(1)}, u32[]{:S(2)}, u32[]{:S(2)}) collective-permute-start(bf16[2,2,5,192,256]{4,3,2,1,0:T(8,128)(2,1)} %get-tuple-element.146), channel_id=1, source_target_pairs={{0,4},{4,0},{8,12},{12,8},{16,20},{20,16},{24,28},{28,24},{1,5},{5... | collective-permute-start | bytes 5898248 | tf_op jit(solution)/shard_map/ppermute | solution.py:412
  314.3 69.3 %collective-permute-start.8 = (bf16[5,64,1536]{2,1,0:T(8,128)(2,1)}, bf16[5,64,1536]{2,1,0:T(8,128)(2,1)}, u32[]{:S(2)}, u32[]{:S(2)}) collective-permute-start(bf16[5,64,1536]{2,1,0:T(8,128)(2,1)} %fusion.6), channel_id=1, source_target_pairs={{0,16},{4,20},{8,24},{12,28},{16,0},{20,4},{24,8},{28,12},{1,17},{... | collective-permute-start | bytes 2949128 | tf_op jit(solution)/shard_map/ppermute | solution.py:412
  397.2 79.0 %collective-permute-start.10 = (bf16[2,2,5,192,256]{4,3,2,1,0:T(8,128)(2,1)}, bf16[2,2,5,192,256]{4,3,2,1,0:T(8,128)(2,1)S(1)}, u32[]{:S(2)}, u32[]{:S(2)}) collective-permute-start(bf16[2,2,5,192,256]{4,3,2,1,0:T(8,128)(2,1)} %get-tuple-element.158), channel_id=1, source_target_pairs={{0,4},{4,0},{8,12},{12,8},{16,20},{20,16},{24,28},{28,24},{1,5},{5... | collective-permute-start | bytes 5898248 | tf_op jit(solution)/shard_map/ppermute | solution.py:412
  398.8 77.5 %collective-permute-start.13 = (bf16[16,48,1536]{2,1,0:T(8,128)(2,1)S(1)}, bf16[16,48,1536]{2,1,0:T(8,128)(2,1)S(1)}, u32[]{:S(2)}, u32[]{:S(2)}) collective-permute-start(bf16[16,48,1536]{2,1,0:T(8,128)(2,1)S(1)} %get-tuple-element.164), channel_id=1, source_target_pairs={{0,1},{1,0},{2,3},{3,2},{4,5},{5,4},{6,7},{7,6},{8,9},{9,8},{10,11... | collective-permute-start | bytes 7077896 | tf_op jit(solution)/shard_map/ppermute | solution.py:412
  401.0 75.3 %collective-permute-start.12 = (bf16[2,320,1536]{2,1,0:T(8,128)(2,1)S(1)}, bf16[2,320,1536]{2,1,0:T(8,128)(2,1)S(1)}, u32[]{:S(2)}, u32[]{:S(2)}) collective-permute-start(bf16[2,320,1536]{2,1,0:T(8,128)(2,1)S(1)} %fusion), channel_id=1, source_target_pairs={{0,2},{1,3},{2,0},{3,1},{4,6},{5,7},{6,4},{7,5},{8,10},{9,11},{10,... | collective-permute-start | bytes 5898248 | tf_op jit(solution)/shard_map/ppermute | solution.py:412
  402.5 73.7 %collective-permute-start.11 = (bf16[2,5,192,256]{3,2,1,0:T(8,128)(2,1)S(1)}, bf16[2,5,192,256]{3,2,1,0:T(8,128)(2,1)S(1)}, u32[]{:S(2)}, u32[]{:S(2)}) collective-permute-start(bf16[2,5,192,256]{3,2,1,0:T(8,128)(2,1)S(1)} %fusion.7), channel_id=1, source_target_pairs={{0,16},{4,20},{8,24},{12,28},{16,0},{20,4},{24,8},{28,12},{1,17},{... | collective-permute-start | bytes 2949128 | tf_op jit(solution)/shard_map/ppermute | solution.py:412
  476.3 59.6 %collective-permute-start.14 = (bf16[2,2,5,192,256]{4,3,2,1,0:T(8,128)(2,1)}, bf16[2,2,5,192,256]{4,3,2,1,0:T(8,128)(2,1)S(1)}, u32[]{:S(2)}, u32[]{:S(2)}) collective-permute-start(bf16[2,2,5,192,256]{4,3,2,1,0:T(8,128)(2,1)} %get-tuple-element.168), channel_id=1, source_target_pairs={{0,4},{4,0},{8,12},{12,8},{16,20},{20,16},{24,28},{28,24},{1,5},{5... | collective-permute-start | bytes 5898248 | tf_op jit(solution)/shard_map/ppermute | solution.py:412
  478.5 50.9 %collective-permute-start.15 = (bf16[2,5,192,256]{3,2,1,0:T(8,128)(2,1)}, bf16[2,5,192,256]{3,2,1,0:T(8,128)(2,1)}, u32[]{:S(2)}, u32[]{:S(2)}) collective-permute-start(bf16[2,5,192,256]{3,2,1,0:T(8,128)(2,1)} %fusion.8), channel_id=1, source_target_pairs={{0,16},{4,20},{8,24},{12,28},{16,0},{20,4},{24,8},{28,12},{1,17},{... | collective-permute-start | bytes 2949128 | tf_op jit(solution)/shard_map/ppermute | solution.py:412
  480.5 48.9 %collective-permute-start.16 = (bf16[5,192,256]{2,1,0:T(8,128)(2,1)}, bf16[5,192,256]{2,1,0:T(8,128)(2,1)S(1)}, u32[]{:S(2)}, u32[]{:S(2)}) collective-permute-start(bf16[5,192,256]{2,1,0:T(8,128)(2,1)} %fusion.15), channel_id=1, source_target_pairs={{0,8},{4,12},{8,0},{12,4},{16,24},{20,28},{24,16},{28,20},{1,9},{5... | collective-permute-start | bytes 1474568 | tf_op jit(solution)/shard_map/ppermute | solution.py:412
  485.3 50.7 %collective-permute-start.17 = (bf16[320,1536]{1,0:T(8,128)(2,1)}, bf16[320,1536]{1,0:T(8,128)(2,1)}, u32[]{:S(2)}, u32[]{:S(2)}) collective-permute-start(bf16[320,1536]{1,0:T(8,128)(2,1)} %fusion.3), channel_id=1, source_target_pairs={{0,8},{4,12},{8,0},{12,4},{16,24},{20,28},{24,16},{28,20},{1,9},{5... | collective-permute-start | bytes 2949128 | tf_op jit(solution)/shard_map/ppermute | solution.py:412
  487.8 48.1 %collective-permute-start.18 = (bf16[2,2,2,48,1536]{4,3,0,2,1:T(8,128)(2,1)}, bf16[2,2,2,48,1536]{4,3,0,2,1:T(8,128)(2,1)}, u32[]{:S(2)}, u32[]{:S(2)}) collective-permute-start(bf16[2,2,2,48,1536]{4,3,0,2,1:T(8,128)(2,1)} %fusion.4), channel_id=1, source_target_pairs={{0,2},{1,3},{2,0},{3,1},{4,6},{5,7},{6,4},{7,5},{8,10},{9,11},{10,... | collective-permute-start | bytes 3538952 | tf_op jit(solution)/shard_map/ppermute | solution.py:412
  537.5 115.7 %collective-permute-start.19 = (bf16[2,2,5,192,256]{4,3,2,1,0:T(8,128)(2,1)}, bf16[2,2,5,192,256]{4,3,2,1,0:T(8,128)(2,1)S(1)}, u32[]{:S(2)}, u32[]{:S(2)}) collective-permute-start(bf16[2,2,5,192,256]{4,3,2,1,0:T(8,128)(2,1)} %get-tuple-element.182), channel_id=1, source_target_pairs={{0,4},{4,0},{8,12},{12,8},{16,20},{20,16},{24,28},{28,24},{1,5},{5... | collective-permute-start | bytes 5898248 | tf_op jit(solution)/shard_map/ppermute | solution.py:412
  540.9 112.3 %collective-permute-start.20 = (bf16[2,5,192,256]{3,2,1,0:T(8,128)(2,1)S(1)}, bf16[2,5,192,256]{3,2,1,0:T(8,128)(2,1)S(1)}, u32[]{:S(2)}, u32[]{:S(2)}) collective-permute-start(bf16[2,5,192,256]{3,2,1,0:T(8,128)(2,1)S(1)} %fusion.9), channel_id=1, source_target_pairs={{0,16},{4,20},{8,24},{12,28},{16,0},{20,4},{24,8},{28,12},{1,17},{... | collective-permute-start | bytes 2949128 | tf_op jit(solution)/shard_map/ppermute | solution.py:412
  653.2 50.6 %collective-permute-start.24 = (bf16[2,5,64,1536]{3,2,1,0:T(8,128)(2,1)}, bf16[2,5,64,1536]{3,2,1,0:T(8,128)(2,1)}, u32[]{:S(2)}, u32[]{:S(2)}) collective-permute-start(bf16[2,5,64,1536]{3,2,1,0:T(8,128)(2,1)} %get-tuple-element.197), channel_id=1, source_target_pairs={{0,4},{4,0},{8,12},{12,8},{16,20},{20,16},{24,28},{28,24},{1,5},{5... | collective-permute-start | bytes 5898248 | tf_op jit(solution)/shard_map/ppermute | solution.py:412
  655.6 48.2 %collective-permute-start.23 = (bf16[2,5,192,256]{3,2,1,0:T(8,128)(2,1)}, bf16[2,5,192,256]{3,2,1,0:T(8,128)(2,1)}, u32[]{:S(2)}, u32[]{:S(2)}) collective-permute-start(bf16[2,5,192,256]{3,2,1,0:T(8,128)(2,1)} %fusion.10), channel_id=1, source_target_pairs={{0,16},{4,20},{8,24},{12,28},{16,0},{20,4},{24,8},{28,12},{1,17},{... | collective-permute-start | bytes 2949128 | tf_op jit(solution)/shard_map/ppermute | solution.py:412
  658.0 45.8 %collective-permute-start.25 = (bf16[5,192,256]{2,1,0:T(8,128)(2,1)}, bf16[5,192,256]{2,1,0:T(8,128)(2,1)S(1)}, u32[]{:S(2)}, u32[]{:S(2)}) collective-permute-start(bf16[5,192,256]{2,1,0:T(8,128)(2,1)} %fusion.13), channel_id=1, source_target_pairs={{0,8},{4,12},{8,0},{12,4},{16,24},{20,28},{24,16},{28,20},{1,9},{5... | collective-permute-start | bytes 1474568 | tf_op jit(solution)/shard_map/ppermute | solution.py:412
  660.8 43.0 %collective-permute-start.26 = (bf16[2,48,1536]{2,1,0:T(8,128)(2,1)}, bf16[2,48,1536]{2,1,0:T(8,128)(2,1)}, u32[]{:S(2)}, u32[]{:S(2)}) collective-permute-start(bf16[2,48,1536]{2,1,0:T(8,128)(2,1)} %fusion.18), channel_id=1, source_target_pairs={{0,4},{4,0},{8,12},{12,8},{16,20},{20,16},{24,28},{28,24},{1,5},{5... | collective-permute-start | bytes 884744 | tf_op jit(solution)/shard_map/ppermute | solution.py:412
  706.5 91.9 %collective-permute-start.27 = (bf16[5,64,1536]{2,1,0:T(8,128)(2,1)}, bf16[5,64,1536]{2,1,0:T(8,128)(2,1)S(1)}, u32[]{:S(2)}, u32[]{:S(2)}) collective-permute-start(bf16[5,64,1536]{2,1,0:T(8,128)(2,1)} %fusion.11), channel_id=1, source_target_pairs={{0,16},{4,20},{8,24},{12,28},{16,0},{20,4},{24,8},{28,12},{1,17},{... | collective-permute-start | bytes 2949128 | tf_op jit(solution)/shard_map/ppermute | solution.py:412
  709.4 89.0 %collective-permute-start.28 = (bf16[5,192,256]{2,1,0:T(8,128)(2,1)}, bf16[5,192,256]{2,1,0:T(8,128)(2,1)}, u32[]{:S(2)}, u32[]{:S(2)}) collective-permute-start(bf16[5,192,256]{2,1,0:T(8,128)(2,1)} %fusion.12), channel_id=1, source_target_pairs={{0,8},{4,12},{8,0},{12,4},{16,24},{20,28},{24,16},{28,20},{1,9},{5... | collective-permute-start | bytes 1474568 | tf_op jit(solution)/shard_map/ppermute | solution.py:412
  712.0 86.4 %collective-permute-start.29 = (bf16[48,1536]{1,0:T(8,128)(2,1)S(1)}, bf16[48,1536]{1,0:T(8,128)(2,1)S(1)}, u32[]{:S(2)}, u32[]{:S(2)}) collective-permute-start(bf16[48,1536]{1,0:T(8,128)(2,1)S(1)} %fusion.22), channel_id=1, source_target_pairs={{0,16},{4,20},{8,24},{12,28},{16,0},{20,4},{24,8},{28,12},{1,17},{... | collective-permute-start | bytes 442376 | tf_op jit(solution)/shard_map/ppermute | solution.py:412
  (73 other events, 1208.0 us)

commit v3 on v2

--- a/solution.py
+++ b/solution.py
@@ -428,8 +428,22 @@
 ZH_BIT = ("dp", BIT_ZH)
 
 
-def pre_kernel(hid_ref, gain_ref, wq_ref, wk_ref, wv_ref, cos_ref, sin_ref, norm_ref, pack_ref):
+def pre_kernel(
+    hid_ref,
+    gain_ref,
+    wq_ref,
+    wk_ref,
+    wv_ref,
+    cos_ref,
+    sin_ref,
+    cot_ref,
+    norm_ref,
+    pack_ref,
+    low_ref,
+):
     tokens = hid_ref.shape[0]
+    half = tokens // 2
+    low_ref[...] = cot_ref[...].astype(BF)
     inputs = hid_ref[...]
     inv = lax.rsqrt(jnp.mean(inputs * inputs, axis=-1, keepdims=True) + EPS)
     normed = (inputs * inv * gain_ref[...]).astype(BF)
@@ -445,36 +459,68 @@
         )
         return (tile * cosine + other * sine).astype(BF)
 
-    def put_heads(tiles, width, start):
-        flat = jnp.concatenate(tiles, axis=1)
-        for g in range(KV_HEADS):
-            pack_ref[g, :, start : start + width] = flat[:, g * width : (g + 1) * width]
-
     tiles = []
     for n in range(wq_ref.shape[1] // CHUNK):
         pre = dot_nn(normed, wq_ref[:, n * CHUNK : (n + 1) * CHUNK])
         tiles += [turn(pre[:, m * LANES : (m + 1) * LANES]) for m in range(CHUNK // LANES)]
-    put_heads(tiles, ROWS_Q, 0)
+    queries = jnp.concatenate(tiles, axis=1)
     pre = dot_nn(normed, wk_ref[...])
-    put_heads(
-        [turn(pre[:, m * LANES : (m + 1) * LANES]) for m in range(pre.shape[1] // LANES)],
-        HEAD_DIM,
-        ROWS_Q,
-    )
-    put_heads([dot_nn(normed, wv_ref[...]).astype(BF)], HEAD_DIM, ROWS_Q + HEAD_DIM)
-
-
-def run_pre(inputs, gain, w_query, w_key, w_value, cos_tab, sin_tab):
+    keys = jnp.concatenate(
+        [turn(pre[:, m * LANES : (m + 1) * LANES]) for m in range(pre.shape[1] // LANES)], axis=1
+    )
+    values = dot_nn(normed, wv_ref[...]).astype(BF)
+    for g in range(KV_HEADS):
+        at = g * ROWS_Q
+        head = slice(g * HEAD_DIM, (g + 1) * HEAD_DIM)
+        pack_ref[g, 0:tokens] = queries[:, at : at + LANES]
+        pack_ref[g, tokens : 2 * tokens] = jnp.concatenate(
+            [queries[:, at + LANES : at + ROWS_Q], keys[:, head]], axis=1
+        )
+        pack_ref[g, 2 * tokens :] = jnp.concatenate(
+            [values[:half, head], values[half:, head]], axis=1
+        )
+
+
+def run_pre(inputs, gain, w_query, w_key, w_value, cos_tab, sin_tab, cotangent):
     tokens = inputs.shape[0]
     return pl.pallas_call(
         pre_kernel,
         out_shape=(
             jax.ShapeDtypeStruct((tokens, WIDTH), BF),
-            jax.ShapeDtypeStruct((KV_HEADS, tokens, PACK), BF),
-        ),
-        compiler_params=params(48),
+            jax.ShapeDtypeStruct((KV_HEADS, tokens * PACK // LANES, LANES), BF),
+            jax.ShapeDtypeStruct((tokens, WIDTH), BF),
+        ),
+        compiler_params=params(60),
         cost_estimate=cost(2 * tokens * WIDTH * 2560, 14e6),
-    )(inputs, gain[None], w_query, w_key, w_value, cos_tab, sin_tab)
+    )(inputs, gain[None], w_query, w_key, w_value, cos_tab, sin_tab, cotangent)
+
+
+def unpack_heads(block_ref, out_ref, row, tokens, column):
+    half = tokens // 2
+    out_ref[row : row + tokens, column : column + LANES] = block_ref[0:tokens]
+    rest = block_ref[tokens : tokens + half]
+    out_ref[row : row + half, column + LANES : column + ROWS_Q] = rest[:, :HEAD_DIM]
+    out_ref[row + half : row + tokens, column + LANES : column + ROWS_Q] = rest[:, HEAD_DIM:]
+
+
+def pack_heads(block_ref, rows, tokens):
+    half = tokens // 2
+    block_ref[0:tokens] = rows[:, 0:LANES]
+    block_ref[tokens : tokens + half] = jnp.concatenate(
+        [rows[:half, LANES:ROWS_Q], rows[half:, LANES:ROWS_Q]], axis=1
+    )
+
+
+def unpack_all(block_ref, q_ref, k_ref, v_ref, row, tokens, q_at=0, k_at=0, v_at=0):
+    half = tokens // 2
+    rows = slice(row, row + tokens)
+    q_ref[rows, q_at : q_at + LANES] = block_ref[0:tokens]
+    two = block_ref[tokens : 2 * tokens]
+    q_ref[rows, q_at + LANES : q_at + ROWS_Q] = two[:, :HEAD_DIM]
+    k_ref[rows, k_at : k_at + HEAD_DIM] = two[:, HEAD_DIM:]
+    rest = block_ref[2 * tokens : 2 * tokens + half]
+    v_ref[row : row + half, v_at : v_at + HEAD_DIM] = rest[:, :HEAD_DIM]
+    v_ref[row + half : row + tokens, v_at : v_at + HEAD_DIM] = rest[:, HEAD_DIM:]
 
 
 def heads_t(block, width):
@@ -496,17 +542,20 @@
     return key_pos <= query_pos
 
 
-def forward_kernel(pack_ref, out_ref, out_t_ref, lse_ref, k_s, vt_s):
+def forward_kernel(pack_ref, out_ref, out_t_ref, lse_ref, q_s, k_s, v_s, vt_s, out_s):
     block = pl.program_id(0)
+    sources = pack_ref.shape[0]
+    tokens = q_s.shape[0] // sources
 
     @pl.when(block == 0)
     def _():
-        k_s[...] = pack_ref[:, ROWS_Q : ROWS_Q + HEAD_DIM]
-        vt_s[...] = pack_ref[:, ROWS_Q + HEAD_DIM : PACK].astype(F32).T.astype(BF)
+        for n in range(sources):
+            unpack_all(pack_ref.at[n], q_s, k_s, v_s, n * tokens, tokens)
+        vt_s[...] = v_s[...].astype(F32).T.astype(BF)
 
     rows = pl.ds(pl.multiple_of(block * BLOCK_Q, BLOCK_Q), BLOCK_Q)
     scale = HEAD_DIM ** (-0.5)
-    q_t = (heads_t(pack_ref[rows, 0:ROWS_Q], PER_KV) * scale).astype(BF)
+    q_t = (heads_t(q_s[rows, :], PER_KV) * scale).astype(BF)
     columns = PER_KV * BLOCK_Q
 
     def step(j, carry, masked):
@@ -533,56 +582,84 @@
     out_t = accum / total
     out_t_ref[0] = out_t
     lse_ref[0] = running + jnp.log(total)
-    out_ref[...] = jnp.concatenate(
+    out_s[rows, :] = jnp.concatenate(
         [out_t[:, h * BLOCK_Q : (h + 1) * BLOCK_Q].T for h in range(PER_KV)], axis=1
     ).astype(BF)
 
+    @pl.when(block == pl.num_programs(0) - 1)
+    def _():
+        for n in range(sources):
+            pack_heads(out_ref.at[n], out_s[n * tokens : (n + 1) * tokens, :], tokens)
+
 
 def run_forward(pack):
-    length = pack.shape[0]
+    sources = pack.shape[0]
+    length = sources * (pack.shape[1] * LANES // PACK)
+    packed = (sources, length // sources * ROWS_Q // LANES, LANES)
     blocks = length // BLOCK_Q
     columns = PER_KV * BLOCK_Q
     return pl.pallas_call(
         forward_kernel,
         grid=(blocks,),
-        in_specs=[pl.BlockSpec((length, PACK), lambda i: (0, 0))],
+        in_specs=[pl.BlockSpec(pack.shape, lambda i: (0, 0, 0))],
         out_specs=(
-            pl.BlockSpec((BLOCK_Q, ROWS_Q), lambda i: (i, 0)),
+            pl.BlockSpec(packed, lambda i: (0, 0, 0)),
             pl.BlockSpec((1, HEAD_DIM, columns), lambda i: (i, 0, 0)),
             pl.BlockSpec((1, 1, columns), lambda i: (i, 0, 0)),
         ),
         out_shape=(
-            jax.ShapeDtypeStruct((length, ROWS_Q), BF),
+            jax.ShapeDtypeStruct(packed, BF),
             jax.ShapeDtypeStruct((blocks, HEAD_DIM, columns), F32),
             jax.ShapeDtypeStruct((blocks, 1, columns), F32),
         ),
-        scratch_shapes=[pltpu.VMEM((length, HEAD_DIM), BF), pltpu.VMEM((HEAD_DIM, length), BF)],
-        compiler_params=params(40, ("arbitrary",)),
+        scratch_shapes=[
+            pltpu.VMEM((length, ROWS_Q), BF),
+            pltpu.VMEM((length, HEAD_DIM), BF),
+            pltpu.VMEM((length, HEAD_DIM), BF),
+            pltpu.VMEM((HEAD_DIM, length), BF),
+            pltpu.VMEM((length, ROWS_Q), BF),
+        ],
+        compiler_params=params(60, ("arbitrary",)),
         cost_estimate=cost(8 * length * length * ROWS_Q, 6e6, length * length * PER_KV),
     )(pack)
 
 
 def backward_kernel(
-    pack_ref, grad_ref, out_t_ref, lse_ref, cos_ref, sin_ref, res_ref, k_s, v_s, kt_s, dk_s, dv_s
+    pack_ref,
+    grad_ref,
+    out_t_ref,
+    lse_ref,
+    cos_ref,
+    sin_ref,
+    res_ref,
+    q_s,
+    do_s,
+    k_s,
+    v_s,
+    kt_s,
+    dk_s,
+    dv_s,
 ):
     block = pl.program_id(0)
+    sources = pack_ref.shape[0]
+    tokens = q_s.shape[0] // sources
 
     @pl.when(block == 0)
     def _():
-        keys = pack_ref[:, ROWS_Q : ROWS_Q + HEAD_DIM]
-        k_s[...] = keys
-        kt_s[...] = keys.astype(F32).T.astype(BF)
-        v_s[...] = pack_ref[:, ROWS_Q + HEAD_DIM : PACK]
+        for n in range(sources):
+            unpack_all(pack_ref.at[n], q_s, k_s, v_s, n * tokens, tokens)
+            unpack_heads(grad_ref.at[n], do_s, n * tokens, tokens, 0)
+        kt_s[...] = k_s[...].astype(F32).T.astype(BF)
         dk_s[...] = jnp.zeros_like(dk_s)
         dv_s[...] = jnp.zeros_like(dv_s)
 
     scale = HEAD_DIM ** (-0.5)
     half = HEAD_DIM // 2
     rows = pl.ds(pl.multiple_of(block * BLOCK_Q, BLOCK_Q), BLOCK_Q)
-    q_block = pack_ref[rows, 0:ROWS_Q]
+    q_block = q_s[rows, :]
     q_t = (heads_t(q_block, PER_KV) * scale).astype(BF)
     q_rows = (heads_rows(q_block, PER_KV).astype(F32) * scale).astype(BF)
-    do_block = grad_ref[...]
+    do_block = do_s[rows, :]
     do_f32 = heads_t(do_block, PER_KV)
     do_t = do_f32.astype(BF)
     do_rows = heads_rows(do_block, PER_KV)
@@ -614,7 +691,7 @@
 
     columns = pl.ds(pl.multiple_of(block * BLOCK_Q, BLOCK_Q), BLOCK_Q)
     cosine, sine = cos_ref[:, columns], sin_ref[:, columns]
-    res_ref[rows, 0:ROWS_Q] = jnp.concatenate(
+    q_s[rows, :] = jnp.concatenate(
         [
             turn_back(dq_t[:, h * BLOCK_Q : (h + 1) * BLOCK_Q], cosine, sine).T
             for h in range(PER_KV)
@@ -624,13 +701,21 @@
 
     @pl.when(block == pl.num_programs(0) - 1)
     def _():
-        dk_t = turn_back(dk_s[...].T, cos_ref[...], sin_ref[...])
-        res_ref[:, ROWS_Q : ROWS_Q + HEAD_DIM] = dk_t.T.astype(BF)
-        res_ref[:, ROWS_Q + HEAD_DIM : PACK] = dv_s[...].astype(BF)
+        dk = turn_back(dk_s[...].T, cos_ref[...], sin_ref[...]).T.astype(BF)
+        half = tokens // 2
+        for n in range(sources):
+            row = n * tokens
+            res_ref[n, 0:tokens] = q_s[row : row + tokens, 0:LANES]
+            res_ref[n, tokens : 2 * tokens] = jnp.concatenate(
+                [q_s[row : row + tokens, LANES:ROWS_Q], dk[row : row + tokens]], axis=1
+            )
+            res_ref[n, 2 * tokens :] = jnp.concatenate(
+                [dv_s[row : row + half, :], dv_s[row + half : row + tokens, :]], axis=1
+            ).astype(BF)
 
 
 def run_backward(pack, grad, out_t, lse, cos_t, sin_t):
-    length = pack.shape[0]
+    length = cos_t.shape[1]
     blocks = length // BLOCK_Q
     columns = PER_KV * BLOCK_Q
     half = HEAD_DIM // 2
@@ -638,30 +723,32 @@
         backward_kernel,
         grid=(blocks,),
         in_specs=[
-            pl.BlockSpec((length, PACK), lambda i: (0, 0)),
-            pl.BlockSpec((BLOCK_Q, ROWS_Q), lambda i: (i, 0)),
+            pl.BlockSpec(pack.shape, lambda i: (0, 0, 0)),
+            pl.BlockSpec(grad.shape, lambda i: (0, 0, 0)),
             pl.BlockSpec((1, HEAD_DIM, columns), lambda i: (i, 0, 0)),
             pl.BlockSpec((1, 1, columns), lambda i: (i, 0, 0)),
             pl.BlockSpec((half, length), lambda i: (0, 0)),
             pl.BlockSpec((half, length), lambda i: (0, 0)),
         ],
-        out_specs=pl.BlockSpec((length, PACK), lambda i: (0, 0)),
-        out_shape=jax.ShapeDtypeStruct((length, PACK), BF),
+        out_specs=pl.BlockSpec(pack.shape, lambda i: (0, 0, 0)),
+        out_shape=jax.ShapeDtypeStruct(pack.shape, BF),
         scratch_shapes=[
+            pltpu.VMEM((length, ROWS_Q), BF),
+            pltpu.VMEM((length, ROWS_Q), BF),
             pltpu.VMEM((length, HEAD_DIM), BF),
             pltpu.VMEM((length, HEAD_DIM), BF),
             pltpu.VMEM((HEAD_DIM, length), BF),
             pltpu.VMEM((length, HEAD_DIM), F32),
             pltpu.VMEM((length, HEAD_DIM), F32),
         ],
-        compiler_params=params(48, ("arbitrary",)),
+        compiler_params=params(60, ("arbitrary",)),
         cost_estimate=cost(20 * length * length * ROWS_Q, 8e6, length * length * PER_KV),
     )(pack, grad, out_t, lse, cos_t, sin_t)
 
 
 def mid_kernel(att_ref, wo_ref, hid_ref, gain_ref, mid_ref, norm_ref, full_ref):
     for g in range(KV_HEADS):
-        full_ref[:, g * ROWS_Q : (g + 1) * ROWS_Q] = att_ref[g]
+        unpack_heads(att_ref.at[g], full_ref, 0, full_ref.shape[0], g * ROWS_Q)
     middle = hid_ref[...] + dot_nn(full_ref[...], wo_ref[...])
     mid_ref[...] = middle
     inv = lax.rsqrt(jnp.mean(middle * middle, axis=-1, keepdims=True) + EPS)
@@ -677,7 +764,7 @@
             jax.ShapeDtypeStruct((tokens, WIDTH), BF),
             jax.ShapeDtypeStruct((tokens, WIDTH), BF),
         ),
-        compiler_params=params(40),
+        compiler_params=params(60),
         cost_estimate=cost(2 * tokens * WIDTH * WIDTH, 12e6),
     )(att, w_output, inputs, gain[None])
 
@@ -708,11 +795,14 @@
     dx_keep,
     dx_send,
     gate_keep,
-    gate_send,
+    gate_send0,
+    gate_send1,
     up_keep,
-    up_send,
+    up_send0,
+    up_send1,
     down_keep,
-    down_send,
+    down_send0,
+    down_send1,
     xs,
     gs,
     gate_s,
@@ -789,7 +879,7 @@
         for z in range(2):
             base = (zh_at ^ z) * 2
             down_keep[z, 0] = wide_s[pl.ds(pl.multiple_of((base + y_at) * part, part), part), :]
-            down_send[z, 0] = wide_s[
+            (down_send0, down_send1)[z][0] = wide_s[
                 pl.ds(pl.multiple_of((base + (1 - y_at)) * part, part), part), :
             ]
 
@@ -801,18 +891,18 @@
                     keep[z, low, 0] = tall_s[
                         pl.ds(pl.multiple_of((base + y_at) * part, part), part), :
                     ]
-                    send[z, low, 0] = tall_s[
+                    send[z][low, 0] = tall_s[
                         pl.ds(pl.multiple_of((base + (1 - y_at)) * part, part), part), :
                     ]
 
         for n in range(count):
             cols = slice(n * CHUNK, (n + 1) * CHUNK)
             tall_s[cols, :] = dot_tn(x[:, cols], d_gate).astype(BF)
-        spread(gate_keep, gate_send)
+        spread(gate_keep, (gate_send0, gate_send1))
         for n in range(count):
             cols = slice(n * CHUNK, (n + 1) * CHUNK)
             tall_s[cols, :] = dot_tn(x[:, cols], d_up).astype(BF)
-        spread(up_keep, up_send)
+        spread(up_keep, (up_send0, up_send1))
         for n in range(count):
             cols = slice(n * CHUNK, (n + 1) * CHUNK)
             d_x = dot_nt(d_gate, w_gate[cols]) + dot_nt(d_up, w_up[cols])
@@ -847,6 +937,10 @@
         source = step - experts - sources - sources // 2
         prior = (None, None) if first else (mix_prior[0], dx_prior[0])
         combine(source, mix_keep, dx_keep, *prior)
+
+
+def less(shape):
+    return jax.ShapeDtypeStruct(shape.shape[1:], shape.dtype)
 
 
 def run_experts(place, x_all, g_all, maps, wr_t, w_gate, w_up, w_down, prior=()):
@@ -890,6 +984,8 @@
         (2, 2, 1, quarter, half), lambda i, p: (0, 0, expert_of(i), 0, 0)
     )
     wide_spec = pl.BlockSpec((2, 1, part, width), lambda i, p: (0, expert_of(i), 0, 0))
+    tall_half = pl.BlockSpec((2, 1, quarter, half), lambda i, p: (0, expert_of(i), 0, 0))
+    wide_half = pl.BlockSpec((1, part, width), lambda i, p: (expert_of(i), 0, 0))
     tall = jax.ShapeDtypeStruct((2, 2, experts, quarter, half), BF)
     wide = jax.ShapeDtypeStruct((2, experts, part, width), BF)
     mixed = jax.ShapeDtypeStruct((sources // 2, tokens, width), BF)
@@ -921,11 +1017,14 @@
             out_specs=(
                 *sums,
                 tall_spec,
+                tall_half,
+                tall_half,
                 tall_spec,
-                tall_spec,
-                tall_spec,
+                tall_half,
+                tall_half,
                 wide_spec,
-                wide_spec,
+                wide_half,
+                wide_half,
             ),
             scratch_shapes=[
                 pltpu.VMEM((experts, slots, width), BF),
@@ -935,8 +1034,10 @@
                 pltpu.VMEM((width, half), BF),
             ],
         ),
-        out_shape=(mixed, mixed, d_x, d_x, tall, tall, tall, tall, wide, wide),
-        compiler_params=params(56, ("arbitrary",)),
+        out_shape=(mixed, mixed, d_x, d_x)
+        + (tall, less(tall), less(tall)) * 2
+        + (wide, less(wide), less(wide)),
+        compiler_params=params(60, ("arbitrary",)),
         cost_estimate=cost(30e9, 60e6),
     )(place, x_all, g_all, maps, wr_t, w_gate, w_gate, w_up, w_up, w_down, w_down, *prior)
 
@@ -980,7 +1081,7 @@
     dlow_ref[...] = d_low
     d_att = dot_nt(d_low, wo_ref[...]).astype(BF)
     for g in range(KV_HEADS):
-        datt_ref[g] = d_att[:, g * ROWS_Q : (g + 1) * ROWS_Q]
+        pack_heads(datt_ref.at[g], d_att[:, g * ROWS_Q : (g + 1) * ROWS_Q], d_att.shape[0])
 
 
 def run_post(dx_sum, middle, cotangent, normed_two, wr_pad, map_rows, gain, w_output):
@@ -988,13 +1089,13 @@
     return pl.pallas_call(
         post_kernel,
         out_shape=(
-            jax.ShapeDtypeStruct((KV_HEADS, tokens, ROWS_Q), BF),
+            jax.ShapeDtypeStruct((KV_HEADS, tokens * ROWS_Q // LANES, LANES), BF),
             jax.ShapeDtypeStruct((tokens, WIDTH), F32),
             jax.ShapeDtypeStruct((tokens, WIDTH), BF),
             jax.ShapeDtypeStruct((tokens, LANES), BF),
             jax.ShapeDtypeStruct((1, WIDTH), F32),
         ),
-        compiler_params=params(48),
+        compiler_params=params(60),
         cost_estimate=cost(2 * tokens * WIDTH * WIDTH, 14e6),
     )(dx_sum, middle, cotangent, normed_two, wr_pad, map_rows, gain[None], w_output)
 
@@ -1032,7 +1133,7 @@
             scratch_shapes=[pltpu.VMEM((rows, 256), BF)],
         ),
         out_shape=(shape, shape),
-        compiler_params=params(32, ("arbitrary",)),
+        compiler_params=params(60, ("arbitrary",)),
         cost_estimate=cost(2 * tokens * rows * cols, 8e6),
     )(place, left, right)
 
@@ -1045,13 +1146,17 @@
         key_at = KV_HEADS * ROWS_Q
         value_at = key_at + KV_HEADS * HEAD_DIM
         for g in range(KV_HEADS):
-            full_ref[:, g * ROWS_Q : (g + 1) * ROWS_Q] = d_ref[g, :, 0:ROWS_Q]
-            full_ref[:, key_at + g * HEAD_DIM : key_at + (g + 1) * HEAD_DIM] = d_ref[
-                g, :, ROWS_Q : ROWS_Q + HEAD_DIM
-            ]
-            full_ref[:, value_at + g * HEAD_DIM : value_at + (g + 1) * HEAD_DIM] = d_ref[
-                g, :, ROWS_Q + HEAD_DIM : PACK
-            ]
+            unpack_all(
+                d_ref.at[g],
+                full_ref,
+                full_ref,
+                full_ref,
+                0,
+                full_ref.shape[0],
+                g * ROWS_Q,
+                key_at + g * HEAD_DIM,
+                value_at + g * HEAD_DIM,
+            )
 
     cols = pl.ds(pl.multiple_of(step * 256, 256), 256)
     held[...] = dot_tn(a_ref[...], full_ref[:, cols]).astype(BF)
@@ -1077,7 +1182,7 @@
             scratch_shapes=[pltpu.VMEM((rows, 256), BF)],
         ),
         out_shape=(jax.ShapeDtypeStruct((tokens, cols), BF), shape, shape),
-        compiler_params=params(40, ("arbitrary",)),
+        compiler_params=params(60, ("arbitrary",)),
         cost_estimate=cost(2 * tokens * rows * cols, 12e6),
     )(place, normed, d_pack)
 
@@ -1107,7 +1212,7 @@
             jax.ShapeDtypeStruct((tokens, WIDTH), F32),
             jax.ShapeDtypeStruct((1, WIDTH), F32),
         ),
-        compiler_params=params(48),
+        compiler_params=params(60),
         cost_estimate=cost(2 * tokens * WIDTH * 2560, 16e6),
     )(d_full, w_query, w_key, w_value, d_middle, inputs, gain[None])
 
@@ -1132,7 +1237,7 @@
         in_specs=[smem] + [vmem] * 4,
         out_shape=(shape, shape),
         scratch_shapes=[pltpu.VMEM((WIDTH, LANES), F32)],
-        compiler_params=params(24),
+        compiler_params=params(60),
         cost_estimate=cost(1e8, 3e6),
     )(place, normed_two, d_log, ggain_mlp, ggain_attn)
 
@@ -1142,6 +1247,7 @@
 
 
 MESH = pl.DeviceIdType.MESH
+hbm = pl.BlockSpec(memory_space=pltpu.HBM)
 
 
 def peer_of(bit):
@@ -1203,49 +1309,46 @@
     own.wait()
 
 
-def gather_kernel(*refs):
-    x_ref, blocks = refs[0], refs[1:5]
-    all_ref, other_ref = refs[5:7]
-    send_sem, recv_sem, more_send, more_recv, local_sem = refs[7:]
+def gather_kernel(x_ref, *refs):
+    blocks, maps_ref = refs[0:4], refs[4]
+    all_ref, other_ref, all_maps_ref = refs[5:8]
+    send_sem, recv_sem, more_send, more_recv, local_sem = refs[8:]
     greet([peer_of(bit) for bit in GATHER_BITS])
-    local = []
-    remote = []
-    for n, block in enumerate(blocks):
+    pairs = [(block, other_ref.at[n], other_ref.at[4 + n]) for n, block in enumerate(blocks)]
+    pairs.append((maps_ref, all_maps_ref.at[pl.ds(0, 4)], all_maps_ref.at[pl.ds(4, 4)]))
+    copies = []
+    for n, (block, here, there) in enumerate(pairs):
         copy = pltpu.make_async_remote_copy(
             src_ref=block,
-            dst_ref=other_ref.at[4 + n],
+            dst_ref=there,
             send_sem=more_send.at[n],
             recv_sem=more_recv.at[n],
             device_id=peer_of(C_BIT),
             device_id_type=MESH,
         )
         copy.start()
-        remote.append(copy)
-        copy = pltpu.make_async_copy(block, other_ref.at[n], local_sem.at[1 + n])
+        copies.append(copy)
+        copy = pltpu.make_async_copy(block, here, local_sem.at[1 + n])
         copy.start()
-        local.append(copy)
+        copies.append(copy)
     gather_steps(x_ref, all_ref, send_sem, recv_sem, local_sem.at[0])
-    for copy in local:
+    for copy in copies:
         copy.wait()
-    for copy in remote:
-        copy.wait()
-
-
-def run_gather(values, blocks):
-    tokens, width = values.shape
-    hbm = pl.BlockSpec(memory_space=pl.ANY)
-    shape = jax.ShapeDtypeStruct((8, tokens, width), values.dtype)
+
+
+def run_gather(values, blocks, maps):
+    shape = jax.ShapeDtypeStruct((8,) + values.shape, values.dtype)
     return pl.pallas_call(
         gather_kernel,
-        in_specs=[hbm] * 5,
-        out_specs=(hbm, hbm),
-        out_shape=(shape, shape),
-        scratch_shapes=[pltpu.SemaphoreType.DMA((n,)) for n in (10, 10, 4, 4, 5)],
+        in_specs=[pl.BlockSpec(memory_space=pltpu.VMEM)] * 6,
+        out_specs=(hbm,) * 3,
+        out_shape=(shape, shape, jax.ShapeDtypeStruct((8,) + maps.shape[1:], maps.dtype)),
+        scratch_shapes=[pltpu.SemaphoreType.DMA((n,)) for n in (10, 10, 5, 5, 6)],
         compiler_params=pltpu.CompilerParams(
-            collective_id=1, has_side_effects=True, vmem_limit_bytes=16 * MIB
+            collective_id=1, has_side_effects=True, vmem_limit_bytes=60 * MIB
         ),
         cost_estimate=cost(0, 150e6),
-    )(values, *blocks)
+    )(values, *blocks, maps)
 
 
 def trade_peers(size):
@@ -1280,32 +1383,107 @@
         copy.wait_send()
 
 
-def trade_kernel(a_ref, out_ref, send_sem, recv_sem, local_sem):
+def ride_pieces(sources, targets, riders, send_sem, recv_sem):
+    starts, copies = [], []
+    for n, (bit, pieces) in enumerate(riders):
+        size = sources[n].shape[0] // pieces
+        for m in range(pieces):
+            at = pl.ds(m * size, size)
+            slot = len(starts)
+
+            def start(n=n, at=at, slot=slot, bit=bit):
+                copy = pltpu.make_async_remote_copy(
+                    src_ref=sources[n].at[at],
+                    dst_ref=targets[n].at[at],
+                    send_sem=send_sem.at[slot],
+                    recv_sem=recv_sem.at[slot],
+                    device_id=peer_of(bit),
+                    device_id_type=MESH,
+                )
+                copy.start()
+                copies.append(copy)
+
+            starts.append(start)
+    return starts, copies
+
+
+def rider_shapes(riders):
+    return tuple(jax.ShapeDtypeStruct(array.shape, array.dtype) for array, _, _ in riders)
+
+
+def all_peers(bits):
+    size = lax.axis_size("dp")
+    return trade_peers(size) + [peer_of(bit) for bit in bits if bit[0] == "expert"]
+
+
+def trade_kernel(*refs, riders):
+    count = len(riders)
+    a_ref, sources = refs[0], refs[1 : 1 + count]
+    out_ref, targets = refs[1 + count], refs[2 + count : 2 + 2 * count]
+    send_sem, recv_sem, local_sem, *more = refs[2 + 2 * count :]
+    greet(all_peers(sorted({bit for bit, _ in riders})))
+    trade = trade_start(a_ref, out_ref, send_sem, recv_sem, local_sem.at[0])
+    copies = []
+    if riders:
+        starts, copies = ride_pieces(sources, targets, riders, *more)
+        for start in starts:
+            start()
+    trade_end(*trade)
+    for copy in copies:
+        copy.wait()
+
+
+def run_trade(values, number, riders=()):
+    size = values.shape[0]
+    count = len(riders)
+    total = sum(rider[2] for rider in riders)
+    sems = [size - 1, size - 1, 1] + [total] * (2 if count else 0)
+    out = pl.pallas_call(
+        functools.partial(trade_kernel, riders=tuple(rider[1:] for rider in riders)),
+        in_specs=[hbm] * (1 + count),
+        out_specs=(hbm,) * (1 + count),
+        out_shape=(jax.ShapeDtypeStruct(values.shape, values.dtype),) + rider_shapes(riders),
+        scratch_shapes=[pltpu.SemaphoreType.DMA((n,)) for n in sems],
+        compiler_params=pltpu.CompilerParams(
+            collective_id=number, has_side_effects=True, vmem_limit_bytes=60 * MIB
+        ),
+        cost_estimate=cost(0, 170e6),
+    )(values, *(rider[0] for rider in riders))
+    return out if count else out[0]
+
+
+def first_kernel(a_ref, rank_ref, turned_ref, out_ref, slot_ref, send_sem, recv_sem, local_sem, *, far):
     greet(trade_peers(a_ref.shape[0]))
-    trade_end(*trade_start(a_ref, out_ref, send_sem, recv_sem, local_sem.at[0]))
-
-
-def run_trade(values, number):
+    trade = trade_start(a_ref, out_ref, send_sem, recv_sem, local_sem.at[0])
+    for e in range(rank_ref.shape[0]):
+        own = rank_ref[e : e + 1, :]
+        smaller = (turned_ref[:, e : e + 1] < own).astype(F32)
+        before = jnp.sum(smaller, axis=0, keepdims=True)
+        slot_ref[e : e + 1, :] = jnp.where(own < far, jnp.minimum(before, SLOTS), -1.0)
+    trade_end(*trade)
+
+
+def run_first(values, rank_map, turned, far):
     size = values.shape[0]
+    vmem = pl.BlockSpec(memory_space=pltpu.VMEM)
     return pl.pallas_call(
-        trade_kernel,
-        in_specs=[pl.BlockSpec(memory_space=pl.ANY)],
-        out_specs=pl.BlockSpec(memory_space=pl.ANY),
-        out_shape=jax.ShapeDtypeStruct(values.shape, values.dtype),
-        scratch_shapes=[
-            pltpu.SemaphoreType.DMA((size - 1,)),
-            pltpu.SemaphoreType.DMA((size - 1,)),
-            pltpu.SemaphoreType.DMA((1,)),
-        ],
+        functools.partial(first_kernel, far=far),
+        in_specs=[hbm, vmem, vmem],
+        out_specs=(hbm, vmem),
+        out_shape=(
+            jax.ShapeDtypeStruct(values.shape, values.dtype),
+            jax.ShapeDtypeStruct(rank_map.shape, F32),
+        ),
+        scratch_shapes=[pltpu.SemaphoreType.DMA((n,)) for n in (size - 1, size - 1, 1)],
         compiler_params=pltpu.CompilerParams(
-            collective_id=number, has_side_effects=True, vmem_limit_bytes=8 * MIB
+            collective_id=2, has_side_effects=True, vmem_limit_bytes=60 * MIB
         ),
         cost_estimate=cost(0, 170e6),
-    )(values)
-
-
-def reduce_chain(job, part, keep_ref, send_ref, out_ref, acc, got, staged, send_sem, recv_sem):
-    bits, row, rows, column, columns, order = part
+    )(values, rank_map, turned)
+
+
+def reduce_chain(slot, part, keep_ref, send_ref, outs, acc, got, staged, send_sem, recv_sem):
+    first, bits, row, rows, column, columns, order = part
     blocks = keep_ref.shape[0]
     stages = len(bits) + 1
     low = send_ref.dtype
@@ -1313,7 +1491,7 @@
     copies = []
 
     def exchange(source, target, bit):
-        n = job * stages + len(copies)
+        n = slot + len(copies)
         copy = pltpu.make_async_remote_copy(
             src_ref=source,
             dst_ref=target,
@@ -1327,7 +1505,7 @@
 
     live = list(range(blocks))
     base_got, base_sent = 0, 0
-    exchange(send_ref.at[(slice(None),) + at], got.at[(pl.ds(0, blocks),) + at], C_BIT)
+    exchange(send_ref.at[(slice(None),) + at], got.at[(pl.ds(0, blocks),) + at], first)
     yield
     for stage in range(stages):
         copies[-1].wait_recv()
@@ -1338,7 +1516,11 @@
             return kept + got[(base_got + position,) + at].astype(F32)
 
         if stage == stages - 1:
-            out_ref[at] = total(0)
+            low_column = 0
+            for out_ref in outs:
+                if low_column <= column < low_column + out_ref.shape[1]:
+                    out_ref[at[0], pl.ds(column - low_column, columns)] = total(0)
+                low_column += out_ref.shape[1]
             break
         mask = 1 << order[stage]
         rest = [i for i in live if not i & mask]
@@ -1359,22 +1541,37 @@
         copy.wait_send()
 
 
-def reduce_kernel(*refs, parts, bits):
-    jobs = len(parts)
-    keeps, sends, outs = refs[:jobs], refs[jobs : 2 * jobs], refs[2 * jobs : 3 * jobs]
-    scratch = refs[3 * jobs :]
-    greet([peer_of(bit) for bit in (C_BIT,) + bits])
-    send_sem, recv_sem = scratch[-2:]
-    chains, number = [], 0
-    for n in range(jobs):
-        buffers = scratch[3 * n : 3 * n + 3]
-        for part in parts[n]:
+def reduce_kernel(*refs, jobs, riders):
+    size, count = len(jobs), len(riders)
+    keeps, sends, sources = refs[:size], refs[size : 2 * size], refs[2 * size : 2 * size + count]
+    refs = refs[2 * size + count :]
+    outs = []
+    for _, _, _, widths in jobs:
+        outs.append(refs[: len(widths)])
+        refs = refs[len(widths) :]
+    targets, scratch = refs[:count], refs[count:]
+    send_sem, recv_sem, ride_send, ride_recv = scratch[3 * size :]
+    used = {bit for first, bits, *_ in jobs for bit in (first,) + bits}
+    used |= {bit for bit, _ in riders}
+    greet([peer_of(bit) for bit in sorted(used)])
+    chains, slot = [], 0
+    for n, (first, bits, parts, _) in enumerate(jobs):
+        for part in parts:
             chains.append(
                 reduce_chain(
-                    number, (bits,) + part, keeps[n], sends[n], outs[n], *buffers, send_sem, recv_sem
+                    slot,
+                    (first, bits) + part,
+                    keeps[n],
+                    sends[n],
+                    outs[n],
+                    *scratch[3 * n : 3 * n + 3],
+                    send_sem,
+                    recv_sem,
                 )
             )
-            number += 1
+            slot += len(bits) + 1
+    starts, copies = ride_pieces(sources, targets, riders, ride_send, ride_recv)
+    turn, plain = 0, sum(pieces == 1 for _, pieces in riders)
     while chains:
         rest = []
         for chain in chains:
@@ -1383,128 +1580,116 @@
                 rest.append(chain)
             except StopIteration:
                 pass
+            if turn >= 2 and starts:
+                starts.pop(0)()
         chains = rest
-
-
-def run_reduce(pairs, parts, bits, number):
-    slots = sum(len(part) for part in parts) * (len(bits) + 1)
+        for _ in range(plain if turn == 0 else 0):
+            starts.pop(0)()
+        if turn <= 1 and starts:
+            starts.pop(0)()
+        turn += 1
+    for start in starts:
+        start()
+    for copy in copies:
+        copy.wait()
+
+
+def run_reduce(pairs, jobs, number, riders=()):
+    slots = sum(len(parts) * (len(bits) + 1) for _, bits, parts, _ in jobs)
     vmem = pl.BlockSpec(memory_space=pltpu.VMEM)
     scratch, shapes = [], []
-    for keep, send in pairs:
+    for (keep, send), (_, _, _, widths) in zip(pairs, jobs):
         blocks, rows, cols = keep.shape
         scratch += [
             pltpu.VMEM((blocks, rows, cols), F32),
             pltpu.VMEM((2 * blocks - 1, rows, cols), send.dtype),
             pltpu.VMEM((max(blocks - 1, 1), rows, cols), send.dtype),
         ]
-        shapes.append(jax.ShapeDtypeStruct((rows, cols), F32))
+        shapes += [jax.ShapeDtypeStruct((rows, width), F32) for width in widths]
+    pieces = max(sum(rider[2] for rider in riders), 1)
+    sems = (slots, slots, pieces, pieces)
     return pl.pallas_call(
-        functools.partial(reduce_kernel, parts=parts, bits=bits),
-        in_specs=[vmem] * len(pairs) + [pl.BlockSpec(memory_space=pl.ANY)] * len(pairs),
-        out_specs=tuple(vmem for _ in pairs),
-        out_shape=tuple(shapes),
-        scratch_shapes=scratch
-        + [pltpu.SemaphoreType.DMA((slots,)), pltpu.SemaphoreType.DMA((slots,))],
+        functools.partial(
+            reduce_kernel, jobs=jobs, riders=tuple(rider[1:] for rider in riders)
+        ),
+        in_specs=[vmem] * len(pairs) + [hbm] * (len(pairs) + len(riders)),
+        out_specs=(vmem,) * len(shapes) + (hbm,) * len(riders),
+        out_shape=tuple(shapes) + rider_shapes(riders),
+        scratch_shapes=scratch + [pltpu.SemaphoreType.DMA((n,)) for n in sems],
         compiler_params=pltpu.CompilerParams(
-            collective_id=number, has_side_effects=True, vmem_limit_bytes=56 * MIB
+            collective_id=number, has_side_effects=True, vmem_limit_bytes=60 * MIB
         ),
         cost_estimate=cost(0, 170e6),
-    )(*(keep for keep, _ in pairs), *(send for _, send in pairs))
+    )(*(keep for keep, _ in pairs), *(send for _, send in pairs), *(rider[0] for rider in riders))
 
 
 def sum_pair(kept, received):
     return kept.astype(F32) + received.astype(F32)
 
 
-def first_sum(keep, got):
-    return sum_pair(keep[1], got[1]).astype(BF)
-
-
-def low_sum(keep, got, more):
-    return (sum_pair(keep[0, 1], got[0, 1]) + more[1].astype(F32)).astype(BF)
-
-
-def join_down_kernel(*refs):
-    out = refs[-1]
-    step = pl.program_id(0)
-    for part in range(2):
-        keep, got, more = refs[3 * part : 3 * part + 3]
-
-        @pl.when((step >= 5 * part) & (step < 5 * part + 5))
-        def _():
-            total = keep[0, 0].astype(F32) + got[0, 0].astype(F32)
-            out[0] = total + more[0].astype(F32)
-
-
-def join_tall_kernel(place_ref, *refs):
-    out = refs[-1]
-    step = pl.program_id(0)
+def add_low(*terms):
+    return sum(term.astype(F32) for term in terms).astype(BF)
+
+
+def join_kernel(place_ref, *refs):
+    outs = refs[-3:]
     zl_at = place_ref[0]
-    for part in range(2):
-        keep, got, more, other = refs[4 * part : 4 * part + 4]
-
-        @pl.when((step >= 5 * part) & (step < 5 * part + 5))
-        def _():
-            total = keep[0, 0, 0].astype(F32) + got[0, 0, 0].astype(F32)
-            total += more[0, 0].astype(F32)
+
+    def total(*terms):
+        return sum(term.astype(F32) for term in terms)
+
+    def work(parts, part):
+        for n in range(2):
+            keep, got, more, other = parts[4 * n : 4 * n + 4]
+            mine = total(keep[0, 0, 0], got[0, 0], more[0])
             across = other[0].astype(F32)
-            for n in range(2):
-                cols = slice(n * LANES, (n + 1) * LANES)
-                mine = pl.multiple_of((2 * n + zl_at) * LANES, LANES)
-                theirs = pl.multiple_of((2 * n + 1 - zl_at) * LANES, LANES)
-                out[0, :, pl.ds(mine, LANES)] = total[:, cols]
-                out[0, :, pl.ds(theirs, LANES)] = across[:, cols]
-
-
-def run_join_down(parts):
-    experts, rows, cols = parts[0][2].shape
+            for m in range(2):
+                cols = slice(m * LANES, (m + 1) * LANES)
+                at = pl.multiple_of((2 * m + zl_at) * LANES, LANES)
+                outs[n][part, 0, :, pl.ds(at, LANES)] = mine[:, cols]
+                at = pl.multiple_of((2 * m + 1 - zl_at) * LANES, LANES)
+                outs[n][part, 0, :, pl.ds(at, LANES)] = across[:, cols]
+        keep, got, more = parts[8:]
+        outs[2][part, 0] = total(keep[0, 0], got[0], more[0])
+
+    work(refs[0:11], 0)
+    work(refs[11:22], 1)
+
+
+def run_join(place, halves):
+    experts, rows, cols = halves[0][2].shape
+    wide_rows, width = halves[0][8].shape[2:]
     specs = []
     for part in range(2):
-        def of(i, part=part):
-            return jnp.clip(i - part * experts, 0, experts - 1)
-
+        tall = [
+            pl.BlockSpec((1, 1, 1, rows, cols), lambda i, p: (0, 0, i, 0, 0)),
+            pl.BlockSpec((1, 1, rows, cols), lambda i, p: (0, i, 0, 0)),
+            pl.BlockSpec((1, rows, cols), lambda i, p: (i, 0, 0)),
+            pl.BlockSpec((1, rows, cols), lambda i, p: (i, 0, 0)),
+        ]
+        specs += tall + tall
         specs += [
-            pl.BlockSpec((1, 1, rows, cols), lambda i, of=of: (0, of(i), 0, 0)),
-            pl.BlockSpec((1, 1, rows, cols), lambda i, of=of: (0, of(i), 0, 0)),
-            pl.BlockSpec((1, rows, cols), lambda i, of=of: (of(i), 0, 0)),
+            pl.BlockSpec((1, 1, wide_rows, width), lambda i, p: (0, i, 0, 0)),
+            pl.BlockSpec((1, wide_rows, width), lambda i, p: (i, 0, 0)),
+            pl.BlockSpec((1, wide_rows, width), lambda i, p: (i, 0, 0)),
         ]
+    shapes = [(rows, 2 * cols), (rows, 2 * cols), (wide_rows, width)]
     return pl.pallas_call(
-        join_down_kernel,
-        grid=(2 * experts,),
-        in_specs=specs,
-        out_specs=pl.BlockSpec((1, rows, cols), lambda i: (i, 0, 0)),
-        out_shape=jax.ShapeDtypeStruct((2 * experts, rows, cols), F32),
-        compiler_params=params(24, ("arbitrary",)),
-        cost_estimate=cost(1e6, 10e6),
-    )(*parts[0], *parts[1])
-
-
-def run_join_tall(place, parts):
-    experts, rows, cols = parts[0][3].shape
-    specs = []
-    for part in range(2):
-        def of(i, part=part):
-            return jnp.clip(i - part * experts, 0, experts - 1)
-
-        wide = pl.BlockSpec((1, 1, 1, rows, cols), lambda i, p, of=of: (0, 0, of(i), 0, 0))
-        specs += [
-            wide,
-            wide,
-            pl.BlockSpec((1, 1, rows, cols), lambda i, p, of=of: (0, of(i), 0, 0)),
-            pl.BlockSpec((1, rows, cols), lambda i, p, of=of: (of(i), 0, 0)),
-        ]
-    return pl.pallas_call(
-        join_tall_kernel,
+        join_kernel,
         grid_spec=pltpu.PrefetchScalarGridSpec(
             num_scalar_prefetch=1,
-            grid=(2 * experts,),
+            grid=(experts,),
             in_specs=specs,
-            out_specs=pl.BlockSpec((1, rows, 2 * cols), lambda i, p: (i, 0, 0)),
-        ),
-        out_shape=jax.ShapeDtypeStruct((2 * experts, rows, 2 * cols), F32),
-        compiler_params=params(24, ("arbitrary",)),
-        cost_estimate=cost(1e6, 12e6),
-    )(place, *parts[0], *parts[1])
+            out_specs=tuple(
+                pl.BlockSpec((2, 1) + shape, lambda i, p: (0, i, 0, 0)) for shape in shapes
+            ),
+        ),
+        out_shape=tuple(
+            jax.ShapeDtypeStruct((2, experts) + shape, F32) for shape in shapes
+        ),
+        compiler_params=params(60, ("arbitrary",)),
+        cost_estimate=cost(1e6, 26e6),
+    )(place, *halves[0], *halves[1])
 
 
 def fast_body(
@@ -1545,11 +1730,15 @@
 
     ranks = slot_order[0, 0].reshape(tokens, top)
     far = tokens * top
-    match = chosen.T[None] == jnp.arange(all_experts, dtype=jnp.int32)[:, None, None]
-    rank_map = jnp.min(jnp.where(match, ranks.T[None], far), axis=1)
-    before = jnp.sum((rank_map[:, None, :] < rank_map[:, :, None]).astype(jnp.int32), axis=-1)
-    slot_map = jnp.where(rank_map < far, jnp.minimum(before, SLOTS), -1).astype(BF)
-    map_rows = jnp.pad(slot_map.T.astype(F32), ((0, 0), (0, LANES - all_experts)), constant_values=-1.0)
+    names = jnp.arange(all_experts, dtype=jnp.int32)
+    match = chosen.T[None] == names[:, None, None]
+    rank_map = jnp.min(jnp.where(match, ranks.T[None], far), axis=1).astype(F32)
+    turned = rank_map.T
+    map_rows = jnp.pad(
+        jnp.where(turned < far, 0.0, -1.0),
+        ((0, 0), (0, LANES - all_experts)),
+        constant_values=-1.0,
+    )
     wr_pad = jnp.pad(w_router, ((0, 0), (0, LANES - all_experts)))
     wr_t = jnp.roll(w_router.T, -column * local_experts, axis=0)
     wr_t = jnp.pad(wr_t, ((0, LANES - all_experts), (0, 0)))
@@ -1563,93 +1752,99 @@
     angles = frequency[:, None] * jnp.arange(length, dtype=jnp.int32).astype(F32)[None]
     cos_t, sin_t = jnp.cos(angles), jnp.sin(angles)
 
-    normed, pack = run_pre(inputs, gain_attn, w_query, w_key, w_value, cos_tab, sin_tab)
-    g_own = cotangent.astype(BF)
-    pack, g_own, slot_map = fence(pack, g_own, slot_map)
+    normed, pack, g_own = run_pre(
+        inputs, gain_attn, w_query, w_key, w_value, cos_tab, sin_tab, cotangent
+    )
+    pack, slot_map = run_first(pack, rank_map, turned, float(far))
+    pack, slot_map, g_late = fence(pack, slot_map, g_own)
     g_x = swap_bit(g_own, X_BIT)
+    g_z = swap_bit(g_late, ZL_BIT)
     maps = stack_swap(slot_map[None], X_BIT)
-    pack = run_trade(pack, 2).reshape(length, PACK)
-    pack, g_x, maps, g_own = fence(pack, g_x, maps, g_own)
-    g_z = swap_bit(g_own, ZL_BIT)
+    out, out_t, lse = run_forward(pack)
+    out, g_x, g_z, maps = fence(out, g_x, g_z, maps)
+    g_zx = swap_bit(g_z, X_BIT)
     maps = stack_swap(maps, ZL_BIT)
-    out, out_t, lse = run_forward(pack)
-    out, g_z, maps = fence(out, g_z, maps)
-    g_zx = swap_bit(g_z, X_BIT)
-    maps = stack_swap(maps, C_BIT)
-    att = run_trade(out.reshape(shards, tokens, ROWS_Q), 3)
+    att = run_trade(out, 3)
     att, g_zx, maps = fence(att, g_zx, maps)
-    maps = jnp.roll(maps.astype(F32), -column * local_experts, axis=1)
     middle, normed_two, att_full = run_mid(att, w_output, inputs, gain_mlp)
-    x_all, g_all = run_gather(normed_two, (g_own, g_x, g_z, g_zx))
+    x_all, g_all, maps = run_gather(normed_two, (g_own, g_x, g_z, g_zx), maps)
+    maps = jnp.roll(maps, -column * local_experts, axis=1)
     expert_args = (place, x_all, g_all, maps, wr_t, w_gate, w_up, w_down)
-    *sums, gate_ka, gate_sa, up_ka, up_sa, down_ka, down_sa = run_experts(*expert_args)
-    down_ga = swap_bit(down_sa, Y_BIT)
-    (
-        mix_keep,
-        mix_send,
-        dx_keep,
-        dx_send,
-        gate_kb,
-        gate_sb,
-        up_kb,
-        up_sb,
-        down_kb,
-        down_sb,
-    ) = run_experts(*expert_args, prior=tuple(sums))
-    dx_send, gate_sa, down_ga, mix_send = fence(dx_send, gate_sa, down_ga, mix_send)
-    down_ma = swap_bit(first_sum(down_ka, down_ga), ZH_BIT)
-    gate_ga = swap_bit(gate_sa, Y_BIT)
+    first = run_experts(*expert_args)
+    gate_ka, gate_s0, gate_s1, up_ka, up_s0, up_s1, down_ka, down_s0, down_s1 = first[4:]
+    down_ya = swap_bit(down_s1, Y_BIT)
+    gate_ya = swap_bit(gate_s1, Y_BIT)
+    mix_keep, mix_send, dx_keep, dx_send, *second = run_experts(*expert_args, prior=first[:4])
+    gate_kb, gate_t0, gate_t1, up_kb, up_t0, up_t1, down_kb, down_t0, down_t1 = second
+    dx_send, down_ya, gate_ya = fence(dx_send, down_ya, gate_ya)
     quarter = tokens // 4
     extra = dx_keep.shape[2]
-    token_parts = tuple((n * quarter, quarter, 0, extra, (0, 1)) for n in range(4))
-    (dx_sum,) = run_reduce(((dx_keep, dx_send),), (token_parts,), (X_BIT, ZL_BIT), 6)
-    dx_sum, gate_ga, down_ma = fence(dx_sum, gate_ga, down_ma)
+    token_parts = tuple(
+        (n * quarter, quarter, 0, extra, (1, 0) if n < 2 else (0, 1)) for n in (2, 0, 3, 1)
+    )
+    dx_sum, up_ya, gate_ga, mix_got, down_ma = run_reduce(
+        ((dx_keep, dx_send),),
+        ((C_BIT, (X_BIT, ZL_BIT), token_parts, (extra,)),),
+        6,
+        riders=(
+            (up_s1, Y_BIT, 1),
+            (gate_s0, Y_BIT, 1),
+            (mix_send, C_BIT, 1),
+            (add_low(down_ka[1], down_ya), ZH_BIT, 5),
+        ),
+    )
+    dx_sum, gate_ya, down_s0 = fence(dx_sum, gate_ya, down_s0)
+    down_ga = swap_bit(down_s0, Y_BIT)
+    gate_za = swap_bit(add_low(gate_ka[1, 1], gate_ya[1]), ZH_BIT)
     d_att, d_middle, d_low, d_log, ggain_mlp = run_post(
         dx_sum, middle, cotangent, normed_two, wr_pad, map_rows, gain_mlp, w_output
     )
-    mix_got = swap_bit(mix_send, C_BIT)
     out_keep, out_send = run_outgrad(place, att_full, d_low, devices)
-    d_att, up_sa, out_send, mix_got = fence(d_att, up_sa, out_send, mix_got)
-    gate_ma = swap_bit(first_sum(gate_ka, gate_ga), ZH_BIT)
-    up_ga = swap_bit(up_sa, Y_BIT)
-    out_got = swap_bit(out_send, C_BIT)
+    d_att, out_send, gate_za, down_ga = fence(d_att, out_send, gate_za, down_ga)
     mix_keep = mix_keep.reshape(2, 2, tokens, WIDTH)
     mix_got = mix_got.reshape(2, 2, tokens, WIDTH)
-    mix_x = swap_bit(sum_pair(mix_keep[:, 1], mix_got[:, 1]).astype(BF), X_BIT)
-    d_out = run_trade(d_att, 4).reshape(length, ROWS_Q)
-    d_out, up_ga, gate_ma, gate_sb, mix_x, out_got = fence(
-        d_out, up_ga, gate_ma, gate_sb, mix_x, out_got
-    )
-    up_ma = swap_bit(first_sum(up_ka, up_ga), ZH_BIT)
-    gate_gb = swap_bit(gate_sb, Y_BIT)
-    gate_oa = swap_bit(low_sum(gate_ka, gate_ga, gate_ma), ZL_BIT)
-    mix_z = swap_bit(
-        (sum_pair(mix_keep[1, 0], mix_got[1, 0]) + mix_x[1].astype(F32)).astype(BF), ZL_BIT
+    d_out, gate_ma, up_za, gate_yb, up_yb, gate_oa, mix_x, out_got = run_trade(
+        d_att,
+        4,
+        riders=(
+            (add_low(gate_ka[1, 0], gate_ya[0]), ZH_BIT, 1),
+            (add_low(up_ka[1, 1], up_ya[1]), ZH_BIT, 1),
+            (gate_t1, Y_BIT, 1),
+            (up_t1, Y_BIT, 1),
+            (add_low(gate_ka[0, 1], gate_ga[1], gate_za), ZL_BIT, 1),
+            (add_low(mix_keep[:, 1], mix_got[:, 1]), X_BIT, 1),
+            (out_send, C_BIT, 1),
+        ),
     )
     split = (2, 2, 2, 2, WIDTH // devices, WIDTH)
     out_keep, out_got = out_keep.reshape(split), out_got.reshape(split)
-    out_x = swap_bit(sum_pair(out_keep[:, :, :, 1], out_got[:, :, :, 1]).astype(BF), X_BIT)
+    both = jnp.stack([add_low(up_ka[1, 0], up_ya[0]), add_low(gate_kb[1, 1], gate_yb[1])])
+    both = swap_bit(both, ZH_BIT)
+    up_ga, down_yb = fence(up_s0, down_t1, d_out)[:2]
+    up_ga = swap_bit(up_ga, Y_BIT)
+    down_yb = swap_bit(down_yb, Y_BIT)
     d_pack = run_backward(pack, d_out, out_t, lse, cos_t, sin_t)
-    d_pack, gate_gb, up_ma, up_sb, gate_oa, mix_z, out_x = fence(
-        d_pack, gate_gb, up_ma, up_sb, gate_oa, mix_z, out_x
-    )
-    gate_mb, up_oa = first_sum(gate_kb, gate_gb), low_sum(up_ka, up_ga, up_ma)
-    out_held = sum_pair(out_keep[:, :, :, 0], out_got[:, :, :, 0]) + out_x.astype(F32)
-    out_z = out_held[:, 1].astype(BF)
-    d_pack, gate_mb, up_oa, out_z = fence(d_pack, gate_mb, up_oa, out_z)
-    gate_mb = swap_bit(gate_mb, ZH_BIT)
-    up_gb = swap_bit(up_sb, Y_BIT)
-    up_oa = swap_bit(up_oa, ZL_BIT)
-    out_z = swap_bit(out_z, ZL_BIT)
-    d_pack = run_trade(d_pack.reshape(shards, tokens, PACK), 5)
-    d_pack, up_gb, gate_mb, down_sb, up_oa, out_z = fence(
-        d_pack, up_gb, gate_mb, down_sb, up_oa, out_z
-    )
-    up_mb = swap_bit(first_sum(up_kb, up_gb), ZH_BIT)
-    down_gb = swap_bit(down_sb, Y_BIT)
-    gate_ob = swap_bit(low_sum(gate_kb, gate_gb, gate_mb), ZL_BIT)
-    out_held = out_held[:, 0] + out_z.astype(F32)
-    out_y = swap_bit(out_held[:, 1].astype(BF), Y_BIT)
+    d_pack, both, up_ga, down_yb = fence(d_pack, both, up_ga, down_yb)
+    up_ma, gate_zb = both[0], both[1]
+    d_pack, gate_mb, up_zb, mix_z, out_x, gate_gb, up_gb, up_oa = run_trade(
+        d_pack,
+        5,
+        riders=(
+            (add_low(gate_kb[1, 0], gate_yb[0]), ZH_BIT, 1),
+            (add_low(up_kb[1, 1], up_yb[1]), ZH_BIT, 1),
+            (add_low(mix_keep[1, 0], mix_got[1, 0], mix_x[1]), ZL_BIT, 1),
+            (add_low(out_keep[:, :, :, 1], out_got[:, :, :, 1]), X_BIT, 1),
+            (gate_t0, Y_BIT, 1),
+            (up_t0, Y_BIT, 1),
+            (add_low(up_ka[0, 1], up_ga[1], up_za), ZL_BIT, 1),
+        ),
+    )
+    d_pack, up_yb, down_yb, gate_gb, down_t0, mix_z, out_x = fence(
+        d_pack, up_yb, down_yb, gate_gb, down_t0, mix_z, out_x
+    )
+    up_mb = swap_bit(add_low(up_kb[1, 0], up_yb[0]), ZH_BIT)
+    down_mb = swap_bit(add_low(down_kb[1], down_yb), ZH_BIT)
+    down_gb = swap_bit(down_t0, Y_BIT)
     d_full, qkv_keep, qkv_send = run_qkvgrad(place, normed, d_pack, devices)
     grad_in, ggain_attn = run_last(
         d_full, w_query, w_key, w_value, d_middle, inputs, gain_attn
@@ -1657,42 +1852,55 @@
     small_keep, small_send = run_small(place, normed_two, d_log, ggain_mlp, ggain_attn, devices)
     mixed = sum_pair(mix_keep[0, 0], mix_got[0, 0]) + sum_pair(mix_x[0], mix_z)
     hidden_out = middle + mixed
-    qkv_send, small_send, up_mb, down_gb, gate_ob, out_y, hidden_out = fence(
-        qkv_send, small_send, up_mb, down_gb, gate_ob, out_y, hidden_out
-    )
-    down_mb = swap_bit(first_sum(down_kb, down_gb), ZH_BIT)
-    up_ob = swap_bit(low_sum(up_kb, up_gb, up_mb), ZL_BIT)
-    out_held = out_held[:, 0] + out_y.astype(F32)
-    out_h = swap_bit(out_held[1].astype(BF), ZH_BIT)
+    out_held = add_low(out_keep[:, :, :, 0], out_got[:, :, :, 0], out_x)
     rows = WIDTH // devices
-    dense_parts = (
+    out_first = out_held[:, :, 0].reshape(4, rows, WIDTH)
+    out_second = out_held[:, :, 1].reshape(4, rows, WIDTH)
+    qkv_send, small_send, out_second, hidden_out = fence(
+        qkv_send, small_send, out_second, hidden_out
+    )
+    qkv_parts = (
         (0, rows, 0, 768, (0, 1, 2, 3)),
-        (0, rows, 768, 768, (1, 2, 0, 3)),
-        (0, rows, 1536, 1024, (2, 0, 1, 3)),
-    )
-    qkv_total, small = run_reduce(
-        ((qkv_keep, qkv_send), (small_keep, small_send)),
-        (dense_parts, ((0, rows, 0, LANES, (0, 1, 2, 3)),)),
-        (X_BIT, Y_BIT, ZL_BIT, ZH_BIT),
+        (0, rows, 768, 768, (1, 0, 2, 3)),
+        (0, rows, 1536, 512, (0, 1, 2, 3)),
+        (0, rows, 2048, 512, (1, 0, 2, 3)),
+    )
+    dense_bits = (X_BIT, Y_BIT, ZL_BIT, ZH_BIT)
+    query_total, key_total, value_total, small, output_total, gate_ob, up_ob = run_reduce(
+        ((qkv_keep, qkv_send), (small_keep, small_send), (out_first, out_second)),
+        (
+            (C_BIT, dense_bits, qkv_parts, (WIDTH, KV_HEADS * HEAD_DIM, KV_HEADS * HEAD_DIM)),
+            (C_BIT, dense_bits, ((0, rows, 0, LANES, (0, 1, 2, 3)),), (LANES,)),
+            (Y_BIT, (ZL_BIT, ZH_BIT), ((0, rows, 0, WIDTH, (0, 1)),), (WIDTH,)),
+        ),
         7,
-    )
-    qkv_total, small, down_mb, up_ob, out_h = fence(qkv_total, small, down_mb, up_ob, out_h)
-    output_total = sum_pair(out_held[0], out_h)
-    down_total = run_join_down(((down_ka, down_ga, down_ma), (down_kb, down_gb, down_mb)))
-    gate_total = run_join_tall(
-        place, ((gate_ka, gate_ga, gate_ma, gate_oa), (gate_kb, gate_gb, gate_mb, gate_ob))
-    )
-    up_total = run_join_tall(
-        place, ((up_ka, up_ga, up_ma, up_oa), (up_kb, up_gb, up_mb, up_ob))
-    )
-    key_width = KV_HEADS * HEAD_DIM
+        riders=(
+            (add_low(gate_kb[0, 1], gate_gb[1], gate_zb), ZL_BIT, 1),
+            (add_low(up_kb[0, 1], up_gb[1], up_zb), ZL_BIT, 1),
+        ),
+    )
+    query_total, small, up_mb, down_mb, down_gb, up_ob = fence(
+        query_total, small, up_mb, down_mb, down_gb, up_ob
+    )
+    joined = run_join(
+        place,
+        (
+            (gate_ka, gate_ga, gate_ma, gate_oa, up_ka, up_ga, up_ma, up_oa)
+            + (down_ka, down_ga, down_ma),
+            (gate_kb, gate_gb, gate_mb, gate_ob, up_kb, up_gb, up_mb, up_ob)
+            + (down_kb, down_gb, down_mb),
+        ),
+    )
+    gate_total, up_total, down_total = [
+        total.reshape((local_experts,) + total.shape[2:]) for total in joined
+    ]
     return (
         hidden_out[None],
         grad_in[None],
         small[:, LANES - 1],
-        qkv_total[:, :WIDTH],
-        qkv_total[:, WIDTH : WIDTH + key_width],
-        qkv_total[:, WIDTH + key_width :],
+        query_total,
+        key_total,
+        value_total,
         output_total,
         small[:, LANES - 2],
         small[:, :all_experts],

time: 831 us -> 761 us (0.916)
  waiting for transfers between devices: 43.4 us -> 0.04 us
  local copies, waits for them, and re-layouts: 41.5 us -> 17.6 us
  starting transfers between devices: 28 us -> 16.5 us
    ppermute x30 -> x15, waiting for transfers between devices: 43.4 us -> 0.04 us  [swap(): return lax.ppermute(values, axis, [(i, i ^ mask) for i in range(size)])]
    unnamed x136 -> x70, local copies, waits for them, and re-layouts: 31.1 us -> 6.27 us
    ppermute x30 -> x15, starting transfers between devices: 28 us -> 16.5 us  [swap(): return lax.ppermute(values, axis, [(i, i ^ mask) for i in range(size)])]
    pallas_call x12 -> x10, Pallas kernels: 507 us -> 496 us  [the longest x3 175 us: run_trade(): pl.pallas_call(functools.partial(trade_kernel, riders=tuple((rider[1:] fo...]
    convert_element_type x15 -> x17, other arithmetic: 24.8 us -> 35.5 us  [the longest x16 35.5 us: add_low(): return sum((term.astype(F32) for term in terms)).astype(BF)]
  transfers between devices with their start and end apart: 30 -> 15, of which waited for: 4 -> 0; matrix products, arithmetic and copies ran while one was open for 4% -> 5% of each run, Pallas kernels for 66% -> 43%
where the time goes in v3:
time: 761 us; the launch traced here: 754 us
  Pallas kernels  668 us (88%)
  other arithmetic  50.2 us (7%)
  local copies, waits for them, and re-layouts  17.6 us (2%)
  starting transfers between devices  16.5 us (2%)
    pallas_call x3, Pallas kernels, run_trade(): pl.pallas_call(functools.partial(trade_kernel, riders=tuple((rider[1:] fo...  175 us
    pallas_call x2, Pallas kernels, run_reduce(): pl.pallas_call(functools.partial(reduce_kernel, jobs=jobs, riders=tuple((...  152 us
    pallas_call x2, Pallas kernels, run_experts(): pl.pallas_call(functools.partial(expert_kernel, first=not prior), grid_sp...  114 us
    pallas_call x1, Pallas kernels, run_first(): pl.pallas_call(functools.partial(first_kernel, far=far), in_specs=[hbm, v...  43.8 us
    pallas_call x1, Pallas kernels, run_backward(): pl.pallas_call(backward_kernel, grid=(blocks,), in_specs=[pl.BlockSpec(pa...  43.5 us
    pallas_call x1, Pallas kernels, run_gather(): pl.pallas_call(gather_kernel, in_specs=[pl.BlockSpec(memory_space=pltpu.V...  38.9 us
    convert_element_type x16, other arithmetic, add_low(): return sum((term.astype(F32) for term in terms)).astype(BF)  35.5 us
    pallas_call x1, Pallas kernels, run_forward(): pl.pallas_call(forward_kernel, grid=(blocks,), in_specs=[pl.BlockSpec(pac...  30.5 us
  transfers between devices with their start and end apart: 15, of which 0 were waited for; matrix products, arithmetic and copies ran while one was open for 5% of the time, Pallas kernels for 43%

profile of v3, /device:TPU:0, one launch (start us, length us, event | category | flops | bytes accessed | tf_op | source)
XLA Modules:
  0.0 753.9 jit_solution(6207872076540644801)
XLA Ops:
  3.7 9.0 %shard_map.229 = (bf16[320,1536]{1,0:T(8,128)(2,1)}, bf16[8,800,128]{2,1,0:T(8,128)(2,1)}, bf16[320,1536]{1,0:T(8,128)(2,1)}) custom-call(f32[320,1536]{1,0:T(8,128)} %bitcast.138, f32[1,1536]{1,0:T(1,128)} %broadcast_in_dim.44.gain_ref, bf16[1536,1536]{1,0:T(8,128)(2,1)} %wq_ref.3, bf16[1536,512]{1,0:T(8,128)(2,1)} %wk_ref.3, bf16[1536,512]{1,0:T(8,128)(2,1)} %wv_ref.3, ...), custom_call_target="tpu_custom_call" | custom-call | flops 2516582400 | bytes 14000000 | tf_op jit(solution)/shard_map/pallas_call | solution.py:486
  12.7 2.9 collective-permute-start
  16.9 43.8 %shard_map.230 = (bf16[8,800,128]{2,1,0:T(8,128)(2,1)}, f32[40,320]{1,0:T(8,128)}) custom-call(bf16[8,800,128]{2,1,0:T(8,128)(2,1)} %get-tuple-element.141.a_ref, f32[40,320]{1,0:T(8,128)} %copy-done.20, f32[320,40]{1,0:T(8,128)} %bitcast.156), custom_call_target="tpu_custom_call" | custom-call | bytes 170000000 | tf_op jit(solution)/shard_map/pallas_call | solution.py:1469
  61.5 30.5 %shard_map.231 = (bf16[8,480,128]{2,1,0:T(8,128)(2,1)}, f32[10,64,768]{2,1,0:T(8,128)}, f32[10,1,768]{2,1,0:T(1,128)}) custom-call(bf16[8,800,128]{2,1,0:T(8,128)(2,1)} %get-tuple-element.145.pack_ref), custom_call_target="tpu_custom_call" | custom-call | flops 10066329600 | bytes 6000000 | tf_op jit(solution)/shard_map/pallas_call | solution.py:601
  104.6 23.9 %shard_map.232.att_ref = bf16[8,480,128]{2,1,0:T(8,128)(2,1)} custom-call(bf16[8,480,128]{2,1,0:T(8,128)(2,1)} %get-tuple-element.149.refs_0_), custom_call_target="tpu_custom_call" | custom-call | bytes 170000000 | tf_op jit(solution)/shard_map/pallas_call | solution.py:1441
  130.2 7.3 shard_map.233
  137.6 38.9 %shard_map.234 = (bf16[8,320,1536]{2,1,0:T(8,128)(2,1)}, bf16[8,320,1536]{2,1,0:T(8,128)(2,1)}, f32[8,40,320]{2,1,0:T(8,128)}) custom-call(bf16[320,1536]{1,0:T(8,128)(2,1)} %get-tuple-element.153.x_ref.norm_ref, bf16[320,1536]{1,0:T(8,128)(2,1)} %get-tuple-element.147.refs_0_, bf16[320,1536]{1,0:T(8,128)(2,1)} %copy-done.14, bf16[320,1536]{1,0:T(8,128)(2,1)} %copy-done.15, ...), custom_call_target="tpu_custom_call" | custom-call | bytes 150000000 | tf_op jit(solution)/shard_map/pallas_call | solution.py:1341
  178.4 55.5 %shard_map.235 = (bf16[4,320,1536]{2,1,0:T(8,128)(2,1)}, bf16[4,320,1536]{2,1,0:T(8,128)(2,1)}, bf16[4,320,1664]{2,1,0:T(8,128)(2,1)}, bf16[4,320,1664]{2,1,0:T(...) custom-call(s32[6]{0:T(128)} %stack.29.place_ref, ...), custom_call_target="tpu_custom_call" | custom-call | flops 30000001024 | bytes 60000000 | tf_op jit(solution)/shard_map/pallas_call | solution.py:999
  236.0 58.8 %shard_map.236 = (bf16[4,320,1536]{2,1,0:T(8,128)(2,1)}, bf16[4,320,1536]{2,1,0:T(8,128)(2,1)}, bf16[4,320,1664]{2,1,0:T(8,128)(2,1)}, bf16[4,320,1664]{2,1,0:T(...) custom-call(s32[6]{0:T(128)} %stack.29.place_ref, ...), custom_call_target="tpu_custom_call" | custom-call | flops 30000001024 | bytes 60000000 | tf_op jit(solution)/shard_map/pallas_call | solution.py:999
  296.1 67.5 %shard_map.237 = (f32[320,1664]{1,0:T(8,128)}, bf16[2,5,192,256]{3,2,1,0:T(8,128)(2,1)}, bf16[2,5,192,256]{3,2,1,0:T(8,128)(2,1)}, bf16[4,320,1536]{2,1,0:T(8,128)(2,1)}, bf16[5,64,1536]{2,1,0:T(8,128)(2,1)}) custom-call(bf16[4,320,1664]{2,1,0:T(8,128)(2,1)} %get-tuple-element.164.refs_0_, bf16[4,320,1664]{2,1,0:T(8,128)(2,1)} %get-tuple-element.168.refs_1_, ...), custom_call_target="tpu_custom_call" | custom-call | bytes 170000000 | tf_op jit(solution)/shard_map/pallas_call | solution.py:1611
  368.7 9.3 %shard_map.238 = (bf16[8,480,128]{2,1,0:T(8,128)(2,1)}, f32[320,1536]{1,0:T(8,128)}, bf16[320,1536]{1,0:T(8,128)(2,1)}, bf16[320,128]{1,0:T(8,128)(2,1)}, f32[1,1536]{1,0:T(1,128)}) custom-call(f32[320,1664]{1,0:T(8,128)} %get-tuple-element.177.dx_ref, f32[320,1536]{1,0:T(8,128)} %get-tuple-element.178.mid_ref, f32[320,1536]{1,0:T(8,128)} %bitcast.142, ...), custom_call_target="tpu_custom_call" | custom-call | flops 1509949440 | bytes 14000000 | tf_op jit(solution)/shard_map/pallas_call | solution.py:1089
  378.0 7.9 %shard_map.239 = (bf16[16,48,1536]{2,1,0:T(8,128)(2,1)}, bf16[16,48,1536]{2,1,0:T(8,128)(2,1)}) custom-call(s32[6]{0:T(128)} %stack.29.place_ref, bf16[320,1536]{1,0:T(8,128)(2,1)} %get-tuple-element.180.a_ref, bf16[320,1536]{1,0:T(8,128)(2,1)} %get-tuple-element.181.b_ref), custom_call_target="tpu_custom_call" | custom-call | flops 1509949440 | bytes 8000000 | tf_op jit(solution)/shard_map/pallas_call | solution.py:1123
  387.9 4.0 fusion.1.refs_6_
  394.0 68.0 %shard_map.240 = (bf16[8,480,128]{2,1,0:T(8,128)(2,1)}, bf16[5,192,256]{2,1,0:T(8,128)(2,1)}, bf16[5,192,256]{2,1,0:T(8,128)(2,1)}, bf16[2,5,192,256]{3,2,1,0:T(...) custom-call(bf16[8,480,128]{2,1,0:T(8,128)(2,1)} %get-tuple-element., ...), custom_call_target="tpu_custom_call" | custom-call | bytes 170000000 | tf_op jit(solution)/shard_map/pallas_call | solution.py:1441
  470.1 43.5 %shard_map.241.refs_0_ = bf16[8,800,128]{2,1,0:T(8,128)(2,1)} custom-call(bf16[8,800,128]{2,1,0:T(8,128)(2,1)} %get-tuple-element.145.pack_ref, bf16[8,480,128]{2,1,0:T(8,128)(2,1)} %get-tuple-element.196.grad_ref, f32[10,64,768]{2,1,0:T(8,128)} %get-tuple-element.197.out_t_ref, f32[10,1,768]{2,1,0:T(1,128)} %get-tuple-element.198.lse_ref, ...), custom_call_target="tpu_custom_call" | custom-call | flops 25165824000 | bytes 8000000 | tf_op jit(solution)/shard_map/pallas_call | solution.py:722
  517.8 2.9 fusion.5.refs_3_
  522.7 82.7 %shard_map.242 = (bf16[8,800,128]{2,1,0:T(8,128)(2,1)}, bf16[5,192,256]{2,1,0:T(8,128)(2,1)}, bf16[5,192,256]{2,1,0:T(8,128)(2,1)}, bf16[320,1536]{1,0:T(8,128)(...) custom-call(bf16[8,800,128]{2,1,0:T(8,128)(2,1)} %shard_map.241.refs, ...), custom_call_target="tpu_custom_call" | custom-call | bytes 170000000 | tf_op jit(solution)/shard_map/pallas_call | solution.py:1441
  610.1 3.5 fusion.4
  619.3 11.6 %shard_map.243 = (bf16[320,2560]{1,0:T(8,128)(2,1)}, bf16[16,48,2560]{2,1,0:T(8,128)(2,1)}, bf16[16,48,2560]{2,1,0:T(8,128)(2,1)}) custom-call(s32[6]{0:T(128)} %stack.29.place_ref, bf16[320,1536]{1,0:T(8,128)(2,1)} %get-tuple-element.140.a_ref, bf16[8,800,128]{2,1,0:T(8,128)(2,1)} %get-tuple-element.221.d_ref), custom_call_target="tpu_custom_call" | custom-call | flops 2516582400 | bytes 12000000 | tf_op jit(solution)/shard_map/pallas_call | solution.py:1172
  630.9 9.4 %shard_map.244 = (f32[320,1536]{1,0:T(8,128)}, f32[1,1536]{1,0:T(1,128)}) custom-call(bf16[320,2560]{1,0:T(8,128)(2,1)} %get-tuple-element.225.d_ref, bf16[1536,1536]{1,0:T(8,128)(2,1)} %wq_ref.3, bf16[1536,512]{1,0:T(8,128)(2,1)} %wk_ref.3, bf16[1536,512]{1,0:T(8,128)(2,1)} %wv_ref.3, f32[320,1536]{1,0:T(8,128)} %get-tuple-element.226.dmid_ref, ...), custom_call_target="tpu_custom_call" | custom-call | flops 2516582400 | bytes 16000000 | tf_op jit(solution)/shard_map/pallas_call | solution.py:1209
  640.3 3.4 shard_map.245
  643.8 2.7 fusion.8
  649.0 84.9 %shard_map.246 = (f32[48,1536]{1,0:T(8,128)}, f32[48,512]{1,0:T(8,128)}, f32[48,512]{1,0:T(8,128)}, f32[48,128]{1,0:T(8,128)}, f32[48,1536]{1,0:T(8,128)}, /*ind...) custom-call(bf16[16,48,2560]{2,1,0:T(8,128)(2,1)} %get-tuple-element.233.refs_0_, ...), custom_call_target="tpu_custom_call" | custom-call | bytes 170000000 | tf_op jit(solution)/shard_map/pallas_call | solution.py:1611
  738.8 12.2 %shard_map.247 = (f32[2,5,192,512]{3,2,1,0:T(8,128)}, f32[2,5,192,512]{3,2,1,0:T(8,128)}, f32[2,5,64,1536]{3,2,1,0:T(8,128)}) custom-call(s32[6]{0:T(128)} %stack.29.place_ref, bf16[2,2,5,192,256]{4,3,2,1,0:T(8,128)(2,1)} %get-tuple-element.183.refs_0_, bf16[2,5,192,256]{3,2,1,0:T(8,128)(2,1)} %get-tuple-element.191.refs_1_, ...), custom_call_target="tpu_custom_call" | custom-call | flops 1000000 | bytes 26000000 | tf_op jit(solution)/shard_map/pallas_call | solution.py:1677
  (139 shorter events, 68.2 us)
Async XLA Ops:
  12.7 48.1 %copy-start.13 = (bf16[320,1536]{1,0:T(8,128)(2,1)S(1)}, bf16[320,1536]{1,0:T(8,128)(2,1)}, u32[]{:S(2)}) copy-start(bf16[320,1536]{1,0:T(8,128)(2,1)} %get-tuple-element.147.refs_0_) | copy-start | bytes 2949124
  12.7 80.0 %collective-permute-start = (bf16[320,1536]{1,0:T(8,128)(2,1)}, bf16[320,1536]{1,0:T(8,128)(2,1)S(1)}, u32[]{:S(2)}, u32[]{:S(2)}) collective-permute-start(bf16[320,1536]{1,0:T(8,128)(2,1)} %get-tuple-element.147.refs_0_), channel_id=1, source_target_pairs={{0,2},{1,3},{2,0},{3,1},{4,6},{5,7},{6,4},{7,5},{8,10},{9,11},{10,... | collective-permute-start | bytes 2949128 | tf_op jit(solution)/shard_map/ppermute | solution.py:412
  16.9 44.5 %copy-start.12 = (f32[40,320]{0,1:T(8,128)S(1)}, f32[40,320]{0,1:T(8,128)}, u32[]{:S(2)}) copy-start(f32[40,320]{0,1:T(8,128)} %copy.49) | copy-start | bytes 153604
  60.7 31.9 %collective-permute-start.1 = (bf16[320,1536]{1,0:T(8,128)(2,1)S(1)}, bf16[320,1536]{1,0:T(8,128)(2,1)S(1)}, u32[]{:S(2)}, u32[]{:S(2)}) collective-permute-start(bf16[320,1536]{1,0:T(8,128)(2,1)S(1)} %copy-done.13), channel_id=1, source_target_pairs={{0,8},{4,12},{8,0},{12,4},{16,24},{20,28},{24,16},{28,20},{1,9},{5... | collective-permute-start | bytes 2949128 | tf_op jit(solution)/shard_map/ppermute | solution.py:412
  60.8 31.2 %collective-permute-start.2 = (f32[1,40,320]{2,1,0:T(8,128)}, f32[1,40,320]{2,1,0:T(8,128)S(1)}, u32[]{:S(2)}, u32[]{:S(2)}) collective-permute-start(f32[1,40,320]{2,1,0:T(8,128)} %bitcast.160), channel_id=1, source_target_pairs={{0,2},{1,3},{2,0},{3,1},{4,6},{5,7},{6,4},{7,5},{8,10},{9,11},{10,... | collective-permute-start | bytes 153608 | tf_op jit(solution)/shard_map/ppermute | solution.py:412
  61.4 36.8 %copy-start.22 = (bf16[1536,40]{0,1:T(8,128)(2,1)S(1)}, bf16[1536,40]{0,1:T(8,128)(2,1)}, u32[]{:S(2)}) copy-start(bf16[1536,40]{0,1:T(8,128)(2,1)} %param.21) | copy-start | bytes 368644
  61.4 38.7 %copy-start.31 = (f32[1536]{0:T(1024)S(1)}, f32[1536]{0:T(1024)}, u32[]{:S(2)}) copy-start(f32[1536]{0:T(1024)} %param.20) | copy-start | bytes 18436
  92.7 35.9 %copy-start.14 = (bf16[320,1536]{1,0:T(8,128)(2,1)}, bf16[320,1536]{1,0:T(8,128)(2,1)S(1)}, u32[]{:S(2)}) copy-start(bf16[320,1536]{1,0:T(8,128)(2,1)S(1)} %collective-permute-done.refs_1_) | copy-start | bytes 2949124
  92.7 35.9 %copy-start.15 = (bf16[320,1536]{1,0:T(8,128)(2,1)}, bf16[320,1536]{1,0:T(8,128)(2,1)S(1)}, u32[]{:S(2)}) copy-start(bf16[320,1536]{1,0:T(8,128)(2,1)S(1)} %collective-permute-done.1.refs_2_) | copy-start | bytes 2949124
  92.7 37.6 %collective-permute-start.3 = (bf16[320,1536]{1,0:T(8,128)(2,1)S(1)}, bf16[320,1536]{1,0:T(8,128)(2,1)S(1)}, u32[]{:S(2)}, u32[]{:S(2)}) collective-permute-start(bf16[320,1536]{1,0:T(8,128)(2,1)S(1)} %collective-permute-done.1.refs_2_), channel_id=1, source_target_pairs={{0,2},{1,3},{2,0},{3,1},{4,6},{5,7},{6,4},{7,5},{8,10},{9,11},{10,... | collective-permute-start | bytes 2949128 | tf_op jit(solution)/shard_map/ppermute | solution.py:412
  96.3 32.3 %collective-permute-start.4 = (f32[2,40,320]{2,1,0:T(8,128)}, f32[2,40,320]{2,1,0:T(8,128)}, u32[]{:S(2)}, u32[]{:S(2)}) collective-permute-start(f32[2,40,320]{2,1,0:T(8,128)} %pad_maximum_fusion.4), channel_id=1, source_target_pairs={{0,8},{4,12},{8,0},{12,4},{16,24},{20,28},{24,16},{28,20},{1,9},{5... | collective-permute-start | bytes 307208 | tf_op jit(solution)/shard_map/ppermute | solution.py:412
  233.9 60.9 %collective-permute-start.5 = (bf16[5,64,1536]{2,1,0:T(8,128)(2,1)}, bf16[5,64,1536]{2,1,0:T(8,128)(2,1)S(1)}, u32[]{:S(2)}, u32[]{:S(2)}) collective-permute-start(bf16[5,64,1536]{2,1,0:T(8,128)(2,1)} %get-tuple-element.166), channel_id=1, source_target_pairs={{0,4},{4,0},{8,12},{12,8},{16,20},{20,16},{24,28},{28,24},{1,5},{5... | collective-permute-start | bytes 2949128 | tf_op jit(solution)/shard_map/ppermute | solution.py:412
  235.5 59.4 %collective-permute-start.6 = (bf16[2,5,192,256]{3,2,1,0:T(8,128)(2,1)}, bf16[2,5,192,256]{3,2,1,0:T(8,128)(2,1)S(1)}, u32[]{:S(2)}, u32[]{:S(2)}) collective-permute-start(bf16[2,5,192,256]{3,2,1,0:T(8,128)(2,1)} %get-tuple-element.167), channel_id=1, source_target_pairs={{0,4},{4,0},{8,12},{12,8},{16,20},{20,16},{24,28},{28,24},{1,5},{5... | collective-permute-start | bytes 2949128 | tf_op jit(solution)/shard_map/ppermute | solution.py:412
  236.0 58.9 %copy-start.5 = (bf16[2,5,64,1536]{3,2,1,0:T(8,128)(2,1)S(1)}, bf16[2,5,64,1536]{3,2,1,0:T(8,128)(2,1)}, u32[]{:S(2)}) copy-start(bf16[2,5,64,1536]{3,2,1,0:T(8,128)(2,1)} %get-tuple-element.172.refs_8_) | copy-start | bytes 5898244
  296.1 67.5 %copy-start.1 = (bf16[2,2,5,192,256]{4,3,2,1,0:T(8,128)(2,1)S(1)}, bf16[2,2,5,192,256]{4,3,2,1,0:T(8,128)(2,1)}, u32[]{:S(2)}) copy-start(bf16[2,2,5,192,256]{4,3,2,1,0:T(8,128)(2,1)} %get-tuple-element.183.refs_0_) | copy-start | bytes 5898244
  366.2 25.7 %collective-permute-start.7 = (bf16[5,192,256]{2,1,0:T(8,128)(2,1)}, bf16[5,192,256]{2,1,0:T(8,128)(2,1)}, u32[]{:S(2)}, u32[]{:S(2)}) collective-permute-start(bf16[5,192,256]{2,1,0:T(8,128)(2,1)} %get-tuple-element.319), channel_id=1, source_target_pairs={{0,16},{4,20},{8,24},{12,28},{16,0},{20,4},{24,8},{28,12},{1,17},{... | collective-permute-start | bytes 1474568 | tf_op jit(solution)/shard_map/ppermute | solution.py:412
  366.4 25.5 %collective-permute-start.8 = (bf16[5,64,1536]{2,1,0:T(8,128)(2,1)}, bf16[5,64,1536]{2,1,0:T(8,128)(2,1)}, u32[]{:S(2)}, u32[]{:S(2)}) collective-permute-start(bf16[5,64,1536]{2,1,0:T(8,128)(2,1)} %get-tuple-element.185), channel_id=1, source_target_pairs={{0,4},{4,0},{8,12},{12,8},{16,20},{20,16},{24,28},{28,24},{1,5},{5... | collective-permute-start | bytes 2949128 | tf_op jit(solution)/shard_map/ppermute | solution.py:412
  394.0 68.0 %copy-start.3 = (bf16[2,2,5,192,256]{4,3,2,1,0:T(8,128)(2,1)S(1)}, bf16[2,2,5,192,256]{4,3,2,1,0:T(8,128)(2,1)}, u32[]{:S(2)}) copy-start(bf16[2,2,5,192,256]{4,3,2,1,0:T(8,128)(2,1)} %get-tuple-element.199.refs_11_) | copy-start | bytes 5898244
  465.4 55.3 %collective-permute-start.9 = (bf16[2,5,192,256]{3,2,1,0:T(8,128)(2,1)}, bf16[2,5,192,256]{3,2,1,0:T(8,128)(2,1)}, u32[]{:S(2)}, u32[]{:S(2)}) collective-permute-start(bf16[2,5,192,256]{3,2,1,0:T(8,128)(2,1)} %pad_maximum_fusion), channel_id=1, source_target_pairs={{0,16},{4,20},{8,24},{12,28},{16,0},{20,4},{24,8},{28,12},{1,17},{... | collective-permute-start | bytes 2949128 | tf_op jit(solution)/shard_map/ppermute | solution.py:412
  465.4 55.3 %collective-permute-start.10 = (bf16[2,5,192,256]{3,2,1,0:T(8,128)(2,1)}, bf16[2,5,192,256]{3,2,1,0:T(8,128)(2,1)}, u32[]{:S(2)}, u32[]{:S(2)}) collective-permute-start(bf16[2,5,192,256]{3,2,1,0:T(8,128)(2,1)} %get-tuple-element.203), channel_id=1, source_target_pairs={{0,4},{4,0},{8,12},{12,8},{16,20},{20,16},{24,28},{28,24},{1,5},{5... | collective-permute-start | bytes 2949128 | tf_op jit(solution)/shard_map/ppermute | solution.py:412
  466.8 53.9 %collective-permute-start.11 = (bf16[5,64,1536]{2,1,0:T(8,128)(2,1)}, bf16[5,64,1536]{2,1,0:T(8,128)(2,1)}, u32[]{:S(2)}, u32[]{:S(2)}) collective-permute-start(bf16[5,64,1536]{2,1,0:T(8,128)(2,1)} %get-tuple-element.204), channel_id=1, source_target_pairs={{0,4},{4,0},{8,12},{12,8},{16,20},{20,16},{24,28},{28,24},{1,5},{5... | collective-permute-start | bytes 2949128 | tf_op jit(solution)/shard_map/ppermute | solution.py:412
  616.1 119.7 %collective-permute-start.13 = (bf16[5,64,1536]{2,1,0:T(8,128)(2,1)}, bf16[5,64,1536]{2,1,0:T(8,128)(2,1)}, u32[]{:S(2)}, u32[]{:S(2)}) collective-permute-start(bf16[5,64,1536]{2,1,0:T(8,128)(2,1)} %fusion.2), channel_id=1, source_target_pairs={{0,16},{4,20},{8,24},{12,28},{16,0},{20,4},{24,8},{28,12},{1,17},{... | collective-permute-start | bytes 2949128 | tf_op jit(solution)/shard_map/ppermute | solution.py:412
  617.8 118.0 %collective-permute-start.14 = (bf16[5,64,1536]{2,1,0:T(8,128)(2,1)}, bf16[5,64,1536]{2,1,0:T(8,128)(2,1)}, u32[]{:S(2)}, u32[]{:S(2)}) collective-permute-start(bf16[5,64,1536]{2,1,0:T(8,128)(2,1)} %get-tuple-element.247), channel_id=1, source_target_pairs={{0,4},{4,0},{8,12},{12,8},{16,20},{20,16},{24,28},{28,24},{1,5},{5... | collective-permute-start | bytes 2949128 | tf_op jit(solution)/shard_map/ppermute | solution.py:412
  646.4 89.3 %collective-permute-start.12 = (bf16[5,192,256]{2,1,0:T(8,128)(2,1)}, bf16[5,192,256]{2,1,0:T(8,128)(2,1)S(1)}, u32[]{:S(2)}, u32[]{:S(2)}) collective-permute-start(bf16[5,192,256]{2,1,0:T(8,128)(2,1)} %get-tuple-element.320), channel_id=1, source_target_pairs={{0,16},{4,20},{8,24},{12,28},{16,0},{20,4},{24,8},{28,12},{1,17},{... | collective-permute-start | bytes 1474568 | tf_op jit(solution)/shard_map/ppermute | solution.py:412
  (23 other events, 174.0 us)

commit v4 on v3

--- a/solution.py
+++ b/solution.py
@@ -1383,32 +1383,106 @@
         copy.wait_send()
 
 
-def ride_pieces(sources, targets, riders, send_sem, recv_sem):
-    starts, copies = [], []
-    for n, (bit, pieces) in enumerate(riders):
-        size = sources[n].shape[0] // pieces
+class Rider:
+    def __init__(self, bit, *terms, pieces=1, turns=(0,)):
+        self.bit, self.pieces, self.turns = bit, pieces, turns
+        self.arrays = [term[0] if isinstance(term, tuple) else term for term in terms]
+        self.parts = [term[1] if isinstance(term, tuple) else None for term in terms]
+        array, part = self.arrays[0], self.parts[0]
+        shape = array.shape
+        if part is not None:
+            kept = [len(range(n)[k]) for k, n in zip(part, shape) if not isinstance(k, int)]
+            shape = tuple(kept) + shape[len(part) :]
+        self.shape = jax.ShapeDtypeStruct(shape, array.dtype)
+        self.direct = len(terms) == 1 and part is None
+
+    def scratch(self):
+        if self.direct:
+            return []
+        buffer = pltpu.VMEM(self.shape.shape, self.shape.dtype)
+        return [buffer] * (len(self.arrays) + 1)
+
+    def plan(self):
+        return (self.bit, self.pieces, self.turns, tuple(self.parts), self.direct)
+
+
+def rider_inputs(riders):
+    return [array for rider in riders for array in rider.arrays]
+
+
+def rider_shapes(riders):
+    return tuple(rider.shape for rider in riders)
+
+
+def rider_scratch(riders):
+    remote = max(sum(rider.pieces for rider in riders), 1)
+    local = max(sum(len(rider.arrays) for rider in riders), 1)
+    buffers = [buffer for rider in riders for buffer in rider.scratch()]
+    return buffers + [pltpu.SemaphoreType.DMA((n,)) for n in (remote, remote, local)]
+
+
+def add_rows(result, buffers):
+    step = 16
+
+    @pl.loop(0, result.shape[1] // step)
+    def _(r):
+        rows = pl.ds(pl.multiple_of(r * step, step), step)
+        for i in range(result.shape[0]):
+            total = buffers[0][i, rows, :].astype(F32)
+            for buffer in buffers[1:]:
+                total += buffer[i, rows, :].astype(F32)
+            result[i, rows, :] = total.astype(result.dtype)
+
+
+def ride_pieces(sources, targets, plans, scratch):
+    send_sem, recv_sem, local_sem = scratch[-3:]
+    starts, finishes, loads, used, source, local = [], [], [], 0, 0, 0
+    for n, (bit, pieces, turns, parts, direct) in enumerate(plans):
+        arrays = sources[source : source + len(parts)]
+        source += len(parts)
+        if direct:
+            held = arrays[0]
+            prepare = None
+        else:
+            buffers = scratch[used : used + len(parts)]
+            held = scratch[used + len(parts)]
+            used += len(parts) + 1
+            copies = []
+            for array, part, buffer in zip(arrays, parts, buffers):
+                view = array if part is None else array.at[part]
+                copy = pltpu.make_async_copy(view, buffer, local_sem.at[local])
+                local += 1
+                loads.append(copy)
+                copies.append(copy)
+
+            def prepare(copies=copies, held=held, buffers=buffers):
+                for copy in copies:
+                    copy.wait()
+                add_rows(held, buffers)
+
+        size = targets[n].shape[0] // pieces
         for m in range(pieces):
             at = pl.ds(m * size, size)
-            slot = len(starts)
-
-            def start(n=n, at=at, slot=slot, bit=bit):
-                copy = pltpu.make_async_remote_copy(
-                    src_ref=sources[n].at[at],
+
+            def remote(n=n, at=at, slot=len(starts), bit=bit, held=held):
+                return pltpu.make_async_remote_copy(
+                    src_ref=held.at[at],
                     dst_ref=targets[n].at[at],
                     send_sem=send_sem.at[slot],
                     recv_sem=recv_sem.at[slot],
                     device_id=peer_of(bit),
                     device_id_type=MESH,
                 )
-                copy.start()
-                copies.append(copy)
-
-            starts.append(start)
-    return starts, copies
-
-
-def rider_shapes(riders):
-    return tuple(jax.ShapeDtypeStruct(array.shape, array.dtype) for array, _, _ in riders)
+
+            def start(remote=remote):
+                remote().start()
+
+            def finish(remote=remote):
+                remote().wait()
+
+            starts.append((prepare if m == 0 else None, start, turns))
+            finishes.append(finish)
+    return starts, finishes, loads
 
 
 def all_peers(bits):
@@ -1416,40 +1490,41 @@
     return trade_peers(size) + [peer_of(bit) for bit in bits if bit[0] == "expert"]
 
 
-def trade_kernel(*refs, riders):
-    count = len(riders)
-    a_ref, sources = refs[0], refs[1 : 1 + count]
-    out_ref, targets = refs[1 + count], refs[2 + count : 2 + 2 * count]
-    send_sem, recv_sem, local_sem, *more = refs[2 + 2 * count :]
-    greet(all_peers(sorted({bit for bit, _ in riders})))
+def trade_kernel(*refs, plans):
+    inputs = sum(len(plan[3]) for plan in plans)
+    a_ref, sources = refs[0], refs[1 : 1 + inputs]
+    out_ref, targets = refs[1 + inputs], refs[2 + inputs : 2 + inputs + len(plans)]
+    send_sem, recv_sem, local_sem, *scratch = refs[2 + inputs + len(plans) :]
+    greet(all_peers(sorted({plan[0] for plan in plans})))
     trade = trade_start(a_ref, out_ref, send_sem, recv_sem, local_sem.at[0])
-    copies = []
-    if riders:
-        starts, copies = ride_pieces(sources, targets, riders, *more)
-        for start in starts:
-            start()
+    starts, finishes, loads = ride_pieces(sources, targets, plans, scratch)
+    for load in loads:
+        load.start()
+    for prepare, start, _ in starts:
+        if prepare is not None:
+            prepare()
+        start()
     trade_end(*trade)
-    for copy in copies:
-        copy.wait()
+    for finish in finishes:
+        finish()
 
 
 def run_trade(values, number, riders=()):
     size = values.shape[0]
-    count = len(riders)
-    total = sum(rider[2] for rider in riders)
-    sems = [size - 1, size - 1, 1] + [total] * (2 if count else 0)
+    inputs = rider_inputs(riders)
     out = pl.pallas_call(
-        functools.partial(trade_kernel, riders=tuple(rider[1:] for rider in riders)),
-        in_specs=[hbm] * (1 + count),
-        out_specs=(hbm,) * (1 + count),
+        functools.partial(trade_kernel, plans=tuple(rider.plan() for rider in riders)),
+        in_specs=[hbm] * (1 + len(inputs)),
+        out_specs=(hbm,) * (1 + len(riders)),
         out_shape=(jax.ShapeDtypeStruct(values.shape, values.dtype),) + rider_shapes(riders),
-        scratch_shapes=[pltpu.SemaphoreType.DMA((n,)) for n in sems],
+        scratch_shapes=[pltpu.SemaphoreType.DMA((n,)) for n in (size - 1, size - 1, 1)]
+        + rider_scratch(riders),
         compiler_params=pltpu.CompilerParams(
             collective_id=number, has_side_effects=True, vmem_limit_bytes=60 * MIB
         ),
         cost_estimate=cost(0, 170e6),
-    )(values, *(rider[0] for rider in riders))
-    return out if count else out[0]
+    )(values, *inputs)
+    return out if riders else out[0]
 
 
 def first_kernel(a_ref, rank_ref, turned_ref, out_ref, slot_ref, send_sem, recv_sem, local_sem, *, far):
@@ -1541,18 +1616,22 @@
         copy.wait_send()
 
 
-def reduce_kernel(*refs, jobs, riders):
-    size, count = len(jobs), len(riders)
-    keeps, sends, sources = refs[:size], refs[size : 2 * size], refs[2 * size : 2 * size + count]
-    refs = refs[2 * size + count :]
+def reduce_kernel(*refs, jobs, plans):
+    size = len(jobs)
+    inputs = sum(len(plan[3]) for plan in plans)
+    keeps, sends, sources = refs[:size], refs[size : 2 * size], refs[2 * size : 2 * size + inputs]
+    refs = refs[2 * size + inputs :]
     outs = []
     for _, _, _, widths in jobs:
         outs.append(refs[: len(widths)])
         refs = refs[len(widths) :]
-    targets, scratch = refs[:count], refs[count:]
-    send_sem, recv_sem, ride_send, ride_recv = scratch[3 * size :]
+    targets, scratch = refs[: len(plans)], refs[len(plans) :]
+    send_sem, recv_sem = scratch[3 * size : 3 * size + 2]
     used = {bit for first, bits, *_ in jobs for bit in (first,) + bits}
-    used |= {bit for bit, _ in riders}
+    used |= {plan[0] for plan in plans}
+    starts, finishes, loads = ride_pieces(sources, targets, plans, scratch[3 * size + 2 :])
+    for load in loads:
+        load.start()
     greet([peer_of(bit) for bit in sorted(used)])
     chains, slot = [], 0
     for n, (first, bits, parts, _) in enumerate(jobs):
@@ -1570,9 +1649,10 @@
                 )
             )
             slot += len(bits) + 1
-    starts, copies = ride_pieces(sources, targets, riders, ride_send, ride_recv)
-    turn, plain = 0, sum(pieces == 1 for _, pieces in riders)
-    while chains:
+    index = lax.axis_index("dp")
+    outer = (index // BIT_ZH) % 2 == (index // BIT_ZL) % 2
+    turn, last = 0, max([0] + [n for _, _, turns in starts for n in turns])
+    while chains or turn <= last:
         rest = []
         for chain in chains:
             try:
@@ -1580,18 +1660,20 @@
                 rest.append(chain)
             except StopIteration:
                 pass
-            if turn >= 2 and starts:
-                starts.pop(0)()
         chains = rest
-        for _ in range(plain if turn == 0 else 0):
-            starts.pop(0)()
-        if turn <= 1 and starts:
-            starts.pop(0)()
+        for prepare, start, turns in starts:
+            if prepare is not None and min(turns) == turn:
+                prepare()
+            if len(set(turns)) == 1:
+                if turns[0] == turn:
+                    start()
+            else:
+                for n, side in enumerate((outer, jnp.logical_not(outer))):
+                    if turns[n] == turn:
+                        pl.when(side)(start)
         turn += 1
-    for start in starts:
-        start()
-    for copy in copies:
-        copy.wait()
+    for finish in finishes:
+        finish()
 
 
 def run_reduce(pairs, jobs, number, riders=()):
@@ -1606,21 +1688,20 @@
             pltpu.VMEM((max(blocks - 1, 1), rows, cols), send.dtype),
         ]
         shapes += [jax.ShapeDtypeStruct((rows, width), F32) for width in widths]
-    pieces = max(sum(rider[2] for rider in riders), 1)
-    sems = (slots, slots, pieces, pieces)
+    inputs = rider_inputs(riders)
     return pl.pallas_call(
-        functools.partial(
-            reduce_kernel, jobs=jobs, riders=tuple(rider[1:] for rider in riders)
-        ),
-        in_specs=[vmem] * len(pairs) + [hbm] * (len(pairs) + len(riders)),
+        functools.partial(reduce_kernel, jobs=jobs, plans=tuple(rider.plan() for rider in riders)),
+        in_specs=[vmem] * len(pairs) + [hbm] * (len(pairs) + len(inputs)),
         out_specs=(vmem,) * len(shapes) + (hbm,) * len(riders),
         out_shape=tuple(shapes) + rider_shapes(riders),
-        scratch_shapes=scratch + [pltpu.SemaphoreType.DMA((n,)) for n in sems],
+        scratch_shapes=scratch
+        + [pltpu.SemaphoreType.DMA((n,)) for n in (slots, slots)]
+        + rider_scratch(riders),
         compiler_params=pltpu.CompilerParams(
             collective_id=number, has_side_effects=True, vmem_limit_bytes=60 * MIB
         ),
         cost_estimate=cost(0, 170e6),
-    )(*(keep for keep, _ in pairs), *(send for _, send in pairs), *(rider[0] for rider in riders))
+    )(*(keep for keep, _ in pairs), *(send for _, send in pairs), *inputs)
 
 
 def sum_pair(kept, received):
@@ -1638,11 +1719,14 @@
     def total(*terms):
         return sum(term.astype(F32) for term in terms)
 
+    def flat(ref):
+        return ref[(0,) * (ref.ndim - 2)]
+
     def work(parts, part):
         for n in range(2):
             keep, got, more, other = parts[4 * n : 4 * n + 4]
-            mine = total(keep[0, 0, 0], got[0, 0], more[0])
-            across = other[0].astype(F32)
+            mine = total(*(flat(term) for term in (keep, got, more)))
+            across = flat(other).astype(F32)
             for m in range(2):
                 cols = slice(m * LANES, (m + 1) * LANES)
                 at = pl.multiple_of((2 * m + zl_at) * LANES, LANES)
@@ -1650,29 +1734,28 @@
                 at = pl.multiple_of((2 * m + 1 - zl_at) * LANES, LANES)
                 outs[n][part, 0, :, pl.ds(at, LANES)] = across[:, cols]
         keep, got, more = parts[8:]
-        outs[2][part, 0] = total(keep[0, 0], got[0], more[0])
+        outs[2][part, 0] = total(*(flat(term) for term in (keep, got, more)))
 
     work(refs[0:11], 0)
     work(refs[11:22], 1)
 
 
 def run_join(place, halves):
-    experts, rows, cols = halves[0][2].shape
+    _, _, experts, rows, cols = halves[0][0].shape
     wide_rows, width = halves[0][8].shape[2:]
-    specs = []
-    for part in range(2):
-        tall = [
-            pl.BlockSpec((1, 1, 1, rows, cols), lambda i, p: (0, 0, i, 0, 0)),
-            pl.BlockSpec((1, 1, rows, cols), lambda i, p: (0, i, 0, 0)),
-            pl.BlockSpec((1, rows, cols), lambda i, p: (i, 0, 0)),
-            pl.BlockSpec((1, rows, cols), lambda i, p: (i, 0, 0)),
-        ]
-        specs += tall + tall
-        specs += [
-            pl.BlockSpec((1, 1, wide_rows, width), lambda i, p: (0, i, 0, 0)),
-            pl.BlockSpec((1, wide_rows, width), lambda i, p: (i, 0, 0)),
-            pl.BlockSpec((1, wide_rows, width), lambda i, p: (i, 0, 0)),
-        ]
+    arrays, specs = [], []
+    for half in halves:
+        for operand in half:
+            array, lead = operand if isinstance(operand, tuple) else (operand, 0)
+            extra = array.ndim - 3
+            at = (lead,) + (0,) * (extra - 1) if extra else ()
+            arrays.append(array)
+            specs.append(
+                pl.BlockSpec(
+                    (1,) * (extra + 1) + array.shape[-2:],
+                    lambda i, p, at=at: at + (i, 0, 0),
+                )
+            )
     shapes = [(rows, 2 * cols), (rows, 2 * cols), (wide_rows, width)]
     return pl.pallas_call(
         join_kernel,
@@ -1684,12 +1767,10 @@
                 pl.BlockSpec((2, 1) + shape, lambda i, p: (0, i, 0, 0)) for shape in shapes
             ),
         ),
-        out_shape=tuple(
-            jax.ShapeDtypeStruct((2, experts) + shape, F32) for shape in shapes
-        ),
+        out_shape=tuple(jax.ShapeDtypeStruct((2, experts) + shape, F32) for shape in shapes),
         compiler_params=params(60, ("arbitrary",)),
         cost_estimate=cost(1e6, 26e6),
-    )(place, *halves[0], *halves[1])
+    )(place, *arrays)
 
 
 def fast_body(
@@ -1774,9 +1855,11 @@
     gate_ka, gate_s0, gate_s1, up_ka, up_s0, up_s1, down_ka, down_s0, down_s1 = first[4:]
     down_ya = swap_bit(down_s1, Y_BIT)
     gate_ya = swap_bit(gate_s1, Y_BIT)
+    early = swap_bit(jnp.stack([gate_ka[1, 1], gate_s1[1]]), ZH_BIT)
     mix_keep, mix_send, dx_keep, dx_send, *second = run_experts(*expert_args, prior=first[:4])
     gate_kb, gate_t0, gate_t1, up_kb, up_t0, up_t1, down_kb, down_t0, down_t1 = second
-    dx_send, down_ya, gate_ya = fence(dx_send, down_ya, gate_ya)
+    dx_send, down_ya, gate_ya, early = fence(dx_send, down_ya, gate_ya, early)
+    gate_s0 = jnp.stack([gate_s0[0], add_low(gate_s0[1], early[1])])
     quarter = tokens // 4
     extra = dx_keep.shape[2]
     token_parts = tuple(
@@ -1787,62 +1870,69 @@
         ((C_BIT, (X_BIT, ZL_BIT), token_parts, (extra,)),),
         6,
         riders=(
-            (up_s1, Y_BIT, 1),
-            (gate_s0, Y_BIT, 1),
-            (mix_send, C_BIT, 1),
-            (add_low(down_ka[1], down_ya), ZH_BIT, 5),
+            Rider(Y_BIT, up_s1),
+            Rider(Y_BIT, gate_s0),
+            Rider(C_BIT, mix_send, turns=(1,)),
+            Rider(ZH_BIT, (down_ka, (1,)), down_ya, turns=(1, 0)),
         ),
     )
-    dx_sum, gate_ya, down_s0 = fence(dx_sum, gate_ya, down_s0)
-    down_ga = swap_bit(down_s0, Y_BIT)
-    gate_za = swap_bit(add_low(gate_ka[1, 1], gate_ya[1]), ZH_BIT)
+    dx_sum, gate_ya, down_s0, gate_t1 = fence(dx_sum, gate_ya, down_s0, gate_t1)
+    gate_ma = swap_bit(add_low(gate_ka[1, 0], gate_ya[0]), ZH_BIT)
+    gate_yb = swap_bit(gate_t1, Y_BIT)
     d_att, d_middle, d_low, d_log, ggain_mlp = run_post(
         dx_sum, middle, cotangent, normed_two, wr_pad, map_rows, gain_mlp, w_output
     )
     out_keep, out_send = run_outgrad(place, att_full, d_low, devices)
-    d_att, out_send, gate_za, down_ga = fence(d_att, out_send, gate_za, down_ga)
+    d_att, out_send, gate_ma, gate_yb = fence(d_att, out_send, gate_ma, gate_yb)
     mix_keep = mix_keep.reshape(2, 2, tokens, WIDTH)
     mix_got = mix_got.reshape(2, 2, tokens, WIDTH)
-    d_out, gate_ma, up_za, gate_yb, up_yb, gate_oa, mix_x, out_got = run_trade(
+    every = slice(None)
+    d_out, up_yb, down_ga, out_got, up_za, gate_oa, mix_x = run_trade(
         d_att,
         4,
         riders=(
-            (add_low(gate_ka[1, 0], gate_ya[0]), ZH_BIT, 1),
-            (add_low(up_ka[1, 1], up_ya[1]), ZH_BIT, 1),
-            (gate_t1, Y_BIT, 1),
-            (up_t1, Y_BIT, 1),
-            (add_low(gate_ka[0, 1], gate_ga[1], gate_za), ZL_BIT, 1),
-            (add_low(mix_keep[:, 1], mix_got[:, 1]), X_BIT, 1),
-            (out_send, C_BIT, 1),
+            Rider(Y_BIT, up_t1),
+            Rider(Y_BIT, down_s0),
+            Rider(C_BIT, out_send),
+            Rider(ZH_BIT, (up_ka, (1, 1)), (up_ya, (1,))),
+            Rider(ZL_BIT, (gate_ka, (0, 1)), (early, (0,)), (gate_ga, (1,))),
+            Rider(X_BIT, (mix_keep, (every, 1)), (mix_got, (every, 1))),
         ),
     )
-    split = (2, 2, 2, 2, WIDTH // devices, WIDTH)
+    split = (8, 2, WIDTH // devices, WIDTH)
     out_keep, out_got = out_keep.reshape(split), out_got.reshape(split)
-    both = jnp.stack([add_low(up_ka[1, 0], up_ya[0]), add_low(gate_kb[1, 1], gate_yb[1])])
+    up_ga, down_yb, up_late, gate_late, _ = fence(up_s0, down_t1, up_ya, gate_yb, d_out)
+    both = jnp.stack([add_low(up_ka[1, 0], up_late[0]), add_low(gate_kb[1, 1], gate_late[1])])
     both = swap_bit(both, ZH_BIT)
-    up_ga, down_yb = fence(up_s0, down_t1, d_out)[:2]
     up_ga = swap_bit(up_ga, Y_BIT)
     down_yb = swap_bit(down_yb, Y_BIT)
     d_pack = run_backward(pack, d_out, out_t, lse, cos_t, sin_t)
     d_pack, both, up_ga, down_yb = fence(d_pack, both, up_ga, down_yb)
-    up_ma, gate_zb = both[0], both[1]
-    d_pack, gate_mb, up_zb, mix_z, out_x, gate_gb, up_gb, up_oa = run_trade(
+    d_pack, gate_gb, up_gb, gate_mb, up_zb, mix_z, out_x, up_oa = run_trade(
         d_pack,
         5,
         riders=(
-            (add_low(gate_kb[1, 0], gate_yb[0]), ZH_BIT, 1),
-            (add_low(up_kb[1, 1], up_yb[1]), ZH_BIT, 1),
-            (add_low(mix_keep[1, 0], mix_got[1, 0], mix_x[1]), ZL_BIT, 1),
-            (add_low(out_keep[:, :, :, 1], out_got[:, :, :, 1]), X_BIT, 1),
-            (gate_t0, Y_BIT, 1),
-            (up_t0, Y_BIT, 1),
-            (add_low(up_ka[0, 1], up_ga[1], up_za), ZL_BIT, 1),
+            Rider(Y_BIT, gate_t0),
+            Rider(Y_BIT, up_t0),
+            Rider(ZH_BIT, (gate_kb, (1, 0)), (gate_yb, (0,))),
+            Rider(ZH_BIT, (up_kb, (1, 1)), (up_yb, (1,))),
+            Rider(
+                ZL_BIT,
+                (mix_keep, (slice(1, 2), 0)),
+                (mix_got, (slice(1, 2), 0)),
+                (mix_x, (slice(1, 2),)),
+            ),
+            Rider(X_BIT, (out_keep, (every, 1)), (out_got, (every, 1))),
+            Rider(ZL_BIT, (up_ka, (0, 1)), (up_ga, (1,)), (up_za, (every,))),
         ),
     )
     d_pack, up_yb, down_yb, gate_gb, down_t0, mix_z, out_x = fence(
         d_pack, up_yb, down_yb, gate_gb, down_t0, mix_z, out_x
     )
-    up_mb = swap_bit(add_low(up_kb[1, 0], up_yb[0]), ZH_BIT)
+    other = jnp.stack(
+        [add_low(gate_kb[0, 1], gate_gb[1], both[1]), add_low(up_kb[0, 1], up_gb[1], up_zb)]
+    )
+    other = swap_bit(other, ZL_BIT)
     down_mb = swap_bit(add_low(down_kb[1], down_yb), ZH_BIT)
     down_gb = swap_bit(down_t0, Y_BIT)
     d_full, qkv_keep, qkv_send = run_qkvgrad(place, normed, d_pack, devices)
@@ -1850,12 +1940,11 @@
         d_full, w_query, w_key, w_value, d_middle, inputs, gain_attn
     )
     small_keep, small_send = run_small(place, normed_two, d_log, ggain_mlp, ggain_attn, devices)
-    mixed = sum_pair(mix_keep[0, 0], mix_got[0, 0]) + sum_pair(mix_x[0], mix_z)
+    mixed = sum_pair(mix_keep[0, 0], mix_got[0, 0]) + sum_pair(mix_x[0], mix_z[0])
     hidden_out = middle + mixed
-    out_held = add_low(out_keep[:, :, :, 0], out_got[:, :, :, 0], out_x)
     rows = WIDTH // devices
-    out_first = out_held[:, :, 0].reshape(4, rows, WIDTH)
-    out_second = out_held[:, :, 1].reshape(4, rows, WIDTH)
+    out_held = add_low(out_keep[:, 0], out_got[:, 0], out_x).reshape(4, 2, rows, WIDTH)
+    out_first, out_second = out_held[:, 0], out_held[:, 1]
     qkv_send, small_send, out_second, hidden_out = fence(
         qkv_send, small_send, out_second, hidden_out
     )
@@ -1866,7 +1955,7 @@
         (0, rows, 2048, 512, (1, 0, 2, 3)),
     )
     dense_bits = (X_BIT, Y_BIT, ZL_BIT, ZH_BIT)
-    query_total, key_total, value_total, small, output_total, gate_ob, up_ob = run_reduce(
+    query_total, key_total, value_total, small, output_total, up_mb = run_reduce(
         ((qkv_keep, qkv_send), (small_keep, small_send), (out_first, out_second)),
         (
             (C_BIT, dense_bits, qkv_parts, (WIDTH, KV_HEADS * HEAD_DIM, KV_HEADS * HEAD_DIM)),
@@ -1874,20 +1963,17 @@
             (Y_BIT, (ZL_BIT, ZH_BIT), ((0, rows, 0, WIDTH, (0, 1)),), (WIDTH,)),
         ),
         7,
-        riders=(
-            (add_low(gate_kb[0, 1], gate_gb[1], gate_zb), ZL_BIT, 1),
-            (add_low(up_kb[0, 1], up_gb[1], up_zb), ZL_BIT, 1),
-        ),
-    )
-    query_total, small, up_mb, down_mb, down_gb, up_ob = fence(
-        query_total, small, up_mb, down_mb, down_gb, up_ob
+        riders=(Rider(ZH_BIT, (up_kb, (1, 0)), (up_yb, (0,))),),
+    )
+    query_total, small, down_mb, down_gb, other = fence(
+        query_total, small, down_mb, down_gb, other
     )
     joined = run_join(
         place,
         (
-            (gate_ka, gate_ga, gate_ma, gate_oa, up_ka, up_ga, up_ma, up_oa)
+            (gate_ka, gate_ga, gate_ma, gate_oa, up_ka, up_ga, (both, 0), up_oa)
             + (down_ka, down_ga, down_ma),
-            (gate_kb, gate_gb, gate_mb, gate_ob, up_kb, up_gb, up_mb, up_ob)
+            (gate_kb, gate_gb, gate_mb, (other, 0), up_kb, up_gb, up_mb, (other, 1))
             + (down_kb, down_gb, down_mb),
         ),
     )

time: 761 us -> 710 us (0.933)
  Pallas kernels: 668 us -> 635 us
  other arithmetic: 50.2 us -> 22.8 us
    pallas_call x5, Pallas kernels: 327 us -> 294 us  [the longest x3 162 us: run_trade(): pl.pallas_call(functools.partial(trade_kernel, plans=tuple((rider.plan()...]
    convert_element_type x16 -> x7, other arithmetic: 35.5 us -> 8.39 us  [add_low(): return sum((term.astype(F32) for term in terms)).astype(BF)]
    ppermute x15 -> x16, starting transfers between devices: 16.5 us -> 22.7 us  [swap(): return lax.ppermute(values, axis, [(i, i ^ mask) for i in range(size)])]
  transfers between devices with their start and end apart: 15 -> 16, of which waited for: 0 -> 1; matrix products, arithmetic and copies ran while one was open for 5% -> 3% of each run, Pallas kernels for 43% -> 44%
where the time goes in v4:
time: 710 us; the launch traced here: 703 us
  Pallas kernels  635 us (89%)
  other arithmetic  22.8 us (3%)
  starting transfers between devices  22.7 us (3%)
  local copies, waits for them, and re-layouts  17.4 us (2%)
    pallas_call x3, Pallas kernels, run_trade(): pl.pallas_call(functools.partial(trade_kernel, plans=tuple((rider.plan()...  162 us
    pallas_call x2, Pallas kernels, run_reduce(): pl.pallas_call(functools.partial(reduce_kernel, jobs=jobs, plans=tuple((r...  132 us
    pallas_call x2, Pallas kernels, run_experts(): pl.pallas_call(functools.partial(expert_kernel, first=not prior), grid_sp...  114 us
    pallas_call x1, Pallas kernels, run_first(): pl.pallas_call(functools.partial(first_kernel, far=far), in_specs=[hbm, v...  43.8 us
    pallas_call x1, Pallas kernels, run_backward(): pl.pallas_call(backward_kernel, grid=(blocks,), in_specs=[pl.BlockSpec(pa...  43.1 us
    pallas_call x1, Pallas kernels, run_gather(): pl.pallas_call(gather_kernel, in_specs=[pl.BlockSpec(memory_space=pltpu.V...  39.2 us
    pallas_call x1, Pallas kernels, run_forward(): pl.pallas_call(forward_kernel, grid=(blocks,), in_specs=[pl.BlockSpec(pac...  30.3 us
    ppermute x16, starting transfers between devices, swap(): return lax.ppermute(values, axis, [(i, i ^ mask) for i in range(size)])  22.7 us
  transfers between devices with their start and end apart: 16, of which 1 were waited for; matrix products, arithmetic and copies ran while one was open for 3% of the time, Pallas kernels for 44%

profile of v4, /device:TPU:0, one launch (start us, length us, event | category | flops | bytes accessed | tf_op | source)
XLA Modules:
  0.0 703.2 jit_solution(8288655600310789410)
XLA Ops:
  3.7 9.0 %shard_map.229 = (bf16[320,1536]{1,0:T(8,128)(2,1)}, bf16[8,800,128]{2,1,0:T(8,128)(2,1)}, bf16[320,1536]{1,0:T(8,128)(2,1)}) custom-call(f32[320,1536]{1,0:T(8,128)} %bitcast.78, f32[1,1536]{1,0:T(1,128)} %broadcast_in_dim.44.gain_ref, bf16[1536,1536]{1,0:T(8,128)(2,1)} %wq_ref.3, bf16[1536,512]{1,0:T(8,128)(2,1)} %wk_ref.3, bf16[1536,512]{1,0:T(8,128)(2,1)} %wv_ref.3, ...), custom_call_target="tpu_custom_call" | custom-call | flops 2516582400 | bytes 14000000 | tf_op jit(solution)/shard_map/pallas_call | solution.py:486
  12.7 2.9 collective-permute-start
  16.9 43.8 %shard_map.230 = (bf16[8,800,128]{2,1,0:T(8,128)(2,1)}, f32[40,320]{1,0:T(8,128)}) custom-call(bf16[8,800,128]{2,1,0:T(8,128)(2,1)} %get-tuple-element.142.a_ref, f32[40,320]{1,0:T(8,128)} %copy-done.22, f32[320,40]{1,0:T(8,128)} %bitcast.89), custom_call_target="tpu_custom_call" | custom-call | bytes 170000000 | tf_op jit(solution)/shard_map/pallas_call | solution.py:1544
  61.4 30.3 %shard_map.231 = (bf16[8,480,128]{2,1,0:T(8,128)(2,1)}, f32[10,64,768]{2,1,0:T(8,128)}, f32[10,1,768]{2,1,0:T(1,128)}) custom-call(bf16[8,800,128]{2,1,0:T(8,128)(2,1)} %get-tuple-element.146.pack_ref), custom_call_target="tpu_custom_call" | custom-call | flops 10066329600 | bytes 6000000 | tf_op jit(solution)/shard_map/pallas_call | solution.py:601
  97.3 23.9 %shard_map.232.att_ref = bf16[8,480,128]{2,1,0:T(8,128)(2,1)} custom-call(bf16[8,480,128]{2,1,0:T(8,128)(2,1)} %get-tuple-element.150.refs_0_), custom_call_target="tpu_custom_call" | custom-call | bytes 170000000 | tf_op jit(solution)/shard_map/pallas_call | solution.py:1515
  122.0 7.3 %shard_map.233 = (f32[320,1536]{1,0:T(8,128)}, bf16[320,1536]{1,0:T(8,128)(2,1)}, bf16[320,1536]{1,0:T(8,128)(2,1)}) custom-call(bf16[8,480,128]{2,1,0:T(8,128)(2,1)} %shard_map.232.att_ref, bf16[1536,1536]{1,0:T(8,128)(2,1)} %wo_ref.3, f32[320,1536]{1,0:T(8,128)} %bitcast.79, f32[1,1536]{1,0:T(1,128)} %broadcast_in_dim.48.gain_ref), custom_call_target="tpu_custom_call" | custom-call | flops 1509949440 | bytes 12000000 | tf_op jit(solution)/shard_map/pallas_call | solution.py:760
  129.3 39.2 %shard_map.234 = (bf16[8,320,1536]{2,1,0:T(8,128)(2,1)}, bf16[8,320,1536]{2,1,0:T(8,128)(2,1)}, f32[8,40,320]{2,1,0:T(8,128)}) custom-call(bf16[320,1536]{1,0:T(8,128)(2,1)} %get-tuple-element.154.x_ref.norm_ref, bf16[320,1536]{1,0:T(8,128)(2,1)} %get-tuple-element.148.refs_0_, bf16[320,1536]{1,0:T(8,128)(2,1)} %copy-done.13, bf16[320,1536]{1,0:T(8,128)(2,1)} %copy-done.14, ...), custom_call_target="tpu_custom_call" | custom-call | bytes 150000000 | tf_op jit(solution)/shard_map/pallas_call | solution.py:1341
  170.5 55.8 %shard_map.235 = (bf16[4,320,1536]{2,1,0:T(8,128)(2,1)}, bf16[4,320,1536]{2,1,0:T(8,128)(2,1)}, bf16[4,320,1664]{2,1,0:T(8,128)(2,1)}, bf16[4,320,1664]{2,1,0:T(...) custom-call(s32[6]{0:T(128)} %stack.43.place_ref, ...), custom_call_target="tpu_custom_call" | custom-call | flops 30000001024 | bytes 60000000 | tf_op jit(solution)/shard_map/pallas_call | solution.py:999
  232.1 58.6 %shard_map.236 = (bf16[4,320,1536]{2,1,0:T(8,128)(2,1)}, bf16[4,320,1536]{2,1,0:T(8,128)(2,1)}, bf16[4,320,1664]{2,1,0:T(8,128)(2,1)}, bf16[4,320,1664]{2,1,0:T(...) custom-call(s32[6]{0:T(128)} %stack.43.place_ref, ...), custom_call_target="tpu_custom_call" | custom-call | flops 30000001024 | bytes 60000000 | tf_op jit(solution)/shard_map/pallas_call | solution.py:999
  292.1 65.1 %shard_map.237 = (f32[320,1664]{1,0:T(8,128)}, bf16[2,5,192,256]{3,2,1,0:T(8,128)(2,1)}, bf16[2,5,192,256]{3,2,1,0:T(8,128)(2,1)}, bf16[4,320,1536]{2,1,0:T(8,128)(2,1)}, bf16[5,64,1536]{2,1,0:T(8,128)(2,1)}) custom-call(bf16[4,320,1664]{2,1,0:T(8,128)(2,1)} %get-tuple-element.165.refs_0_, bf16[4,320,1664]{2,1,0:T(8,128)(2,1)} %get-tuple-element.170.refs_1_, ...), custom_call_target="tpu_custom_call" | custom-call | bytes 170000000 | tf_op jit(solution)/shard_map/pallas_call | solution.py:1692
  358.6 2.2 multiply_sine_fusion
  363.2 3.5 collective-permute-start.8
  367.4 9.3 %shard_map.238 = (bf16[8,480,128]{2,1,0:T(8,128)(2,1)}, f32[320,1536]{1,0:T(8,128)}, bf16[320,1536]{1,0:T(8,128)(2,1)}, bf16[320,128]{1,0:T(8,128)(2,1)}, f32[1,1536]{1,0:T(1,128)}) custom-call(f32[320,1664]{1,0:T(8,128)} %get-tuple-element.181.dx_ref, f32[320,1536]{1,0:T(8,128)} %get-tuple-element.182.mid_ref, f32[320,1536]{1,0:T(8,128)} %bitcast.82, ...), custom_call_target="tpu_custom_call" | custom-call | flops 1509949440 | bytes 14000000 | tf_op jit(solution)/shard_map/pallas_call | solution.py:1089
  376.7 7.9 %shard_map.239 = (bf16[16,48,1536]{2,1,0:T(8,128)(2,1)}, bf16[16,48,1536]{2,1,0:T(8,128)(2,1)}) custom-call(s32[6]{0:T(128)} %stack.43.place_ref, bf16[320,1536]{1,0:T(8,128)(2,1)} %get-tuple-element.184.a_ref, bf16[320,1536]{1,0:T(8,128)(2,1)} %get-tuple-element.185.b_ref), custom_call_target="tpu_custom_call" | custom-call | flops 1509949440 | bytes 8000000 | tf_op jit(solution)/shard_map/pallas_call | solution.py:1123
  384.6 3.8 collective-permute-done.8.refs_2_
  388.5 56.3 %shard_map.240 = (bf16[8,480,128]{2,1,0:T(8,128)(2,1)}, bf16[2,5,192,256]{3,2,1,0:T(8,128)(2,1)}, bf16[5,64,1536]{2,1,0:T(8,128)(2,1)}, bf16[16,48,1536]{2,1,0:T...) custom-call(bf16[8,480,128]{2,1,0:T(8,128)(2,1)} %get-tuple-element.189.refs, ...), custom_call_target="tpu_custom_call" | custom-call | bytes 170000000 | tf_op jit(solution)/shard_map/pallas_call | solution.py:1515
  450.6 43.1 %shard_map.241.refs_0_ = bf16[8,800,128]{2,1,0:T(8,128)(2,1)} custom-call(bf16[8,800,128]{2,1,0:T(8,128)(2,1)} %get-tuple-element.146.pack_ref, bf16[8,480,128]{2,1,0:T(8,128)(2,1)} %get-tuple-element.198.grad_ref, f32[10,64,768]{2,1,0:T(8,128)} %get-tuple-element.199.out_t_ref, f32[10,1,768]{2,1,0:T(1,128)} %get-tuple-element.200.lse_ref, ...), custom_call_target="tpu_custom_call" | custom-call | flops 25165824000 | bytes 8000000 | tf_op jit(solution)/shard_map/pallas_call | solution.py:722
  495.2 82.1 %shard_map.242 = (bf16[8,800,128]{2,1,0:T(8,128)(2,1)}, bf16[2,5,192,256]{3,2,1,0:T(8,128)(2,1)}, bf16[2,5,192,256]{3,2,1,0:T(8,128)(2,1)}, bf16[5,192,256]{2,1,...) custom-call(bf16[8,800,128]{2,1,0:T(8,128)(2,1)} %shard_map.241.refs, ...), custom_call_target="tpu_custom_call" | custom-call | bytes 170000000 | tf_op jit(solution)/shard_map/pallas_call | solution.py:1515
  588.4 11.7 %shard_map.243 = (bf16[320,2560]{1,0:T(8,128)(2,1)}, bf16[16,48,2560]{2,1,0:T(8,128)(2,1)}, bf16[16,48,2560]{2,1,0:T(8,128)(2,1)}) custom-call(s32[6]{0:T(128)} %stack.43.place_ref, bf16[320,1536]{1,0:T(8,128)(2,1)} %get-tuple-element.141.a_ref, bf16[8,800,128]{2,1,0:T(8,128)(2,1)} %get-tuple-element.225.d_ref), custom_call_target="tpu_custom_call" | custom-call | flops 2516582400 | bytes 12000000 | tf_op jit(solution)/shard_map/pallas_call | solution.py:1172
  600.1 9.3 %shard_map.244 = (f32[320,1536]{1,0:T(8,128)}, f32[1,1536]{1,0:T(1,128)}) custom-call(bf16[320,2560]{1,0:T(8,128)(2,1)} %get-tuple-element.229.d_ref, bf16[1536,1536]{1,0:T(8,128)(2,1)} %wq_ref.3, bf16[1536,512]{1,0:T(8,128)(2,1)} %wk_ref.3, bf16[1536,512]{1,0:T(8,128)(2,1)} %wv_ref.3, f32[320,1536]{1,0:T(8,128)} %get-tuple-element.230.dmid_ref, ...), custom_call_target="tpu_custom_call" | custom-call | flops 2516582400 | bytes 16000000 | tf_op jit(solution)/shard_map/pallas_call | solution.py:1209
  609.4 3.6 shard_map.245
  614.6 3.7 fusion.2
  618.3 66.5 %shard_map.246 = (f32[48,1536]{1,0:T(8,128)}, f32[48,512]{1,0:T(8,128)}, f32[48,512]{1,0:T(8,128)}, f32[48,128]{1,0:T(8,128)}, f32[48,1536]{1,0:T(8,128)}, /*index=5*/bf16[5,192,256]{2,1,0:T(8,128)(2,1)}) custom-call(bf16[16,48,2560]{2,1,0:T(8,128)(2,1)} %get-tuple-element.237.refs_0_, f32[16,48,128]{2,1,0:T(8,128)} %get-tuple-element.238.refs_1_, ...), custom_call_target="tpu_custom_call" | custom-call | bytes 170000000 | tf_op jit(solution)/shard_map/pallas_call | solution.py:1692
  687.8 12.2 %shard_map.247 = (f32[2,5,192,512]{3,2,1,0:T(8,128)}, f32[2,5,192,512]{3,2,1,0:T(8,128)}, f32[2,5,64,1536]{3,2,1,0:T(8,128)}) custom-call(s32[6]{0:T(128)} %stack.43.place_ref, bf16[2,2,5,192,256]{4,3,2,1,0:T(8,128)(2,1)} %get-tuple-element.169.refs_6_.refs_0_, bf16[2,5,192,256]{3,2,1,0:T(8,128)(2,1)} %get-tuple-element.195.refs_8_.refs_1_, ...), custom_call_target="tpu_custom_call" | custom-call | flops 1000000 | bytes 26000000 | tf_op jit(solution)/shard_map/pallas_call | solution.py:1760
  (144 shorter events, 50.5 us)
Async XLA Ops:
  12.7 48.0 %copy-start.12 = (bf16[320,1536]{1,0:T(8,128)(2,1)S(1)}, bf16[320,1536]{1,0:T(8,128)(2,1)}, u32[]{:S(2)}) copy-start(bf16[320,1536]{1,0:T(8,128)(2,1)} %get-tuple-element.148.refs_0_) | copy-start | bytes 2949124
  12.7 79.0 %collective-permute-start = (bf16[320,1536]{1,0:T(8,128)(2,1)}, bf16[320,1536]{1,0:T(8,128)(2,1)S(1)}, u32[]{:S(2)}, u32[]{:S(2)}) collective-permute-start(bf16[320,1536]{1,0:T(8,128)(2,1)} %get-tuple-element.148.refs_0_), channel_id=1, source_target_pairs={{0,2},{1,3},{2,0},{3,1},{4,6},{5,7},{6,4},{7,5},{8,10},{9,11},{10,... | collective-permute-start | bytes 2949128 | tf_op jit(solution)/shard_map/ppermute | solution.py:412
  60.7 31.0 %collective-permute-start.1 = (bf16[320,1536]{1,0:T(8,128)(2,1)S(1)}, bf16[320,1536]{1,0:T(8,128)(2,1)S(1)}, u32[]{:S(2)}, u32[]{:S(2)}) collective-permute-start(bf16[320,1536]{1,0:T(8,128)(2,1)S(1)} %copy-done.12), channel_id=1, source_target_pairs={{0,8},{4,12},{8,0},{12,4},{16,24},{20,28},{24,16},{28,20},{1,9},{5... | collective-permute-start | bytes 2949128 | tf_op jit(solution)/shard_map/ppermute | solution.py:412
  60.8 30.9 %collective-permute-start.2 = (f32[1,40,320]{2,1,0:T(8,128)}, f32[1,40,320]{2,1,0:T(8,128)S(1)}, u32[]{:S(2)}, u32[]{:S(2)}) collective-permute-start(f32[1,40,320]{2,1,0:T(8,128)} %bitcast.93), channel_id=1, source_target_pairs={{0,2},{1,3},{2,0},{3,1},{4,6},{5,7},{6,4},{7,5},{8,10},{9,11},{10,... | collective-permute-start | bytes 153608 | tf_op jit(solution)/shard_map/ppermute | solution.py:412
  91.7 30.3 %collective-permute-start.3 = (bf16[320,1536]{1,0:T(8,128)(2,1)S(1)}, bf16[320,1536]{1,0:T(8,128)(2,1)S(1)}, u32[]{:S(2)}, u32[]{:S(2)}) collective-permute-start(bf16[320,1536]{1,0:T(8,128)(2,1)S(1)} %collective-permute-done.1.refs_2_), channel_id=1, source_target_pairs={{0,2},{1,3},{2,0},{3,1},{4,6},{5,7},{6,4},{7,5},{8,10},{9,11},{10,... | collective-permute-start | bytes 2949128 | tf_op jit(solution)/shard_map/ppermute | solution.py:412
  95.4 25.9 %collective-permute-start.4 = (f32[2,40,320]{2,1,0:T(8,128)S(1)}, f32[2,40,320]{2,1,0:T(8,128)S(1)}, u32[]{:S(2)}, u32[]{:S(2)}) collective-permute-start(f32[2,40,320]{2,1,0:T(8,128)S(1)} %pad_maximum_fusion.7), channel_id=1, source_target_pairs={{0,8},{4,12},{8,0},{12,4},{16,24},{20,28},{24,16},{28,20},{1,9},{5... | collective-permute-start | bytes 307208 | tf_op jit(solution)/shard_map/ppermute | solution.py:412
  226.3 64.4 %collective-permute-start.6 = (bf16[2,5,192,256]{3,2,1,0:T(8,128)(2,1)}, bf16[2,5,192,256]{3,2,1,0:T(8,128)(2,1)}, u32[]{:S(2)}, u32[]{:S(2)}) collective-permute-start(bf16[2,5,192,256]{3,2,1,0:T(8,128)(2,1)} %get-tuple-element.168), channel_id=1, source_target_pairs={{0,4},{4,0},{8,12},{12,8},{16,20},{20,16},{24,28},{28,24},{1,5},{5... | collective-permute-start | bytes 2949128 | tf_op jit(solution)/shard_map/ppermute | solution.py:412
  229.0 61.7 %collective-permute-start.5 = (bf16[5,64,1536]{2,1,0:T(8,128)(2,1)}, bf16[5,64,1536]{2,1,0:T(8,128)(2,1)S(1)}, u32[]{:S(2)}, u32[]{:S(2)}) collective-permute-start(bf16[5,64,1536]{2,1,0:T(8,128)(2,1)} %get-tuple-element.167), channel_id=1, source_target_pairs={{0,4},{4,0},{8,12},{12,8},{16,20},{20,16},{24,28},{28,24},{1,5},{5... | collective-permute-start | bytes 2949128 | tf_op jit(solution)/shard_map/ppermute | solution.py:412
  230.7 60.0 %collective-permute-start.7 = (bf16[2,5,192,256]{3,2,1,0:T(8,128)(2,1)S(1)}, bf16[2,5,192,256]{3,2,1,0:T(8,128)(2,1)S(1)}, u32[]{:S(2)}, u32[]{:S(2)}) collective-permute-start(bf16[2,5,192,256]{3,2,1,0:T(8,128)(2,1)S(1)} %pad_maximum_fusion), channel_id=1, source_target_pairs={{0,16},{4,20},{8,24},{12,28},{16,0},{20,4},{24,8},{28,12},{1,17},{... | collective-permute-start | bytes 2949128 | tf_op jit(solution)/shard_map/ppermute | solution.py:412
  232.1 58.6 %copy-start.18 = (bf16[2,5,192,256]{3,2,1,0:T(8,128)(2,1)S(1)}, bf16[2,5,192,256]{3,2,1,0:T(8,128)(2,1)}, u32[]{:S(2)}) copy-start(bf16[2,5,192,256]{3,2,1,0:T(8,128)(2,1)} %get-tuple-element.172) | copy-start | bytes 2949124
  290.7 66.5 %copy-start.4 = (bf16[2,5,192,256]{3,2,1,0:T(8,128)(2,1)}, bf16[2,5,192,256]{3,2,1,0:T(8,128)(2,1)S(1)}, u32[]{:S(2)}) copy-start(bf16[2,5,192,256]{3,2,1,0:T(8,128)(2,1)S(1)} %collective-permute-done.7.refs_7_) | copy-start | bytes 2949124
  292.1 65.1 %copy-start.34 = (bf16[2,5,192,256]{3,2,1,0:T(8,128)(2,1)S(1)}, bf16[2,5,192,256]{3,2,1,0:T(8,128)(2,1)}, u32[]{:S(2)}) copy-start(bf16[2,5,192,256]{3,2,1,0:T(8,128)(2,1)} %get-tuple-element.188) | copy-start | bytes 2949124
  357.2 31.3 %collective-permute-start.9 = (bf16[2,5,192,256]{3,2,1,0:T(8,128)(2,1)S(1)}, bf16[2,5,192,256]{3,2,1,0:T(8,128)(2,1)S(1)}, u32[]{:S(2)}, u32[]{:S(2)}) collective-permute-start(bf16[2,5,192,256]{3,2,1,0:T(8,128)(2,1)S(1)} %copy-done.34), channel_id=1, source_target_pairs={{0,4},{4,0},{8,12},{12,8},{16,20},{20,16},{24,28},{28,24},{1,5},{5... | collective-permute-start | bytes 2949128 | tf_op jit(solution)/shard_map/ppermute | solution.py:412
  363.2 25.3 %collective-permute-start.8 = (bf16[5,192,256]{2,1,0:T(8,128)(2,1)S(1)}, bf16[5,192,256]{2,1,0:T(8,128)(2,1)S(1)}, u32[]{:S(2)}, u32[]{:S(2)}) collective-permute-start(bf16[5,192,256]{2,1,0:T(8,128)(2,1)S(1)} %fusion.9), channel_id=1, source_target_pairs={{0,16},{4,20},{8,24},{12,28},{16,0},{20,4},{24,8},{28,12},{1,17},{... | collective-permute-start | bytes 1474568 | tf_op jit(solution)/shard_map/ppermute | solution.py:412
  388.5 56.3 %copy-start.23 = (bf16[5,192,256]{2,1,0:T(8,128)(2,1)}, bf16[5,192,256]{2,1,0:T(8,128)(2,1)S(1)}, u32[]{:S(2)}) copy-start(bf16[5,192,256]{2,1,0:T(8,128)(2,1)S(1)} %collective-permute-done.8.refs_2_) | copy-start | bytes 1474564
  388.5 57.5 %copy-start.10 = (bf16[2,5,192,256]{3,2,1,0:T(8,128)(2,1)}, bf16[2,5,192,256]{3,2,1,0:T(8,128)(2,1)S(1)}, u32[]{:S(2)}) copy-start(bf16[2,5,192,256]{3,2,1,0:T(8,128)(2,1)S(1)} %collective-permute-done.9.refs_4_) | copy-start | bytes 2949124
  388.5 56.3 %copy-start.5 = (bf16[2,5,192,256]{3,2,1,0:T(8,128)(2,1)S(1)}, bf16[2,5,192,256]{3,2,1,0:T(8,128)(2,1)}, u32[]{:S(2)}) copy-start(bf16[2,5,192,256]{3,2,1,0:T(8,128)(2,1)} %get-tuple-element.204.refs_5_) | copy-start | bytes 2949124
  447.2 46.5 %collective-permute-start.10 = (bf16[2,5,192,256]{3,2,1,0:T(8,128)(2,1)S(1)}, bf16[2,5,192,256]{3,2,1,0:T(8,128)(2,1)S(1)}, u32[]{:S(2)}, u32[]{:S(2)}) collective-permute-start(bf16[2,5,192,256]{3,2,1,0:T(8,128)(2,1)S(1)} %pad_maximum_fusion.2), channel_id=1, source_target_pairs={{0,16},{4,20},{8,24},{12,28},{16,0},{20,4},{24,8},{28,12},{1,17},{... | collective-permute-start | bytes 2949128 | tf_op jit(solution)/shard_map/ppermute | solution.py:412
  448.6 45.1 %collective-permute-start.11 = (bf16[2,5,192,256]{3,2,1,0:T(8,128)(2,1)}, bf16[2,5,192,256]{3,2,1,0:T(8,128)(2,1)S(1)}, u32[]{:S(2)}, u32[]{:S(2)}) collective-permute-start(bf16[2,5,192,256]{3,2,1,0:T(8,128)(2,1)} %get-tuple-element.207), channel_id=1, source_target_pairs={{0,4},{4,0},{8,12},{12,8},{16,20},{20,16},{24,28},{28,24},{1,5},{5... | collective-permute-start | bytes 2949128 | tf_op jit(solution)/shard_map/ppermute | solution.py:412
  449.3 44.3 %collective-permute-start.12 = (bf16[5,64,1536]{2,1,0:T(8,128)(2,1)}, bf16[5,64,1536]{2,1,0:T(8,128)(2,1)S(1)}, u32[]{:S(2)}, u32[]{:S(2)}) collective-permute-start(bf16[5,64,1536]{2,1,0:T(8,128)(2,1)} %get-tuple-element.208), channel_id=1, source_target_pairs={{0,4},{4,0},{8,12},{12,8},{16,20},{20,16},{24,28},{28,24},{1,5},{5... | collective-permute-start | bytes 2949128 | tf_op jit(solution)/shard_map/ppermute | solution.py:412
  495.2 82.1 %copy-start.1 = (bf16[16,48,1536]{2,1,0:T(8,128)(2,1)S(1)}, bf16[16,48,1536]{2,1,0:T(8,128)(2,1)}, u32[]{:S(2)}) copy-start(bf16[16,48,1536]{2,1,0:T(8,128)(2,1)} %get-tuple-element.215) | copy-start | bytes 7077892
  581.1 103.7 %collective-permute-start.13 = (bf16[5,64,1536]{2,1,0:T(8,128)(2,1)}, bf16[5,64,1536]{2,1,0:T(8,128)(2,1)S(1)}, u32[]{:S(2)}, u32[]{:S(2)}) collective-permute-start(bf16[5,64,1536]{2,1,0:T(8,128)(2,1)} %fusion.1), channel_id=1, source_target_pairs={{0,16},{4,20},{8,24},{12,28},{16,0},{20,4},{24,8},{28,12},{1,17},{... | collective-permute-start | bytes 2949128 | tf_op jit(solution)/shard_map/ppermute | solution.py:412
  583.1 101.7 %collective-permute-start.14 = (bf16[5,64,1536]{2,1,0:T(8,128)(2,1)}, bf16[5,64,1536]{2,1,0:T(8,128)(2,1)}, u32[]{:S(2)}, u32[]{:S(2)}) collective-permute-start(bf16[5,64,1536]{2,1,0:T(8,128)(2,1)} %get-tuple-element.247), channel_id=1, source_target_pairs={{0,4},{4,0},{8,12},{12,8},{16,20},{20,16},{24,28},{28,24},{1,5},{5... | collective-permute-start | bytes 2949128 | tf_op jit(solution)/shard_map/ppermute | solution.py:412
  587.9 96.9 %collective-permute-start.15 = (bf16[2,5,192,256]{3,2,1,0:T(8,128)(2,1)}, bf16[2,5,192,256]{3,2,1,0:T(8,128)(2,1)}, u32[]{:S(2)}, u32[]{:S(2)}) collective-permute-start(bf16[2,5,192,256]{3,2,1,0:T(8,128)(2,1)} %pad_maximum_fusion.3), channel_id=1, source_target_pairs={{0,8},{4,12},{8,0},{12,4},{16,24},{20,28},{24,16},{28,20},{1,9},{5... | collective-permute-start | bytes 2949128 | tf_op jit(solution)/shard_map/ppermute | solution.py:412
  (27 other events, 306.9 us)

commit v5 on v4

--- a/solution.py
+++ b/solution.py
@@ -1109,35 +1109,6 @@
         send[b] = held[pl.ds(pl.multiple_of(other * part, part), part), :]
 
 
-def outgrad_kernel(place_ref, a_ref, b_ref, keep, send, held):
-    held[...] = dot_tn(a_ref[...], b_ref[...]).astype(BF)
-    put_rows(place_ref, held, keep, send)
-
-
-def run_outgrad(place, left, right, blocks):
-    tokens, rows = left.shape
-    cols = right.shape[1]
-    part = rows // blocks
-    spec = pl.BlockSpec((blocks // 2, part, 256), lambda i, p: (0, 0, i))
-    shape = jax.ShapeDtypeStruct((blocks // 2, part, cols), BF)
-    return pl.pallas_call(
-        outgrad_kernel,
-        grid_spec=pltpu.PrefetchScalarGridSpec(
-            num_scalar_prefetch=1,
-            grid=(cols // 256,),
-            in_specs=[
-                pl.BlockSpec((tokens, rows), lambda i, p: (0, 0)),
-                pl.BlockSpec((tokens, 256), lambda i, p: (0, i)),
-            ],
-            out_specs=(spec, spec),
-            scratch_shapes=[pltpu.VMEM((rows, 256), BF)],
-        ),
-        out_shape=(shape, shape),
-        compiler_params=params(60, ("arbitrary",)),
-        cost_estimate=cost(2 * tokens * rows * cols, 8e6),
-    )(place, left, right)
-
-
 def qkvgrad_kernel(place_ref, a_ref, d_ref, full_ref, keep, send, held):
     step = pl.program_id(0)
 
@@ -1187,59 +1158,72 @@
     )(place, normed, d_pack)
 
 
-def last_kernel(d_ref, wq_ref, wk_ref, wv_ref, dmid_ref, hid_ref, gain_ref, out_ref, ggain_ref):
+def last_work(inputs, outputs, scratch):
+    gain_ref, gmlp_ref, sources = inputs[0], inputs[1], inputs[2:]
+    (out_ref,) = outputs
+    keep, send, held = scratch[:3]
+    buffers, load_sem = scratch[3:-1], scratch[-1]
+    loads = [
+        pltpu.make_async_copy(source, buffer, load_sem.at[n])
+        for n, (source, buffer) in enumerate(zip(sources, buffers))
+    ]
+    for load in loads:
+        load.start()
+    d_ref, wq_ref, wk_ref, wv_ref, dmid_ref, hid_ref, norm_ref, dlog_ref = buffers
     key_at = KV_HEADS * ROWS_Q
     value_at = key_at + KV_HEADS * HEAD_DIM
-    d_norm = dot_nt(d_ref[:, 0:key_at], wq_ref[...])
-    d_norm += dot_nt(d_ref[:, key_at:value_at], wk_ref[...])
-    d_norm += dot_nt(d_ref[:, value_at:], wv_ref[...])
-    inputs = hid_ref[...]
-    inv = lax.rsqrt(jnp.mean(inputs * inputs, axis=-1, keepdims=True) + EPS)
-    scaled = d_norm * gain_ref[...]
-    ggain_ref[...] = jnp.sum(d_norm * inputs * inv, axis=0, keepdims=True)
-    out_ref[...] = (
-        dmid_ref[...]
-        + inv * scaled
-        - inputs * inv**3 * jnp.mean(inputs * scaled, axis=-1, keepdims=True)
-    )
-
-
-def run_last(d_full, w_query, w_key, w_value, d_middle, inputs, gain):
-    tokens = inputs.shape[0]
-    return pl.pallas_call(
-        last_kernel,
-        out_shape=(
-            jax.ShapeDtypeStruct((tokens, WIDTH), F32),
-            jax.ShapeDtypeStruct((1, WIDTH), F32),
-        ),
-        compiler_params=params(60),
-        cost_estimate=cost(2 * tokens * WIDTH * 2560, 16e6),
-    )(d_full, w_query, w_key, w_value, d_middle, inputs, gain[None])
-
-
-def small_kernel(place_ref, norm_ref, dlog_ref, gmlp_ref, gattn_ref, keep, send, held):
-    columns = dot_tn(norm_ref[...], dlog_ref[...])
-    lane = lax.broadcasted_iota(jnp.int32, columns.shape, 1)
-    for n, ref in enumerate((gmlp_ref, gattn_ref)):
-        turned = jnp.broadcast_to(ref[...], (8, ref.shape[1])).T[:, 0:1]
-        columns = jnp.where(lane == LANES - 2 + n, turned, columns)
-    held[...] = columns
-    put_rows(place_ref, held, keep, send)
-
-
-def run_small(place, normed_two, d_log, ggain_mlp, ggain_attn, blocks):
-    part = WIDTH // blocks
-    shape = jax.ShapeDtypeStruct((blocks // 2, part, LANES), F32)
-    smem = pl.BlockSpec(memory_space=pltpu.SMEM)
+    device = lax.axis_index("dp") * lax.axis_size("expert") + lax.axis_index("expert")
+
+    def compute():
+        for load in loads:
+            load.wait()
+        tokens = hid_ref.shape[0]
+        size = tokens // 4
+        ggain = jnp.zeros(gain_ref.shape, F32)
+        for r in range(4):
+            rows = slice(r * size, (r + 1) * size)
+            d_norm = dot_nt(d_ref[rows, 0:key_at], wq_ref[...])
+            d_norm += dot_nt(d_ref[rows, key_at:value_at], wk_ref[...])
+            d_norm += dot_nt(d_ref[rows, value_at:], wv_ref[...])
+            values = hid_ref[rows, :]
+            inv = lax.rsqrt(jnp.mean(values * values, axis=-1, keepdims=True) + EPS)
+            scaled = d_norm * gain_ref[...]
+            ggain += jnp.sum(d_norm * values * inv, axis=0, keepdims=True)
+            out_ref[rows, :] = (
+                dmid_ref[rows, :]
+                + inv * scaled
+                - values * inv**3 * jnp.mean(values * scaled, axis=-1, keepdims=True)
+            )
+        columns = dot_tn(norm_ref[...], dlog_ref[...])
+        lane = lax.broadcasted_iota(jnp.int32, columns.shape, 1)
+        for n, row in enumerate((gmlp_ref[...], ggain)):
+            turned = jnp.broadcast_to(row, (8, row.shape[1])).T[:, 0:1]
+            columns = jnp.where(lane == LANES - 2 + n, turned, columns)
+        held[...] = columns
+        part = keep.shape[1]
+        for b in range(keep.shape[0]):
+            own = (2 * b) ^ device
+            keep[b] = held[pl.ds(pl.multiple_of(own * part, part), part), :]
+            own = own ^ 1
+            send[b] = held[pl.ds(pl.multiple_of(own * part, part), part), :]
+
+    return compute
+
+
+def plan_last(arrays, gain, ggain_mlp, blocks):
     vmem = pl.BlockSpec(memory_space=pltpu.VMEM)
-    return pl.pallas_call(
-        small_kernel,
-        in_specs=[smem] + [vmem] * 4,
-        out_shape=(shape, shape),
-        scratch_shapes=[pltpu.VMEM((WIDTH, LANES), F32)],
-        compiler_params=params(60),
-        cost_estimate=cost(1e8, 3e6),
-    )(place, normed_two, d_log, ggain_mlp, ggain_attn)
+    tokens = arrays[0].shape[0]
+    small = pltpu.VMEM((blocks // 2, WIDTH // blocks, LANES), F32)
+    scratch = [small, small, pltpu.VMEM((WIDTH, LANES), F32)]
+    scratch += [pltpu.VMEM(array.shape, array.dtype) for array in arrays]
+    scratch.append(pltpu.SemaphoreType.DMA((len(arrays),)))
+    return (
+        (gain[None], ggain_mlp) + arrays,
+        [vmem] * 2 + [hbm] * len(arrays),
+        [jax.ShapeDtypeStruct((tokens, WIDTH), F32)],
+        scratch,
+        last_work,
+    )
 
 
 def stack_swap(values, bit):
@@ -1490,41 +1474,112 @@
     return trade_peers(size) + [peer_of(bit) for bit in bits if bit[0] == "expert"]
 
 
-def trade_kernel(*refs, plans):
+def trade_kernel(*refs, plans, work):
     inputs = sum(len(plan[3]) for plan in plans)
+    more = 2 if work else 0
     a_ref, sources = refs[0], refs[1 : 1 + inputs]
-    out_ref, targets = refs[1 + inputs], refs[2 + inputs : 2 + inputs + len(plans)]
-    send_sem, recv_sem, local_sem, *scratch = refs[2 + inputs + len(plans) :]
-    greet(all_peers(sorted({plan[0] for plan in plans})))
+    work_in, refs = refs[1 + inputs : 1 + inputs + more], refs[1 + inputs + more :]
+    out_ref, targets = refs[0], refs[1 : 1 + len(plans)]
+    work_out, refs = refs[1 + len(plans) : 1 + len(plans) + more], refs[1 + len(plans) + more :]
+    send_sem, recv_sem, local_sem, *scratch = refs
+    work_scratch = scratch[-6:] if work else ()
+    scratch = scratch[:-6] if work else scratch
+    bits = {plan[0] for plan in plans} | ({C_BIT} if work else set())
+    greet(all_peers(sorted(bits)))
     trade = trade_start(a_ref, out_ref, send_sem, recv_sem, local_sem.at[0])
     starts, finishes, loads = ride_pieces(sources, targets, plans, scratch)
     for load in loads:
         load.start()
+    if work:
+        finishes.append(weight_grad(work_in, work_out, work_scratch))
     for prepare, start, _ in starts:
         if prepare is not None:
             prepare()
         start()
+    if work:
+        finishes[-1] = finishes[-1]()
     trade_end(*trade)
     for finish in finishes:
         finish()
 
 
-def run_trade(values, number, riders=()):
+def weight_grad(inputs, outputs, scratch):
+    keep, got = outputs
+    left, right, sent, held, load_sem, cross_sem = scratch
+    loads = [
+        pltpu.make_async_copy(source, target, load_sem.at[n])
+        for n, (source, target) in enumerate(zip(inputs, (left, right)))
+    ]
+    for load in loads:
+        load.start()
+    blocks, part, width = keep.shape
+    step = held.shape[1]
+    device = lax.axis_index("dp") * lax.axis_size("expert") + lax.axis_index("expert")
+
+    def compute():
+        for load in loads:
+            load.wait()
+
+        @pl.loop(0, width // step)
+        def _(n):
+            cols = pl.ds(pl.multiple_of(n * step, step), step)
+            held[...] = dot_tn(left[...], right[:, cols]).astype(BF)
+            for b in range(blocks):
+                own = (2 * b) ^ device
+                keep[b, :, cols] = held[pl.ds(pl.multiple_of(own * part, part), part), :]
+                own = own ^ 1
+                sent[b, :, cols] = held[pl.ds(pl.multiple_of(own * part, part), part), :]
+
+        copy = pltpu.make_async_remote_copy(
+            src_ref=sent,
+            dst_ref=got,
+            send_sem=cross_sem.at[0],
+            recv_sem=cross_sem.at[1],
+            device_id=peer_of(C_BIT),
+            device_id_type=MESH,
+        )
+        copy.start()
+        return copy.wait
+
+    return compute
+
+
+def run_trade(values, number, riders=(), work=(), blocks=0):
     size = values.shape[0]
     inputs = rider_inputs(riders)
+    vmem = pl.BlockSpec(memory_space=pltpu.VMEM)
+    shapes, specs, scratch = [], [], []
+    if work:
+        left, right = work
+        rows, width = left.shape[1], right.shape[1]
+        half = jax.ShapeDtypeStruct((blocks // 2, rows // blocks, width), BF)
+        shapes, specs = [half, half], [vmem, hbm]
+        scratch = [
+            pltpu.VMEM(left.shape, left.dtype),
+            pltpu.VMEM(right.shape, right.dtype),
+            pltpu.VMEM(half.shape, BF),
+            pltpu.VMEM((rows, 256), BF),
+            pltpu.SemaphoreType.DMA((2,)),
+            pltpu.SemaphoreType.DMA((2,)),
+        ]
     out = pl.pallas_call(
-        functools.partial(trade_kernel, plans=tuple(rider.plan() for rider in riders)),
-        in_specs=[hbm] * (1 + len(inputs)),
-        out_specs=(hbm,) * (1 + len(riders)),
-        out_shape=(jax.ShapeDtypeStruct(values.shape, values.dtype),) + rider_shapes(riders),
+        functools.partial(
+            trade_kernel, plans=tuple(rider.plan() for rider in riders), work=bool(work)
+        ),
+        in_specs=[hbm] * (1 + len(inputs) + len(work)),
+        out_specs=(hbm,) * (1 + len(riders)) + tuple(specs),
+        out_shape=(jax.ShapeDtypeStruct(values.shape, values.dtype),)
+        + rider_shapes(riders)
+        + tuple(shapes),
         scratch_shapes=[pltpu.SemaphoreType.DMA((n,)) for n in (size - 1, size - 1, 1)]
-        + rider_scratch(riders),
+        + rider_scratch(riders)
+        + scratch,
         compiler_params=pltpu.CompilerParams(
             collective_id=number, has_side_effects=True, vmem_limit_bytes=60 * MIB
         ),
         cost_estimate=cost(0, 170e6),
-    )(values, *inputs)
-    return out if riders else out[0]
+    )(values, *inputs, *work)
+    return out if riders or work else out[0]
 
 
 def first_kernel(a_ref, rank_ref, turned_ref, out_ref, slot_ref, send_sem, recv_sem, local_sem, *, far):
@@ -1616,11 +1671,21 @@
         copy.wait_send()
 
 
-def reduce_kernel(*refs, jobs, plans):
+def reduce_kernel(*refs, jobs, plans, work):
     size = len(jobs)
+    given = size - 1 if work else size
     inputs = sum(len(plan[3]) for plan in plans)
-    keeps, sends, sources = refs[:size], refs[size : 2 * size], refs[2 * size : 2 * size + inputs]
-    refs = refs[2 * size + inputs :]
+    keeps, sends, refs = list(refs[:given]), list(refs[given : 2 * given]), refs[2 * given :]
+    sources, refs = refs[:inputs], refs[inputs:]
+    compute = None
+    if work:
+        counts, body = work
+        work_in, refs = refs[: counts[0]], refs[counts[0] :]
+        work_out, refs = refs[: counts[1]], refs[counts[1] :]
+        work_scratch, refs = refs[-counts[2] :], refs[: -counts[2]]
+        compute = body(work_in, work_out, work_scratch)
+        keeps.append(work_scratch[0])
+        sends.append(work_scratch[1])
     outs = []
     for _, _, _, widths in jobs:
         outs.append(refs[: len(widths)])
@@ -1633,10 +1698,10 @@
     for load in loads:
         load.start()
     greet([peer_of(bit) for bit in sorted(used)])
-    chains, slot = [], 0
+    chains, late, slot = [], [], 0
     for n, (first, bits, parts, _) in enumerate(jobs):
         for part in parts:
-            chains.append(
+            (late if n >= given else chains).append(
                 reduce_chain(
                     slot,
                     (first, bits) + part,
@@ -1671,16 +1736,21 @@
                 for n, side in enumerate((outer, jnp.logical_not(outer))):
                     if turns[n] == turn:
                         pl.when(side)(start)
+        if turn == 0 and work:
+            compute()
+            chains += late
         turn += 1
     for finish in finishes:
         finish()
 
 
-def run_reduce(pairs, jobs, number, riders=()):
+def run_reduce(pairs, jobs, number, riders=(), work=None):
     slots = sum(len(parts) * (len(bits) + 1) for _, bits, parts, _ in jobs)
     vmem = pl.BlockSpec(memory_space=pltpu.VMEM)
     scratch, shapes = [], []
-    for (keep, send), (_, _, _, widths) in zip(pairs, jobs):
+    arrays, work_specs, work_shapes, work_scratch, body = work or ((), (), (), (), None)
+    late = [(shape, shape) for shape in work_scratch[:1]]
+    for (keep, send), (_, _, _, widths) in zip(list(pairs) + late, jobs):
         blocks, rows, cols = keep.shape
         scratch += [
             pltpu.VMEM((blocks, rows, cols), F32),
@@ -1690,18 +1760,24 @@
         shapes += [jax.ShapeDtypeStruct((rows, width), F32) for width in widths]
     inputs = rider_inputs(riders)
     return pl.pallas_call(
-        functools.partial(reduce_kernel, jobs=jobs, plans=tuple(rider.plan() for rider in riders)),
-        in_specs=[vmem] * len(pairs) + [hbm] * (len(pairs) + len(inputs)),
-        out_specs=(vmem,) * len(shapes) + (hbm,) * len(riders),
-        out_shape=tuple(shapes) + rider_shapes(riders),
+        functools.partial(
+            reduce_kernel,
+            jobs=jobs,
+            plans=tuple(rider.plan() for rider in riders),
+            work=((len(arrays), len(work_shapes), len(work_scratch)), body) if work else None,
+        ),
+        in_specs=[vmem] * len(pairs) + [hbm] * (len(pairs) + len(inputs)) + list(work_specs),
+        out_specs=(vmem,) * (len(work_shapes) + len(shapes)) + (hbm,) * len(riders),
+        out_shape=tuple(work_shapes) + tuple(shapes) + rider_shapes(riders),
         scratch_shapes=scratch
         + [pltpu.SemaphoreType.DMA((n,)) for n in (slots, slots)]
-        + rider_scratch(riders),
+        + rider_scratch(riders)
+        + list(work_scratch),
         compiler_params=pltpu.CompilerParams(
             collective_id=number, has_side_effects=True, vmem_limit_bytes=60 * MIB
         ),
         cost_estimate=cost(0, 170e6),
-    )(*(keep for keep, _ in pairs), *(send for _, send in pairs), *inputs)
+    )(*(keep for keep, _ in pairs), *(send for _, send in pairs), *inputs, *arrays)
 
 
 def sum_pair(kept, received):
@@ -1858,6 +1934,7 @@
     early = swap_bit(jnp.stack([gate_ka[1, 1], gate_s1[1]]), ZH_BIT)
     mix_keep, mix_send, dx_keep, dx_send, *second = run_experts(*expert_args, prior=first[:4])
     gate_kb, gate_t0, gate_t1, up_kb, up_t0, up_t1, down_kb, down_t0, down_t1 = second
+    down_ga = swap_bit(down_s0, Y_BIT)
     dx_send, down_ya, gate_ya, early = fence(dx_send, down_ya, gate_ya, early)
     gate_s0 = jnp.stack([gate_s0[0], add_low(gate_s0[1], early[1])])
     quarter = tokens // 4
@@ -1876,24 +1953,23 @@
             Rider(ZH_BIT, (down_ka, (1,)), down_ya, turns=(1, 0)),
         ),
     )
-    dx_sum, gate_ya, down_s0, gate_t1 = fence(dx_sum, gate_ya, down_s0, gate_t1)
+    dx_sum, gate_ya, down_ga, gate_t1 = fence(dx_sum, gate_ya, down_ga, gate_t1)
     gate_ma = swap_bit(add_low(gate_ka[1, 0], gate_ya[0]), ZH_BIT)
     gate_yb = swap_bit(gate_t1, Y_BIT)
     d_att, d_middle, d_low, d_log, ggain_mlp = run_post(
         dx_sum, middle, cotangent, normed_two, wr_pad, map_rows, gain_mlp, w_output
     )
-    out_keep, out_send = run_outgrad(place, att_full, d_low, devices)
-    d_att, out_send, gate_ma, gate_yb = fence(d_att, out_send, gate_ma, gate_yb)
+    d_att, gate_ma, gate_yb = fence(d_att, gate_ma, gate_yb)
     mix_keep = mix_keep.reshape(2, 2, tokens, WIDTH)
     mix_got = mix_got.reshape(2, 2, tokens, WIDTH)
     every = slice(None)
-    d_out, up_yb, down_ga, out_got, up_za, gate_oa, mix_x = run_trade(
+    d_out, up_yb, up_za, gate_oa, mix_x, out_keep, out_got = run_trade(
         d_att,
         4,
+        work=(att_full, d_low),
+        blocks=devices,
         riders=(
             Rider(Y_BIT, up_t1),
-            Rider(Y_BIT, down_s0),
-            Rider(C_BIT, out_send),
             Rider(ZH_BIT, (up_ka, (1, 1)), (up_ya, (1,))),
             Rider(ZL_BIT, (gate_ka, (0, 1)), (early, (0,)), (gate_ga, (1,))),
             Rider(X_BIT, (mix_keep, (every, 1)), (mix_got, (every, 1))),
@@ -1936,18 +2012,12 @@
     down_mb = swap_bit(add_low(down_kb[1], down_yb), ZH_BIT)
     down_gb = swap_bit(down_t0, Y_BIT)
     d_full, qkv_keep, qkv_send = run_qkvgrad(place, normed, d_pack, devices)
-    grad_in, ggain_attn = run_last(
-        d_full, w_query, w_key, w_value, d_middle, inputs, gain_attn
-    )
-    small_keep, small_send = run_small(place, normed_two, d_log, ggain_mlp, ggain_attn, devices)
     mixed = sum_pair(mix_keep[0, 0], mix_got[0, 0]) + sum_pair(mix_x[0], mix_z[0])
     hidden_out = middle + mixed
     rows = WIDTH // devices
     out_held = add_low(out_keep[:, 0], out_got[:, 0], out_x).reshape(4, 2, rows, WIDTH)
     out_first, out_second = out_held[:, 0], out_held[:, 1]
-    qkv_send, small_send, out_second, hidden_out = fence(
-        qkv_send, small_send, out_second, hidden_out
-    )
+    qkv_send, out_second, hidden_out = fence(qkv_send, out_second, hidden_out)
     qkv_parts = (
         (0, rows, 0, 768, (0, 1, 2, 3)),
         (0, rows, 768, 768, (1, 0, 2, 3)),
@@ -1955,15 +2025,17 @@
         (0, rows, 2048, 512, (1, 0, 2, 3)),
     )
     dense_bits = (X_BIT, Y_BIT, ZL_BIT, ZH_BIT)
-    query_total, key_total, value_total, small, output_total, up_mb = run_reduce(
-        ((qkv_keep, qkv_send), (small_keep, small_send), (out_first, out_second)),
+    last = (d_full, w_query, w_key, w_value, d_middle, inputs, normed_two, d_log)
+    grad_in, query_total, key_total, value_total, output_total, small, up_mb = run_reduce(
+        ((qkv_keep, qkv_send), (out_first, out_second)),
         (
             (C_BIT, dense_bits, qkv_parts, (WIDTH, KV_HEADS * HEAD_DIM, KV_HEADS * HEAD_DIM)),
+            (Y_BIT, (ZL_BIT, ZH_BIT), ((0, rows, 0, WIDTH, (0, 1)),), (WIDTH,)),
             (C_BIT, dense_bits, ((0, rows, 0, LANES, (0, 1, 2, 3)),), (LANES,)),
-            (Y_BIT, (ZL_BIT, ZH_BIT), ((0, rows, 0, WIDTH, (0, 1)),), (WIDTH,)),
         ),
         7,
         riders=(Rider(ZH_BIT, (up_kb, (1, 0)), (up_yb, (0,))),),
+        work=plan_last(last, gain_attn, ggain_mlp, devices),
     )
     query_total, small, down_mb, down_gb, other = fence(
         query_total, small, down_mb, down_gb, other

time: 710 us -> 699 us (0.985)
  Pallas kernels: 635 us -> 613 us
    pallas_call x3 -> x0, Pallas kernels: 20.8 us -> none  [the longest x1 9.31 us: run_last(): pl.pallas_call(last_kernel, out_shape=(jax.ShapeDtypeStruct((tokens, WIDT...]
    ppermute x16 -> x17, starting transfers between devices: 22.7 us -> 22.6 us  [swap(): return lax.ppermute(values, axis, [(i, i ^ mask) for i in range(size)])]
  transfers between devices with their start and end apart: 16 -> 17, of which waited for: 1 -> 1; matrix products, arithmetic and copies ran while one was open for 3% -> 4% of each run, Pallas kernels for 44% -> 51%
where the time goes in v5:
time: 699 us; the launch traced here: 693 us
  Pallas kernels  613 us (88%)
  other arithmetic  26.1 us (4%)
  starting transfers between devices  22.6 us (3%)
  local copies, waits for them, and re-layouts  19.1 us (3%)
  waiting for transfers between devices  10.5 us (2%)
    pallas_call x3, Pallas kernels, run_trade(): pl.pallas_call(functools.partial(trade_kernel, plans=tuple((rider.plan()...  157 us
    pallas_call x2, Pallas kernels, run_reduce(): pl.pallas_call(functools.partial(reduce_kernel, jobs=jobs, plans=tuple((r...  135 us
    pallas_call x2, Pallas kernels, run_experts(): pl.pallas_call(functools.partial(expert_kernel, first=not prior), grid_sp...  114 us
    pallas_call x1, Pallas kernels, run_first(): pl.pallas_call(functools.partial(first_kernel, far=far), in_specs=[hbm, v...  43.8 us
    pallas_call x1, Pallas kernels, run_backward(): pl.pallas_call(backward_kernel, grid=(blocks,), in_specs=[pl.BlockSpec(pa...  43.1 us
    pallas_call x1, Pallas kernels, run_gather(): pl.pallas_call(gather_kernel, in_specs=[pl.BlockSpec(memory_space=pltpu.V...  39.3 us
    pallas_call x1, Pallas kernels, run_forward(): pl.pallas_call(forward_kernel, grid=(blocks,), in_specs=[pl.BlockSpec(pac...  30.3 us
    ppermute x17, starting transfers between devices, swap(): return lax.ppermute(values, axis, [(i, i ^ mask) for i in range(size)])  22.6 us
  transfers between devices with their start and end apart: 17, of which 1 were waited for; matrix products, arithmetic and copies ran while one was open for 4% of the time, Pallas kernels for 51%

profile of v5, /device:TPU:0, one launch (start us, length us, event | category | flops | bytes accessed | tf_op | source)
XLA Modules:
  0.0 692.8 jit_solution(9427025483149026337)
XLA Ops:
  3.7 9.0 %shard_map.229 = (bf16[320,1536]{1,0:T(8,128)(2,1)}, bf16[8,800,128]{2,1,0:T(8,128)(2,1)}, bf16[320,1536]{1,0:T(8,128)(2,1)}) custom-call(f32[320,1536]{1,0:T(8,128)} %bitcast.78, f32[1,1536]{1,0:T(1,128)} %broadcast_in_dim.44.gain_ref.refs_6_, bf16[1536,1536]{1,0:T(8,128)(2,1)} %refs_9_.1, bf16[1536,512]{1,0:T(8,128)(2,1)} %refs_10_.1, ...), custom_call_target="tpu_custom_call" | custom-call | flops 2516582400 | bytes 14000000 | tf_op jit(solution)/shard_map/pallas_call | solution.py:486
  12.7 2.9 collective-permute-start
  16.9 43.8 %shard_map.230 = (bf16[8,800,128]{2,1,0:T(8,128)(2,1)}, f32[40,320]{1,0:T(8,128)}) custom-call(bf16[8,800,128]{2,1,0:T(8,128)(2,1)} %get-tuple-element.135.a_ref, f32[40,320]{1,0:T(8,128)} %copy-done.23, f32[320,40]{1,0:T(8,128)} %bitcast.90), custom_call_target="tpu_custom_call" | custom-call | bytes 170000000 | tf_op jit(solution)/shard_map/pallas_call | solution.py:1599
  61.4 30.3 %shard_map.231 = (bf16[8,480,128]{2,1,0:T(8,128)(2,1)}, f32[10,64,768]{2,1,0:T(8,128)}, f32[10,1,768]{2,1,0:T(1,128)}) custom-call(bf16[8,800,128]{2,1,0:T(8,128)(2,1)} %get-tuple-element.139.pack_ref), custom_call_target="tpu_custom_call" | custom-call | flops 10066329600 | bytes 6000000 | tf_op jit(solution)/shard_map/pallas_call | solution.py:601
  101.6 23.9 %shard_map.232.att_ref = bf16[8,480,128]{2,1,0:T(8,128)(2,1)} custom-call(bf16[8,480,128]{2,1,0:T(8,128)(2,1)} %get-tuple-element.143.refs_0_), custom_call_target="tpu_custom_call" | custom-call | bytes 170000000 | tf_op jit(solution)/shard_map/pallas_call | solution.py:1565
  127.2 7.3 %shard_map.233 = (f32[320,1536]{1,0:T(8,128)}, bf16[320,1536]{1,0:T(8,128)(2,1)}, bf16[320,1536]{1,0:T(8,128)(2,1)}) custom-call(bf16[8,480,128]{2,1,0:T(8,128)(2,1)} %shard_map.232.att_ref, bf16[1536,1536]{1,0:T(8,128)(2,1)} %wo_ref.3, f32[320,1536]{1,0:T(8,128)} %bitcast.79, f32[1,1536]{1,0:T(1,128)} %broadcast_in_dim.48.gain_ref), custom_call_target="tpu_custom_call" | custom-call | flops 1509949440 | bytes 12000000 | tf_op jit(solution)/shard_map/pallas_call | solution.py:760
  134.5 39.3 %shard_map.234 = (bf16[8,320,1536]{2,1,0:T(8,128)(2,1)}, bf16[8,320,1536]{2,1,0:T(8,128)(2,1)}, f32[8,40,320]{2,1,0:T(8,128)}) custom-call(bf16[320,1536]{1,0:T(8,128)(2,1)} %get-tuple-element.147.x_ref.norm_ref.refs_14_, bf16[320,1536]{1,0:T(8,128)(2,1)} %get-tuple-element.141.refs_0_, bf16[320,1536]{1,0:T(8,128)(2,1)} %copy-done.15, ...), custom_call_target="tpu_custom_call" | custom-call | bytes 150000000 | tf_op jit(solution)/shard_map/pallas_call | solution.py:1325
  173.8 2.0 fusion.11.map_ref
  175.7 55.9 %shard_map.235 = (bf16[4,320,1536]{2,1,0:T(8,128)(2,1)}, bf16[4,320,1536]{2,1,0:T(8,128)(2,1)}, bf16[4,320,1664]{2,1,0:T(8,128)(2,1)}, bf16[4,320,1664]{2,1,0:T(...) custom-call(s32[6]{0:T(128)} %stack.43.place_ref, ...), custom_call_target="tpu_custom_call" | custom-call | flops 30000001024 | bytes 60000000 | tf_op jit(solution)/shard_map/pallas_call | solution.py:999
  239.6 58.6 %shard_map.236 = (bf16[4,320,1536]{2,1,0:T(8,128)(2,1)}, bf16[4,320,1536]{2,1,0:T(8,128)(2,1)}, bf16[4,320,1664]{2,1,0:T(8,128)(2,1)}, bf16[4,320,1664]{2,1,0:T(...) custom-call(s32[6]{0:T(128)} %stack.43.place_ref, ...), custom_call_target="tpu_custom_call" | custom-call | flops 30000001024 | bytes 60000000 | tf_op jit(solution)/shard_map/pallas_call | solution.py:999
  299.6 64.4 %shard_map.237 = (f32[320,1664]{1,0:T(8,128)}, bf16[2,5,192,256]{3,2,1,0:T(8,128)(2,1)}, bf16[2,5,192,256]{3,2,1,0:T(8,128)(2,1)}, bf16[4,320,1536]{2,1,0:T(8,128)(2,1)}, bf16[5,64,1536]{2,1,0:T(8,128)(2,1)}) custom-call(bf16[4,320,1664]{2,1,0:T(8,128)(2,1)} %get-tuple-element.158.refs_0_, bf16[4,320,1664]{2,1,0:T(8,128)(2,1)} %get-tuple-element.163.refs_1_, ...), custom_call_target="tpu_custom_call" | custom-call | bytes 170000000 | tf_op jit(solution)/shard_map/pallas_call | solution.py:1762
  366.0 3.6 collective-permute-start.9
  369.6 2.3 multiply_sine_fusion
  371.8 9.3 %shard_map.238 = (bf16[8,480,128]{2,1,0:T(8,128)(2,1)}, f32[320,1536]{1,0:T(8,128)}, bf16[320,1536]{1,0:T(8,128)(2,1)}, bf16[320,128]{1,0:T(8,128)(2,1)}, f32[1,1536]{1,0:T(1,128)}) custom-call(f32[320,1664]{1,0:T(8,128)} %get-tuple-element.174.dx_ref, f32[320,1536]{1,0:T(8,128)} %get-tuple-element.175.mid_ref, f32[320,1536]{1,0:T(8,128)} %bitcast.82, ...), custom_call_target="tpu_custom_call" | custom-call | flops 1509949440 | bytes 14000000 | tf_op jit(solution)/shard_map/pallas_call | solution.py:1089
  381.1 10.5 %collective-permute-done.9.refs_2_ = bf16[5,192,256]{2,1,0:T(8,128)(2,1)S(1)} collective-permute-done((bf16[5,192,256]{2,1,0:T(8,128)(2,1)S(1)}, bf16[5,192,256]{2,1,0:T(8,128)(2,1)S(1)}, u32[]{:S(2)}, u32[]{:S(2)}) %collective-permute-start.9) | collective-permute-done | bytes 491552 | tf_op jit(solution)/shard_map/ppermute | solution.py:412
  391.6 51.6 %shard_map.239 = (bf16[8,480,128]{2,1,0:T(8,128)(2,1)}, bf16[2,5,192,256]{3,2,1,0:T(8,128)(2,1)}, bf16[5,192,256]{2,1,0:T(8,128)(2,1)}, bf16[5,192,256]{2,1,0:T(...) custom-call(bf16[8,480,128]{2,1,0:T(8,128)(2,1)} %get-tuple-element.179.ref, ...), custom_call_target="tpu_custom_call" | custom-call | bytes 170000000 | tf_op jit(solution)/shard_map/pallas_call | solution.py:1565
  448.6 43.1 %shard_map.240.refs_0_ = bf16[8,800,128]{2,1,0:T(8,128)(2,1)} custom-call(bf16[8,800,128]{2,1,0:T(8,128)(2,1)} %get-tuple-element.139.pack_ref, bf16[8,480,128]{2,1,0:T(8,128)(2,1)} %get-tuple-element.188.grad_ref, f32[10,64,768]{2,1,0:T(8,128)} %get-tuple-element.189.out_t_ref, f32[10,1,768]{2,1,0:T(1,128)} %get-tuple-element.190.lse_ref, ...), custom_call_target="tpu_custom_call" | custom-call | flops 25165824000 | bytes 8000000 | tf_op jit(solution)/shard_map/pallas_call | solution.py:722
  493.3 81.5 %shard_map.241 = (bf16[8,800,128]{2,1,0:T(8,128)(2,1)}, bf16[2,5,192,256]{3,2,1,0:T(8,128)(2,1)}, bf16[2,5,192,256]{3,2,1,0:T(8,128)(2,1)}, bf16[5,192,256]{2,1,...) custom-call(bf16[8,800,128]{2,1,0:T(8,128)(2,1)} %shard_map.240.refs, ...), custom_call_target="tpu_custom_call" | custom-call | bytes 170000000 | tf_op jit(solution)/shard_map/pallas_call | solution.py:1565
  574.8 2.2 fusion
  578.5 2.1 collective-permute-start.14
  586.7 11.9 %shard_map.242 = (bf16[320,2560]{1,0:T(8,128)(2,1)}, bf16[16,48,2560]{2,1,0:T(8,128)(2,1)}, bf16[16,48,2560]{2,1,0:T(8,128)(2,1)}) custom-call(s32[6]{0:T(128)} %stack.43.place_ref, bf16[320,1536]{1,0:T(8,128)(2,1)} %get-tuple-element.134.a_ref, bf16[8,800,128]{2,1,0:T(8,128)(2,1)} %get-tuple-element.215.d_ref), custom_call_target="tpu_custom_call" | custom-call | flops 2516582400 | bytes 12000000 | tf_op jit(solution)/shard_map/pallas_call | solution.py:1143
  598.6 3.7 fusion.2
  602.3 70.9 %shard_map.243 = (f32[320,1536]{1,0:T(8,128)}, f32[48,1536]{1,0:T(8,128)}, f32[48,512]{1,0:T(8,128)}, f32[48,512]{1,0:T(8,128)}, f32[48,1536]{1,0:T(8,128)}, /*i...) custom-call(bf16[16,48,2560]{2,1,0:T(8,128)(2,1)} %get-tuple-element.220.refs_0_, ...), custom_call_target="tpu_custom_call" | custom-call | bytes 170000000 | tf_op jit(solution)/shard_map/pallas_call | solution.py:1762
  676.2 12.2 %shard_map.244 = (f32[2,5,192,512]{3,2,1,0:T(8,128)}, f32[2,5,192,512]{3,2,1,0:T(8,128)}, f32[2,5,64,1536]{3,2,1,0:T(8,128)}) custom-call(s32[6]{0:T(128)} %stack.43.place_ref, bf16[2,2,5,192,256]{4,3,2,1,0:T(8,128)(2,1)} %get-tuple-element.162.refs_4_.refs_0_, bf16[2,5,192,256]{3,2,1,0:T(8,128)(2,1)} %get-tuple-element.183.refs_6_.refs_1_, ...), custom_call_target="tpu_custom_call" | custom-call | flops 1000000 | bytes 26000000 | tf_op jit(solution)/shard_map/pallas_call | solution.py:1836
  (144 shorter events, 49.1 us)
Async XLA Ops:
  12.7 79.7 %collective-permute-start = (bf16[320,1536]{1,0:T(8,128)(2,1)}, bf16[320,1536]{1,0:T(8,128)(2,1)S(1)}, u32[]{:S(2)}, u32[]{:S(2)}) collective-permute-start(bf16[320,1536]{1,0:T(8,128)(2,1)} %get-tuple-element.141.refs_0_), channel_id=1, source_target_pairs={{0,2},{1,3},{2,0},{3,1},{4,6},{5,7},{6,4},{7,5},{8,10},{9,11},{10,... | collective-permute-start | bytes 2949128 | tf_op jit(solution)/shard_map/ppermute | solution.py:412
  60.7 31.6 %collective-permute-start.1 = (bf16[320,1536]{1,0:T(8,128)(2,1)S(1)}, bf16[320,1536]{1,0:T(8,128)(2,1)S(1)}, u32[]{:S(2)}, u32[]{:S(2)}) collective-permute-start(bf16[320,1536]{1,0:T(8,128)(2,1)S(1)} %copy-done.14), channel_id=1, source_target_pairs={{0,8},{4,12},{8,0},{12,4},{16,24},{20,28},{24,16},{28,20},{1,9},{5... | collective-permute-start | bytes 2949128 | tf_op jit(solution)/shard_map/ppermute | solution.py:412
  60.8 30.9 %collective-permute-start.2 = (f32[1,40,320]{2,1,0:T(8,128)}, f32[1,40,320]{2,1,0:T(8,128)S(1)}, u32[]{:S(2)}, u32[]{:S(2)}) collective-permute-start(f32[1,40,320]{2,1,0:T(8,128)} %bitcast.94), channel_id=1, source_target_pairs={{0,2},{1,3},{2,0},{3,1},{4,6},{5,7},{6,4},{7,5},{8,10},{9,11},{10,... | collective-permute-start | bytes 153608 | tf_op jit(solution)/shard_map/ppermute | solution.py:412
  92.3 34.8 %collective-permute-start.3 = (bf16[320,1536]{1,0:T(8,128)(2,1)S(1)}, bf16[320,1536]{1,0:T(8,128)(2,1)S(1)}, u32[]{:S(2)}, u32[]{:S(2)}) collective-permute-start(bf16[320,1536]{1,0:T(8,128)(2,1)S(1)} %collective-permute-done.1.refs_2_), channel_id=1, source_target_pairs={{0,2},{1,3},{2,0},{3,1},{4,6},{5,7},{6,4},{7,5},{8,10},{9,11},{10,... | collective-permute-start | bytes 2949128 | tf_op jit(solution)/shard_map/ppermute | solution.py:412
  99.7 25.9 %collective-permute-start.4 = (f32[2,40,320]{2,1,0:T(8,128)}, f32[2,40,320]{2,1,0:T(8,128)S(1)}, u32[]{:S(2)}, u32[]{:S(2)}) collective-permute-start(f32[2,40,320]{2,1,0:T(8,128)} %pad_maximum_fusion.7), channel_id=1, source_target_pairs={{0,8},{4,12},{8,0},{12,4},{16,24},{20,28},{24,16},{28,20},{1,9},{5... | collective-permute-start | bytes 307208 | tf_op jit(solution)/shard_map/ppermute | solution.py:412
  231.6 66.6 %collective-permute-start.6 = (bf16[2,5,192,256]{3,2,1,0:T(8,128)(2,1)}, bf16[2,5,192,256]{3,2,1,0:T(8,128)(2,1)}, u32[]{:S(2)}, u32[]{:S(2)}) collective-permute-start(bf16[2,5,192,256]{3,2,1,0:T(8,128)(2,1)} %get-tuple-element.161), channel_id=1, source_target_pairs={{0,4},{4,0},{8,12},{12,8},{16,20},{20,16},{24,28},{28,24},{1,5},{5... | collective-permute-start | bytes 2949128 | tf_op jit(solution)/shard_map/ppermute | solution.py:412
  234.3 63.9 %collective-permute-start.5 = (bf16[5,64,1536]{2,1,0:T(8,128)(2,1)}, bf16[5,64,1536]{2,1,0:T(8,128)(2,1)S(1)}, u32[]{:S(2)}, u32[]{:S(2)}) collective-permute-start(bf16[5,64,1536]{2,1,0:T(8,128)(2,1)} %get-tuple-element.160), channel_id=1, source_target_pairs={{0,4},{4,0},{8,12},{12,8},{16,20},{20,16},{24,28},{28,24},{1,5},{5... | collective-permute-start | bytes 2949128 | tf_op jit(solution)/shard_map/ppermute | solution.py:412
  237.0 61.2 %collective-permute-start.7 = (bf16[2,5,192,256]{3,2,1,0:T(8,128)(2,1)}, bf16[2,5,192,256]{3,2,1,0:T(8,128)(2,1)S(1)}, u32[]{:S(2)}, u32[]{:S(2)}) collective-permute-start(bf16[2,5,192,256]{3,2,1,0:T(8,128)(2,1)} %pad_maximum_fusion), channel_id=1, source_target_pairs={{0,16},{4,20},{8,24},{12,28},{16,0},{20,4},{24,8},{28,12},{1,17},{... | collective-permute-start | bytes 2949128 | tf_op jit(solution)/shard_map/ppermute | solution.py:412
  238.1 125.9 %collective-permute-start.8 = (bf16[5,64,1536]{2,1,0:T(8,128)(2,1)}, bf16[5,64,1536]{2,1,0:T(8,128)(2,1)S(1)}, u32[]{:S(2)}, u32[]{:S(2)}) collective-permute-start(bf16[5,64,1536]{2,1,0:T(8,128)(2,1)} %get-tuple-element.172), channel_id=1, source_target_pairs={{0,4},{4,0},{8,12},{12,8},{16,20},{20,16},{24,28},{28,24},{1,5},{5... | collective-permute-start | bytes 2949128 | tf_op jit(solution)/shard_map/ppermute | solution.py:412
  239.6 58.6 %copy-start.19 = (bf16[2,5,192,256]{3,2,1,0:T(8,128)(2,1)S(1)}, bf16[2,5,192,256]{3,2,1,0:T(8,128)(2,1)}, u32[]{:S(2)}) copy-start(bf16[2,5,192,256]{3,2,1,0:T(8,128)(2,1)} %get-tuple-element.165) | copy-start | bytes 2949124
  298.2 65.8 %copy-start.5 = (bf16[2,5,192,256]{3,2,1,0:T(8,128)(2,1)}, bf16[2,5,192,256]{3,2,1,0:T(8,128)(2,1)S(1)}, u32[]{:S(2)}) copy-start(bf16[2,5,192,256]{3,2,1,0:T(8,128)(2,1)S(1)} %collective-permute-done.7.refs_5_) | copy-start | bytes 2949124
  299.6 64.5 %copy-start.34 = (bf16[2,5,192,256]{3,2,1,0:T(8,128)(2,1)S(1)}, bf16[2,5,192,256]{3,2,1,0:T(8,128)(2,1)}, u32[]{:S(2)}) copy-start(bf16[2,5,192,256]{3,2,1,0:T(8,128)(2,1)} %get-tuple-element.178) | copy-start | bytes 2949124
  364.1 27.5 %collective-permute-start.10 = (bf16[2,5,192,256]{3,2,1,0:T(8,128)(2,1)S(1)}, bf16[2,5,192,256]{3,2,1,0:T(8,128)(2,1)S(1)}, u32[]{:S(2)}, u32[]{:S(2)}) collective-permute-start(bf16[2,5,192,256]{3,2,1,0:T(8,128)(2,1)S(1)} %copy-done.34), channel_id=1, source_target_pairs={{0,4},{4,0},{8,12},{12,8},{16,20},{20,16},{24,28},{28,24},{1,5},{5... | collective-permute-start | bytes 2949128 | tf_op jit(solution)/shard_map/ppermute | solution.py:412
  366.0 25.6 %collective-permute-start.9 = (bf16[5,192,256]{2,1,0:T(8,128)(2,1)S(1)}, bf16[5,192,256]{2,1,0:T(8,128)(2,1)S(1)}, u32[]{:S(2)}, u32[]{:S(2)}) collective-permute-start(bf16[5,192,256]{2,1,0:T(8,128)(2,1)S(1)} %fusion.9), channel_id=1, source_target_pairs={{0,16},{4,20},{8,24},{12,28},{16,0},{20,4},{24,8},{28,12},{1,17},{... | collective-permute-start | bytes 1474568 | tf_op jit(solution)/shard_map/ppermute | solution.py:412
  391.6 51.7 %copy-start.24 = (bf16[5,192,256]{2,1,0:T(8,128)(2,1)}, bf16[5,192,256]{2,1,0:T(8,128)(2,1)S(1)}, u32[]{:S(2)}) copy-start(bf16[5,192,256]{2,1,0:T(8,128)(2,1)S(1)} %collective-permute-done.9.refs_2_) | copy-start | bytes 1474564
  391.6 52.8 %copy-start.11 = (bf16[2,5,192,256]{3,2,1,0:T(8,128)(2,1)}, bf16[2,5,192,256]{3,2,1,0:T(8,128)(2,1)S(1)}, u32[]{:S(2)}) copy-start(bf16[2,5,192,256]{3,2,1,0:T(8,128)(2,1)S(1)} %collective-permute-done.10.refs_4_) | copy-start | bytes 2949124
  391.6 51.7 %copy-start.6 = (bf16[2,5,192,256]{3,2,1,0:T(8,128)(2,1)S(1)}, bf16[2,5,192,256]{3,2,1,0:T(8,128)(2,1)}, u32[]{:S(2)}) copy-start(bf16[2,5,192,256]{3,2,1,0:T(8,128)(2,1)} %get-tuple-element.194.refs_3_) | copy-start | bytes 2949124
  445.7 46.0 %collective-permute-start.11 = (bf16[2,5,192,256]{3,2,1,0:T(8,128)(2,1)S(1)}, bf16[2,5,192,256]{3,2,1,0:T(8,128)(2,1)S(1)}, u32[]{:S(2)}, u32[]{:S(2)}) collective-permute-start(bf16[2,5,192,256]{3,2,1,0:T(8,128)(2,1)S(1)} %pad_maximum_fusion.2), channel_id=1, source_target_pairs={{0,16},{4,20},{8,24},{12,28},{16,0},{20,4},{24,8},{28,12},{1,17},{... | collective-permute-start | bytes 2949128 | tf_op jit(solution)/shard_map/ppermute | solution.py:412
  446.6 45.1 %collective-permute-start.12 = (bf16[2,5,192,256]{3,2,1,0:T(8,128)(2,1)}, bf16[2,5,192,256]{3,2,1,0:T(8,128)(2,1)S(1)}, u32[]{:S(2)}, u32[]{:S(2)}) collective-permute-start(bf16[2,5,192,256]{3,2,1,0:T(8,128)(2,1)} %get-tuple-element.197), channel_id=1, source_target_pairs={{0,4},{4,0},{8,12},{12,8},{16,20},{20,16},{24,28},{28,24},{1,5},{5... | collective-permute-start | bytes 2949128 | tf_op jit(solution)/shard_map/ppermute | solution.py:412
  447.5 44.2 %collective-permute-start.13 = (bf16[5,64,1536]{2,1,0:T(8,128)(2,1)}, bf16[5,64,1536]{2,1,0:T(8,128)(2,1)S(1)}, u32[]{:S(2)}, u32[]{:S(2)}) collective-permute-start(bf16[5,64,1536]{2,1,0:T(8,128)(2,1)} %get-tuple-element.198), channel_id=1, source_target_pairs={{0,4},{4,0},{8,12},{12,8},{16,20},{20,16},{24,28},{28,24},{1,5},{5... | collective-permute-start | bytes 2949128 | tf_op jit(solution)/shard_map/ppermute | solution.py:412
  493.3 81.5 %copy-start.1 = (bf16[16,48,1536]{2,1,0:T(8,128)(2,1)S(1)}, bf16[16,48,1536]{2,1,0:T(8,128)(2,1)}, u32[]{:S(2)}) copy-start(bf16[16,48,1536]{2,1,0:T(8,128)(2,1)} %get-tuple-element.205) | copy-start | bytes 7077892
  578.5 94.7 %collective-permute-start.14 = (bf16[5,64,1536]{2,1,0:T(8,128)(2,1)}, bf16[5,64,1536]{2,1,0:T(8,128)(2,1)}, u32[]{:S(2)}, u32[]{:S(2)}) collective-permute-start(bf16[5,64,1536]{2,1,0:T(8,128)(2,1)} %fusion.1), channel_id=1, source_target_pairs={{0,16},{4,20},{8,24},{12,28},{16,0},{20,4},{24,8},{28,12},{1,17},{... | collective-permute-start | bytes 2949128 | tf_op jit(solution)/shard_map/ppermute | solution.py:412
  580.5 92.6 %collective-permute-start.15 = (bf16[5,64,1536]{2,1,0:T(8,128)(2,1)}, bf16[5,64,1536]{2,1,0:T(8,128)(2,1)}, u32[]{:S(2)}, u32[]{:S(2)}) collective-permute-start(bf16[5,64,1536]{2,1,0:T(8,128)(2,1)} %get-tuple-element.233), channel_id=1, source_target_pairs={{0,4},{4,0},{8,12},{12,8},{16,20},{20,16},{24,28},{28,24},{1,5},{5... | collective-permute-start | bytes 2949128 | tf_op jit(solution)/shard_map/ppermute | solution.py:412
  585.0 88.2 %collective-permute-start.16 = (bf16[2,5,192,256]{3,2,1,0:T(8,128)(2,1)}, bf16[2,5,192,256]{3,2,1,0:T(8,128)(2,1)}, u32[]{:S(2)}, u32[]{:S(2)}) collective-permute-start(bf16[2,5,192,256]{3,2,1,0:T(8,128)(2,1)} %pad_maximum_fusion.3), channel_id=1, source_target_pairs={{0,8},{4,12},{8,0},{12,4},{16,24},{20,28},{24,16},{28,20},{1,9},{5... | collective-permute-start | bytes 2949128 | tf_op jit(solution)/shard_map/ppermute | solution.py:412
  (28 other events, 309.7 us)

commit v6 on v5

--- a/solution.py
+++ b/solution.py
@@ -383,6 +383,7 @@
 SLOTS = 64
 CHUNK = 512
 MIB = 1 << 20
+hbm = pl.BlockSpec(memory_space=pltpu.HBM)
 
 
 def dot_nn(a, b):
@@ -773,8 +774,8 @@
     place_ref,
     x_ref,
     g_ref,
+    gates_ref,
     map_ref,
-    wr_ref,
     wg0_ref,
     wg1_ref,
     wu0_ref,
@@ -813,43 +814,16 @@
     sources = map_ref.shape[0]
     experts = xs.shape[0]
     low = 0 if first else experts
-    tokens = x_ref.shape[1]
     rows = experts * SLOTS
     count = WIDTH // CHUNK
 
-    def one_hot(source):
-        slots = map_ref[source, low : low + experts, :]
-        wide = jnp.broadcast_to(slots[:, None, :], (experts, SLOTS, tokens))
-        rank = lax.broadcasted_iota(jnp.int32, (experts, SLOTS, tokens), 1).astype(F32)
-        return (wide == rank).astype(F32).reshape(rows, tokens)
-
-    @pl.when(step < sources)
+    def pick_of(source):
+        return one_hot(map_ref[source, low : low + experts, :], rows)
+
+    @pl.when(step < experts)
     def _():
-        slot_map = map_ref[step]
-        chosen = slot_map >= 0.0
-        logits = dot_nt(wr_ref[...], x_ref[0])[0 : slot_map.shape[0]]
-        logits = jnp.where(chosen, logits, MASKED)
-        raised = jnp.exp(logits - jnp.max(logits, axis=0, keepdims=True))
-        raised = jnp.where(chosen, raised, 0.0)
-        gates = raised / jnp.sum(raised, axis=0, keepdims=True)
-        pick = one_hot(step)
-        wide = jnp.broadcast_to(gates[low : low + experts, None, :], (experts, SLOTS, tokens))
-        gate_rows = jnp.sum(pick * wide.reshape(rows, tokens), axis=1, keepdims=True)
-        pick = pick.astype(BF)
-        here = pl.ds(pl.multiple_of(step * SLOTS, SLOTS), SLOTS)
-        for e in range(experts):
-            gate_s[e, here, :] = gate_rows[e * SLOTS : (e + 1) * SLOTS]
-        for n in range(count):
-            cols = slice(n * CHUNK, (n + 1) * CHUNK)
-            got = dot_nn(pick, x_ref[0, :, cols]).astype(BF)
-            xs[:, here, cols] = got.reshape(experts, SLOTS, CHUNK)
-            got = dot_nn(pick, g_ref[0, :, cols]).astype(BF)
-            gs[:, here, cols] = got.reshape(experts, SLOTS, CHUNK)
-
-    @pl.when((step >= sources) & (step < sources + experts))
-    def _():
-        e = step - sources
-        x = xs[e]
+        e = step
+        x = x_ref[0]
         w_gate = jnp.concatenate([wg0_ref[0], wg1_ref[0]], axis=1)
         w_up = jnp.concatenate([wu0_ref[0], wu1_ref[0]], axis=1)
         gate_pre = dot_nn(x, w_gate)
@@ -857,13 +831,13 @@
         sig = jax.nn.sigmoid(gate_pre)
         silu = gate_pre * sig
         hidden = (silu * up_pre).astype(BF)
-        gate = gate_s[e]
+        gate = gates_ref[0]
         d_hidden = jnp.zeros(hidden.shape, F32)
         d_gates = jnp.zeros(gate.shape, F32)
         for n in range(count):
             cols = slice(n * CHUNK, (n + 1) * CHUNK)
             w_down = jnp.concatenate([wd0_ref[0, :, cols], wd1_ref[0, :, cols]], axis=0)
-            grad = gs[e, :, cols].astype(F32)
+            grad = g_ref[0, :, cols].astype(F32)
             d_y = (gate * grad).astype(BF)
             y = dot_nn(hidden, w_down)
             d_gates += jnp.sum(y * grad, axis=1, keepdims=True)
@@ -915,7 +889,7 @@
             out[0, :, cols] = values.astype(BF)
 
         here = pl.ds(pl.multiple_of(source * SLOTS, SLOTS), SLOTS)
-        pick = one_hot(source).astype(BF)
+        pick = pick_of(source).astype(BF)
         for n in range(count):
             cols = slice(n * CHUNK, (n + 1) * CHUNK)
             put(dx_out, dx_in, cols, dot_tn(pick, xs[:, here, cols].reshape(rows, CHUNK)))
@@ -926,15 +900,15 @@
         spread_out = jnp.where(column == owner + (place_ref[4] + low), values, 0.0).astype(BF)
         put(dx_out, dx_in, slice(WIDTH, WIDTH + LANES), dot_tn(pick, spread_out))
 
-    @pl.when((step >= sources + experts) & (step < sources + experts + sources // 2))
+    @pl.when((step >= experts) & (step < experts + sources // 2))
+    def _():
+        source = step - experts + sources // 2
+        prior = (None, None) if first else (mix_prior[1], dx_prior[1])
+        combine(source, mix_send, dx_send, *prior)
+
+    @pl.when(step >= experts + sources // 2)
     def _():
         source = step - experts - sources // 2
-        prior = (None, None) if first else (mix_prior[1], dx_prior[1])
-        combine(source, mix_send, dx_send, *prior)
-
-    @pl.when(step >= sources + experts + sources // 2)
-    def _():
-        source = step - experts - sources - sources // 2
         prior = (None, None) if first else (mix_prior[0], dx_prior[0])
         combine(source, mix_keep, dx_keep, *prior)
 
@@ -943,8 +917,9 @@
     return jax.ShapeDtypeStruct(shape.shape[1:], shape.dtype)
 
 
-def run_experts(place, x_all, g_all, maps, wr_t, w_gate, w_up, w_down, prior=()):
-    sources, tokens, width = x_all.shape
+def run_experts(place, x_slots, g_slots, gates, maps, w_gate, w_up, w_down, prior=()):
+    sources, _, tokens = maps.shape
+    width = x_slots.shape[2]
     experts = w_gate.shape[0] // 2
     low = experts if prior else 0
     ffe = w_gate.shape[2]
@@ -953,14 +928,14 @@
     half = ffe // 2
     slots = sources * SLOTS
     extra = width + LANES
-    second = sources + experts
+    second = experts
     third = second + sources // 2
 
     def at(i, low, size):
         return jnp.clip(i - low, 0, size - 1)
 
     def expert_of(i):
-        return at(i, sources, experts)
+        return at(i, 0, experts)
 
     def w_cols(block):
         return pl.BlockSpec(
@@ -972,10 +947,7 @@
             (1, LANES, width), lambda i, p: (expert_of(i) + low, p[0] + 2 * block, 0)
         )
 
-    token_spec = pl.BlockSpec(
-        (1, tokens, width),
-        lambda i, p: (at(i, 0, sources), 0, 0),
-    )
+    slot_spec = pl.BlockSpec((1, slots, width), lambda i, p: (expert_of(i) + low, 0, 0))
 
     def out_tokens(low, cols):
         return pl.BlockSpec((1, tokens, cols), lambda i, p: (at(i, low, sources // 2), 0, 0))
@@ -1002,10 +974,10 @@
             num_scalar_prefetch=1,
             grid=(third + sources // 2,),
             in_specs=[
-                token_spec,
-                token_spec,
+                slot_spec,
+                slot_spec,
+                pl.BlockSpec((1, slots, 1), lambda i, p: (expert_of(i) + low, 0, 0)),
                 pl.BlockSpec(maps.shape, lambda i, p: (0, 0, 0)),
-                pl.BlockSpec(wr_t.shape, lambda i, p: (0, 0)),
                 w_cols(0),
                 w_cols(1),
                 w_cols(0),
@@ -1039,7 +1011,7 @@
         + (wide, less(wide), less(wide)),
         compiler_params=params(60, ("arbitrary",)),
         cost_estimate=cost(30e9, 60e6),
-    )(place, x_all, g_all, maps, wr_t, w_gate, w_gate, w_up, w_up, w_down, w_down, *prior)
+    )(place, x_slots, g_slots, gates, maps, w_gate, w_gate, w_up, w_up, w_down, w_down, *prior)
 
 
 def post_kernel(
@@ -1231,7 +1203,6 @@
 
 
 MESH = pl.DeviceIdType.MESH
-hbm = pl.BlockSpec(memory_space=pltpu.HBM)
 
 
 def peer_of(bit):
@@ -1249,10 +1220,20 @@
 GATHER_BITS = (X_BIT, ZL_BIT, C_BIT)
 
 
-def gather_steps(x_ref, all_ref, send_sem, recv_sem, local_sem):
+def one_hot(slots, rows):
+    experts, tokens = slots.shape
+    wide = jnp.broadcast_to(slots[:, None, :], (experts, SLOTS, tokens))
+    rank = lax.broadcasted_iota(jnp.int32, (experts, SLOTS, tokens), 1).astype(F32)
+    return (wide == rank).astype(F32).reshape(rows, tokens)
+
+
+def gather_kernel(x_ref, *refs):
+    blocks, maps_ref, wr_ref = refs[0:4], refs[4], refs[5]
+    x_slots, g_slots, gates_ref, local_ref = refs[6:10]
+    all_ref, other, all_maps_ref, stage = refs[10:14]
+    send_sem, recv_sem, more_send, more_recv, store_sem = refs[14:]
+    greet([peer_of(bit) for bit in GATHER_BITS])
     half = x_ref.shape[0] // 2
-    own = pltpu.make_async_copy(x_ref, all_ref.at[0], local_sem)
-    own.start()
     copies = []
 
     def send(source, slot, rows, bit):
@@ -1274,34 +1255,10 @@
     z_low = send(x_ref, 2, low, ZL_BIT)
     x_low = send(x_ref, 1, low, X_BIT)
     z_top = send(x_ref, 2, top, ZL_BIT)
-    last = [send(x_ref, 4, None, C_BIT)]
-    x_top.wait_recv()
-    far_top = send(all_ref.at[1], 3, top, ZL_BIT)
-    z_low.wait_recv()
-    far_low = send(all_ref.at[2], 3, low, X_BIT)
-    x_low.wait_recv()
-    last.append(send(all_ref.at[1], 5, None, C_BIT))
-    z_top.wait_recv()
-    last.append(send(all_ref.at[2], 6, None, C_BIT))
-    far_top.wait_recv()
-    far_low.wait_recv()
-    last.append(send(all_ref.at[3], 7, None, C_BIT))
-    for copy in last:
-        copy.wait_recv()
-    for copy in copies:
-        copy.wait_send()
-    own.wait()
-
-
-def gather_kernel(x_ref, *refs):
-    blocks, maps_ref = refs[0:4], refs[4]
-    all_ref, other_ref, all_maps_ref = refs[5:8]
-    send_sem, recv_sem, more_send, more_recv, local_sem = refs[8:]
-    greet([peer_of(bit) for bit in GATHER_BITS])
-    pairs = [(block, other_ref.at[n], other_ref.at[4 + n]) for n, block in enumerate(blocks)]
-    pairs.append((maps_ref, all_maps_ref.at[pl.ds(0, 4)], all_maps_ref.at[pl.ds(4, 4)]))
-    copies = []
-    for n, (block, here, there) in enumerate(pairs):
+    pairs = [(maps_ref, all_maps_ref.at[pl.ds(4, 4)])]
+    pairs += [(block, other.at[n]) for n, block in enumerate(blocks)]
+    crossed = []
+    for n, (block, there) in enumerate(pairs):
         copy = pltpu.make_async_remote_copy(
             src_ref=block,
             dst_ref=there,
@@ -1311,28 +1268,120 @@
             device_id_type=MESH,
         )
         copy.start()
-        copies.append(copy)
-        copy = pltpu.make_async_copy(block, here, local_sem.at[1 + n])
-        copy.start()
-        copies.append(copy)
-    gather_steps(x_ref, all_ref, send_sem, recv_sem, local_sem.at[0])
-    for copy in copies:
-        copy.wait()
-
-
-def run_gather(values, blocks, maps):
-    shape = jax.ShapeDtypeStruct((8,) + values.shape, values.dtype)
+        crossed.append(copy)
+    cross_own = send(x_ref, 4, None, C_BIT)
+    all_maps_ref[0:4] = maps_ref[...]
+    column = lax.axis_index("expert")
+    experts = x_slots.shape[0]
+    rows = experts * SLOTS
+    depth = stage.shape[0]
+    stores = []
+
+    def own_rows(table):
+        picked = jnp.zeros((experts, table.shape[1]), F32)
+        for n in range(table.shape[0] // experts):
+            picked = jnp.where(column == n, table[n * experts : (n + 1) * experts], picked)
+        return picked
+
+    def put(source, values, target, pick):
+        side = len(stores) % depth
+        if len(stores) >= depth:
+            stores[-depth].wait()
+        for n in range(WIDTH // CHUNK):
+            cols = slice(n * CHUNK, (n + 1) * CHUNK)
+            got = dot_nn(pick, values[:, cols]).astype(BF)
+            stage[side, :, :, cols] = got.reshape(experts, SLOTS, CHUNK)
+        store = pltpu.make_async_copy(
+            stage.at[side], target.at[:, pl.ds(source * SLOTS, SLOTS)], store_sem.at[side]
+        )
+        store.start()
+        stores.append(store)
+
+    def put_g(source, values):
+        pick = one_hot(own_rows(all_maps_ref[source]), rows)
+        put(source, values, g_slots, pick.astype(BF))
+
+    def put_x(source, values):
+        slot_map = all_maps_ref[source]
+        chosen = slot_map >= 0.0
+        logits = dot_nt(wr_ref[...], values[...])[0 : slot_map.shape[0]]
+        logits = jnp.where(chosen, logits, MASKED)
+        raised = jnp.exp(logits - jnp.max(logits, axis=0, keepdims=True))
+        raised = jnp.where(chosen, raised, 0.0)
+        gates = own_rows(raised / jnp.sum(raised, axis=0, keepdims=True))
+        slots = own_rows(slot_map)
+        local_ref[source] = slots
+        pick = one_hot(slots, rows)
+        wide = jnp.broadcast_to(gates[:, None, :], (experts, SLOTS, gates.shape[1]))
+        of_rows = jnp.sum(pick * wide.reshape(rows, gates.shape[1]), axis=1, keepdims=True)
+        gates_ref[:, source * SLOTS : (source + 1) * SLOTS, :] = of_rows.reshape(experts, SLOTS, 1)
+        put(source, values, x_slots, pick.astype(BF))
+
+    put_x(0, x_ref)
+    put_g(0, blocks[0])
+    put_g(1, blocks[1])
+    x_top.wait_recv()
+    far_top = send(all_ref.at[1], 3, top, ZL_BIT)
+    z_low.wait_recv()
+    far_low = send(all_ref.at[2], 3, low, X_BIT)
+    put_g(2, blocks[2])
+    put_g(3, blocks[3])
+    for copy in crossed:
+        copy.wait_recv()
+    cross_own.wait_recv()
+    put_x(4, all_ref.at[4])
+    put_g(4, other.at[0])
+    x_low.wait_recv()
+    cross_x = send(all_ref.at[1], 5, None, C_BIT)
+    z_top.wait_recv()
+    cross_z = send(all_ref.at[2], 6, None, C_BIT)
+    put_x(1, all_ref.at[1])
+    put_x(2, all_ref.at[2])
+    put_g(5, other.at[1])
+    cross_x.wait_recv()
+    cross_z.wait_recv()
+    put_x(5, all_ref.at[5])
+    far_top.wait_recv()
+    far_low.wait_recv()
+    cross_far = send(all_ref.at[3], 7, None, C_BIT)
+    put_x(6, all_ref.at[6])
+    put_g(6, other.at[2])
+    put_g(7, other.at[3])
+    put_x(3, all_ref.at[3])
+    cross_far.wait_recv()
+    put_x(7, all_ref.at[7])
+    for store in stores[-depth:]:
+        store.wait()
+    for copy in copies + crossed:
+        copy.wait_send()
+
+
+def run_gather(values, blocks, maps, wr_t, experts):
+    vmem = pl.BlockSpec(memory_space=pltpu.VMEM)
+    tokens, width = values.shape
+    slots = jax.ShapeDtypeStruct((experts, 8 * SLOTS, width), values.dtype)
     return pl.pallas_call(
         gather_kernel,
-        in_specs=[pl.BlockSpec(memory_space=pltpu.VMEM)] * 6,
-        out_specs=(hbm,) * 3,
-        out_shape=(shape, shape, jax.ShapeDtypeStruct((8,) + maps.shape[1:], maps.dtype)),
-        scratch_shapes=[pltpu.SemaphoreType.DMA((n,)) for n in (10, 10, 5, 5, 6)],
+        in_specs=[vmem] * 7,
+        out_specs=(hbm, hbm, vmem, vmem),
+        out_shape=(
+            slots,
+            slots,
+            jax.ShapeDtypeStruct((experts, 8 * SLOTS, 1), F32),
+            jax.ShapeDtypeStruct((8, experts, tokens), F32),
+        ),
+        scratch_shapes=[
+            pltpu.VMEM((8, tokens, width), values.dtype),
+            pltpu.VMEM((4, tokens, width), values.dtype),
+            pltpu.VMEM((8,) + maps.shape[1:], maps.dtype),
+            pltpu.VMEM((4, experts, SLOTS, width), values.dtype),
+        ]
+        + [pltpu.SemaphoreType.DMA((n,)) for n in (10, 10, 5, 5, 4)],
         compiler_params=pltpu.CompilerParams(
             collective_id=1, has_side_effects=True, vmem_limit_bytes=60 * MIB
         ),
         cost_estimate=cost(0, 150e6),
-    )(values, *blocks, maps)
+    )(values, *blocks, maps, wr_t)
 
 
 def trade_peers(size):
@@ -1897,8 +1946,7 @@
         constant_values=-1.0,
     )
     wr_pad = jnp.pad(w_router, ((0, 0), (0, LANES - all_experts)))
-    wr_t = jnp.roll(w_router.T, -column * local_experts, axis=0)
-    wr_t = jnp.pad(wr_t, ((0, LANES - all_experts), (0, 0)))
+    wr_t = jnp.pad(w_router.T, ((0, LANES - all_experts), (0, 0)))
 
     half = HEAD_DIM // 2
     frequency = jnp.exp(-math.log(10000.0) * jnp.arange(half, dtype=F32) * 2.0 / HEAD_DIM)
@@ -1924,9 +1972,10 @@
     att = run_trade(out, 3)
     att, g_zx, maps = fence(att, g_zx, maps)
     middle, normed_two, att_full = run_mid(att, w_output, inputs, gain_mlp)
-    x_all, g_all, maps = run_gather(normed_two, (g_own, g_x, g_z, g_zx), maps)
-    maps = jnp.roll(maps, -column * local_experts, axis=1)
-    expert_args = (place, x_all, g_all, maps, wr_t, w_gate, w_up, w_down)
+    x_slots, g_slots, gates, maps = run_gather(
+        normed_two, (g_own, g_x, g_z, g_zx), maps, wr_t, local_experts
+    )
+    expert_args = (place, x_slots, g_slots, gates, maps, w_gate, w_up, w_down)
     first = run_experts(*expert_args)
     gate_ka, gate_s0, gate_s1, up_ka, up_s0, up_s1, down_ka, down_s0, down_s1 = first[4:]
     down_ya = swap_bit(down_s1, Y_BIT)

time: 699 us -> 679 us (0.971)
  Pallas kernels: 613 us -> 593 us
    pallas_call x2, Pallas kernels: 114 us -> 86.5 us  [run_experts(): pl.pallas_call(functools.partial(expert_kernel, first=not prior), grid_sp...]
    pallas_call x1, Pallas kernels: 39.3 us -> 47.7 us  [run_gather(): pl.pallas_call(gather_kernel, in_specs=[vmem] * 7, out_specs=(hbm, hbm, v...]
where the time goes in v6:
time: 679 us; the launch traced here: 672 us
  Pallas kernels  593 us (87%)
  other arithmetic  23.5 us (3%)
  starting transfers between devices  23.1 us (3%)
  local copies, waits for them, and re-layouts  20 us (3%)
  waiting for transfers between devices  10.3 us (2%)
    pallas_call x3, Pallas kernels, run_trade(): pl.pallas_call(functools.partial(trade_kernel, plans=tuple((rider.plan()...  157 us
    pallas_call x2, Pallas kernels, run_reduce(): pl.pallas_call(functools.partial(reduce_kernel, jobs=jobs, plans=tuple((r...  135 us
    pallas_call x2, Pallas kernels, run_experts(): pl.pallas_call(functools.partial(expert_kernel, first=not prior), grid_sp...  86.5 us
    pallas_call x1, Pallas kernels, run_gather(): pl.pallas_call(gather_kernel, in_specs=[vmem] * 7, out_specs=(hbm, hbm, v...  47.7 us
    pallas_call x1, Pallas kernels, run_first(): pl.pallas_call(functools.partial(first_kernel, far=far), in_specs=[hbm, v...  43.8 us
    pallas_call x1, Pallas kernels, run_backward(): pl.pallas_call(backward_kernel, grid=(blocks,), in_specs=[pl.BlockSpec(pa...  43.1 us
    pallas_call x1, Pallas kernels, run_forward(): pl.pallas_call(forward_kernel, grid=(blocks,), in_specs=[pl.BlockSpec(pac...  30.4 us
    ppermute x17, starting transfers between devices, swap(): return lax.ppermute(values, axis, [(i, i ^ mask) for i in range(size)])  23.1 us
  transfers between devices with their start and end apart: 17, of which 1 were waited for; matrix products, arithmetic and copies ran while one was open for 4% of the time, Pallas kernels for 51%

profile of v6, /device:TPU:0, one launch (start us, length us, event | category | flops | bytes accessed | tf_op | source)
XLA Modules:
  0.0 671.6 jit_solution(2713907809997897468)
XLA Ops:
  3.7 9.1 %shard_map.229 = (bf16[320,1536]{1,0:T(8,128)(2,1)}, bf16[8,800,128]{2,1,0:T(8,128)(2,1)}, bf16[320,1536]{1,0:T(8,128)(2,1)}) custom-call(f32[320,1536]{1,0:T(8,128)} %bitcast.78, f32[1,1536]{1,0:T(1,128)} %broadcast_in_dim.44.gain_ref.refs_6_, bf16[1536,1536]{1,0:T(8,128)(2,1)} %refs_9_.1, bf16[1536,512]{1,0:T(8,128)(2,1)} %refs_10_.1, ...), custom_call_target="tpu_custom_call" | custom-call | flops 2516582400 | bytes 14000000 | tf_op jit(solution)/shard_map/pallas_call | solution.py:487
  12.7 2.9 collective-permute-start
  17.0 43.8 %shard_map.230 = (bf16[8,800,128]{2,1,0:T(8,128)(2,1)}, f32[40,320]{1,0:T(8,128)}) custom-call(bf16[8,800,128]{2,1,0:T(8,128)(2,1)} %get-tuple-element.136.a_ref, f32[40,320]{1,0:T(8,128)} %copy-done.23, f32[320,40]{1,0:T(8,128)} %bitcast.90), custom_call_target="tpu_custom_call" | custom-call | bytes 170000000 | tf_op jit(solution)/shard_map/pallas_call | solution.py:1648
  61.5 30.4 %shard_map.231 = (bf16[8,480,128]{2,1,0:T(8,128)(2,1)}, f32[10,64,768]{2,1,0:T(8,128)}, f32[10,1,768]{2,1,0:T(1,128)}) custom-call(bf16[8,800,128]{2,1,0:T(8,128)(2,1)} %get-tuple-element.140.pack_ref), custom_call_target="tpu_custom_call" | custom-call | flops 10066329600 | bytes 6000000 | tf_op jit(solution)/shard_map/pallas_call | solution.py:602
  99.7 1.9 collective-permute-start.4
  101.6 24.0 %shard_map.232.att_ref = bf16[8,480,128]{2,1,0:T(8,128)(2,1)} custom-call(bf16[8,480,128]{2,1,0:T(8,128)(2,1)} %get-tuple-element.144.refs_0_), custom_call_target="tpu_custom_call" | custom-call | bytes 170000000 | tf_op jit(solution)/shard_map/pallas_call | solution.py:1614
  127.2 7.4 %shard_map.233 = (f32[320,1536]{1,0:T(8,128)}, bf16[320,1536]{1,0:T(8,128)(2,1)}, bf16[320,1536]{1,0:T(8,128)(2,1)}) custom-call(bf16[8,480,128]{2,1,0:T(8,128)(2,1)} %shard_map.232.att_ref, bf16[1536,1536]{1,0:T(8,128)(2,1)} %wo_ref.3, f32[320,1536]{1,0:T(8,128)} %bitcast.79, f32[1,1536]{1,0:T(1,128)} %broadcast_in_dim.48.gain_ref), custom_call_target="tpu_custom_call" | custom-call | flops 1509949440 | bytes 12000000 | tf_op jit(solution)/shard_map/pallas_call | solution.py:761
  134.6 47.7 %shard_map.234 = (bf16[10,512,1536]{2,1,0:T(8,128)(2,1)}, bf16[10,512,1536]{2,1,0:T(8,128)(2,1)}, f32[10,512,1]{2,1,0:T(8,128)}, f32[8,10,320]{2,1,0:T(8,128)}) custom-call(bf16[320,1536]{1,0:T(8,128)(2,1)} %get-tuple-element.148.x_ref.norm_ref.refs_14_, bf16[320,1536]{1,0:T(8,128)(2,1)} %get-tuple-element.142.refs_0_, bf16[320,1536]{1,0:T(8,128)(2,1)} %copy-done.16, ...), custom_call_target="tpu_custom_call" | custom-call | bytes 150000000 | tf_op jit(solution)/shard_map/pallas_call | solution.py:1363
  182.3 42.1 %shard_map.235 = (bf16[4,320,1536]{2,1,0:T(8,128)(2,1)}, bf16[4,320,1536]{2,1,0:T(8,128)(2,1)}, bf16[4,320,1664]{2,1,0:T(8,128)(2,1)}, bf16[4,320,1664]{2,1,0:T(...) custom-call(s32[6]{0:T(128)} %stack.43.place_ref, ...), custom_call_target="tpu_custom_call" | custom-call | flops 30000001024 | bytes 60000000 | tf_op jit(solution)/shard_map/pallas_call | solution.py:971
  232.4 44.4 %shard_map.236 = (bf16[4,320,1536]{2,1,0:T(8,128)(2,1)}, bf16[4,320,1536]{2,1,0:T(8,128)(2,1)}, bf16[4,320,1664]{2,1,0:T(8,128)(2,1)}, bf16[4,320,1664]{2,1,0:T(...) custom-call(s32[6]{0:T(128)} %stack.43.place_ref, ...), custom_call_target="tpu_custom_call" | custom-call | flops 30000001024 | bytes 60000000 | tf_op jit(solution)/shard_map/pallas_call | solution.py:971
  278.3 64.0 %shard_map.237 = (f32[320,1664]{1,0:T(8,128)}, bf16[2,5,192,256]{3,2,1,0:T(8,128)(2,1)}, bf16[2,5,192,256]{3,2,1,0:T(8,128)(2,1)}, bf16[4,320,1536]{2,1,0:T(8,128)(2,1)}, bf16[5,64,1536]{2,1,0:T(8,128)(2,1)}) custom-call(bf16[4,320,1664]{2,1,0:T(8,128)(2,1)} %get-tuple-element.160.refs_0_, bf16[4,320,1664]{2,1,0:T(8,128)(2,1)} %get-tuple-element.165.refs_1_, ...), custom_call_target="tpu_custom_call" | custom-call | bytes 170000000 | tf_op jit(solution)/shard_map/pallas_call | solution.py:1811
  344.2 4.2 collective-permute-start.9
  348.5 2.5 multiply_sine_fusion
  351.0 9.3 %shard_map.238 = (bf16[8,480,128]{2,1,0:T(8,128)(2,1)}, f32[320,1536]{1,0:T(8,128)}, bf16[320,1536]{1,0:T(8,128)(2,1)}, bf16[320,128]{1,0:T(8,128)(2,1)}, f32[1,1536]{1,0:T(1,128)}) custom-call(f32[320,1664]{1,0:T(8,128)} %get-tuple-element.176.dx_ref, f32[320,1536]{1,0:T(8,128)} %get-tuple-element.177.mid_ref, f32[320,1536]{1,0:T(8,128)} %bitcast.82, ...), custom_call_target="tpu_custom_call" | custom-call | flops 1509949440 | bytes 14000000 | tf_op jit(solution)/shard_map/pallas_call | solution.py:1061
  360.3 10.2 %collective-permute-done.9.refs_2_ = bf16[5,192,256]{2,1,0:T(8,128)(2,1)S(1)} collective-permute-done((bf16[5,192,256]{2,1,0:T(8,128)(2,1)S(1)}, bf16[5,192,256]{2,1,0:T(8,128)(2,1)S(1)}, u32[]{:S(2)}, u32[]{:S(2)}) %collective-permute-start.9) | collective-permute-done | bytes 491552 | tf_op jit(solution)/shard_map/ppermute | solution.py:413
  370.5 51.3 %shard_map.239 = (bf16[8,480,128]{2,1,0:T(8,128)(2,1)}, bf16[2,5,192,256]{3,2,1,0:T(8,128)(2,1)}, bf16[5,192,256]{2,1,0:T(8,128)(2,1)}, bf16[5,192,256]{2,1,0:T(...) custom-call(bf16[8,480,128]{2,1,0:T(8,128)(2,1)} %get-tuple-element.181.ref, ...), custom_call_target="tpu_custom_call" | custom-call | bytes 170000000 | tf_op jit(solution)/shard_map/pallas_call | solution.py:1614
  427.3 43.1 %shard_map.240.refs_0_ = bf16[8,800,128]{2,1,0:T(8,128)(2,1)} custom-call(bf16[8,800,128]{2,1,0:T(8,128)(2,1)} %get-tuple-element.140.pack_ref, bf16[8,480,128]{2,1,0:T(8,128)(2,1)} %get-tuple-element.190.grad_ref, f32[10,64,768]{2,1,0:T(8,128)} %get-tuple-element.191.out_t_ref, f32[10,1,768]{2,1,0:T(1,128)} %get-tuple-element.192.lse_ref, ...), custom_call_target="tpu_custom_call" | custom-call | flops 25165824000 | bytes 8000000 | tf_op jit(solution)/shard_map/pallas_call | solution.py:723
  472.1 81.5 %shard_map.241 = (bf16[8,800,128]{2,1,0:T(8,128)(2,1)}, bf16[2,5,192,256]{3,2,1,0:T(8,128)(2,1)}, bf16[2,5,192,256]{3,2,1,0:T(8,128)(2,1)}, bf16[5,192,256]{2,1,...) custom-call(bf16[8,800,128]{2,1,0:T(8,128)(2,1)} %shard_map.240.refs, ...), custom_call_target="tpu_custom_call" | custom-call | bytes 170000000 | tf_op jit(solution)/shard_map/pallas_call | solution.py:1614
  553.7 2.2 fusion
  557.4 2.0 collective-permute-start.14
  565.3 11.9 %shard_map.242 = (bf16[320,2560]{1,0:T(8,128)(2,1)}, bf16[16,48,2560]{2,1,0:T(8,128)(2,1)}, bf16[16,48,2560]{2,1,0:T(8,128)(2,1)}) custom-call(s32[6]{0:T(128)} %stack.43.place_ref, bf16[320,1536]{1,0:T(8,128)(2,1)} %get-tuple-element.135.a_ref, bf16[8,800,128]{2,1,0:T(8,128)(2,1)} %get-tuple-element.217.d_ref), custom_call_target="tpu_custom_call" | custom-call | flops 2516582400 | bytes 12000000 | tf_op jit(solution)/shard_map/pallas_call | solution.py:1115
  577.2 3.7 fusion.2
  580.9 71.3 %shard_map.243 = (f32[320,1536]{1,0:T(8,128)}, f32[48,1536]{1,0:T(8,128)}, f32[48,512]{1,0:T(8,128)}, f32[48,512]{1,0:T(8,128)}, f32[48,1536]{1,0:T(8,128)}, /*i...) custom-call(bf16[16,48,2560]{2,1,0:T(8,128)(2,1)} %get-tuple-element.222.refs_0_, ...), custom_call_target="tpu_custom_call" | custom-call | bytes 170000000 | tf_op jit(solution)/shard_map/pallas_call | solution.py:1811
  655.2 12.2 %shard_map.244 = (f32[2,5,192,512]{3,2,1,0:T(8,128)}, f32[2,5,192,512]{3,2,1,0:T(8,128)}, f32[2,5,64,1536]{3,2,1,0:T(8,128)}) custom-call(s32[6]{0:T(128)} %stack.43.place_ref, bf16[2,2,5,192,256]{4,3,2,1,0:T(8,128)(2,1)} %get-tuple-element.164.refs_4_.refs_0_, bf16[2,5,192,256]{3,2,1,0:T(8,128)(2,1)} %get-tuple-element.185.refs_6_.refs_1_, ...), custom_call_target="tpu_custom_call" | custom-call | flops 1000000 | bytes 26000000 | tf_op jit(solution)/shard_map/pallas_call | solution.py:1885
  (142 shorter events, 47.2 us)
Async XLA Ops:
  12.7 48.0 %copy-start.15 = (bf16[320,1536]{1,0:T(8,128)(2,1)S(1)}, bf16[320,1536]{1,0:T(8,128)(2,1)}, u32[]{:S(2)}) copy-start(bf16[320,1536]{1,0:T(8,128)(2,1)} %get-tuple-element.142.refs_0_) | copy-start | bytes 2949124
  12.7 79.8 %collective-permute-start = (bf16[320,1536]{1,0:T(8,128)(2,1)}, bf16[320,1536]{1,0:T(8,128)(2,1)S(1)}, u32[]{:S(2)}, u32[]{:S(2)}) collective-permute-start(bf16[320,1536]{1,0:T(8,128)(2,1)} %get-tuple-element.142.refs_0_), channel_id=1, source_target_pairs={{0,2},{1,3},{2,0},{3,1},{4,6},{5,7},{6,4},{7,5},{8,10},{9,11},{10,... | collective-permute-start | bytes 2949128 | tf_op jit(solution)/shard_map/ppermute | solution.py:413
  60.8 31.8 %collective-permute-start.1 = (bf16[320,1536]{1,0:T(8,128)(2,1)S(1)}, bf16[320,1536]{1,0:T(8,128)(2,1)S(1)}, u32[]{:S(2)}, u32[]{:S(2)}) collective-permute-start(bf16[320,1536]{1,0:T(8,128)(2,1)S(1)} %copy-done.15), channel_id=1, source_target_pairs={{0,8},{4,12},{8,0},{12,4},{16,24},{20,28},{24,16},{28,20},{1,9},{5... | collective-permute-start | bytes 2949128 | tf_op jit(solution)/shard_map/ppermute | solution.py:413
  60.9 31.0 %collective-permute-start.2 = (f32[1,40,320]{2,1,0:T(8,128)}, f32[1,40,320]{2,1,0:T(8,128)S(1)}, u32[]{:S(2)}, u32[]{:S(2)}) collective-permute-start(f32[1,40,320]{2,1,0:T(8,128)} %bitcast.94), channel_id=1, source_target_pairs={{0,2},{1,3},{2,0},{3,1},{4,6},{5,7},{6,4},{7,5},{8,10},{9,11},{10,... | collective-permute-start | bytes 153608 | tf_op jit(solution)/shard_map/ppermute | solution.py:413
  92.6 34.6 %collective-permute-start.3 = (bf16[320,1536]{1,0:T(8,128)(2,1)S(1)}, bf16[320,1536]{1,0:T(8,128)(2,1)S(1)}, u32[]{:S(2)}, u32[]{:S(2)}) collective-permute-start(bf16[320,1536]{1,0:T(8,128)(2,1)S(1)} %collective-permute-done.1.refs_2_), channel_id=1, source_target_pairs={{0,2},{1,3},{2,0},{3,1},{4,6},{5,7},{6,4},{7,5},{8,10},{9,11},{10,... | collective-permute-start | bytes 2949128 | tf_op jit(solution)/shard_map/ppermute | solution.py:413
  99.7 25.9 %collective-permute-start.4 = (f32[2,40,320]{2,1,0:T(8,128)}, f32[2,40,320]{2,1,0:T(8,128)S(1)}, u32[]{:S(2)}, u32[]{:S(2)}) collective-permute-start(f32[2,40,320]{2,1,0:T(8,128)} %pad_maximum_fusion.7), channel_id=1, source_target_pairs={{0,8},{4,12},{8,0},{12,4},{16,24},{20,28},{24,16},{28,20},{1,9},{5... | collective-permute-start | bytes 307208 | tf_op jit(solution)/shard_map/ppermute | solution.py:413
  224.4 52.5 %collective-permute-start.6 = (bf16[2,5,192,256]{3,2,1,0:T(8,128)(2,1)}, bf16[2,5,192,256]{3,2,1,0:T(8,128)(2,1)}, u32[]{:S(2)}, u32[]{:S(2)}) collective-permute-start(bf16[2,5,192,256]{3,2,1,0:T(8,128)(2,1)} %get-tuple-element.163), channel_id=1, source_target_pairs={{0,4},{4,0},{8,12},{12,8},{16,20},{20,16},{24,28},{28,24},{1,5},{5... | collective-permute-start | bytes 2949128 | tf_op jit(solution)/shard_map/ppermute | solution.py:413
  227.0 49.9 %collective-permute-start.5 = (bf16[5,64,1536]{2,1,0:T(8,128)(2,1)}, bf16[5,64,1536]{2,1,0:T(8,128)(2,1)S(1)}, u32[]{:S(2)}, u32[]{:S(2)}) collective-permute-start(bf16[5,64,1536]{2,1,0:T(8,128)(2,1)} %get-tuple-element.162), channel_id=1, source_target_pairs={{0,4},{4,0},{8,12},{12,8},{16,20},{20,16},{24,28},{28,24},{1,5},{5... | collective-permute-start | bytes 2949128 | tf_op jit(solution)/shard_map/ppermute | solution.py:413
  229.8 47.2 %collective-permute-start.7 = (bf16[2,5,192,256]{3,2,1,0:T(8,128)(2,1)}, bf16[2,5,192,256]{3,2,1,0:T(8,128)(2,1)S(1)}, u32[]{:S(2)}, u32[]{:S(2)}) collective-permute-start(bf16[2,5,192,256]{3,2,1,0:T(8,128)(2,1)} %pad_maximum_fusion), channel_id=1, source_target_pairs={{0,16},{4,20},{8,24},{12,28},{16,0},{20,4},{24,8},{28,12},{1,17},{... | collective-permute-start | bytes 2949128 | tf_op jit(solution)/shard_map/ppermute | solution.py:413
  231.0 111.3 %collective-permute-start.8 = (bf16[5,64,1536]{2,1,0:T(8,128)(2,1)}, bf16[5,64,1536]{2,1,0:T(8,128)(2,1)S(1)}, u32[]{:S(2)}, u32[]{:S(2)}) collective-permute-start(bf16[5,64,1536]{2,1,0:T(8,128)(2,1)} %get-tuple-element.174), channel_id=1, source_target_pairs={{0,4},{4,0},{8,12},{12,8},{16,20},{20,16},{24,28},{28,24},{1,5},{5... | collective-permute-start | bytes 2949128 | tf_op jit(solution)/shard_map/ppermute | solution.py:413
  276.9 65.3 %copy-start.5 = (bf16[2,5,192,256]{3,2,1,0:T(8,128)(2,1)}, bf16[2,5,192,256]{3,2,1,0:T(8,128)(2,1)S(1)}, u32[]{:S(2)}) copy-start(bf16[2,5,192,256]{3,2,1,0:T(8,128)(2,1)S(1)} %collective-permute-done.7.refs_5_) | copy-start | bytes 2949124
  278.3 64.0 %copy-start.34 = (bf16[2,5,192,256]{3,2,1,0:T(8,128)(2,1)S(1)}, bf16[2,5,192,256]{3,2,1,0:T(8,128)(2,1)}, u32[]{:S(2)}) copy-start(bf16[2,5,192,256]{3,2,1,0:T(8,128)(2,1)} %get-tuple-element.180) | copy-start | bytes 2949124
  342.3 28.2 %collective-permute-start.10 = (bf16[2,5,192,256]{3,2,1,0:T(8,128)(2,1)S(1)}, bf16[2,5,192,256]{3,2,1,0:T(8,128)(2,1)S(1)}, u32[]{:S(2)}, u32[]{:S(2)}) collective-permute-start(bf16[2,5,192,256]{3,2,1,0:T(8,128)(2,1)S(1)} %copy-done.34), channel_id=1, source_target_pairs={{0,4},{4,0},{8,12},{12,8},{16,20},{20,16},{24,28},{28,24},{1,5},{5... | collective-permute-start | bytes 2949128 | tf_op jit(solution)/shard_map/ppermute | solution.py:413
  344.2 26.3 %collective-permute-start.9 = (bf16[5,192,256]{2,1,0:T(8,128)(2,1)S(1)}, bf16[5,192,256]{2,1,0:T(8,128)(2,1)S(1)}, u32[]{:S(2)}, u32[]{:S(2)}) collective-permute-start(bf16[5,192,256]{2,1,0:T(8,128)(2,1)S(1)} %fusion.9), channel_id=1, source_target_pairs={{0,16},{4,20},{8,24},{12,28},{16,0},{20,4},{24,8},{28,12},{1,17},{... | collective-permute-start | bytes 1474568 | tf_op jit(solution)/shard_map/ppermute | solution.py:413
  370.5 51.3 %copy-start.24 = (bf16[5,192,256]{2,1,0:T(8,128)(2,1)}, bf16[5,192,256]{2,1,0:T(8,128)(2,1)S(1)}, u32[]{:S(2)}) copy-start(bf16[5,192,256]{2,1,0:T(8,128)(2,1)S(1)} %collective-permute-done.9.refs_2_) | copy-start | bytes 1474564
  370.5 52.4 %copy-start.11 = (bf16[2,5,192,256]{3,2,1,0:T(8,128)(2,1)}, bf16[2,5,192,256]{3,2,1,0:T(8,128)(2,1)S(1)}, u32[]{:S(2)}) copy-start(bf16[2,5,192,256]{3,2,1,0:T(8,128)(2,1)S(1)} %collective-permute-done.10.refs_4_) | copy-start | bytes 2949124
  370.5 51.3 %copy-start.6 = (bf16[2,5,192,256]{3,2,1,0:T(8,128)(2,1)S(1)}, bf16[2,5,192,256]{3,2,1,0:T(8,128)(2,1)}, u32[]{:S(2)}) copy-start(bf16[2,5,192,256]{3,2,1,0:T(8,128)(2,1)} %get-tuple-element.196.refs_3_) | copy-start | bytes 2949124
  424.2 46.2 %collective-permute-start.11 = (bf16[2,5,192,256]{3,2,1,0:T(8,128)(2,1)S(1)}, bf16[2,5,192,256]{3,2,1,0:T(8,128)(2,1)S(1)}, u32[]{:S(2)}, u32[]{:S(2)}) collective-permute-start(bf16[2,5,192,256]{3,2,1,0:T(8,128)(2,1)S(1)} %pad_maximum_fusion.2), channel_id=1, source_target_pairs={{0,16},{4,20},{8,24},{12,28},{16,0},{20,4},{24,8},{28,12},{1,17},{... | collective-permute-start | bytes 2949128 | tf_op jit(solution)/shard_map/ppermute | solution.py:413
  425.3 45.1 %collective-permute-start.12 = (bf16[2,5,192,256]{3,2,1,0:T(8,128)(2,1)}, bf16[2,5,192,256]{3,2,1,0:T(8,128)(2,1)S(1)}, u32[]{:S(2)}, u32[]{:S(2)}) collective-permute-start(bf16[2,5,192,256]{3,2,1,0:T(8,128)(2,1)} %get-tuple-element.199), channel_id=1, source_target_pairs={{0,4},{4,0},{8,12},{12,8},{16,20},{20,16},{24,28},{28,24},{1,5},{5... | collective-permute-start | bytes 2949128 | tf_op jit(solution)/shard_map/ppermute | solution.py:413
  426.2 44.2 %collective-permute-start.13 = (bf16[5,64,1536]{2,1,0:T(8,128)(2,1)}, bf16[5,64,1536]{2,1,0:T(8,128)(2,1)S(1)}, u32[]{:S(2)}, u32[]{:S(2)}) collective-permute-start(bf16[5,64,1536]{2,1,0:T(8,128)(2,1)} %get-tuple-element.200), channel_id=1, source_target_pairs={{0,4},{4,0},{8,12},{12,8},{16,20},{20,16},{24,28},{28,24},{1,5},{5... | collective-permute-start | bytes 2949128 | tf_op jit(solution)/shard_map/ppermute | solution.py:413
  472.1 81.6 %copy-start.1 = (bf16[16,48,1536]{2,1,0:T(8,128)(2,1)S(1)}, bf16[16,48,1536]{2,1,0:T(8,128)(2,1)}, u32[]{:S(2)}) copy-start(bf16[16,48,1536]{2,1,0:T(8,128)(2,1)} %get-tuple-element.207) | copy-start | bytes 7077892
  557.4 94.8 %collective-permute-start.14 = (bf16[5,64,1536]{2,1,0:T(8,128)(2,1)}, bf16[5,64,1536]{2,1,0:T(8,128)(2,1)}, u32[]{:S(2)}, u32[]{:S(2)}) collective-permute-start(bf16[5,64,1536]{2,1,0:T(8,128)(2,1)} %fusion.1), channel_id=1, source_target_pairs={{0,16},{4,20},{8,24},{12,28},{16,0},{20,4},{24,8},{28,12},{1,17},{... | collective-permute-start | bytes 2949128 | tf_op jit(solution)/shard_map/ppermute | solution.py:413
  559.4 92.8 %collective-permute-start.15 = (bf16[5,64,1536]{2,1,0:T(8,128)(2,1)}, bf16[5,64,1536]{2,1,0:T(8,128)(2,1)}, u32[]{:S(2)}, u32[]{:S(2)}) collective-permute-start(bf16[5,64,1536]{2,1,0:T(8,128)(2,1)} %get-tuple-element.235), channel_id=1, source_target_pairs={{0,4},{4,0},{8,12},{12,8},{16,20},{20,16},{24,28},{28,24},{1,5},{5... | collective-permute-start | bytes 2949128 | tf_op jit(solution)/shard_map/ppermute | solution.py:413
  563.6 88.6 %collective-permute-start.16 = (bf16[2,5,192,256]{3,2,1,0:T(8,128)(2,1)}, bf16[2,5,192,256]{3,2,1,0:T(8,128)(2,1)}, u32[]{:S(2)}, u32[]{:S(2)}) collective-permute-start(bf16[2,5,192,256]{3,2,1,0:T(8,128)(2,1)} %pad_maximum_fusion.3), channel_id=1, source_target_pairs={{0,8},{4,12},{8,0},{12,4},{16,24},{20,28},{24,16},{28,20},{1,9},{5... | collective-permute-start | bytes 2949128 | tf_op jit(solution)/shard_map/ppermute | solution.py:413
  (28 other events, 306.1 us)

commit v7 on v6

--- a/solution.py
+++ b/solution.py
@@ -798,6 +798,7 @@
     gate_keep,
     gate_send0,
     gate_send1,
+    early,
     up_keep,
     up_send0,
     up_send1,
@@ -873,6 +874,8 @@
             cols = slice(n * CHUNK, (n + 1) * CHUNK)
             tall_s[cols, :] = dot_tn(x[:, cols], d_gate).astype(BF)
         spread(gate_keep, (gate_send0, gate_send1))
+        early[0, 0] = gate_keep[1, 1, 0]
+        early[1, 0] = gate_send1[1, 0]
         for n in range(count):
             cols = slice(n * CHUNK, (n + 1) * CHUNK)
             tall_s[cols, :] = dot_tn(x[:, cols], d_up).astype(BF)
@@ -991,6 +994,7 @@
                 tall_spec,
                 tall_half,
                 tall_half,
+                tall_half,
                 tall_spec,
                 tall_half,
                 tall_half,
@@ -1007,7 +1011,8 @@
             ],
         ),
         out_shape=(mixed, mixed, d_x, d_x)
-        + (tall, less(tall), less(tall)) * 2
+        + (tall, less(tall), less(tall), less(tall))
+        + (tall, less(tall), less(tall))
         + (wide, less(wide), less(wide)),
         compiler_params=params(60, ("arbitrary",)),
         cost_estimate=cost(30e9, 60e6),
@@ -1977,12 +1982,12 @@
     )
     expert_args = (place, x_slots, g_slots, gates, maps, w_gate, w_up, w_down)
     first = run_experts(*expert_args)
-    gate_ka, gate_s0, gate_s1, up_ka, up_s0, up_s1, down_ka, down_s0, down_s1 = first[4:]
+    gate_ka, gate_s0, gate_s1, early, up_ka, up_s0, up_s1, down_ka, down_s0, down_s1 = first[4:]
     down_ya = swap_bit(down_s1, Y_BIT)
     gate_ya = swap_bit(gate_s1, Y_BIT)
-    early = swap_bit(jnp.stack([gate_ka[1, 1], gate_s1[1]]), ZH_BIT)
+    early = swap_bit(early, ZH_BIT)
     mix_keep, mix_send, dx_keep, dx_send, *second = run_experts(*expert_args, prior=first[:4])
-    gate_kb, gate_t0, gate_t1, up_kb, up_t0, up_t1, down_kb, down_t0, down_t1 = second
+    gate_kb, gate_t0, gate_t1, _, up_kb, up_t0, up_t1, down_kb, down_t0, down_t1 = second
     down_ga = swap_bit(down_s0, Y_BIT)
     dx_send, down_ya, gate_ya, early = fence(dx_send, down_ya, gate_ya, early)
     gate_s0 = jnp.stack([gate_s0[0], add_low(gate_s0[1], early[1])])
@@ -2008,7 +2013,6 @@
     d_att, d_middle, d_low, d_log, ggain_mlp = run_post(
         dx_sum, middle, cotangent, normed_two, wr_pad, map_rows, gain_mlp, w_output
     )
-    d_att, gate_ma, gate_yb = fence(d_att, gate_ma, gate_yb)
     mix_keep = mix_keep.reshape(2, 2, tokens, WIDTH)
     mix_got = mix_got.reshape(2, 2, tokens, WIDTH)
     every = slice(None)
@@ -2026,7 +2030,9 @@
     )
     split = (8, 2, WIDTH // devices, WIDTH)
     out_keep, out_got = out_keep.reshape(split), out_got.reshape(split)
-    up_ga, down_yb, up_late, gate_late, _ = fence(up_s0, down_t1, up_ya, gate_yb, d_out)
+    up_ga, down_yb, up_late, gate_late, gate_ma, d_out = fence(
+        up_s0, down_t1, up_ya, gate_yb, gate_ma, d_out
+    )
     both = jnp.stack([add_low(up_ka[1, 0], up_late[0]), add_low(gate_kb[1, 1], gate_late[1])])
     both = swap_bit(both, ZH_BIT)
     up_ga = swap_bit(up_ga, Y_BIT)

time: 679 us -> 670 us (0.987)
  waiting for transfers between devices: 10.3 us -> 0.04 us
    ppermute x17, waiting for transfers between devices: 10.3 us -> 0.04 us  [swap(): return lax.ppermute(values, axis, [(i, i ^ mask) for i in range(size)])]
  transfers between devices with their start and end apart: 17 -> 17, of which waited for: 1 -> 0; matrix products, arithmetic and copies ran while one was open for 4% -> 3% of each run, Pallas kernels for 51% -> 60%
where the time goes in v7:
time: 670 us; the launch traced here: 662 us
  Pallas kernels  598 us (89%)
  other arithmetic  22.8 us (3%)
  starting transfers between devices  22 us (3%)
  local copies, waits for them, and re-layouts  17.9 us (3%)
    pallas_call x3, Pallas kernels, run_trade(): pl.pallas_call(functools.partial(trade_kernel, plans=tuple((rider.plan()...  161 us
    pallas_call x2, Pallas kernels, run_reduce(): pl.pallas_call(functools.partial(reduce_kernel, jobs=jobs, plans=tuple((r...  136 us
    pallas_call x2, Pallas kernels, run_experts(): pl.pallas_call(functools.partial(expert_kernel, first=not prior), grid_sp...  86.5 us
    pallas_call x1, Pallas kernels, run_gather(): pl.pallas_call(gather_kernel, in_specs=[vmem] * 7, out_specs=(hbm, hbm, v...  47.7 us
    pallas_call x1, Pallas kernels, run_first(): pl.pallas_call(functools.partial(first_kernel, far=far), in_specs=[hbm, v...  43.8 us
    pallas_call x1, Pallas kernels, run_backward(): pl.pallas_call(backward_kernel, grid=(blocks,), in_specs=[pl.BlockSpec(pa...  43.1 us
    pallas_call x1, Pallas kernels, run_forward(): pl.pallas_call(forward_kernel, grid=(blocks,), in_specs=[pl.BlockSpec(pac...  30.4 us
    ppermute x17, starting transfers between devices, swap(): return lax.ppermute(values, axis, [(i, i ^ mask) for i in range(size)])  22 us
  transfers between devices with their start and end apart: 17, of which 0 were waited for; matrix products, arithmetic and copies ran while one was open for 3% of the time, Pallas kernels for 60%

profile of v7, /device:TPU:0, one launch (start us, length us, event | category | flops | bytes accessed | tf_op | source)
XLA Modules:
  0.0 662.5 jit_solution(14022976908143271976)
XLA Ops:
  3.7 9.1 %shard_map.229 = (bf16[320,1536]{1,0:T(8,128)(2,1)}, bf16[8,800,128]{2,1,0:T(8,128)(2,1)}, bf16[320,1536]{1,0:T(8,128)(2,1)}) custom-call(f32[320,1536]{1,0:T(8,128)} %bitcast.76, f32[1,1536]{1,0:T(1,128)} %broadcast_in_dim.44.gain_ref.refs_6_, bf16[1536,1536]{1,0:T(8,128)(2,1)} %refs_9_.1, bf16[1536,512]{1,0:T(8,128)(2,1)} %refs_10_.1, ...), custom_call_target="tpu_custom_call" | custom-call | flops 2516582400 | bytes 14000000 | tf_op jit(solution)/shard_map/pallas_call | solution.py:487
  12.7 2.9 collective-permute-start
  17.0 43.8 %shard_map.230 = (bf16[8,800,128]{2,1,0:T(8,128)(2,1)}, f32[40,320]{1,0:T(8,128)}) custom-call(bf16[8,800,128]{2,1,0:T(8,128)(2,1)} %get-tuple-element.136.a_ref, f32[40,320]{1,0:T(8,128)} %copy-done.23, f32[320,40]{1,0:T(8,128)} %bitcast.88), custom_call_target="tpu_custom_call" | custom-call | bytes 170000000 | tf_op jit(solution)/shard_map/pallas_call | solution.py:1653
  61.5 30.4 %shard_map.231 = (bf16[8,480,128]{2,1,0:T(8,128)(2,1)}, f32[10,64,768]{2,1,0:T(8,128)}, f32[10,1,768]{2,1,0:T(1,128)}) custom-call(bf16[8,800,128]{2,1,0:T(8,128)(2,1)} %get-tuple-element.140.pack_ref), custom_call_target="tpu_custom_call" | custom-call | flops 10066329600 | bytes 6000000 | tf_op jit(solution)/shard_map/pallas_call | solution.py:602
  95.9 1.7 pad.12.refs_5_
  99.7 1.9 collective-permute-start.4
  101.6 24.0 %shard_map.232.att_ref = bf16[8,480,128]{2,1,0:T(8,128)(2,1)} custom-call(bf16[8,480,128]{2,1,0:T(8,128)(2,1)} %get-tuple-element.144.refs_0_), custom_call_target="tpu_custom_call" | custom-call | bytes 170000000 | tf_op jit(solution)/shard_map/pallas_call | solution.py:1619
  127.2 7.4 %shard_map.233 = (f32[320,1536]{1,0:T(8,128)}, bf16[320,1536]{1,0:T(8,128)(2,1)}, bf16[320,1536]{1,0:T(8,128)(2,1)}) custom-call(bf16[8,480,128]{2,1,0:T(8,128)(2,1)} %shard_map.232.att_ref, bf16[1536,1536]{1,0:T(8,128)(2,1)} %wo_ref.3, f32[320,1536]{1,0:T(8,128)} %bitcast.77, f32[1,1536]{1,0:T(1,128)} %broadcast_in_dim.48.gain_ref), custom_call_target="tpu_custom_call" | custom-call | flops 1509949440 | bytes 12000000 | tf_op jit(solution)/shard_map/pallas_call | solution.py:761
  134.6 47.7 %shard_map.234 = (bf16[10,512,1536]{2,1,0:T(8,128)(2,1)}, bf16[10,512,1536]{2,1,0:T(8,128)(2,1)}, f32[10,512,1]{2,1,0:T(8,128)}, f32[8,10,320]{2,1,0:T(8,128)}) custom-call(bf16[320,1536]{1,0:T(8,128)(2,1)} %get-tuple-element.148.x_ref.norm_ref.refs_14_, bf16[320,1536]{1,0:T(8,128)(2,1)} %get-tuple-element.142.refs_0_, bf16[320,1536]{1,0:T(8,128)(2,1)} %copy-done.16, ...), custom_call_target="tpu_custom_call" | custom-call | bytes 150000000 | tf_op jit(solution)/shard_map/pallas_call | solution.py:1368
  182.3 42.1 %shard_map.235 = (bf16[4,320,1536]{2,1,0:T(8,128)(2,1)}, bf16[4,320,1536]{2,1,0:T(8,128)(2,1)}, bf16[4,320,1664]{2,1,0:T(8,128)(2,1)}, bf16[4,320,1664]{2,1,0:T(...) custom-call(s32[6]{0:T(128)} %stack.40.place_ref, ...), custom_call_target="tpu_custom_call" | custom-call | flops 30000001024 | bytes 60000000 | tf_op jit(solution)/shard_map/pallas_call | solution.py:974
  229.1 44.4 %shard_map.236 = (bf16[4,320,1536]{2,1,0:T(8,128)(2,1)}, bf16[4,320,1536]{2,1,0:T(8,128)(2,1)}, bf16[4,320,1664]{2,1,0:T(8,128)(2,1)}, bf16[4,320,1664]{2,1,0:T(...) custom-call(s32[6]{0:T(128)} %stack.40.place_ref, ...), custom_call_target="tpu_custom_call" | custom-call | flops 30000001024 | bytes 60000000 | tf_op jit(solution)/shard_map/pallas_call | solution.py:974
  275.0 63.9 %shard_map.237 = (f32[320,1664]{1,0:T(8,128)}, bf16[2,5,192,256]{3,2,1,0:T(8,128)(2,1)}, bf16[2,5,192,256]{3,2,1,0:T(8,128)(2,1)}, bf16[4,320,1536]{2,1,0:T(8,128)(2,1)}, bf16[5,64,1536]{2,1,0:T(8,128)(2,1)}) custom-call(bf16[4,320,1664]{2,1,0:T(8,128)(2,1)} %get-tuple-element.162.refs_0_, bf16[4,320,1664]{2,1,0:T(8,128)(2,1)} %get-tuple-element.167.refs_1_, ...), custom_call_target="tpu_custom_call" | custom-call | bytes 170000000 | tf_op jit(solution)/shard_map/pallas_call | solution.py:1816
  341.0 4.3 collective-permute-start.10
  345.2 2.4 multiply_sine_fusion
  347.7 9.3 %shard_map.238 = (bf16[8,480,128]{2,1,0:T(8,128)(2,1)}, f32[320,1536]{1,0:T(8,128)}, bf16[320,1536]{1,0:T(8,128)(2,1)}, bf16[320,128]{1,0:T(8,128)(2,1)}, f32[1,1536]{1,0:T(1,128)}) custom-call(f32[320,1664]{1,0:T(8,128)} %get-tuple-element.182.dx_ref, f32[320,1536]{1,0:T(8,128)} %get-tuple-element.183.mid_ref, f32[320,1536]{1,0:T(8,128)} %bitcast.80, ...), custom_call_target="tpu_custom_call" | custom-call | flops 1509949440 | bytes 14000000 | tf_op jit(solution)/shard_map/pallas_call | solution.py:1066
  357.0 54.4 %shard_map.239 = (bf16[8,480,128]{2,1,0:T(8,128)(2,1)}, bf16[2,5,192,256]{3,2,1,0:T(8,128)(2,1)}, bf16[5,192,256]{2,1,0:T(8,128)(2,1)}, bf16[5,192,256]{2,1,0:T(...) custom-call(bf16[8,480,128]{2,1,0:T(8,128)(2,1)} %get-tuple-element.184.ref, ...), custom_call_target="tpu_custom_call" | custom-call | bytes 170000000 | tf_op jit(solution)/shard_map/pallas_call | solution.py:1619
  416.4 43.1 %shard_map.240.refs_0_ = bf16[8,800,128]{2,1,0:T(8,128)(2,1)} custom-call(bf16[8,800,128]{2,1,0:T(8,128)(2,1)} %get-tuple-element.140.pack_ref, bf16[8,480,128]{2,1,0:T(8,128)(2,1)} %get-tuple-element.193.grad_ref, f32[10,64,768]{2,1,0:T(8,128)} %get-tuple-element.194.out_t_ref, f32[10,1,768]{2,1,0:T(1,128)} %get-tuple-element.195.lse_ref, ...), custom_call_target="tpu_custom_call" | custom-call | flops 25165824000 | bytes 8000000 | tf_op jit(solution)/shard_map/pallas_call | solution.py:723
  461.2 83.1 %shard_map.241 = (bf16[8,800,128]{2,1,0:T(8,128)(2,1)}, bf16[2,5,192,256]{3,2,1,0:T(8,128)(2,1)}, bf16[2,5,192,256]{3,2,1,0:T(8,128)(2,1)}, bf16[5,192,256]{2,1,...) custom-call(bf16[8,800,128]{2,1,0:T(8,128)(2,1)} %shard_map.240.refs, ...), custom_call_target="tpu_custom_call" | custom-call | bytes 170000000 | tf_op jit(solution)/shard_map/pallas_call | solution.py:1619
  544.3 2.2 fusion
  548.0 1.7 collective-permute-start.14
  555.8 11.9 %shard_map.242 = (bf16[320,2560]{1,0:T(8,128)(2,1)}, bf16[16,48,2560]{2,1,0:T(8,128)(2,1)}, bf16[16,48,2560]{2,1,0:T(8,128)(2,1)}) custom-call(s32[6]{0:T(128)} %stack.40.place_ref, bf16[320,1536]{1,0:T(8,128)(2,1)} %get-tuple-element.135.a_ref, bf16[8,800,128]{2,1,0:T(8,128)(2,1)} %get-tuple-element.217.d_ref), custom_call_target="tpu_custom_call" | custom-call | flops 2516582400 | bytes 12000000 | tf_op jit(solution)/shard_map/pallas_call | solution.py:1120
  567.8 3.7 fusion.2
  571.4 71.7 %shard_map.243 = (f32[320,1536]{1,0:T(8,128)}, f32[48,1536]{1,0:T(8,128)}, f32[48,512]{1,0:T(8,128)}, f32[48,512]{1,0:T(8,128)}, f32[48,1536]{1,0:T(8,128)}, /*i...) custom-call(bf16[16,48,2560]{2,1,0:T(8,128)(2,1)} %get-tuple-element.222.refs_0_, ...), custom_call_target="tpu_custom_call" | custom-call | bytes 170000000 | tf_op jit(solution)/shard_map/pallas_call | solution.py:1816
  646.1 12.2 %shard_map.244 = (f32[2,5,192,512]{3,2,1,0:T(8,128)}, f32[2,5,192,512]{3,2,1,0:T(8,128)}, f32[2,5,64,1536]{3,2,1,0:T(8,128)}) custom-call(s32[6]{0:T(128)} %stack.40.place_ref, bf16[2,2,5,192,256]{4,3,2,1,0:T(8,128)(2,1)} %get-tuple-element.180.refs_4_.refs_0_, bf16[2,5,192,256]{3,2,1,0:T(8,128)(2,1)} %get-tuple-element.187.refs_6_.refs_1_, ...), custom_call_target="tpu_custom_call" | custom-call | flops 1000000 | bytes 26000000 | tf_op jit(solution)/shard_map/pallas_call | solution.py:1890
  (139 shorter events, 41.9 us)
Async XLA Ops:
  12.7 48.0 %copy-start.15 = (bf16[320,1536]{1,0:T(8,128)(2,1)S(1)}, bf16[320,1536]{1,0:T(8,128)(2,1)}, u32[]{:S(2)}) copy-start(bf16[320,1536]{1,0:T(8,128)(2,1)} %get-tuple-element.142.refs_0_) | copy-start | bytes 2949124
  12.7 79.8 %collective-permute-start = (bf16[320,1536]{1,0:T(8,128)(2,1)}, bf16[320,1536]{1,0:T(8,128)(2,1)S(1)}, u32[]{:S(2)}, u32[]{:S(2)}) collective-permute-start(bf16[320,1536]{1,0:T(8,128)(2,1)} %get-tuple-element.142.refs_0_), channel_id=1, source_target_pairs={{0,2},{1,3},{2,0},{3,1},{4,6},{5,7},{6,4},{7,5},{8,10},{9,11},{10,... | collective-permute-start | bytes 2949128 | tf_op jit(solution)/shard_map/ppermute | solution.py:413
  60.8 31.8 %collective-permute-start.1 = (bf16[320,1536]{1,0:T(8,128)(2,1)S(1)}, bf16[320,1536]{1,0:T(8,128)(2,1)S(1)}, u32[]{:S(2)}, u32[]{:S(2)}) collective-permute-start(bf16[320,1536]{1,0:T(8,128)(2,1)S(1)} %copy-done.15), channel_id=1, source_target_pairs={{0,8},{4,12},{8,0},{12,4},{16,24},{20,28},{24,16},{28,20},{1,9},{5... | collective-permute-start | bytes 2949128 | tf_op jit(solution)/shard_map/ppermute | solution.py:413
  60.9 33.3 %copy-start.33 = (f32[1536]{0:T(1024)S(1)}, f32[1536]{0:T(1024)}, u32[]{:S(2)}) copy-start(f32[1536]{0:T(1024)} %param.20) | copy-start | bytes 18436
  60.9 31.0 %collective-permute-start.2 = (f32[1,40,320]{2,1,0:T(8,128)}, f32[1,40,320]{2,1,0:T(8,128)S(1)}, u32[]{:S(2)}, u32[]{:S(2)}) collective-permute-start(f32[1,40,320]{2,1,0:T(8,128)} %bitcast.92), channel_id=1, source_target_pairs={{0,2},{1,3},{2,0},{3,1},{4,6},{5,7},{6,4},{7,5},{8,10},{9,11},{10,... | collective-permute-start | bytes 153608 | tf_op jit(solution)/shard_map/ppermute | solution.py:413
  92.6 34.6 %collective-permute-start.3 = (bf16[320,1536]{1,0:T(8,128)(2,1)S(1)}, bf16[320,1536]{1,0:T(8,128)(2,1)S(1)}, u32[]{:S(2)}, u32[]{:S(2)}) collective-permute-start(bf16[320,1536]{1,0:T(8,128)(2,1)S(1)} %collective-permute-done.1.refs_2_), channel_id=1, source_target_pairs={{0,2},{1,3},{2,0},{3,1},{4,6},{5,7},{6,4},{7,5},{8,10},{9,11},{10,... | collective-permute-start | bytes 2949128 | tf_op jit(solution)/shard_map/ppermute | solution.py:413
  99.7 25.9 %collective-permute-start.4 = (f32[2,40,320]{2,1,0:T(8,128)}, f32[2,40,320]{2,1,0:T(8,128)S(1)}, u32[]{:S(2)}, u32[]{:S(2)}) collective-permute-start(f32[2,40,320]{2,1,0:T(8,128)} %pad_maximum_fusion.6), channel_id=1, source_target_pairs={{0,8},{4,12},{8,0},{12,4},{16,24},{20,28},{24,16},{28,20},{1,9},{5... | collective-permute-start | bytes 307208 | tf_op jit(solution)/shard_map/ppermute | solution.py:413
  224.4 49.3 %collective-permute-start.5 = (bf16[5,64,1536]{2,1,0:T(8,128)(2,1)}, bf16[5,64,1536]{2,1,0:T(8,128)(2,1)S(1)}, u32[]{:S(2)}, u32[]{:S(2)}) collective-permute-start(bf16[5,64,1536]{2,1,0:T(8,128)(2,1)} %get-tuple-element.164), channel_id=1, source_target_pairs={{0,4},{4,0},{8,12},{12,8},{16,20},{20,16},{24,28},{28,24},{1,5},{5... | collective-permute-start | bytes 2949128 | tf_op jit(solution)/shard_map/ppermute | solution.py:413
  225.9 47.7 %collective-permute-start.6 = (bf16[2,5,192,256]{3,2,1,0:T(8,128)(2,1)}, bf16[2,5,192,256]{3,2,1,0:T(8,128)(2,1)}, u32[]{:S(2)}, u32[]{:S(2)}) collective-permute-start(bf16[2,5,192,256]{3,2,1,0:T(8,128)(2,1)} %get-tuple-element.165), channel_id=1, source_target_pairs={{0,4},{4,0},{8,12},{12,8},{16,20},{20,16},{24,28},{28,24},{1,5},{5... | collective-permute-start | bytes 2949128 | tf_op jit(solution)/shard_map/ppermute | solution.py:413
  226.5 47.2 %collective-permute-start.7 = (bf16[2,5,192,256]{3,2,1,0:T(8,128)(2,1)}, bf16[2,5,192,256]{3,2,1,0:T(8,128)(2,1)S(1)}, u32[]{:S(2)}, u32[]{:S(2)}) collective-permute-start(bf16[2,5,192,256]{3,2,1,0:T(8,128)(2,1)} %get-tuple-element.166), channel_id=1, source_target_pairs={{0,16},{4,20},{8,24},{12,28},{16,0},{20,4},{24,8},{28,12},{1,17},{... | collective-permute-start | bytes 2949128 | tf_op jit(solution)/shard_map/ppermute | solution.py:413
  227.7 111.3 %collective-permute-start.8 = (bf16[5,64,1536]{2,1,0:T(8,128)(2,1)}, bf16[5,64,1536]{2,1,0:T(8,128)(2,1)S(1)}, u32[]{:S(2)}, u32[]{:S(2)}) collective-permute-start(bf16[5,64,1536]{2,1,0:T(8,128)(2,1)} %get-tuple-element.177), channel_id=1, source_target_pairs={{0,4},{4,0},{8,12},{12,8},{16,20},{20,16},{24,28},{28,24},{1,5},{5... | collective-permute-start | bytes 2949128 | tf_op jit(solution)/shard_map/ppermute | solution.py:413
  229.1 44.5 %copy-start.19 = (bf16[2,5,192,256]{3,2,1,0:T(8,128)(2,1)S(1)}, bf16[2,5,192,256]{3,2,1,0:T(8,128)(2,1)}, u32[]{:S(2)}) copy-start(bf16[2,5,192,256]{3,2,1,0:T(8,128)(2,1)} %get-tuple-element.169) | copy-start | bytes 2949124
  273.7 65.3 %copy-start.5 = (bf16[2,5,192,256]{3,2,1,0:T(8,128)(2,1)}, bf16[2,5,192,256]{3,2,1,0:T(8,128)(2,1)S(1)}, u32[]{:S(2)}) copy-start(bf16[2,5,192,256]{3,2,1,0:T(8,128)(2,1)S(1)} %collective-permute-done.7.refs_5_) | copy-start | bytes 2949124
  275.0 64.0 %copy-start.34 = (bf16[2,5,192,256]{3,2,1,0:T(8,128)(2,1)S(1)}, bf16[2,5,192,256]{3,2,1,0:T(8,128)(2,1)}, u32[]{:S(2)}) copy-start(bf16[2,5,192,256]{3,2,1,0:T(8,128)(2,1)} %get-tuple-element.179) | copy-start | bytes 2949124
  339.0 72.4 %collective-permute-start.9 = (bf16[2,5,192,256]{3,2,1,0:T(8,128)(2,1)S(1)}, bf16[2,5,192,256]{3,2,1,0:T(8,128)(2,1)S(1)}, u32[]{:S(2)}, u32[]{:S(2)}) collective-permute-start(bf16[2,5,192,256]{3,2,1,0:T(8,128)(2,1)S(1)} %copy-done.34), channel_id=1, source_target_pairs={{0,4},{4,0},{8,12},{12,8},{16,20},{20,16},{24,28},{28,24},{1,5},{5... | collective-permute-start | bytes 2949128 | tf_op jit(solution)/shard_map/ppermute | solution.py:413
  341.0 70.4 %collective-permute-start.10 = (bf16[5,192,256]{2,1,0:T(8,128)(2,1)S(1)}, bf16[5,192,256]{2,1,0:T(8,128)(2,1)S(1)}, u32[]{:S(2)}, u32[]{:S(2)}) collective-permute-start(bf16[5,192,256]{2,1,0:T(8,128)(2,1)S(1)} %fusion.9), channel_id=1, source_target_pairs={{0,16},{4,20},{8,24},{12,28},{16,0},{20,4},{24,8},{28,12},{1,17},{... | collective-permute-start | bytes 1474568 | tf_op jit(solution)/shard_map/ppermute | solution.py:413
  357.0 54.4 %copy-start.6 = (bf16[2,5,192,256]{3,2,1,0:T(8,128)(2,1)S(1)}, bf16[2,5,192,256]{3,2,1,0:T(8,128)(2,1)}, u32[]{:S(2)}) copy-start(bf16[2,5,192,256]{3,2,1,0:T(8,128)(2,1)} %get-tuple-element.196.refs_3_) | copy-start | bytes 2949124
  414.2 45.2 %collective-permute-start.11 = (bf16[2,5,192,256]{3,2,1,0:T(8,128)(2,1)S(1)}, bf16[2,5,192,256]{3,2,1,0:T(8,128)(2,1)S(1)}, u32[]{:S(2)}, u32[]{:S(2)}) collective-permute-start(bf16[2,5,192,256]{3,2,1,0:T(8,128)(2,1)S(1)} %pad_maximum_fusion.1), channel_id=1, source_target_pairs={{0,16},{4,20},{8,24},{12,28},{16,0},{20,4},{24,8},{28,12},{1,17},{... | collective-permute-start | bytes 2949128 | tf_op jit(solution)/shard_map/ppermute | solution.py:413
  414.3 45.2 %collective-permute-start.12 = (bf16[2,5,192,256]{3,2,1,0:T(8,128)(2,1)}, bf16[2,5,192,256]{3,2,1,0:T(8,128)(2,1)S(1)}, u32[]{:S(2)}, u32[]{:S(2)}) collective-permute-start(bf16[2,5,192,256]{3,2,1,0:T(8,128)(2,1)} %get-tuple-element.199), channel_id=1, source_target_pairs={{0,4},{4,0},{8,12},{12,8},{16,20},{20,16},{24,28},{28,24},{1,5},{5... | collective-permute-start | bytes 2949128 | tf_op jit(solution)/shard_map/ppermute | solution.py:413
  415.9 43.6 %collective-permute-start.13 = (bf16[5,64,1536]{2,1,0:T(8,128)(2,1)}, bf16[5,64,1536]{2,1,0:T(8,128)(2,1)S(1)}, u32[]{:S(2)}, u32[]{:S(2)}) collective-permute-start(bf16[5,64,1536]{2,1,0:T(8,128)(2,1)} %get-tuple-element.200), channel_id=1, source_target_pairs={{0,4},{4,0},{8,12},{12,8},{16,20},{20,16},{24,28},{28,24},{1,5},{5... | collective-permute-start | bytes 2949128 | tf_op jit(solution)/shard_map/ppermute | solution.py:413
  461.2 83.1 %copy-start.1 = (bf16[16,48,1536]{2,1,0:T(8,128)(2,1)S(1)}, bf16[16,48,1536]{2,1,0:T(8,128)(2,1)}, u32[]{:S(2)}) copy-start(bf16[16,48,1536]{2,1,0:T(8,128)(2,1)} %get-tuple-element.207) | copy-start | bytes 7077892
  548.0 95.2 %collective-permute-start.14 = (bf16[5,64,1536]{2,1,0:T(8,128)(2,1)}, bf16[5,64,1536]{2,1,0:T(8,128)(2,1)}, u32[]{:S(2)}, u32[]{:S(2)}) collective-permute-start(bf16[5,64,1536]{2,1,0:T(8,128)(2,1)} %fusion.1), channel_id=1, source_target_pairs={{0,16},{4,20},{8,24},{12,28},{16,0},{20,4},{24,8},{28,12},{1,17},{... | collective-permute-start | bytes 2949128 | tf_op jit(solution)/shard_map/ppermute | solution.py:413
  549.6 93.5 %collective-permute-start.15 = (bf16[5,64,1536]{2,1,0:T(8,128)(2,1)}, bf16[5,64,1536]{2,1,0:T(8,128)(2,1)}, u32[]{:S(2)}, u32[]{:S(2)}) collective-permute-start(bf16[5,64,1536]{2,1,0:T(8,128)(2,1)} %get-tuple-element.235), channel_id=1, source_target_pairs={{0,4},{4,0},{8,12},{12,8},{16,20},{20,16},{24,28},{28,24},{1,5},{5... | collective-permute-start | bytes 2949128 | tf_op jit(solution)/shard_map/ppermute | solution.py:413
  554.2 89.0 %collective-permute-start.16 = (bf16[2,5,192,256]{3,2,1,0:T(8,128)(2,1)}, bf16[2,5,192,256]{3,2,1,0:T(8,128)(2,1)}, u32[]{:S(2)}, u32[]{:S(2)}) collective-permute-start(bf16[2,5,192,256]{3,2,1,0:T(8,128)(2,1)} %pad_maximum_fusion.2), channel_id=1, source_target_pairs={{0,8},{4,12},{8,0},{12,4},{16,24},{20,28},{24,16},{28,20},{1,9},{5... | collective-permute-start | bytes 2949128 | tf_op jit(solution)/shard_map/ppermute | solution.py:413
  (28 other events, 233.6 us)

commit v8 on v7

--- a/solution.py
+++ b/solution.py
@@ -765,7 +765,7 @@
             jax.ShapeDtypeStruct((tokens, WIDTH), BF),
             jax.ShapeDtypeStruct((tokens, WIDTH), BF),
         ),
-        compiler_params=params(60),
+        compiler_params=params(24),
         cost_estimate=cost(2 * tokens * WIDTH * WIDTH, 12e6),
     )(att, w_output, inputs, gain[None])
 
@@ -1336,22 +1336,22 @@
     cross_own.wait_recv()
     put_x(4, all_ref.at[4])
     put_g(4, other.at[0])
+    put_g(5, other.at[1])
+    put_g(6, other.at[2])
     x_low.wait_recv()
     cross_x = send(all_ref.at[1], 5, None, C_BIT)
     z_top.wait_recv()
     cross_z = send(all_ref.at[2], 6, None, C_BIT)
     put_x(1, all_ref.at[1])
     put_x(2, all_ref.at[2])
-    put_g(5, other.at[1])
     cross_x.wait_recv()
     cross_z.wait_recv()
     put_x(5, all_ref.at[5])
+    put_x(6, all_ref.at[6])
+    put_g(7, other.at[3])
     far_top.wait_recv()
     far_low.wait_recv()
     cross_far = send(all_ref.at[3], 7, None, C_BIT)
-    put_x(6, all_ref.at[6])
-    put_g(6, other.at[2])
-    put_g(7, other.at[3])
     put_x(3, all_ref.at[3])
     cross_far.wait_recv()
     put_x(7, all_ref.at[7])
@@ -1598,7 +1598,7 @@
     return compute
 
 
-def run_trade(values, number, riders=(), work=(), blocks=0):
+def run_trade(values, number, riders=(), work=(), blocks=0, mib=60):
     size = values.shape[0]
     inputs = rider_inputs(riders)
     vmem = pl.BlockSpec(memory_space=pltpu.VMEM)
@@ -1629,7 +1629,7 @@
         + rider_scratch(riders)
         + scratch,
         compiler_params=pltpu.CompilerParams(
-            collective_id=number, has_side_effects=True, vmem_limit_bytes=60 * MIB
+            collective_id=number, has_side_effects=True, vmem_limit_bytes=mib * MIB
         ),
         cost_estimate=cost(0, 170e6),
     )(values, *inputs, *work)
@@ -1974,7 +1974,7 @@
     out, g_x, g_z, maps = fence(out, g_x, g_z, maps)
     g_zx = swap_bit(g_z, X_BIT)
     maps = stack_swap(maps, ZL_BIT)
-    att = run_trade(out, 3)
+    att = run_trade(out, 3, mib=16)
     att, g_zx, maps = fence(att, g_zx, maps)
     middle, normed_two, att_full = run_mid(att, w_output, inputs, gain_mlp)
     x_slots, g_slots, gates, maps = run_gather(

time: 670 us -> 665 us (level)
  Pallas kernels: 598 us -> 588 us
    unnamed x77 -> x85, local copies, waits for them, and re-layouts: 8.55 us -> 14.1 us
where the time goes in v8:
time: 665 us; the launch traced here: 656 us
  Pallas kernels  588 us (88%)
  local copies, waits for them, and re-layouts  22.9 us (3%)
  other arithmetic  22.7 us (3%)
  starting transfers between devices  21.7 us (3%)
    pallas_call x3, Pallas kernels, run_trade(): pl.pallas_call(functools.partial(trade_kernel, plans=tuple((rider.plan()...  161 us
    pallas_call x2, Pallas kernels, run_reduce(): pl.pallas_call(functools.partial(reduce_kernel, jobs=jobs, plans=tuple((r...  135 us
    pallas_call x2, Pallas kernels, run_experts(): pl.pallas_call(functools.partial(expert_kernel, first=not prior), grid_sp...  86.6 us
    pallas_call x1, Pallas kernels, run_first(): pl.pallas_call(functools.partial(first_kernel, far=far), in_specs=[hbm, v...  43.7 us
    pallas_call x1, Pallas kernels, run_gather(): pl.pallas_call(gather_kernel, in_specs=[vmem] * 7, out_specs=(hbm, hbm, v...  43.4 us
    pallas_call x1, Pallas kernels, run_backward(): pl.pallas_call(backward_kernel, grid=(blocks,), in_specs=[pl.BlockSpec(pa...  43.1 us
    pallas_call x1, Pallas kernels, run_forward(): pl.pallas_call(forward_kernel, grid=(blocks,), in_specs=[pl.BlockSpec(pac...  30 us
    ppermute x17, starting transfers between devices, swap(): return lax.ppermute(values, axis, [(i, i ^ mask) for i in range(size)])  21.7 us
  transfers between devices with their start and end apart: 17, of which 0 were waited for; matrix products, arithmetic and copies ran while one was open for 3% of the time, Pallas kernels for 60%

profile of v8, /device:TPU:0, one launch (start us, length us, event | category | flops | bytes accessed | tf_op | source)
XLA Modules:
  0.0 656.4 jit_solution(9014372961091608830)
XLA Ops:
  3.7 9.1 %shard_map.229 = (bf16[320,1536]{1,0:T(8,128)(2,1)}, bf16[8,800,128]{2,1,0:T(8,128)(2,1)}, bf16[320,1536]{1,0:T(8,128)(2,1)}) custom-call(f32[320,1536]{1,0:T(8,128)} %bitcast.70, f32[1,1536]{1,0:T(1,128)} %broadcast_in_dim.44.gain_ref.refs_6_, bf16[1536,1536]{1,0:T(8,128)(2,1)} %refs_9_.1, bf16[1536,512]{1,0:T(8,128)(2,1)} %refs_10_.1, ...), custom_call_target="tpu_custom_call" | custom-call | flops 2516582400 | bytes 14000000 | tf_op jit(solution)/shard_map/pallas_call | solution.py:487
  12.7 2.9 collective-permute-start
  17.0 43.7 %shard_map.230 = (bf16[8,800,128]{2,1,0:T(8,128)(2,1)}, f32[40,320]{1,0:T(8,128)}) custom-call(bf16[8,800,128]{2,1,0:T(8,128)(2,1)} %get-tuple-element.136.a_ref, f32[40,320]{1,0:T(8,128)} %copy-done.28, f32[320,40]{1,0:T(8,128)} %bitcast.88), custom_call_target="tpu_custom_call" | custom-call | bytes 170000000 | tf_op jit(solution)/shard_map/pallas_call | solution.py:1653
  61.5 30.0 %shard_map.231 = (bf16[8,480,128]{2,1,0:T(8,128)(2,1)}, f32[10,64,768]{2,1,0:T(8,128)}, f32[10,1,768]{2,1,0:T(1,128)}) custom-call(bf16[8,800,128]{2,1,0:T(8,128)(2,1)} %get-tuple-element.140.pack_ref), custom_call_target="tpu_custom_call" | custom-call | flops 10066329600 | bytes 6000000 | tf_op jit(solution)/shard_map/pallas_call | solution.py:602
  94.8 1.7 pad.12.refs_5_
  98.6 1.9 collective-permute-start.4
  100.6 23.6 %shard_map.232.att_ref = bf16[8,480,128]{2,1,0:T(8,128)(2,1)S(1)} custom-call(bf16[8,480,128]{2,1,0:T(8,128)(2,1)S(1)} %copy-done.6), custom_call_target="tpu_custom_call" | custom-call | bytes 170000000 | tf_op jit(solution)/shard_map/pallas_call | solution.py:1619
  125.8 2.3 copy-done
  128.2 2.0 shard_map.233
  133.4 43.4 %shard_map.234 = (bf16[10,512,1536]{2,1,0:T(8,128)(2,1)}, bf16[10,512,1536]{2,1,0:T(8,128)(2,1)}, f32[10,512,1]{2,1,0:T(8,128)}, f32[8,10,320]{2,1,0:T(8,128)}) custom-call(bf16[320,1536]{1,0:T(8,128)(2,1)} %copy-done.2, bf16[320,1536]{1,0:T(8,128)(2,1)} %get-tuple-element.142.refs_0_, bf16[320,1536]{1,0:T(8,128)(2,1)} %copy-done.23, ...), custom_call_target="tpu_custom_call" | custom-call | bytes 150000000 | tf_op jit(solution)/shard_map/pallas_call | solution.py:1368
  176.8 42.1 %shard_map.235 = (bf16[4,320,1536]{2,1,0:T(8,128)(2,1)}, bf16[4,320,1536]{2,1,0:T(8,128)(2,1)}, bf16[4,320,1664]{2,1,0:T(8,128)(2,1)}, bf16[4,320,1664]{2,1,0:T(...) custom-call(s32[6]{0:T(128)} %stack.40.place_ref, ...), custom_call_target="tpu_custom_call" | custom-call | flops 30000001024 | bytes 60000000 | tf_op jit(solution)/shard_map/pallas_call | solution.py:974
  223.7 44.5 %shard_map.236 = (bf16[4,320,1536]{2,1,0:T(8,128)(2,1)}, bf16[4,320,1536]{2,1,0:T(8,128)(2,1)}, bf16[4,320,1664]{2,1,0:T(8,128)(2,1)}, bf16[4,320,1664]{2,1,0:T(...) custom-call(s32[6]{0:T(128)} %stack.40.place_ref, ...), custom_call_target="tpu_custom_call" | custom-call | flops 30000001024 | bytes 60000000 | tf_op jit(solution)/shard_map/pallas_call | solution.py:974
  269.7 64.4 %shard_map.237 = (f32[320,1664]{1,0:T(8,128)}, bf16[2,5,192,256]{3,2,1,0:T(8,128)(2,1)}, bf16[2,5,192,256]{3,2,1,0:T(8,128)(2,1)}, bf16[4,320,1536]{2,1,0:T(8,128)(2,1)}, bf16[5,64,1536]{2,1,0:T(8,128)(2,1)}) custom-call(bf16[4,320,1664]{2,1,0:T(8,128)(2,1)} %get-tuple-element.162.refs_0_, bf16[4,320,1664]{2,1,0:T(8,128)(2,1)} %get-tuple-element.167.refs_1_, ...), custom_call_target="tpu_custom_call" | custom-call | bytes 170000000 | tf_op jit(solution)/shard_map/pallas_call | solution.py:1816
  336.0 3.8 collective-permute-start.10
  339.8 2.4 multiply_sine_fusion
  342.3 9.3 %shard_map.238 = (bf16[8,480,128]{2,1,0:T(8,128)(2,1)}, f32[320,1536]{1,0:T(8,128)}, bf16[320,1536]{1,0:T(8,128)(2,1)}, bf16[320,128]{1,0:T(8,128)(2,1)}, f32[1,1536]{1,0:T(1,128)}) custom-call(f32[320,1664]{1,0:T(8,128)} %get-tuple-element.182.dx_ref, f32[320,1536]{1,0:T(8,128)} %copy-done.3, f32[320,1536]{1,0:T(8,128)} %bitcast.80, ...), custom_call_target="tpu_custom_call" | custom-call | flops 1509949440 | bytes 14000000 | tf_op jit(solution)/shard_map/pallas_call | solution.py:1066
  351.6 54.4 %shard_map.239 = (bf16[8,480,128]{2,1,0:T(8,128)(2,1)}, bf16[2,5,192,256]{3,2,1,0:T(8,128)(2,1)}, bf16[5,192,256]{2,1,0:T(8,128)(2,1)}, bf16[5,192,256]{2,1,0:T(...) custom-call(bf16[8,480,128]{2,1,0:T(8,128)(2,1)} %get-tuple-element.184.ref, ...), custom_call_target="tpu_custom_call" | custom-call | bytes 170000000 | tf_op jit(solution)/shard_map/pallas_call | solution.py:1619
  411.0 43.1 %shard_map.240.refs_0_ = bf16[8,800,128]{2,1,0:T(8,128)(2,1)} custom-call(bf16[8,800,128]{2,1,0:T(8,128)(2,1)} %get-tuple-element.140.pack_ref, bf16[8,480,128]{2,1,0:T(8,128)(2,1)} %get-tuple-element.193.grad_ref, f32[10,64,768]{2,1,0:T(8,128)} %get-tuple-element.194.out_t_ref, f32[10,1,768]{2,1,0:T(1,128)} %get-tuple-element.195.lse_ref, ...), custom_call_target="tpu_custom_call" | custom-call | flops 25165824000 | bytes 8000000 | tf_op jit(solution)/shard_map/pallas_call | solution.py:723
  455.8 83.1 %shard_map.241 = (bf16[8,800,128]{2,1,0:T(8,128)(2,1)}, bf16[2,5,192,256]{3,2,1,0:T(8,128)(2,1)}, bf16[2,5,192,256]{3,2,1,0:T(8,128)(2,1)}, bf16[5,192,256]{2,1,...) custom-call(bf16[8,800,128]{2,1,0:T(8,128)(2,1)} %shard_map.240.refs, ...), custom_call_target="tpu_custom_call" | custom-call | bytes 170000000 | tf_op jit(solution)/shard_map/pallas_call | solution.py:1619
  538.9 2.2 fusion
  550.5 11.9 %shard_map.242 = (bf16[320,2560]{1,0:T(8,128)(2,1)}, bf16[16,48,2560]{2,1,0:T(8,128)(2,1)}, bf16[16,48,2560]{2,1,0:T(8,128)(2,1)}) custom-call(s32[6]{0:T(128)} %stack.40.place_ref, bf16[320,1536]{1,0:T(8,128)(2,1)} %get-tuple-element.135.a_ref, bf16[8,800,128]{2,1,0:T(8,128)(2,1)} %get-tuple-element.217.d_ref), custom_call_target="tpu_custom_call" | custom-call | flops 2516582400 | bytes 12000000 | tf_op jit(solution)/shard_map/pallas_call | solution.py:1120
  562.4 3.7 fusion.2
  566.1 71.0 %shard_map.243 = (f32[320,1536]{1,0:T(8,128)}, f32[48,1536]{1,0:T(8,128)}, f32[48,512]{1,0:T(8,128)}, f32[48,512]{1,0:T(8,128)}, f32[48,1536]{1,0:T(8,128)}, /*i...) custom-call(bf16[16,48,2560]{2,1,0:T(8,128)(2,1)} %get-tuple-element.222.refs_0_, ...), custom_call_target="tpu_custom_call" | custom-call | bytes 170000000 | tf_op jit(solution)/shard_map/pallas_call | solution.py:1816
  640.0 12.2 %shard_map.244 = (f32[2,5,192,512]{3,2,1,0:T(8,128)}, f32[2,5,192,512]{3,2,1,0:T(8,128)}, f32[2,5,64,1536]{3,2,1,0:T(8,128)}) custom-call(s32[6]{0:T(128)} %stack.40.place_ref, bf16[2,2,5,192,256]{4,3,2,1,0:T(8,128)(2,1)} %get-tuple-element.180.refs_4_.refs_0_, bf16[2,5,192,256]{3,2,1,0:T(8,128)(2,1)} %get-tuple-element.187.refs_6_.refs_1_, ...), custom_call_target="tpu_custom_call" | custom-call | flops 1000000 | bytes 26000000 | tf_op jit(solution)/shard_map/pallas_call | solution.py:1890
  (147 shorter events, 46.3 us)
Async XLA Ops:
  12.7 48.0 %copy-start.22 = (bf16[320,1536]{1,0:T(8,128)(2,1)S(1)}, bf16[320,1536]{1,0:T(8,128)(2,1)}, u32[]{:S(2)}) copy-start(bf16[320,1536]{1,0:T(8,128)(2,1)} %get-tuple-element.142.refs_0_) | copy-start | bytes 2949124
  12.7 79.4 %collective-permute-start = (bf16[320,1536]{1,0:T(8,128)(2,1)}, bf16[320,1536]{1,0:T(8,128)(2,1)S(1)}, u32[]{:S(2)}, u32[]{:S(2)}) collective-permute-start(bf16[320,1536]{1,0:T(8,128)(2,1)} %get-tuple-element.142.refs_0_), channel_id=1, source_target_pairs={{0,2},{1,3},{2,0},{3,1},{4,6},{5,7},{6,4},{7,5},{8,10},{9,11},{10,... | collective-permute-start | bytes 2949128 | tf_op jit(solution)/shard_map/ppermute | solution.py:413
  60.7 31.4 %collective-permute-start.1 = (bf16[320,1536]{1,0:T(8,128)(2,1)S(1)}, bf16[320,1536]{1,0:T(8,128)(2,1)}, u32[]{:S(2)}, u32[]{:S(2)}) collective-permute-start(bf16[320,1536]{1,0:T(8,128)(2,1)S(1)} %copy-done.22), channel_id=1, source_target_pairs={{0,8},{4,12},{8,0},{12,4},{16,24},{20,28},{24,16},{28,20},{1,9},{5... | collective-permute-start | bytes 2949128 | tf_op jit(solution)/shard_map/ppermute | solution.py:413
  60.8 32.8 %copy-start.38 = (f32[1536]{0:T(1024)S(1)}, f32[1536]{0:T(1024)}, u32[]{:S(2)}) copy-start(f32[1536]{0:T(1024)} %param.20) | copy-start | bytes 18436
  60.8 30.6 %collective-permute-start.2 = (f32[1,40,320]{2,1,0:T(8,128)}, f32[1,40,320]{2,1,0:T(8,128)S(1)}, u32[]{:S(2)}, u32[]{:S(2)}) collective-permute-start(f32[1,40,320]{2,1,0:T(8,128)} %bitcast.92), channel_id=1, source_target_pairs={{0,2},{1,3},{2,0},{3,1},{4,6},{5,7},{6,4},{7,5},{8,10},{9,11},{10,... | collective-permute-start | bytes 153608 | tf_op jit(solution)/shard_map/ppermute | solution.py:413
  92.1 33.7 %collective-permute-start.3 = (bf16[320,1536]{1,0:T(8,128)(2,1)}, bf16[320,1536]{1,0:T(8,128)(2,1)}, u32[]{:S(2)}, u32[]{:S(2)}) collective-permute-start(bf16[320,1536]{1,0:T(8,128)(2,1)} %collective-permute-done.1.refs_2_), channel_id=1, source_target_pairs={{0,2},{1,3},{2,0},{3,1},{4,6},{5,7},{6,4},{7,5},{8,10},{9,11},{10,... | collective-permute-start | bytes 2949128 | tf_op jit(solution)/shard_map/ppermute | solution.py:413
  93.7 32.2 %copy-start.7 = (f32[1,1536]{1,0:T(1,128)}, f32[1,1536]{1,0:T(1,128)S(1)}, u32[]{:S(2)}) copy-start(f32[1,1536]{1,0:T(1,128)S(1)} %broadcast_in_dim.48.gain_ref) | copy-start | bytes 18436
  98.6 25.6 %collective-permute-start.4 = (f32[2,40,320]{2,1,0:T(8,128)}, f32[2,40,320]{2,1,0:T(8,128)S(1)}, u32[]{:S(2)}, u32[]{:S(2)}) collective-permute-start(f32[2,40,320]{2,1,0:T(8,128)} %pad_maximum_fusion.6), channel_id=1, source_target_pairs={{0,8},{4,12},{8,0},{12,4},{16,24},{20,28},{24,16},{28,20},{1,9},{5... | collective-permute-start | bytes 307208 | tf_op jit(solution)/shard_map/ppermute | solution.py:413
  218.9 49.4 %collective-permute-start.5 = (bf16[5,64,1536]{2,1,0:T(8,128)(2,1)}, bf16[5,64,1536]{2,1,0:T(8,128)(2,1)S(1)}, u32[]{:S(2)}, u32[]{:S(2)}) collective-permute-start(bf16[5,64,1536]{2,1,0:T(8,128)(2,1)} %get-tuple-element.164), channel_id=1, source_target_pairs={{0,4},{4,0},{8,12},{12,8},{16,20},{20,16},{24,28},{28,24},{1,5},{5... | collective-permute-start | bytes 2949128 | tf_op jit(solution)/shard_map/ppermute | solution.py:413
  220.4 47.9 %collective-permute-start.6 = (bf16[2,5,192,256]{3,2,1,0:T(8,128)(2,1)}, bf16[2,5,192,256]{3,2,1,0:T(8,128)(2,1)}, u32[]{:S(2)}, u32[]{:S(2)}) collective-permute-start(bf16[2,5,192,256]{3,2,1,0:T(8,128)(2,1)} %get-tuple-element.165), channel_id=1, source_target_pairs={{0,4},{4,0},{8,12},{12,8},{16,20},{20,16},{24,28},{28,24},{1,5},{5... | collective-permute-start | bytes 2949128 | tf_op jit(solution)/shard_map/ppermute | solution.py:413
  221.0 47.3 %collective-permute-start.7 = (bf16[2,5,192,256]{3,2,1,0:T(8,128)(2,1)}, bf16[2,5,192,256]{3,2,1,0:T(8,128)(2,1)S(1)}, u32[]{:S(2)}, u32[]{:S(2)}) collective-permute-start(bf16[2,5,192,256]{3,2,1,0:T(8,128)(2,1)} %get-tuple-element.166), channel_id=1, source_target_pairs={{0,16},{4,20},{8,24},{12,28},{16,0},{20,4},{24,8},{28,12},{1,17},{... | collective-permute-start | bytes 2949128 | tf_op jit(solution)/shard_map/ppermute | solution.py:413
  222.2 111.8 %collective-permute-start.8 = (bf16[5,64,1536]{2,1,0:T(8,128)(2,1)}, bf16[5,64,1536]{2,1,0:T(8,128)(2,1)S(1)}, u32[]{:S(2)}, u32[]{:S(2)}) collective-permute-start(bf16[5,64,1536]{2,1,0:T(8,128)(2,1)} %get-tuple-element.177), channel_id=1, source_target_pairs={{0,4},{4,0},{8,12},{12,8},{16,20},{20,16},{24,28},{28,24},{1,5},{5... | collective-permute-start | bytes 2949128 | tf_op jit(solution)/shard_map/ppermute | solution.py:413
  223.7 44.5 %copy-start.24 = (bf16[2,5,192,256]{3,2,1,0:T(8,128)(2,1)S(1)}, bf16[2,5,192,256]{3,2,1,0:T(8,128)(2,1)}, u32[]{:S(2)}) copy-start(bf16[2,5,192,256]{3,2,1,0:T(8,128)(2,1)} %get-tuple-element.169) | copy-start | bytes 2949124
  268.3 65.7 %copy-start.12 = (bf16[2,5,192,256]{3,2,1,0:T(8,128)(2,1)}, bf16[2,5,192,256]{3,2,1,0:T(8,128)(2,1)S(1)}, u32[]{:S(2)}) copy-start(bf16[2,5,192,256]{3,2,1,0:T(8,128)(2,1)S(1)} %collective-permute-done.7.refs_5_) | copy-start | bytes 2949124
  334.1 72.0 %collective-permute-start.9 = (bf16[2,5,192,256]{3,2,1,0:T(8,128)(2,1)}, bf16[2,5,192,256]{3,2,1,0:T(8,128)(2,1)S(1)}, u32[]{:S(2)}, u32[]{:S(2)}) collective-permute-start(bf16[2,5,192,256]{3,2,1,0:T(8,128)(2,1)} %get-tuple-element.179), channel_id=1, source_target_pairs={{0,4},{4,0},{8,12},{12,8},{16,20},{20,16},{24,28},{28,24},{1,5},{5... | collective-permute-start | bytes 2949128 | tf_op jit(solution)/shard_map/ppermute | solution.py:413
  336.0 70.0 %collective-permute-start.10 = (bf16[5,192,256]{2,1,0:T(8,128)(2,1)S(1)}, bf16[5,192,256]{2,1,0:T(8,128)(2,1)S(1)}, u32[]{:S(2)}, u32[]{:S(2)}) collective-permute-start(bf16[5,192,256]{2,1,0:T(8,128)(2,1)S(1)} %fusion.9), channel_id=1, source_target_pairs={{0,16},{4,20},{8,24},{12,28},{16,0},{20,4},{24,8},{28,12},{1,17},{... | collective-permute-start | bytes 1474568 | tf_op jit(solution)/shard_map/ppermute | solution.py:413
  351.5 54.5 %copy-start.13 = (bf16[2,5,192,256]{3,2,1,0:T(8,128)(2,1)S(1)}, bf16[2,5,192,256]{3,2,1,0:T(8,128)(2,1)}, u32[]{:S(2)}) copy-start(bf16[2,5,192,256]{3,2,1,0:T(8,128)(2,1)} %get-tuple-element.196.refs_3_) | copy-start | bytes 2949124
  408.9 45.2 %collective-permute-start.11 = (bf16[2,5,192,256]{3,2,1,0:T(8,128)(2,1)S(1)}, bf16[2,5,192,256]{3,2,1,0:T(8,128)(2,1)S(1)}, u32[]{:S(2)}, u32[]{:S(2)}) collective-permute-start(bf16[2,5,192,256]{3,2,1,0:T(8,128)(2,1)S(1)} %pad_maximum_fusion.1), channel_id=1, source_target_pairs={{0,16},{4,20},{8,24},{12,28},{16,0},{20,4},{24,8},{28,12},{1,17},{... | collective-permute-start | bytes 2949128 | tf_op jit(solution)/shard_map/ppermute | solution.py:413
  408.9 45.2 %collective-permute-start.12 = (bf16[2,5,192,256]{3,2,1,0:T(8,128)(2,1)}, bf16[2,5,192,256]{3,2,1,0:T(8,128)(2,1)S(1)}, u32[]{:S(2)}, u32[]{:S(2)}) collective-permute-start(bf16[2,5,192,256]{3,2,1,0:T(8,128)(2,1)} %get-tuple-element.199), channel_id=1, source_target_pairs={{0,4},{4,0},{8,12},{12,8},{16,20},{20,16},{24,28},{28,24},{1,5},{5... | collective-permute-start | bytes 2949128 | tf_op jit(solution)/shard_map/ppermute | solution.py:413
  410.5 43.6 %collective-permute-start.13 = (bf16[5,64,1536]{2,1,0:T(8,128)(2,1)}, bf16[5,64,1536]{2,1,0:T(8,128)(2,1)S(1)}, u32[]{:S(2)}, u32[]{:S(2)}) collective-permute-start(bf16[5,64,1536]{2,1,0:T(8,128)(2,1)} %get-tuple-element.200), channel_id=1, source_target_pairs={{0,4},{4,0},{8,12},{12,8},{16,20},{20,16},{24,28},{28,24},{1,5},{5... | collective-permute-start | bytes 2949128 | tf_op jit(solution)/shard_map/ppermute | solution.py:413
  455.8 83.1 %copy-start.8 = (bf16[16,48,1536]{2,1,0:T(8,128)(2,1)S(1)}, bf16[16,48,1536]{2,1,0:T(8,128)(2,1)}, u32[]{:S(2)}) copy-start(bf16[16,48,1536]{2,1,0:T(8,128)(2,1)} %get-tuple-element.207) | copy-start | bytes 7077892
  542.6 94.5 %collective-permute-start.14 = (bf16[5,64,1536]{2,1,0:T(8,128)(2,1)}, bf16[5,64,1536]{2,1,0:T(8,128)(2,1)}, u32[]{:S(2)}, u32[]{:S(2)}) collective-permute-start(bf16[5,64,1536]{2,1,0:T(8,128)(2,1)} %fusion.1), channel_id=1, source_target_pairs={{0,16},{4,20},{8,24},{12,28},{16,0},{20,4},{24,8},{28,12},{1,17},{... | collective-permute-start | bytes 2949128 | tf_op jit(solution)/shard_map/ppermute | solution.py:413
  544.1 93.0 %collective-permute-start.15 = (bf16[5,64,1536]{2,1,0:T(8,128)(2,1)}, bf16[5,64,1536]{2,1,0:T(8,128)(2,1)}, u32[]{:S(2)}, u32[]{:S(2)}) collective-permute-start(bf16[5,64,1536]{2,1,0:T(8,128)(2,1)} %get-tuple-element.235), channel_id=1, source_target_pairs={{0,4},{4,0},{8,12},{12,8},{16,20},{20,16},{24,28},{28,24},{1,5},{5... | collective-permute-start | bytes 2949128 | tf_op jit(solution)/shard_map/ppermute | solution.py:413
  548.8 88.3 %collective-permute-start.16 = (bf16[2,5,192,256]{3,2,1,0:T(8,128)(2,1)}, bf16[2,5,192,256]{3,2,1,0:T(8,128)(2,1)}, u32[]{:S(2)}, u32[]{:S(2)}) collective-permute-start(bf16[2,5,192,256]{3,2,1,0:T(8,128)(2,1)} %pad_maximum_fusion.2), channel_id=1, source_target_pairs={{0,8},{4,12},{8,0},{12,4},{16,24},{20,28},{24,16},{28,20},{1,9},{5... | collective-permute-start | bytes 2949128 | tf_op jit(solution)/shard_map/ppermute | solution.py:413
  (32 other events, 205.4 us)

commit v9 on v8

--- a/solution.py
+++ b/solution.py
@@ -1994,7 +1994,7 @@
     quarter = tokens // 4
     extra = dx_keep.shape[2]
     token_parts = tuple(
-        (n * quarter, quarter, 0, extra, (1, 0) if n < 2 else (0, 1)) for n in (2, 0, 3, 1)
+        (n * quarter, quarter, 0, extra, (1, 0) if n < 2 else (0, 1)) for n in (0, 2, 1, 3)
     )
     dx_sum, up_ya, gate_ga, mix_got, down_ma = run_reduce(
         ((dx_keep, dx_send),),

time: 665 us -> 663 us (level)
  no operation moved by 1% of the time
where the time goes in v9:
time: 663 us; the launch traced here: 655 us
  Pallas kernels  586 us (88%)
  local copies, waits for them, and re-layouts  22.9 us (3%)
  other arithmetic  22.7 us (3%)
  starting transfers between devices  21.7 us (3%)
    pallas_call x3, Pallas kernels, run_trade(): pl.pallas_call(functools.partial(trade_kernel, plans=tuple((rider.plan()...  161 us
    pallas_call x2, Pallas kernels, run_reduce(): pl.pallas_call(functools.partial(reduce_kernel, jobs=jobs, plans=tuple((r...  134 us
    pallas_call x2, Pallas kernels, run_experts(): pl.pallas_call(functools.partial(expert_kernel, first=not prior), grid_sp...  86.6 us
    pallas_call x1, Pallas kernels, run_first(): pl.pallas_call(functools.partial(first_kernel, far=far), in_specs=[hbm, v...  43.7 us
    pallas_call x1, Pallas kernels, run_gather(): pl.pallas_call(gather_kernel, in_specs=[vmem] * 7, out_specs=(hbm, hbm, v...  43.4 us
    pallas_call x1, Pallas kernels, run_backward(): pl.pallas_call(backward_kernel, grid=(blocks,), in_specs=[pl.BlockSpec(pa...  43.1 us
    pallas_call x1, Pallas kernels, run_forward(): pl.pallas_call(forward_kernel, grid=(blocks,), in_specs=[pl.BlockSpec(pac...  30 us
    ppermute x17, starting transfers between devices, swap(): return lax.ppermute(values, axis, [(i, i ^ mask) for i in range(size)])  21.7 us
  transfers between devices with their start and end apart: 17, of which 0 were waited for; matrix products, arithmetic and copies ran while one was open for 3% of the time, Pallas kernels for 60%

profile of v9, /device:TPU:0, one launch (start us, length us, event | category | flops | bytes accessed | tf_op | source)
XLA Modules:
  0.0 654.9 jit_solution(18426410458933171792)
XLA Ops:
  3.7 9.1 %shard_map.229 = (bf16[320,1536]{1,0:T(8,128)(2,1)}, bf16[8,800,128]{2,1,0:T(8,128)(2,1)}, bf16[320,1536]{1,0:T(8,128)(2,1)}) custom-call(f32[320,1536]{1,0:T(8,128)} %bitcast.70, f32[1,1536]{1,0:T(1,128)} %broadcast_in_dim.44.gain_ref.refs_6_, bf16[1536,1536]{1,0:T(8,128)(2,1)} %refs_9_.1, bf16[1536,512]{1,0:T(8,128)(2,1)} %refs_10_.1, ...), custom_call_target="tpu_custom_call" | custom-call | flops 2516582400 | bytes 14000000 | tf_op jit(solution)/shard_map/pallas_call | solution.py:487
  12.7 2.9 collective-permute-start
  17.0 43.7 %shard_map.230 = (bf16[8,800,128]{2,1,0:T(8,128)(2,1)}, f32[40,320]{1,0:T(8,128)}) custom-call(bf16[8,800,128]{2,1,0:T(8,128)(2,1)} %get-tuple-element.136.a_ref, f32[40,320]{1,0:T(8,128)} %copy-done.28, f32[320,40]{1,0:T(8,128)} %bitcast.88), custom_call_target="tpu_custom_call" | custom-call | bytes 170000000 | tf_op jit(solution)/shard_map/pallas_call | solution.py:1653
  61.5 30.0 %shard_map.231 = (bf16[8,480,128]{2,1,0:T(8,128)(2,1)}, f32[10,64,768]{2,1,0:T(8,128)}, f32[10,1,768]{2,1,0:T(1,128)}) custom-call(bf16[8,800,128]{2,1,0:T(8,128)(2,1)} %get-tuple-element.140.pack_ref), custom_call_target="tpu_custom_call" | custom-call | flops 10066329600 | bytes 6000000 | tf_op jit(solution)/shard_map/pallas_call | solution.py:602
  94.8 1.7 pad.12.refs_5_
  98.6 1.9 collective-permute-start.4
  100.6 23.6 %shard_map.232.att_ref = bf16[8,480,128]{2,1,0:T(8,128)(2,1)S(1)} custom-call(bf16[8,480,128]{2,1,0:T(8,128)(2,1)S(1)} %copy-done.6), custom_call_target="tpu_custom_call" | custom-call | bytes 170000000 | tf_op jit(solution)/shard_map/pallas_call | solution.py:1619
  125.8 2.3 copy-done
  128.2 2.0 shard_map.233
  133.4 43.4 %shard_map.234 = (bf16[10,512,1536]{2,1,0:T(8,128)(2,1)}, bf16[10,512,1536]{2,1,0:T(8,128)(2,1)}, f32[10,512,1]{2,1,0:T(8,128)}, f32[8,10,320]{2,1,0:T(8,128)}) custom-call(bf16[320,1536]{1,0:T(8,128)(2,1)} %copy-done.2, bf16[320,1536]{1,0:T(8,128)(2,1)} %get-tuple-element.142.refs_0_, bf16[320,1536]{1,0:T(8,128)(2,1)} %copy-done.23, ...), custom_call_target="tpu_custom_call" | custom-call | bytes 150000000 | tf_op jit(solution)/shard_map/pallas_call | solution.py:1368
  176.8 42.1 %shard_map.235 = (bf16[4,320,1536]{2,1,0:T(8,128)(2,1)}, bf16[4,320,1536]{2,1,0:T(8,128)(2,1)}, bf16[4,320,1664]{2,1,0:T(8,128)(2,1)}, bf16[4,320,1664]{2,1,0:T(...) custom-call(s32[6]{0:T(128)} %stack.40.place_ref, ...), custom_call_target="tpu_custom_call" | custom-call | flops 30000001024 | bytes 60000000 | tf_op jit(solution)/shard_map/pallas_call | solution.py:974
  223.7 44.5 %shard_map.236 = (bf16[4,320,1536]{2,1,0:T(8,128)(2,1)}, bf16[4,320,1536]{2,1,0:T(8,128)(2,1)}, bf16[4,320,1664]{2,1,0:T(8,128)(2,1)}, bf16[4,320,1664]{2,1,0:T(...) custom-call(s32[6]{0:T(128)} %stack.40.place_ref, ...), custom_call_target="tpu_custom_call" | custom-call | flops 30000001024 | bytes 60000000 | tf_op jit(solution)/shard_map/pallas_call | solution.py:974
  269.7 62.8 %shard_map.237 = (f32[320,1664]{1,0:T(8,128)}, bf16[2,5,192,256]{3,2,1,0:T(8,128)(2,1)}, bf16[2,5,192,256]{3,2,1,0:T(8,128)(2,1)}, bf16[4,320,1536]{2,1,0:T(8,128)(2,1)}, bf16[5,64,1536]{2,1,0:T(8,128)(2,1)}) custom-call(bf16[4,320,1664]{2,1,0:T(8,128)(2,1)} %get-tuple-element.162.refs_0_, bf16[4,320,1664]{2,1,0:T(8,128)(2,1)} %get-tuple-element.167.refs_1_, ...), custom_call_target="tpu_custom_call" | custom-call | bytes 170000000 | tf_op jit(solution)/shard_map/pallas_call | solution.py:1816
  334.5 3.8 collective-permute-start.10
  338.3 2.4 multiply_sine_fusion
  340.7 9.3 %shard_map.238 = (bf16[8,480,128]{2,1,0:T(8,128)(2,1)}, f32[320,1536]{1,0:T(8,128)}, bf16[320,1536]{1,0:T(8,128)(2,1)}, bf16[320,128]{1,0:T(8,128)(2,1)}, f32[1,1536]{1,0:T(1,128)}) custom-call(f32[320,1664]{1,0:T(8,128)} %get-tuple-element.182.dx_ref, f32[320,1536]{1,0:T(8,128)} %copy-done.3, f32[320,1536]{1,0:T(8,128)} %bitcast.80, ...), custom_call_target="tpu_custom_call" | custom-call | flops 1509949440 | bytes 14000000 | tf_op jit(solution)/shard_map/pallas_call | solution.py:1066
  350.0 54.5 %shard_map.239 = (bf16[8,480,128]{2,1,0:T(8,128)(2,1)}, bf16[2,5,192,256]{3,2,1,0:T(8,128)(2,1)}, bf16[5,192,256]{2,1,0:T(8,128)(2,1)}, bf16[5,192,256]{2,1,0:T(...) custom-call(bf16[8,480,128]{2,1,0:T(8,128)(2,1)} %get-tuple-element.184.ref, ...), custom_call_target="tpu_custom_call" | custom-call | bytes 170000000 | tf_op jit(solution)/shard_map/pallas_call | solution.py:1619
  409.5 43.1 %shard_map.240.refs_0_ = bf16[8,800,128]{2,1,0:T(8,128)(2,1)} custom-call(bf16[8,800,128]{2,1,0:T(8,128)(2,1)} %get-tuple-element.140.pack_ref, bf16[8,480,128]{2,1,0:T(8,128)(2,1)} %get-tuple-element.193.grad_ref, f32[10,64,768]{2,1,0:T(8,128)} %get-tuple-element.194.out_t_ref, f32[10,1,768]{2,1,0:T(1,128)} %get-tuple-element.195.lse_ref, ...), custom_call_target="tpu_custom_call" | custom-call | flops 25165824000 | bytes 8000000 | tf_op jit(solution)/shard_map/pallas_call | solution.py:723
  454.2 83.1 %shard_map.241 = (bf16[8,800,128]{2,1,0:T(8,128)(2,1)}, bf16[2,5,192,256]{3,2,1,0:T(8,128)(2,1)}, bf16[2,5,192,256]{3,2,1,0:T(8,128)(2,1)}, bf16[5,192,256]{2,1,...) custom-call(bf16[8,800,128]{2,1,0:T(8,128)(2,1)} %shard_map.240.refs, ...), custom_call_target="tpu_custom_call" | custom-call | bytes 170000000 | tf_op jit(solution)/shard_map/pallas_call | solution.py:1619
  537.3 2.2 fusion
  548.9 11.9 %shard_map.242 = (bf16[320,2560]{1,0:T(8,128)(2,1)}, bf16[16,48,2560]{2,1,0:T(8,128)(2,1)}, bf16[16,48,2560]{2,1,0:T(8,128)(2,1)}) custom-call(s32[6]{0:T(128)} %stack.40.place_ref, bf16[320,1536]{1,0:T(8,128)(2,1)} %get-tuple-element.135.a_ref, bf16[8,800,128]{2,1,0:T(8,128)(2,1)} %get-tuple-element.217.d_ref), custom_call_target="tpu_custom_call" | custom-call | flops 2516582400 | bytes 12000000 | tf_op jit(solution)/shard_map/pallas_call | solution.py:1120
  560.8 3.7 fusion.2
  564.5 71.0 %shard_map.243 = (f32[320,1536]{1,0:T(8,128)}, f32[48,1536]{1,0:T(8,128)}, f32[48,512]{1,0:T(8,128)}, f32[48,512]{1,0:T(8,128)}, f32[48,1536]{1,0:T(8,128)}, /*i...) custom-call(bf16[16,48,2560]{2,1,0:T(8,128)(2,1)} %get-tuple-element.222.refs_0_, ...), custom_call_target="tpu_custom_call" | custom-call | bytes 170000000 | tf_op jit(solution)/shard_map/pallas_call | solution.py:1816
  638.5 12.2 %shard_map.244 = (f32[2,5,192,512]{3,2,1,0:T(8,128)}, f32[2,5,192,512]{3,2,1,0:T(8,128)}, f32[2,5,64,1536]{3,2,1,0:T(8,128)}) custom-call(s32[6]{0:T(128)} %stack.40.place_ref, bf16[2,2,5,192,256]{4,3,2,1,0:T(8,128)(2,1)} %get-tuple-element.180.refs_4_.refs_0_, bf16[2,5,192,256]{3,2,1,0:T(8,128)(2,1)} %get-tuple-element.187.refs_6_.refs_1_, ...), custom_call_target="tpu_custom_call" | custom-call | flops 1000000 | bytes 26000000 | tf_op jit(solution)/shard_map/pallas_call | solution.py:1890
  (147 shorter events, 46.3 us)
Async XLA Ops:
  12.7 48.0 %copy-start.22 = (bf16[320,1536]{1,0:T(8,128)(2,1)S(1)}, bf16[320,1536]{1,0:T(8,128)(2,1)}, u32[]{:S(2)}) copy-start(bf16[320,1536]{1,0:T(8,128)(2,1)} %get-tuple-element.142.refs_0_) | copy-start | bytes 2949124
  12.7 79.4 %collective-permute-start = (bf16[320,1536]{1,0:T(8,128)(2,1)}, bf16[320,1536]{1,0:T(8,128)(2,1)S(1)}, u32[]{:S(2)}, u32[]{:S(2)}) collective-permute-start(bf16[320,1536]{1,0:T(8,128)(2,1)} %get-tuple-element.142.refs_0_), channel_id=1, source_target_pairs={{0,2},{1,3},{2,0},{3,1},{4,6},{5,7},{6,4},{7,5},{8,10},{9,11},{10,... | collective-permute-start | bytes 2949128 | tf_op jit(solution)/shard_map/ppermute | solution.py:413
  60.7 31.4 %collective-permute-start.1 = (bf16[320,1536]{1,0:T(8,128)(2,1)S(1)}, bf16[320,1536]{1,0:T(8,128)(2,1)}, u32[]{:S(2)}, u32[]{:S(2)}) collective-permute-start(bf16[320,1536]{1,0:T(8,128)(2,1)S(1)} %copy-done.22), channel_id=1, source_target_pairs={{0,8},{4,12},{8,0},{12,4},{16,24},{20,28},{24,16},{28,20},{1,9},{5... | collective-permute-start | bytes 2949128 | tf_op jit(solution)/shard_map/ppermute | solution.py:413
  60.8 32.8 %copy-start.38 = (f32[1536]{0:T(1024)S(1)}, f32[1536]{0:T(1024)}, u32[]{:S(2)}) copy-start(f32[1536]{0:T(1024)} %param.20) | copy-start | bytes 18436
  60.8 30.6 %collective-permute-start.2 = (f32[1,40,320]{2,1,0:T(8,128)}, f32[1,40,320]{2,1,0:T(8,128)S(1)}, u32[]{:S(2)}, u32[]{:S(2)}) collective-permute-start(f32[1,40,320]{2,1,0:T(8,128)} %bitcast.92), channel_id=1, source_target_pairs={{0,2},{1,3},{2,0},{3,1},{4,6},{5,7},{6,4},{7,5},{8,10},{9,11},{10,... | collective-permute-start | bytes 153608 | tf_op jit(solution)/shard_map/ppermute | solution.py:413
  92.1 33.7 %collective-permute-start.3 = (bf16[320,1536]{1,0:T(8,128)(2,1)}, bf16[320,1536]{1,0:T(8,128)(2,1)}, u32[]{:S(2)}, u32[]{:S(2)}) collective-permute-start(bf16[320,1536]{1,0:T(8,128)(2,1)} %collective-permute-done.1.refs_2_), channel_id=1, source_target_pairs={{0,2},{1,3},{2,0},{3,1},{4,6},{5,7},{6,4},{7,5},{8,10},{9,11},{10,... | collective-permute-start | bytes 2949128 | tf_op jit(solution)/shard_map/ppermute | solution.py:413
  93.7 32.2 %copy-start.7 = (f32[1,1536]{1,0:T(1,128)}, f32[1,1536]{1,0:T(1,128)S(1)}, u32[]{:S(2)}) copy-start(f32[1,1536]{1,0:T(1,128)S(1)} %broadcast_in_dim.48.gain_ref) | copy-start | bytes 18436
  98.6 25.6 %collective-permute-start.4 = (f32[2,40,320]{2,1,0:T(8,128)}, f32[2,40,320]{2,1,0:T(8,128)S(1)}, u32[]{:S(2)}, u32[]{:S(2)}) collective-permute-start(f32[2,40,320]{2,1,0:T(8,128)} %pad_maximum_fusion.6), channel_id=1, source_target_pairs={{0,8},{4,12},{8,0},{12,4},{16,24},{20,28},{24,16},{28,20},{1,9},{5... | collective-permute-start | bytes 307208 | tf_op jit(solution)/shard_map/ppermute | solution.py:413
  218.9 49.4 %collective-permute-start.5 = (bf16[5,64,1536]{2,1,0:T(8,128)(2,1)}, bf16[5,64,1536]{2,1,0:T(8,128)(2,1)S(1)}, u32[]{:S(2)}, u32[]{:S(2)}) collective-permute-start(bf16[5,64,1536]{2,1,0:T(8,128)(2,1)} %get-tuple-element.164), channel_id=1, source_target_pairs={{0,4},{4,0},{8,12},{12,8},{16,20},{20,16},{24,28},{28,24},{1,5},{5... | collective-permute-start | bytes 2949128 | tf_op jit(solution)/shard_map/ppermute | solution.py:413
  220.4 47.9 %collective-permute-start.6 = (bf16[2,5,192,256]{3,2,1,0:T(8,128)(2,1)}, bf16[2,5,192,256]{3,2,1,0:T(8,128)(2,1)}, u32[]{:S(2)}, u32[]{:S(2)}) collective-permute-start(bf16[2,5,192,256]{3,2,1,0:T(8,128)(2,1)} %get-tuple-element.165), channel_id=1, source_target_pairs={{0,4},{4,0},{8,12},{12,8},{16,20},{20,16},{24,28},{28,24},{1,5},{5... | collective-permute-start | bytes 2949128 | tf_op jit(solution)/shard_map/ppermute | solution.py:413
  221.0 47.3 %collective-permute-start.7 = (bf16[2,5,192,256]{3,2,1,0:T(8,128)(2,1)}, bf16[2,5,192,256]{3,2,1,0:T(8,128)(2,1)S(1)}, u32[]{:S(2)}, u32[]{:S(2)}) collective-permute-start(bf16[2,5,192,256]{3,2,1,0:T(8,128)(2,1)} %get-tuple-element.166), channel_id=1, source_target_pairs={{0,16},{4,20},{8,24},{12,28},{16,0},{20,4},{24,8},{28,12},{1,17},{... | collective-permute-start | bytes 2949128 | tf_op jit(solution)/shard_map/ppermute | solution.py:413
  222.2 110.2 %collective-permute-start.8 = (bf16[5,64,1536]{2,1,0:T(8,128)(2,1)}, bf16[5,64,1536]{2,1,0:T(8,128)(2,1)S(1)}, u32[]{:S(2)}, u32[]{:S(2)}) collective-permute-start(bf16[5,64,1536]{2,1,0:T(8,128)(2,1)} %get-tuple-element.177), channel_id=1, source_target_pairs={{0,4},{4,0},{8,12},{12,8},{16,20},{20,16},{24,28},{28,24},{1,5},{5... | collective-permute-start | bytes 2949128 | tf_op jit(solution)/shard_map/ppermute | solution.py:413
  223.7 44.5 %copy-start.24 = (bf16[2,5,192,256]{3,2,1,0:T(8,128)(2,1)S(1)}, bf16[2,5,192,256]{3,2,1,0:T(8,128)(2,1)}, u32[]{:S(2)}) copy-start(bf16[2,5,192,256]{3,2,1,0:T(8,128)(2,1)} %get-tuple-element.169) | copy-start | bytes 2949124
  268.3 64.1 %copy-start.12 = (bf16[2,5,192,256]{3,2,1,0:T(8,128)(2,1)}, bf16[2,5,192,256]{3,2,1,0:T(8,128)(2,1)S(1)}, u32[]{:S(2)}) copy-start(bf16[2,5,192,256]{3,2,1,0:T(8,128)(2,1)S(1)} %collective-permute-done.7.refs_5_) | copy-start | bytes 2949124
  332.5 72.0 %collective-permute-start.9 = (bf16[2,5,192,256]{3,2,1,0:T(8,128)(2,1)}, bf16[2,5,192,256]{3,2,1,0:T(8,128)(2,1)S(1)}, u32[]{:S(2)}, u32[]{:S(2)}) collective-permute-start(bf16[2,5,192,256]{3,2,1,0:T(8,128)(2,1)} %get-tuple-element.179), channel_id=1, source_target_pairs={{0,4},{4,0},{8,12},{12,8},{16,20},{20,16},{24,28},{28,24},{1,5},{5... | collective-permute-start | bytes 2949128 | tf_op jit(solution)/shard_map/ppermute | solution.py:413
  334.5 70.0 %collective-permute-start.10 = (bf16[5,192,256]{2,1,0:T(8,128)(2,1)S(1)}, bf16[5,192,256]{2,1,0:T(8,128)(2,1)S(1)}, u32[]{:S(2)}, u32[]{:S(2)}) collective-permute-start(bf16[5,192,256]{2,1,0:T(8,128)(2,1)S(1)} %fusion.9), channel_id=1, source_target_pairs={{0,16},{4,20},{8,24},{12,28},{16,0},{20,4},{24,8},{28,12},{1,17},{... | collective-permute-start | bytes 1474568 | tf_op jit(solution)/shard_map/ppermute | solution.py:413
  350.0 54.5 %copy-start.13 = (bf16[2,5,192,256]{3,2,1,0:T(8,128)(2,1)S(1)}, bf16[2,5,192,256]{3,2,1,0:T(8,128)(2,1)}, u32[]{:S(2)}) copy-start(bf16[2,5,192,256]{3,2,1,0:T(8,128)(2,1)} %get-tuple-element.196.refs_3_) | copy-start | bytes 2949124
  407.3 45.2 %collective-permute-start.11 = (bf16[2,5,192,256]{3,2,1,0:T(8,128)(2,1)S(1)}, bf16[2,5,192,256]{3,2,1,0:T(8,128)(2,1)S(1)}, u32[]{:S(2)}, u32[]{:S(2)}) collective-permute-start(bf16[2,5,192,256]{3,2,1,0:T(8,128)(2,1)S(1)} %pad_maximum_fusion.1), channel_id=1, source_target_pairs={{0,16},{4,20},{8,24},{12,28},{16,0},{20,4},{24,8},{28,12},{1,17},{... | collective-permute-start | bytes 2949128 | tf_op jit(solution)/shard_map/ppermute | solution.py:413
  407.4 45.2 %collective-permute-start.12 = (bf16[2,5,192,256]{3,2,1,0:T(8,128)(2,1)}, bf16[2,5,192,256]{3,2,1,0:T(8,128)(2,1)S(1)}, u32[]{:S(2)}, u32[]{:S(2)}) collective-permute-start(bf16[2,5,192,256]{3,2,1,0:T(8,128)(2,1)} %get-tuple-element.199), channel_id=1, source_target_pairs={{0,4},{4,0},{8,12},{12,8},{16,20},{20,16},{24,28},{28,24},{1,5},{5... | collective-permute-start | bytes 2949128 | tf_op jit(solution)/shard_map/ppermute | solution.py:413
  408.9 43.6 %collective-permute-start.13 = (bf16[5,64,1536]{2,1,0:T(8,128)(2,1)}, bf16[5,64,1536]{2,1,0:T(8,128)(2,1)S(1)}, u32[]{:S(2)}, u32[]{:S(2)}) collective-permute-start(bf16[5,64,1536]{2,1,0:T(8,128)(2,1)} %get-tuple-element.200), channel_id=1, source_target_pairs={{0,4},{4,0},{8,12},{12,8},{16,20},{20,16},{24,28},{28,24},{1,5},{5... | collective-permute-start | bytes 2949128 | tf_op jit(solution)/shard_map/ppermute | solution.py:413
  454.2 83.1 %copy-start.8 = (bf16[16,48,1536]{2,1,0:T(8,128)(2,1)S(1)}, bf16[16,48,1536]{2,1,0:T(8,128)(2,1)}, u32[]{:S(2)}) copy-start(bf16[16,48,1536]{2,1,0:T(8,128)(2,1)} %get-tuple-element.207) | copy-start | bytes 7077892
  541.0 94.5 %collective-permute-start.14 = (bf16[5,64,1536]{2,1,0:T(8,128)(2,1)}, bf16[5,64,1536]{2,1,0:T(8,128)(2,1)}, u32[]{:S(2)}, u32[]{:S(2)}) collective-permute-start(bf16[5,64,1536]{2,1,0:T(8,128)(2,1)} %fusion.1), channel_id=1, source_target_pairs={{0,16},{4,20},{8,24},{12,28},{16,0},{20,4},{24,8},{28,12},{1,17},{... | collective-permute-start | bytes 2949128 | tf_op jit(solution)/shard_map/ppermute | solution.py:413
  542.5 93.0 %collective-permute-start.15 = (bf16[5,64,1536]{2,1,0:T(8,128)(2,1)}, bf16[5,64,1536]{2,1,0:T(8,128)(2,1)}, u32[]{:S(2)}, u32[]{:S(2)}) collective-permute-start(bf16[5,64,1536]{2,1,0:T(8,128)(2,1)} %get-tuple-element.235), channel_id=1, source_target_pairs={{0,4},{4,0},{8,12},{12,8},{16,20},{20,16},{24,28},{28,24},{1,5},{5... | collective-permute-start | bytes 2949128 | tf_op jit(solution)/shard_map/ppermute | solution.py:413
  547.2 88.3 %collective-permute-start.16 = (bf16[2,5,192,256]{3,2,1,0:T(8,128)(2,1)}, bf16[2,5,192,256]{3,2,1,0:T(8,128)(2,1)}, u32[]{:S(2)}, u32[]{:S(2)}) collective-permute-start(bf16[2,5,192,256]{3,2,1,0:T(8,128)(2,1)} %pad_maximum_fusion.2), channel_id=1, source_target_pairs={{0,8},{4,12},{8,0},{12,4},{16,24},{20,28},{24,16},{28,20},{1,9},{5... | collective-permute-start | bytes 2949128 | tf_op jit(solution)/shard_map/ppermute | solution.py:413
  (32 other events, 205.3 us)
